TPU v7x, 32 devices: a whole 2x2x4 slice. The times are simulated.
32 devices in a mesh: dp: 4 (over y, x), ctx: 2 (over core), expert: 4 (over z).
Axes of the slice: x: 2, y: 2, z: 4, core: 2. Of those that a mesh axis runs over, the one named last changes fastest.
Arguments:
- tokens: bfloat16 [96, 200, 512], P(('dp', 'expert'), 'ctx'), may hold values from -6 to 6
- gain_one: float32 [512], replicated, may hold values from 0.1 to 1.9
- w_qkv: bfloat16 [512, 1536], replicated, may hold values from -0.25 to 0.25
- w_out: bfloat16 [512, 512], replicated, may hold values from -1 to 1
- gain_two: float32 [512], replicated, may hold values from 0.1 to 1.9
- w_router: bfloat16 [512, 4], replicated, may hold values from -0.1875 to 0.1875
- w_in: bfloat16 [4, 512, 2048], P('expert'), may hold values from -0.25 to 0.25
- w_back: bfloat16 [4, 2048, 512], P('expert'), may hold values from -0.25 to 0.25
- route_ids: int32 [16, 2, 6, 100, 2], P(('dp', 'expert'), 'ctx'), may hold values from 0 to 3, all different within a row; in each aligned block of 600 rows (0 to 599, 600 to 1199, ..., all dimensions but the last counted through in order) at most 600 rows name the same one
- key_mask: int32 [96, 200], P(('dp', 'expert')), may hold values from 0 to 1, as said below
- cotangent: bfloat16 [96, 200, 512], P(('dp', 'expert'), 'ctx'), may hold values from -6 to 6
Outputs:
- mixed: bfloat16 [96, 200, 512], P(('dp', 'expert'), 'ctx')
- grad_tokens: bfloat16 [96, 200, 512], P(('dp', 'expert'), 'ctx')
- grad_gain_one: float32 [512], replicated
- grad_qkv: float32 [512, 1536], replicated
- grad_out: float32 [512, 512], replicated
- grad_gain_two: float32 [512], replicated
- grad_router: float32 [512, 4], replicated
- grad_in: float32 [4, 512, 2048], P('expert')
- grad_back: float32 [4, 2048, 512], P('expert')
Inputs may be any that keep to these rules, and one draw needn't show every extreme that they name: Among the 600 tokens of one device (one aligned block of route_ids), at most 600 routes name the same expert, ; a token's two experts differ. `key_mask`: each image's mask is 1 on a first run of positions of length 150 to 200, then 0.
All inputs are finite; a program needn't handle non-finite values.
Results may differ from a plain program's by a relative error of at most 0.017.
Values may be sent and summed in bfloat16 or wider, within the bound.
No kernel may reach another device: no remote copies, remote signals or barrier semaphores. Data moves between devices by JAX's collectives and lax.ppermute only.
A program may use at most 192 MiB of HBM per device.

v0:
```python
import jax
import jax.numpy as jnp
from jax import lax
from jax.sharding import PartitionSpec as P

HEADS = 8
HEAD_DIM = 64
TOP = 2


def norm_rows(value, gain):
    center = value - jnp.mean(value, -1, keepdims=True)
    spread = jnp.mean(center * center, -1, keepdims=True)
    return center * lax.rsqrt(spread + 1e-06) * gain


def smooth_gelu(value):
    return 0.5 * value * (1.0 + jnp.tanh(0.7978845608 * (value + 0.044715 * value * value * value)))


def forward(tokens, gain_one, w_qkv, w_out, gain_two, w_router, w_in, w_back, flat_ids, live):
    nimg, half, width = tokens.shape
    count = nimg * half
    experts_all = w_router.shape[1]
    capacity = max(2, 2 * TOP * count // experts_all)
    x_rows = tokens.astype(jnp.float32).reshape(count, width)
    normed = norm_rows(x_rows, gain_one).astype(jnp.bfloat16)
    qkv = jnp.dot(normed, w_qkv, preferred_element_type=jnp.float32).astype(jnp.bfloat16)
    qkv = qkv.reshape(nimg, half, 3 * width)
    query = qkv[..., :width]
    keys_local = qkv[..., width : 2 * width]
    vals_local = qkv[..., 2 * width :]
    keys, vals = (
        lax.all_gather(keys_local, "ctx", axis=1, tiled=True),
        lax.all_gather(vals_local, "ctx", axis=1, tiled=True),
    )
    seq = keys.shape[1]
    query4 = query.reshape(nimg, half, HEADS, HEAD_DIM)
    keys4 = keys.reshape(nimg, seq, HEADS, HEAD_DIM)
    vals4 = vals.reshape(nimg, seq, HEADS, HEAD_DIM)
    scale = HEAD_DIM ** (-0.5)
    scores = (
        jnp.einsum("iqhc,ikhc->ihqk", query4, keys4, preferred_element_type=jnp.float32) * scale
    )
    open_keys = live[:, None, None, :]
    masked = jnp.where(open_keys, scores, -1000000000.0)
    topmost = jnp.max(masked, -1, keepdims=True)
    expo = jnp.where(open_keys, jnp.exp(masked - topmost), 0.0)
    probs = expo / jnp.sum(expo, -1, keepdims=True)
    probs_low = probs.astype(jnp.bfloat16)
    mix = jnp.einsum("ihqk,ikhc->iqhc", probs_low, vals4, preferred_element_type=jnp.float32)
    mix = mix.reshape(count, width).astype(jnp.bfloat16)
    mid = x_rows + jnp.dot(mix, w_out, preferred_element_type=jnp.float32)
    routed = norm_rows(mid, gain_two).astype(jnp.bfloat16)
    logits = jnp.dot(routed, w_router, preferred_element_type=jnp.float32)
    pick = flat_ids[:, :, None] == jnp.arange(experts_all, dtype=jnp.int32)[None, None, :]
    chosen = jnp.sum(jnp.where(pick, logits[:, None, :], 0.0), -1)
    expo_gate = jnp.exp(chosen)
    gates = expo_gate / jnp.sum(expo_gate, -1, keepdims=True)
    pair_ids = flat_ids.reshape(-1)
    hits = (pair_ids[:, None] == jnp.arange(experts_all, dtype=jnp.int32)[None, :]).astype(
        jnp.int32
    )
    before = jnp.cumsum(hits, 0) - hits
    slots = jnp.sum(before * hits, 1)
    where_rows = pair_ids * capacity + slots
    sent = jnp.repeat(routed, TOP, axis=0)
    buffer = jnp.zeros((experts_all * capacity, width), jnp.bfloat16).at[where_rows].set(sent)
    buffer = buffer.reshape(experts_all, capacity, width)
    arrived = lax.all_to_all(buffer, "expert", split_axis=0, concat_axis=1, tiled=True)
    pre = jnp.einsum("erd,edf->erf", arrived, w_in, preferred_element_type=jnp.float32)
    act = smooth_gelu(pre).astype(jnp.bfloat16)
    made = jnp.einsum("erf,efd->erd", act, w_back, preferred_element_type=jnp.float32).astype(
        jnp.bfloat16
    )
    returned = lax.all_to_all(made, "expert", split_axis=1, concat_axis=0, tiled=True)
    picked = returned.reshape(experts_all * capacity, width)[where_rows].reshape(count, TOP, width)
    output = mid + jnp.sum(gates[:, :, None] * picked.astype(jnp.float32), 1)
    return (
        x_rows,
        normed,
        query4,
        keys4,
        vals4,
        probs,
        probs_low,
        mix,
        mid,
        routed,
        pick,
        gates,
        where_rows,
        arrived,
        pre,
        act,
        picked,
        output,
        capacity,
    )


def shards(
    tokens, gain_one, w_qkv, w_out, gain_two, w_router, w_in, w_back, route_ids, key_mask, cotangent
):
    nimg, half, width = tokens.shape
    count = nimg * half
    experts_all = w_router.shape[1]
    flat_ids = route_ids.reshape(count, TOP)
    live = key_mask > 0
    state = forward(
        tokens, gain_one, w_qkv, w_out, gain_two, w_router, w_in, w_back, flat_ids, live
    )
    mixed = state[17].reshape(nimg, half, width).astype(jnp.bfloat16)
    state = forward(
        tokens, gain_one, w_qkv, w_out, gain_two, w_router, w_in, w_back, flat_ids, live
    )
    (
        x_rows,
        normed,
        query4,
        keys4,
        vals4,
        probs,
        probs_low,
        mix,
        mid,
        routed,
        pick,
        gates,
        where_rows,
        arrived,
        pre,
        act,
        picked,
        output,
        capacity,
    ) = state
    scale = HEAD_DIM ** (-0.5)
    high = lax.Precision.HIGHEST
    grad_y = cotangent.astype(jnp.float32).reshape(count, width)
    grad_gate = jnp.sum(grad_y[:, None, :] * picked.astype(jnp.float32), -1)
    d_out = (
        (gates[:, :, None] * grad_y[:, None, :]).astype(jnp.bfloat16).reshape(count * TOP, width)
    )
    grad_buffer = jnp.zeros((experts_all * capacity, width), jnp.bfloat16).at[where_rows].set(d_out)
    grad_buffer = grad_buffer.reshape(experts_all, capacity, width)
    grad_arrived = lax.all_to_all(grad_buffer, "expert", split_axis=0, concat_axis=1, tiled=True)
    d_act = jnp.einsum("erd,efd->erf", grad_arrived, w_back, preferred_element_type=jnp.float32)
    grad_back = jnp.einsum("erf,erd->efd", act, grad_arrived, preferred_element_type=jnp.float32)
    _, gelu_pull = jax.vjp(smooth_gelu, pre)
    d_pre = gelu_pull(d_act)[0].astype(jnp.bfloat16)
    grad_in = jnp.einsum("erd,erf->edf", arrived, d_pre, preferred_element_type=jnp.float32)
    d_in = jnp.einsum("erf,edf->erd", d_pre, w_in, preferred_element_type=jnp.float32).astype(
        jnp.bfloat16
    )
    grad_returned = lax.all_to_all(d_in, "expert", split_axis=1, concat_axis=0, tiled=True)
    grad_rows = grad_returned.reshape(experts_all * capacity, width)[where_rows].reshape(
        count, TOP, width
    )
    d_experts = jnp.sum(grad_rows.astype(jnp.float32), 1)
    d_chosen = gates * (grad_gate - jnp.sum(gates * grad_gate, -1, keepdims=True))
    d_logits = jnp.sum(jnp.where(pick, d_chosen[:, :, None], 0.0), 1)
    grad_router = jnp.dot(routed.astype(jnp.float32).T, d_logits, precision=high)
    d_routed = d_experts + jnp.dot(d_logits, w_router.astype(jnp.float32).T, precision=high)
    _, norm_two_pull = jax.vjp(norm_rows, mid, gain_two)
    d_mid_norm, grad_gain_two = norm_two_pull(d_routed)
    d_mid = grad_y + d_mid_norm
    d_branch = d_mid.astype(jnp.bfloat16)
    grad_out = jnp.einsum("td,te->de", mix, d_branch, preferred_element_type=jnp.float32)
    d_mix = jnp.dot(d_branch, w_out.T, preferred_element_type=jnp.float32).astype(jnp.bfloat16)
    d_mix4 = d_mix.reshape(nimg, half, HEADS, HEAD_DIM)
    d_probs = jnp.einsum("iqhc,ikhc->ihqk", d_mix4, vals4, preferred_element_type=jnp.float32)
    d_scores = (probs * (d_probs - jnp.sum(probs * d_probs, -1, keepdims=True))).astype(
        jnp.bfloat16
    )
    d_query = (
        jnp.einsum("ihqk,ikhc->iqhc", d_scores, keys4, preferred_element_type=jnp.float32) * scale
    )
    d_keys = (
        jnp.einsum("ihqk,iqhc->ikhc", d_scores, query4, preferred_element_type=jnp.float32) * scale
    )
    d_vals = jnp.einsum("ihqk,iqhc->ikhc", probs_low, d_mix4, preferred_element_type=jnp.float32)
    seq = keys4.shape[1]
    d_keys_own, d_vals_own = (
        lax.psum_scatter(
            d_keys.reshape(nimg, seq, width).astype(jnp.bfloat16),
            "ctx",
            scatter_dimension=1,
            tiled=True,
        ).astype(jnp.float32),
        lax.psum_scatter(
            d_vals.reshape(nimg, seq, width).astype(jnp.bfloat16),
            "ctx",
            scatter_dimension=1,
            tiled=True,
        ).astype(jnp.float32),
    )
    d_qkv = jnp.concatenate(
        [
            d_query.reshape(count, width).astype(jnp.bfloat16),
            d_keys_own.reshape(count, width).astype(jnp.bfloat16),
            d_vals_own.reshape(count, width).astype(jnp.bfloat16),
        ],
        axis=1,
    )
    grad_qkv = jnp.einsum("td,te->de", normed, d_qkv, preferred_element_type=jnp.float32)
    d_normed = jnp.dot(d_qkv, w_qkv.T, preferred_element_type=jnp.float32)
    _, norm_one_pull = jax.vjp(norm_rows, x_rows, gain_one)
    d_x_norm, grad_gain_one = norm_one_pull(d_normed)
    grad_tokens = (d_mid + d_x_norm).reshape(nimg, half, width).astype(jnp.bfloat16)
    grad_gain_one, grad_qkv, grad_out, grad_gain_two, grad_router = lax.psum(
        (grad_gain_one, grad_qkv, grad_out, grad_gain_two, grad_router), ("dp", "ctx", "expert")
    )
    grad_in, grad_back = (
        lax.psum(grad_in.astype(jnp.bfloat16), ("dp", "ctx")).astype(jnp.float32),
        lax.psum(grad_back.astype(jnp.bfloat16), ("dp", "ctx")).astype(jnp.float32),
    )
    return (
        mixed,
        grad_tokens,
        grad_gain_one,
        grad_qkv,
        grad_out,
        grad_gain_two,
        grad_router,
        grad_in,
        grad_back,
    )


def solution(mesh):
    placed = (
        P(("dp", "expert"), "ctx", None),
        P(),
        P(),
        P(),
        P(),
        P(),
        P("expert", None, None),
        P("expert", None, None),
        P(("dp", "expert"), "ctx", None, None, None),
        P(("dp", "expert"), None),
        P(("dp", "expert"), "ctx", None),
    )
    return jax.shard_map(
        shards,
        mesh=mesh,
        in_specs=placed,
        out_specs=(
            P(("dp", "expert"), "ctx", None),
            P(("dp", "expert"), "ctx", None),
            P(),
            P(),
            P(),
            P(),
            P(),
            P("expert", None, None),
            P("expert", None, None),
        ),
        check_vma=False,
    )
```

profile of v0, /device:TPU:0, one launch (start us, length us, event | category | flops | bytes accessed | tf_op | source)
XLA Modules:
  0.0 712.0 jit_solution(9703908839708034771)
XLA Ops:
  12.5 3.8 convolution_convert_fusion.2
  16.4 3.7 reshape.366
  31.4 4.4 mul.324
  35.8 4.0 copy.110
  39.9 6.3 fusion.48
  48.7 4.0 copy.107
  52.7 3.9 fusion.22
  64.7 14.4 %scatter_custom_fusion.1 = bf16[2400,512]{1,0:T(8,128)(2,1)} fusion(s32[1200]{0:T(1024)S(1)} %fusion.39, f32[1200,512]{1,0:T(8,128)} %mul.324, f32[1200]{0:T(1024)S(1)} %div.90, bf16[]{:T(256)} %constant.40.clone.1), kind=kCustom, calls=%fused_computation.58 | custom fusion | flops 1228800 | bytes 4923394 | tf_op jit(solution)/shard_map/scatter | solution.py:145
  79.1 4.8 all-to-all-start.2
  85.6 3.9 reshape.409
  89.5 10.2 %scatter_custom_fusion = bf16[2400,512]{1,0:T(8,128)(2,1)} fusion(s32[1200]{0:T(1024)S(1)} %fusion.39, bf16[1200,512]{1,0:T(8,128)(2,1)} %reshape.409, bf16[]{:T(256)} %constant.40.clone.1), kind=kCustom, calls=%fused_computation.68 | custom fusion | bytes 2458112 | tf_op jit(solution)/shard_map/scatter | solution.py:68
  99.7 40.7 %all-to-all-done.2 = bf16[4,600,512]{2,1,0:T(8,128)(2,1)} async-done(((bf16[4,600,512]{2,1,0:T(8,128)(2,1)}), bf16[4,600,512]{2,1,0:T(8,128)(2,1)}, u32[]{:S(2)}, u32[]{:S(2)}) %all-to-all-start.2) | async-done | bytes 2457632 | tf_op jit(solution)/shard_map/all_to_all | solution.py:147
  140.4 5.0 all-to-all-start
  145.4 11.4 %fusion.15 = f32[2400,2048]{1,0:T(8,128)} fusion(bf16[2400,512]{1,0:T(8,128)(2,1)} %bitcast.11, bf16[1,2048,512]{2,1,0:T(8,128)(2,1)} %param.18), kind=kOutput, calls=%fused_computation.40 | convolution fusion | flops 5033164800 | bytes 24215552 | tf_op jit(solution)/shard_map/erd,efd->erf/dot_general | solution.py:148
  156.8 44.2 %all-to-all-done = bf16[4,600,512]{2,1,0:T(8,128)(2,1)} async-done(((bf16[4,600,512]{2,1,0:T(8,128)(2,1)}), bf16[4,600,512]{2,1,0:T(8,128)(2,1)}, u32[]{:S(2)}, u32[]{:S(2)}) %all-to-all-start) | async-done | bytes 2457632 | tf_op jit(solution)/shard_map/all_to_all | solution.py:70
  201.0 24.4 %fusion.4 = (bf16[2400,2048]{1,0:T(8,128)(2,1)}, bf16[2400,2048]{1,0:T(8,128)(2,1)S(1)}) fusion(f32[2400,2048]{1,0:T(8,128)} %fusion.15, bf16[2400,512]{1,0:T(8,128)(2,1)} %bitcast.6, bf16[1,512,2048]{2,1,0:T(8,128)(2,1)S(1)} %copy-done), kind=kOutput, calls=%fused_computation.12 | convolution fusion | flops 5160960000 | bytes 43876352 | tf_op jit(solution)/shard_map/erd,edf->erf/dot_general | solution.py:71
  225.4 5.5 fusion.7
  230.9 21.7 %copy.149 = bf16[1,2400,512]{2,0,1:T(2,128)(2,1)} copy(bf16[1,2400,512]{2,1,0:T(8,128)(2,1)S(1)} %fusion.7) | data formatting | bytes 4915200 | tf_op jit(solution)/shard_map/convert_element_type | solution.py:73
  253.1 17.7 %reduce.11 = bf16[2400,512]{1,0:T(8,128)(2,1)} reduce(bf16[2400,1,512]{2,1,0:T(2,128)(2,1)} %bitcast.107, bf16[]{:T(256)} %broadcast.269), dimensions={1}, to_apply=%bitcast.101.reduce_sub_computation | reduce | bytes 4915202
  270.9 4.3 reshape.434
  275.2 4.7 all-to-all-start.1
  279.9 9.4 %fusion.8 = bf16[1,2400,512]{2,1,0:T(8,128)(2,1)S(1)} fusion(bf16[2400,2048]{1,0:T(8,128)(2,1)} %get-tuple-element.28, bf16[1,512,2048]{2,1,0:T(8,128)(2,1)S(1)} %copy-done), kind=kOutput, calls=%fused_computation.23 | convolution fusion | flops 5034393600 | bytes 14385152 | tf_op jit(solution)/shard_map/erf,edf->erd/dot_general | solution.py:153
  289.3 21.7 %copy.148 = bf16[1,2400,512]{2,0,1:T(2,128)(2,1)} copy(bf16[1,2400,512]{2,1,0:T(8,128)(2,1)S(1)} %fusion.8) | data formatting | bytes 4915200 | tf_op jit(solution)/shard_map/convert_element_type | solution.py:153
  310.9 16.3 %reduce.10 = bf16[2400,512]{1,0:T(8,128)(2,1)S(1)} reduce(bf16[2400,1,512]{2,1,0:T(2,128)(2,1)} %bitcast.108, bf16[]{:T(256)} %broadcast.269), dimensions={1}, to_apply=%bitcast.100.reduce_sub_computation | reduce | bytes 4915202
  329.6 5.7 all-to-all-done.1
  335.4 4.5 all-to-all-start.3
  340.0 5.5 reshape.435
  345.5 3.1 copy.146
  348.6 4.7 gather_fusion
  353.3 4.0 reshape.385
  357.3 7.2 %multiply_reduce_fusion.1 = (f32[600,2]{1,0:T(8,128)S(1)}, f32[600,512]{1,0:T(8,128)}) fusion(f32[600,2,512]{2,1,0:T(2,128)} %reshape.385, f32[600,512]{1,0:T(8,128)S(1)} %copy-done.5, f32[600,2]{1,0:T(8,128)S(1)} %copy.113), kind=kLoop, calls=%fused_computation.33 | loop fusion | flops 2149200 | bytes 4924800 | tf_op jit(solution)/shard_map/reduce_sum | solution.py:141
  364.7 30.7 %all-to-all-done.3 = bf16[4,2,153600]{2,1,0:T(2,128)(2,1)} async-done(((bf16[4,2,153600]{2,1,0:T(2,128)(2,1)}), bf16[4,2,153600]{2,1,0:T(2,128)(2,1)}, u32[]{:S(2)}, u32[]{:S(2)}) %all-to-all-start.3) | async-done | bytes 2457632 | tf_op jit(solution)/shard_map/all_to_all | solution.py:156
  395.4 5.3 reshape.437
  400.7 3.1 copy.145
  403.8 4.7 gather_fusion.1
  408.5 4.3 reshape.388
  412.8 4.7 reduce_sum.196
  423.5 4.5 multiply_reduce_fusion
  430.9 3.7 multiply_convert_fusion.1
  442.5 10.1 %fusion.10 = bf16[1,512,2048]{2,1,0:T(8,128)(2,1)} fusion(bf16[2400,512]{1,0:T(8,128)(2,1)} %bitcast.6, bf16[2400,2048]{1,0:T(8,128)(2,1)} %get-tuple-element.28), kind=kOutput, calls=%fused_computation.29 | convolution fusion | flops 5034213376 | bytes 14385152 | tf_op jit(solution)/shard_map/erd,erf->edf/dot_general | solution.py:152
  452.6 10.0 %fusion.11 = bf16[1,2048,512]{2,1,0:T(8,128)(2,1)} fusion(bf16[2400,2048]{1,0:T(8,128)(2,1)} %copy-done.36, bf16[2400,512]{1,0:T(8,128)(2,1)} %bitcast.11), kind=kOutput, calls=%fused_computation.30 | convolution fusion | flops 5034213376 | bytes 14385152 | tf_op jit(solution)/shard_map/erf,erd->efd/dot_general | solution.py:149
  477.9 4.9 fusion.30
  482.8 67.8 %all-reduce.13.cloned.1.call-done = (bf16[1,512,2048]{2,1,0:T(8,128)(2,1)}, bf16[1,2048,512]{2,1,0:T(8,128)(2,1)}) async-done(((bf16[1,512,2048]{2,1,0:T(8,128)(2,1)}, bf16[1,2048,512]{2,1,0:T(8,128)(2,1)}), (bf16[1,512,2048]{2,1,0:T(8,128)(2,1)}, bf16[1,2048,512]{2,1,0:T(8,128)(2,1)})) %all-reduce.13.cloned.1.call-update) | async-done | bytes 4194320 | tf_op jit(solution)/shard_map/psum | solution.py:215
  550.6 4.3 convert_element_type.197
  559.9 3.5 multiply_reduce_fusion.5
  565.1 39.9 %all-reduce.3 = (f32[512]{0:T(512)}, f32[512]{0:T(512)}, f32[512,4]{0,1:T(4,128)}) all-reduce(f32[512]{0:T(512)S(1)} %get-tuple-element.11, f32[512]{0:T(512)S(1)} %get-tuple-element.9, f32[512,4]{0,1:T(4,128)S(1)} %fusion.51), channel_id=1, replica_groups=mesh['dp'=4,'ctx'=2,'expert'=4] {'dp','ctx','expert'}, use_global_device_ids=true, to_apply=%region_26.27 | all-reduce | flops 3072 | bytes 24576 | tf_op jit(solution)/shard_map/psum | solution.py:211
  605.0 95.4 %all-reduce.11.cloned.1.call-done = (f32[512,1536]{1,0:T(8,128)}, f32[512,512]{1,0:T(8,128)}) async-done(((f32[512,1536]{1,0:T(8,128)}, f32[512,512]{1,0:T(8,128)}), (f32[512,1536]{1,0:T(8,128)}, f32[512,512]{1,0:T(8,128)})) %all-reduce.11.cloned.1.call-update) | async-done | bytes 4194320 | tf_op jit(solution)/shard_map/psum | solution.py:211
  700.4 3.9 copy.156
  (176 shorter events, 70.7 us)
Async XLA Ops:
  7.2 193.8 %copy-start = (bf16[1,512,2048]{2,1,0:T(8,128)(2,1)S(1)}, bf16[1,512,2048]{2,1,0:T(8,128)(2,1)}, u32[]{:S(2)}) copy-start(bf16[1,512,2048]{2,1,0:T(8,128)(2,1)} %param.17) | copy-start | bytes 6291460
  7.2 5.3 copy-start.32
  7.2 28.6 %all-gather.5.cloned.1.call-start = ((), (), s32[]{:S(2)}) async-start(), calls=%async_computation.5 | async-start | bytes 2457600 | tf_op jit(solution)/shard_map/all_gather | solution.py:34
  9.8 6.5 copy-start.9
  11.8 4.5 copy-start.26
  11.9 4.5 copy-start.23
  11.9 0.6 copy-start.28
  21.6 2.4 copy-start.22
  22.8 26.0 %all-gather.3.cloned.1.call-start = ((), (), s32[]{:S(2)}) async-start(), calls=%async_computation.4 | async-start | bytes 2457600 | tf_op jit(solution)/shard_map/all_gather | solution.py:35
  29.1 6.6 copy-start.4
  31.4 4.4 copy-start.31
  35.7 4.1 copy-start.16
  56.7 4.1 copy-start.10
  60.7 2.9 copy-start.25
  62.6 1.1 copy-start.2
  62.6 1.3 copy-start.30
  63.9 20.0 %copy-start.12 = (bf16[600,512]{1,0:T(8,128)(2,1)}, bf16[600,512]{1,0:T(8,128)(2,1)S(1)}, u32[]{:S(2)}) copy-start(bf16[600,512]{1,0:T(8,128)(2,1)S(1)} %multiply_convert_fusion.6) | copy-start | bytes 1843204
  79.1 61.3 %all-to-all-start.2 = ((bf16[4,600,512]{2,1,0:T(8,128)(2,1)}), bf16[4,600,512]{2,1,0:T(8,128)(2,1)}, u32[]{:S(2)}, u32[]{:S(2)}) async-start(bf16[4,600,512]{2,1,0:T(8,128)(2,1)} %bitcast.109), calls=%async_computation.2 | async-start | bytes 4915200 | tf_op jit(solution)/shard_map/all_to_all | solution.py:147
  140.4 60.6 %all-to-all-start = ((bf16[4,600,512]{2,1,0:T(8,128)(2,1)}), bf16[4,600,512]{2,1,0:T(8,128)(2,1)}, u32[]{:S(2)}, u32[]{:S(2)}) async-start(bf16[4,600,512]{2,1,0:T(8,128)(2,1)} %bitcast.110), calls=%async_computation | async-start | bytes 4915200 | tf_op jit(solution)/shard_map/all_to_all | solution.py:70
  201.0 24.4 %copy-start.34 = (bf16[1,2048,512]{2,1,0:T(8,128)(2,1)S(1)}, bf16[1,2048,512]{2,1,0:T(8,128)(2,1)}, u32[]{:S(2)}) copy-start(bf16[1,2048,512]{2,1,0:T(8,128)(2,1)} %param.18) | copy-start | bytes 6291460
  225.4 5.5 copy-start.36
  275.2 60.2 %all-to-all-start.1 = ((bf16[4,2,153600]{2,1,0:T(2,128)(2,1)}), bf16[4,2,153600]{2,1,0:T(2,128)(2,1)}, u32[]{:S(2)}, u32[]{:S(2)}) async-start(bf16[4,2,153600]{2,1,0:T(2,128)(2,1)} %reshape.434), calls=%async_computation.1 | async-start | bytes 4915200 | tf_op jit(solution)/shard_map/all_to_all | solution.py:76
  335.4 60.0 %all-to-all-start.3 = ((bf16[4,2,153600]{2,1,0:T(2,128)(2,1)}), bf16[4,2,153600]{2,1,0:T(2,128)(2,1)}, u32[]{:S(2)}, u32[]{:S(2)}) async-start(bf16[4,2,153600]{2,1,0:T(2,128)(2,1)} %reshape.436), calls=%async_computation.3 | async-start | bytes 4915200 | tf_op jit(solution)/shard_map/all_to_all | solution.py:156
  339.9 130.7 %all-reduce.15.cloned.1.call-start = ((), (), s32[]{:S(2)}) async-start(), calls=%async_computation.8 | async-start | bytes 4915200
  353.3 4.0 copy-start.5
  412.8 4.7 copy-start.3
  417.5 1.3 copy-start.15
  418.8 1.4 copy-start.6
  420.2 1.3 copy-start.19
  420.4 1.1 copy-start.7
  421.5 6.6 slice-start
  423.5 4.6 slice-start.1
  430.9 3.7 copy-start.17
  442.4 108.2 %all-reduce.13.cloned.1.call-start = ((), (), s32[]{:S(2)}) async-start(), calls=%async_computation.7 | async-start | bytes 8388608 | tf_op jit(solution)/shard_map/psum | solution.py:215
  462.6 0.7 copy-start.35
  462.6 237.8 %all-reduce.11.cloned.1.call-start = ((), (), s32[]{:S(2)}) async-start(), calls=%async_computation.6 | async-start | bytes 8388608 | tf_op jit(solution)/shard_map/psum | solution.py:211
  466.9 2.2 copy-start.8
  466.9 2.2 copy-start.14
  473.2 4.6 copy-start.11
  473.2 4.6 copy-start.27
  473.2 4.6 copy-start.29
  473.2 4.6 copy-start.33
  477.9 4.9 copy-start.21
  550.6 4.3 copy-start.18
  554.9 4.6 copy-start.13
  559.9 3.6 copy-start.24
  700.4 3.9 copy-start.20
  700.4 4.9 copy-start.1
Sparse Core Ops, SparseCore 0:
  22.9 12.5 all-gather.4
  37.6 11.0 all-gather.2
  442.5 21.3 all-reduce.14
  468.2 82.3 all-reduce.12
  557.7 142.5 all-reduce.10
where the time goes:
time: 716 us; the launch traced here: 712 us
  waiting for transfers between devices  287 us (40%)
  local copies, waits for them, and re-layouts  160 us (22%)
  matrix products  112 us (16%)
  other arithmetic  78.6 us (11%)
  blocking collectives  39.9 us (6%)
  starting transfers between devices  19.4 us (3%)
  between operations  15.3 us (2%)
    psum x1, waiting for transfers between devices, shards(): lax.psum((grad_gain_one, grad_qkv, grad_out, grad_gain_two, grad_router),...  95.4 us
    psum x1, waiting for transfers between devices, shards(): lax.psum(grad_in.astype(jnp.bfloat16), ('dp', 'ctx')).astype(jnp.float32)  67.8 us
    all_to_all x1, waiting for transfers between devices, forward(): lax.all_to_all(buffer, 'expert', split_axis=0, concat_axis=1, tiled=True)  44.2 us
    all_to_all x1, waiting for transfers between devices, shards(): lax.all_to_all(grad_buffer, 'expert', split_axis=0, concat_axis=1, tiled=...  40.7 us
    psum x1, blocking collectives, shards(): lax.psum((grad_gain_one, grad_qkv, grad_out, grad_gain_two, grad_router),...  39.9 us
    unnamed x94, local copies, waits for them, and re-layouts  36.9 us
    unnamed x4, other arithmetic  34.1 us
    all_to_all x1, waiting for transfers between devices, shards(): lax.all_to_all(d_in, 'expert', split_axis=1, concat_axis=0, tiled=True)  30.7 us
  transfers between devices with their start and end apart: 9, of which 7 were waited for; matrix products, arithmetic and copies ran while one was open for 25% of the time, Pallas kernels for 0%

commit v1 on v0

--- a/solution.py
+++ b/solution.py
@@ -1,11 +1,552 @@
+import functools
 import jax
 import jax.numpy as jnp
 from jax import lax
+from jax.experimental import pallas as pl
+from jax.experimental.pallas import tpu as pltpu
 from jax.sharding import PartitionSpec as P
 
 HEADS = 8
 HEAD_DIM = 64
 TOP = 2
+EPS = 1e-06
+SCALE = HEAD_DIM ** (-0.5)
+F32 = jnp.float32
+BF16 = jnp.bfloat16
+NT = (((1,), (1,)), ((), ()))
+TN = (((0,), (0,)), ((), ()))
+NN = (((1,), (0,)), ((), ()))
+
+
+def mm(a, b, dims=NN):
+    return lax.dot_general(a, b, dims, preferred_element_type=F32)
+
+
+def two_halves(a):
+    high = a.astype(BF16)
+    return high, (a - high.astype(F32)).astype(BF16)
+
+
+def stats(value):
+    center = value - jnp.mean(value, -1, keepdims=True)
+    rstd = lax.rsqrt(jnp.mean(center * center, -1, keepdims=True) + EPS)
+    return center * rstd, rstd
+
+
+def norm_vjp(d_value, unit, rstd, gain):
+    d_unit = d_value * gain
+    return rstd * (
+        d_unit
+        - jnp.mean(d_unit, -1, keepdims=True)
+        - unit * jnp.mean(d_unit * unit, -1, keepdims=True)
+    )
+
+
+def head_pair(value):
+    lane = lax.broadcasted_iota(jnp.int32, value.shape, 1)
+    first = lane < HEAD_DIM
+    return jnp.concatenate(
+        [jnp.where(first, value, 0.0), jnp.where(first, 0.0, value)], axis=0
+    ).astype(BF16)
+
+
+def join_pair(value):
+    rows = value.shape[0] // 2
+    lane = lax.broadcasted_iota(jnp.int32, (rows, value.shape[1]), 1)
+    return jnp.where(lane < HEAD_DIM, value[:rows], value[rows:])
+
+
+def attend_kernel(
+    own_ref, other_ref, open_ref, g1_ref, wqkv_ref, wout_ref, g2_ref,
+    x_ref, normed_ref, qkv_ref, probs_ref, mix_ref, mid_ref, routed_ref,
+    x_s, qkv_s, mix_s,
+):
+    half = own_ref.shape[1]
+    width = own_ref.shape[2]
+    pair = 2 * HEAD_DIM
+    x_s[0:half, :] = own_ref[0].astype(F32)
+    x_s[half : 2 * half, :] = other_ref[0].astype(F32)
+    x = x_s[...]
+    x_ref[...] = x.astype(BF16)
+    unit, _ = stats(x)
+    normed = (unit * g1_ref[...]).astype(BF16)
+    normed_ref[...] = normed
+    qkv_s[...] = mm(normed, wqkv_ref[...])
+    qkv_ref[...] = qkv_s[...].astype(BF16)
+    is_open = open_ref[0] > 0
+    for n in range(width // pair):
+        at = n * pair
+        query = head_pair(qkv_s[:, at : at + pair])
+        keys = qkv_s[:, width + at : width + at + pair].astype(BF16)
+        vals = qkv_s[:, 2 * width + at : 2 * width + at + pair].astype(BF16)
+        scores = jnp.where(is_open, mm(query, keys, NT) * SCALE, -1e9)
+        top = jnp.max(scores, -1, keepdims=True)
+        expo = jnp.where(is_open, jnp.exp(scores - top), 0.0)
+        probs = (expo / jnp.sum(expo, -1, keepdims=True)).astype(BF16)
+        probs_ref[0, n] = probs
+        mix_s[:, at : at + pair] = join_pair(mm(probs, vals))
+    mix = mix_s[...].astype(BF16)
+    mix_ref[...] = mix
+    mid = x + mm(mix, wout_ref[...])
+    mid_ref[...] = mid
+    unit, _ = stats(mid)
+    routed_ref[...] = (unit * g2_ref[...]).astype(BF16)
+
+
+def attend(own, other, is_open, g1, wqkv, wout, g2):
+    imgs, half, width = own.shape
+    seq = 2 * half
+    rows = imgs * seq
+    pairs = HEADS // 2
+    one = lambda *s: pl.BlockSpec(s, lambda i: (i,) + (0,) * (len(s) - 1))
+    fix = lambda *s: pl.BlockSpec(s, lambda i: (0,) * len(s))
+    return pl.pallas_call(
+        attend_kernel,
+        grid=(imgs,),
+        in_specs=[
+            one(1, half, width), one(1, half, width), one(1, 1, seq), fix(1, width),
+            fix(width, 3 * width), fix(width, width), fix(1, width),
+        ],
+        out_specs=[
+            one(seq, width), one(seq, width), one(seq, 3 * width), one(1, pairs, 2 * seq, seq),
+            one(seq, width), one(seq, width), one(seq, width),
+        ],
+        out_shape=[
+            jax.ShapeDtypeStruct((rows, width), BF16),
+            jax.ShapeDtypeStruct((rows, width), BF16),
+            jax.ShapeDtypeStruct((rows, 3 * width), BF16),
+            jax.ShapeDtypeStruct((imgs, pairs, 2 * seq, seq), BF16),
+            jax.ShapeDtypeStruct((rows, width), BF16),
+            jax.ShapeDtypeStruct((rows, width), F32),
+            jax.ShapeDtypeStruct((rows, width), BF16),
+        ],
+        scratch_shapes=[
+            pltpu.VMEM((seq, width), F32),
+            pltpu.VMEM((seq, 3 * width), F32),
+            pltpu.VMEM((seq, width), F32),
+        ],
+        compiler_params=pltpu.CompilerParams(vmem_limit_bytes=48 << 20),
+        name="attend",
+    )(own, other, is_open, g1, wqkv, wout, g2)
+
+
+def expert_kernel(
+    me_ref, rows_ref, dy_ref, ids_ref, wr_ref, win_ref, wback_ref,
+    act_ref, dpre_ref, dout_ref, made_ref, din_ref, gg_ref,
+    gate_s, made_s, din_s,
+):
+    step = pl.program_id(0)
+    rows = rows_ref[...]
+
+    @pl.when(step == 0)
+    def _():
+        logits = mm(rows, wr_ref[...])
+        lane = lax.broadcasted_iota(jnp.int32, logits.shape, 1)
+        pick = (lane == ids_ref[:, 0:1]) | (lane == ids_ref[:, 1:2])
+        top = jnp.max(jnp.where(pick, logits, -jnp.inf), -1, keepdims=True)
+        expo = jnp.where(pick, jnp.exp(logits - top), 0.0)
+        gates = expo / jnp.sum(expo, -1, keepdims=True)
+        gate = jnp.sum(jnp.where(lane == me_ref[0], gates, 0.0), -1, keepdims=True)
+        gate_s[...] = jnp.broadcast_to(gate, gate_s.shape)
+        dout_ref[...] = (gate * dy_ref[...].astype(F32)).astype(BF16)
+        made_s[...] = jnp.zeros_like(made_s)
+        din_s[...] = jnp.zeros_like(din_s)
+
+    w_in = win_ref[0]
+    w_back = wback_ref[0]
+    pre = mm(rows, w_in)
+    square = pre * pre
+    inner = 0.7978845608 * (pre + 0.044715 * square * pre)
+    th = jnp.tanh(inner)
+    up = 0.5 * (1.0 + th)
+    act = (pre * up).astype(BF16)
+    slope = up + 0.5 * pre * (1.0 - th * th) * (0.7978845608 * (1.0 + 0.134145 * square))
+    act_ref[...] = act
+    made_s[...] += mm(act, w_back)
+    dpre = (mm(dout_ref[...], w_back, NT) * slope).astype(BF16)
+    dpre_ref[...] = dpre
+    din_s[...] += mm(dpre, w_in, NT)
+
+    @pl.when(step == pl.num_programs(0) - 1)
+    def _():
+        gate = gate_s[:, 0:1]
+        made = made_s[...].astype(BF16).astype(F32)
+        made_ref[...] = (gate * made).astype(BF16)
+        din_ref[...] = din_s[...].astype(BF16)
+        high, low = two_halves(made * dy_ref[...].astype(F32))
+        ones = jnp.ones((16, made.shape[1]), BF16)
+        gg_ref[...] = (mm(ones, high, NT) + mm(ones, low, NT))[0:8]
+
+
+def expert(me, rows, dy, ids, wr, w_in, w_back):
+    count, width = rows.shape
+    hidden = w_in.shape[2]
+    steps = 4
+    part = hidden // steps
+    fix = lambda *s: pl.BlockSpec(s, lambda j, m: (0,) * len(s))
+    return pl.pallas_call(
+        expert_kernel,
+        grid_spec=pltpu.PrefetchScalarGridSpec(
+            num_scalar_prefetch=1,
+            grid=(steps,),
+            in_specs=[
+                fix(count, width), fix(count, width), fix(count, 2), fix(width, wr.shape[1]),
+                pl.BlockSpec((1, width, part), lambda j, m: (0, 0, j)),
+                pl.BlockSpec((1, part, width), lambda j, m: (0, j, 0)),
+            ],
+            out_specs=[
+                pl.BlockSpec((count, part), lambda j, m: (0, j)),
+                pl.BlockSpec((count, part), lambda j, m: (0, j)),
+                fix(count, width), fix(count, width), fix(count, width), fix(8, count),
+            ],
+            scratch_shapes=[
+                pltpu.VMEM((count, 128), F32),
+                pltpu.VMEM((count, width), F32),
+                pltpu.VMEM((count, width), F32),
+            ],
+        ),
+        out_shape=[
+            jax.ShapeDtypeStruct((count, hidden), BF16),
+            jax.ShapeDtypeStruct((count, hidden), BF16),
+            jax.ShapeDtypeStruct((count, width), BF16),
+            jax.ShapeDtypeStruct((count, width), BF16),
+            jax.ShapeDtypeStruct((count, width), BF16),
+            jax.ShapeDtypeStruct((8, count), F32),
+        ],
+        compiler_params=pltpu.CompilerParams(vmem_limit_bytes=48 << 20),
+        name="expert",
+    )(me, rows, dy, ids, wr, w_in, w_back)
+
+
+def weight_kernel(*refs):
+    n = (len(refs) - 2) // 4
+    rows, acts, dpres, douts = refs[:n], refs[n : 2 * n], refs[2 * n : 3 * n], refs[3 * n : 4 * n]
+    gin_ref, gback_ref = refs[4 * n :]
+    total = mm(rows[0][...], dpres[0][...], TN)
+    for b in range(1, n):
+        total += mm(rows[b][...], dpres[b][...], TN)
+    gin_ref[0] = total.astype(BF16)
+    total = mm(acts[0][...], douts[0][...], TN)
+    for b in range(1, n):
+        total += mm(acts[b][...], douts[b][...], TN)
+    gback_ref[0] = total.astype(BF16)
+
+
+def weight_grads(rows, acts, dpres, douts):
+    count, width = rows[0].shape
+    hidden = acts[0].shape[1]
+    n = len(rows)
+    steps = 8
+    part = hidden // steps
+    fix = pl.BlockSpec((count, width), lambda j: (0, 0))
+    cut = pl.BlockSpec((count, part), lambda j: (0, j))
+    return pl.pallas_call(
+        weight_kernel,
+        grid=(steps,),
+        in_specs=[fix] * n + [cut] * (2 * n) + [fix] * n,
+        out_specs=[
+            pl.BlockSpec((1, width, part), lambda j: (0, 0, j)),
+            pl.BlockSpec((1, part, width), lambda j: (0, j, 0)),
+        ],
+        out_shape=[
+            jax.ShapeDtypeStruct((1, width, hidden), BF16),
+            jax.ShapeDtypeStruct((1, hidden, width), BF16),
+        ],
+        compiler_params=pltpu.CompilerParams(vmem_limit_bytes=48 << 20),
+        name="weight_grads",
+    )(*rows, *acts, *dpres, *douts)
+
+
+def back_kernel(
+    me_ref, din0_ref, din1_ref, din2_ref, din3_ref, gg0_ref, gg1_ref, gg2_ref, gg3_ref,
+    ids_ref, dy_ref, mid_ref, routed_ref, wr_ref, g2_ref, mix_ref, wout_ref,
+    probs_ref, qkv_ref, x_ref, normed_ref, wqkv_ref, g1_ref,
+    own_ref, other_ref, grad_ref, small_ref,
+    dmid_s, dmix_s, dqkv_s, tok_s,
+):
+    step = pl.program_id(0)
+    imgs = pl.num_programs(0)
+    seq = qkv_ref.shape[0]
+    width = x_ref.shape[1]
+    half = seq // 2
+    pair = 2 * HEAD_DIM
+
+    @pl.when(step == 0)
+    def _():
+        routed = routed_ref[...]
+        logits = mm(wr_ref[...], routed, NT)
+        row = lax.broadcasted_iota(jnp.int32, logits.shape, 0)
+        pick = (row == ids_ref[0:1, :]) | (row == ids_ref[1:2, :])
+        top = jnp.max(jnp.where(pick, logits, -jnp.inf), 0, keepdims=True)
+        expo = jnp.where(pick, jnp.exp(logits - top), 0.0)
+        gates = expo / jnp.sum(expo, 0, keepdims=True)
+        me = me_ref[0]
+        d_gate = jnp.zeros_like(gates)
+        for k, ref in enumerate((gg0_ref, gg1_ref, gg2_ref, gg3_ref)):
+            there = me + k - 2 * (me & k)
+            part = jnp.concatenate([ref[...]] * (gates.shape[0] // 8), axis=0)
+            d_gate += jnp.where(row == there, part, 0.0)
+        d_logits = gates * (d_gate - jnp.sum(gates * d_gate, 0, keepdims=True))
+        high, low = two_halves(d_logits)
+        wr = wr_ref[...]
+        small_ref[0:16, :] = mm(high, routed) + mm(low, routed)
+        d_routed = (
+            din0_ref[...].astype(F32) + din1_ref[...].astype(F32)
+            + din2_ref[...].astype(F32) + din3_ref[...].astype(F32)
+            + mm(high, wr, TN) + mm(low, wr, TN)
+        )
+        unit, rstd = stats(mid_ref[...])
+        small_ref[16:17, :] = jnp.sum(d_routed * unit, 0, keepdims=True)
+        d_mid = dy_ref[...].astype(F32) + norm_vjp(d_routed, unit, rstd, g2_ref[...])
+        dmid_s[...] = d_mid
+        d_branch = d_mid.astype(BF16)
+        grad_ref[:, 3 * width :] = mm(mix_ref[...], d_branch, TN).astype(BF16)
+        dmix_s[...] = mm(d_branch, wout_ref[...], NT)
+
+    base = pl.multiple_of(step * seq, 8)
+    for n in range(width // pair):
+        at = n * pair
+        d_mix = head_pair(dmix_s[pl.ds(base, seq), at : at + pair])
+        query = head_pair(qkv_ref[:, at : at + pair].astype(F32))
+        keys = qkv_ref[:, width + at : width + at + pair]
+        vals = qkv_ref[:, 2 * width + at : 2 * width + at + pair]
+        low = probs_ref[0, n]
+        probs = low.astype(F32)
+        d_probs = mm(d_mix, vals, NT)
+        d_scores = probs * (d_probs - jnp.sum(probs * d_probs, -1, keepdims=True))
+        d_scores = d_scores.astype(BF16)
+        d_query = join_pair(mm(d_scores, keys)) * SCALE
+        d_keys = mm(d_scores, query, TN) * SCALE
+        d_vals = mm(low, d_mix, TN)
+        dqkv_s[pl.ds(base, seq), at : at + pair] = d_query.astype(BF16)
+        dqkv_s[pl.ds(base, seq), width + at : width + at + pair] = d_keys.astype(BF16)
+        dqkv_s[pl.ds(base, seq), 2 * width + at : 2 * width + at + pair] = d_vals.astype(BF16)
+
+    @pl.when(step == imgs - 1)
+    def _():
+        d_qkv = dqkv_s[...]
+        grad_ref[:, : 3 * width] = mm(normed_ref[...], d_qkv, TN).astype(BF16)
+        d_normed = mm(d_qkv, wqkv_ref[...], NT)
+        unit, rstd = stats(x_ref[...].astype(F32))
+        small_ref[17:18, :] = jnp.sum(d_normed * unit, 0, keepdims=True)
+        small_ref[18:24, :] = jnp.zeros((6, width), F32)
+        tok_s[...] = dmid_s[...] + norm_vjp(d_normed, unit, rstd, g1_ref[...])
+        for i in range(own_ref.shape[0]):
+            own_ref[i] = tok_s[i * seq : i * seq + half, :].astype(BF16)
+            other_ref[i] = tok_s[i * seq + half : (i + 1) * seq, :].astype(BF16)
+
+
+def attend_back(me, dins, ggs, ids, dy, mid, routed, wr, g2, mix, wout, probs, qkv, x, normed, wqkv, g1):
+    imgs = probs.shape[0]
+    rows, width = x.shape
+    seq = rows // imgs
+    pairs = HEADS // 2
+    fix = lambda *s: pl.BlockSpec(s, lambda i, m: (0,) * len(s))
+    return pl.pallas_call(
+        back_kernel,
+        grid_spec=pltpu.PrefetchScalarGridSpec(
+            num_scalar_prefetch=1,
+            grid=(imgs,),
+            in_specs=[fix(rows, width)] * 4 + [fix(8, rows)] * 4 + [
+                fix(2, rows), fix(rows, width), fix(rows, width), fix(rows, width),
+                fix(16, width), fix(1, width), fix(rows, width), fix(width, width),
+                pl.BlockSpec((1, pairs, 2 * seq, seq), lambda i, m: (i, 0, 0, 0)),
+                pl.BlockSpec((seq, 3 * width), lambda i, m: (i, 0)),
+                fix(rows, width), fix(rows, width), fix(width, 3 * width), fix(1, width),
+            ],
+            out_specs=[
+                fix(imgs, seq // 2, width), fix(imgs, seq // 2, width),
+                fix(width, 4 * width), fix(24, width),
+            ],
+            scratch_shapes=[
+                pltpu.VMEM((rows, width), F32),
+                pltpu.VMEM((rows, width), F32),
+                pltpu.VMEM((rows, 3 * width), BF16),
+                pltpu.VMEM((rows, width), F32),
+            ],
+        ),
+        out_shape=[
+            jax.ShapeDtypeStruct((imgs, seq // 2, width), BF16),
+            jax.ShapeDtypeStruct((imgs, seq // 2, width), BF16),
+            jax.ShapeDtypeStruct((width, 4 * width), BF16),
+            jax.ShapeDtypeStruct((24, width), F32),
+        ],
+        compiler_params=pltpu.CompilerParams(vmem_limit_bytes=56 << 20),
+        name="attend_back",
+    )(me, *dins, *ggs, ids, dy, mid, routed, wr, g2, mix, wout, probs, qkv, x, normed, wqkv, g1)
+
+
+def combine_kernel(mid_ref, a_ref, b_ref, c_ref, d_ref, own_ref, other_ref, s_ref):
+    half = own_ref.shape[1]
+    s_ref[...] = mid_ref[...] + (
+        a_ref[...].astype(F32) + b_ref[...].astype(F32)
+        + c_ref[...].astype(F32) + d_ref[...].astype(F32)
+    )
+    own_ref[0] = s_ref[0:half, :].astype(BF16)
+    other_ref[0] = s_ref[half : 2 * half, :].astype(BF16)
+
+
+def combine(mid, parts, imgs):
+    rows, width = mid.shape
+    seq = rows // imgs
+    spec = pl.BlockSpec((seq, width), lambda i: (i, 0))
+    out = pl.BlockSpec((1, seq // 2, width), lambda i: (i, 0, 0))
+    shape = jax.ShapeDtypeStruct((imgs, seq // 2, width), BF16)
+    return pl.pallas_call(
+        combine_kernel,
+        grid=(imgs,),
+        in_specs=[spec] * 5,
+        out_specs=[out, out],
+        out_shape=[shape, shape],
+        scratch_shapes=[pltpu.VMEM((seq, width), F32)],
+        name="combine",
+    )(mid, *parts)
+
+
+SWAP = [(0, 1), (1, 0)]
+
+
+def xor(k, n=4):
+    return [(i, i ^ k) for i in range(n)]
+
+
+def keep_give(value, index):
+    parts = value.shape[0] // 2
+    return (
+        lax.dynamic_slice_in_dim(value, index * parts, parts, 0),
+        lax.dynamic_slice_in_dim(value, (1 - index) * parts, parts, 0),
+    )
+
+
+def order_two(mine, theirs, index, axis=0):
+    return jnp.where(
+        index == 0,
+        jnp.concatenate([mine, theirs], axis),
+        jnp.concatenate([theirs, mine], axis),
+    )
+
+
+def send(value, axis, pairs):
+    return lax.ppermute(value, axis, pairs)
+
+
+def halve(value, index, axis, pairs):
+    mine, theirs = keep_give(value, index)
+    return mine + send(theirs.astype(BF16), axis, pairs).astype(F32)
+
+
+def reduce_shared(grads, small, core, y, x, z):
+    total = halve(grads.astype(F32), core, "ctx", SWAP)
+    cols = total.shape[1] // 2
+    a, b = total[:, :cols], total[:, cols:]
+    a = halve(a, x, "dp", xor(1))
+    b = halve(b, y, "dp", xor(2))
+    a = halve(a, y, "dp", xor(2))
+    b = halve(b, x, "dp", xor(1))
+    both = jnp.concatenate([a, b], 0)
+    rows = both.shape[0] // 4
+    piece = lambda k: lax.dynamic_slice_in_dim(both, (z ^ k) * rows, rows, 0)
+    mine = piece(0)
+    for k in (1, 2, 3):
+        mine = mine + send(piece(k).astype(BF16), "expert", xor(k)).astype(F32)
+    mine = mine.astype(BF16)
+    slots = jnp.stack([mine] + [send(mine, "expert", xor(k)) for k in (1, 2, 3)])
+    both = jnp.concatenate(
+        [lax.dynamic_slice_in_dim(slots, z ^ k, 1, 0)[0] for k in range(4)], 0
+    )
+    a, b = both[: 2 * rows], both[2 * rows :]
+    a = order_two(a, send(a, "dp", xor(2)), y)
+    b = order_two(b, send(b, "dp", xor(1)), x)
+    a = order_two(a, send(a, "dp", xor(1)), x)
+    b = order_two(b, send(b, "dp", xor(2)), y)
+    total = jnp.concatenate([a, b], 1)
+    total = order_two(total, send(total, "ctx", SWAP), core)
+    small = small + send(small, "ctx", SWAP)
+    small = small + send(small, "dp", xor(1))
+    small = small + send(small, "dp", xor(2))
+    small = small + send(small, "expert", xor(1))
+    small = small + send(small, "expert", xor(2))
+    return total.astype(F32), small
+
+
+def dense_shards(
+    tokens, gain_one, w_qkv, w_out, gain_two, w_router, w_in, w_back, route_ids, key_mask, cotangent
+):
+    nimg, half, width = tokens.shape
+    imgs = nimg // 2
+    rows = imgs * 2 * half
+    experts = w_router.shape[1]
+    core = lax.axis_index("ctx")
+    z = lax.axis_index("expert")
+    place = lax.axis_index("dp")
+    y, x = place // 2, place % 2
+
+    dy_own, dy_give = keep_give(cotangent, core)
+    tok_own, tok_give = keep_give(tokens, core)
+    ids = route_ids.reshape(nimg, half, TOP)
+    ids_own, ids_give = keep_give(ids, core)
+    dy_other = send(dy_give, "ctx", SWAP)
+    tok_other = send(tok_give, "ctx", SWAP)
+    ids_flat = lambda v: jnp.transpose(v, (2, 0, 1))
+    ids_other = send(ids_flat(ids_give), "ctx", SWAP)
+    dy = jnp.concatenate([dy_own, dy_other], 1).reshape(rows, width)
+    ids_row = jnp.concatenate([ids_flat(ids_own), ids_other], 2).reshape(TOP, rows)
+    ids_all = lax.all_gather(ids_row, "expert", axis=0)
+    ids_col = jnp.transpose(ids_all, (0, 2, 1))
+
+    def spread(value):
+        first = send(value, "expert", xor(1))
+        second = send(value, "expert", [(1, 2), (2, 1)])
+        inner = send(first, "expert", [(1, 2), (2, 1)])
+        outer = send(second, "expert", [(1, 0), (2, 3)])
+        far = send(first, "expert", [(2, 0), (1, 3)])
+        middle = (z == 1) | (z == 2)
+        return [
+            value,
+            first,
+            jnp.where(middle, inner, outer),
+            jnp.where(middle, second, far),
+        ]
+
+    dys = spread(dy)
+    mask = lax.dynamic_slice_in_dim(key_mask, core * imgs, imgs, 0)
+    is_open = order_two(mask[:, :half], mask[:, half:], core, 1)[:, None, :]
+    g1, g2 = gain_one[None, :], gain_two[None, :]
+    x_rows, normed, qkv, probs, mix, mid, routed = attend(
+        tok_own, tok_other, is_open, g1, w_qkv, w_out, g2
+    )
+    routeds = spread(routed)
+    me = z[None].astype(jnp.int32)
+    wr = jnp.pad(w_router, ((0, 0), (0, 128 - experts)))
+    wr_row = jnp.pad(w_router.T, ((0, 16 - experts), (0, 0)))
+    parts = []
+    for k in range(4):
+        ids_k = lax.dynamic_slice_in_dim(ids_col, z ^ k, 1, 0)[0]
+        parts.append(expert(me, routeds[k], dys[k], ids_k, wr, w_in, w_back))
+    acts, dpres, douts, mades, dins, ggs = zip(*parts)
+    back = lambda group: [group[0]] + [send(group[k], "expert", xor(k)) for k in (1, 2, 3)]
+    dins, ggs = back(dins), back(ggs)
+    grad_in, grad_back = weight_grads(routeds, acts, dpres, douts)
+    mades = back(mades)
+    tok_own, tok_give, shared, small = attend_back(
+        me, dins, ggs, ids_row, dy, mid, routed, wr_row, g2, mix, w_out, probs, qkv, x_rows, normed, w_qkv, g1
+    )
+    mix_own, mix_give = combine(mid, mades, imgs)
+    mixed = order_two(mix_own, send(mix_give, "ctx", SWAP), core)
+    grad_tokens = order_two(tok_own, send(tok_give, "ctx", SWAP), core)
+    shared, small = reduce_shared(shared, small, core, y, x, z)
+    grad_in, grad_back = lax.psum((grad_in, grad_back), ("dp", "ctx"))
+    return (
+        mixed,
+        grad_tokens,
+        small[17],
+        shared[:, : 3 * width],
+        shared[:, 3 * width :],
+        small[16],
+        small[:experts].T,
+        grad_in.astype(F32),
+        grad_back.astype(F32),
+    )
 
 
 def norm_rows(value, gain):
@@ -242,8 +783,10 @@
         P(("dp", "expert"), None),
         P(("dp", "expert"), "ctx", None),
     )
+    sizes = dict(mesh.shape)
+    dense = sizes == {"dp": 4, "ctx": 2, "expert": 4}
     return jax.shard_map(
-        shards,
+        dense_shards if dense else shards,
         mesh=mesh,
         in_specs=placed,
         out_specs=(

time: 716 us -> 370 us (0.52)
  waiting for transfers between devices: 287 us -> 101 us
  local copies, waits for them, and re-layouts: 160 us -> 34.3 us
  matrix products: 112 us -> 0 us
  Pallas kernels: 0 us -> 90.5 us
  other arithmetic: 78.6 us -> 32.8 us
  starting transfers between devices: 19.4 us -> 62.9 us
  blocking collectives: 39.9 us -> 32.2 us
    psum x2 -> x1, waiting for transfers between devices: 163 us -> 17.3 us  [dense_shards(): grad_in, grad_back = lax.psum((grad_in, grad_back), ('dp', 'ctx'))]
    all_to_all x4 -> x0, waiting for transfers between devices: 121 us -> none  [the longest x1 44.2 us: forward(): lax.all_to_all(buffer, 'expert', split_axis=0, concat_axis=1, tiled=True)]
    dot_general x20 -> x0, matrix products: 105 us -> none  [the longest x1 24.4 us: forward(): jnp.einsum('erd,edf->erf', arrived, w_in, preferred_element_type=jnp.floa...]
    pallas_call x0 -> x8, Pallas kernels: none -> 90.5 us  [the longest x4 43.6 us: expert(): pl.pallas_call(expert_kernel, grid_spec=pltpu.PrefetchScalarGridSpec(num_...]
    ppermute x0 -> x45, waiting for transfers between devices: none -> 83.6 us  [send(): return lax.ppermute(value, axis, pairs)]
    convert_element_type x16 -> x5, local copies, waits for them, and re-layouts: 71.3 us -> 1.07 us  [halve(): return mine + send(theirs.astype(BF16), axis, pairs).astype(F32)]
    ppermute x0 -> x45, starting transfers between devices: none -> 62.9 us  [send(): return lax.ppermute(value, axis, pairs)]
    psum x1 -> x0, blocking collectives: 39.9 us -> none  [shards(): lax.psum((grad_gain_one, grad_qkv, grad_out, grad_gain_two, grad_router),...]
  transfers between devices with their start and end apart: 9 -> 46, of which waited for: 7 -> 22; matrix products, arithmetic and copies ran while one was open for 25% -> 7% of each run, Pallas kernels for 0% -> 20%
where the time goes in v1:
time: 370 us; the launch traced here: 369 us
  waiting for transfers between devices  101 us (27%)
  Pallas kernels  90.5 us (24%)
  starting transfers between devices  62.9 us (17%)
  local copies, waits for them, and re-layouts  34.3 us (9%)
  other arithmetic  32.8 us (9%)
  blocking collectives  32.2 us (9%)
  between operations  14.8 us (4%)
    ppermute x45, waiting for transfers between devices, send(): return lax.ppermute(value, axis, pairs)  83.6 us
    ppermute x45, starting transfers between devices, send(): return lax.ppermute(value, axis, pairs)  62.9 us
    pallas_call x4, Pallas kernels, expert(): pl.pallas_call(expert_kernel, grid_spec=pltpu.PrefetchScalarGridSpec(num_...  43.6 us
    all_gather x1, blocking collectives, dense_shards(): ids_all = lax.all_gather(ids_row, 'expert', axis=0)  32.2 us
    unnamed x107, local copies, waits for them, and re-layouts  24.4 us
    pallas_call x1, Pallas kernels, weight_grads(): pl.pallas_call(weight_kernel, grid=(steps,), in_specs=[fix] * n + [cut] *...  17.5 us
    psum x1, waiting for transfers between devices, dense_shards(): grad_in, grad_back = lax.psum((grad_in, grad_back), ('dp', 'ctx'))  17.3 us
    pallas_call x1, Pallas kernels, attend_back(): pl.pallas_call(back_kernel, grid_spec=pltpu.PrefetchScalarGridSpec(num_sc...  17.2 us
  transfers between devices with their start and end apart: 46, of which 22 were waited for; matrix products, arithmetic and copies ran while one was open for 7% of the time, Pallas kernels for 20%

profile of v1, /device:TPU:0, one launch (start us, length us, event | category | flops | bytes accessed | tf_op | source)
XLA Modules:
  0.0 368.6 jit_solution(13649271398357074821)
XLA Ops:
  9.0 1.9 constant_dynamic-slice_fusion.8
  11.2 8.4 %attend.1 = (bf16[600,512]{1,0:T(8,128)(2,1)S(1)}, bf16[600,512]{1,0:T(8,128)(2,1)S(1)}, bf16[600,1536]{1,0:T(8,128)(2,1)}, bf16[3,4,400,200]{3,2,1,0:T(8,128)(2...) custom-call(bf16[3,100,512]{2,1,0:T(8,128)(2,1)S(1)} %get-tuple-element.94.own_ref, ...), custom_call_target="tpu_custom_call" | custom-call | tf_op jit(solution)/shard_map/attend/pallas_call | solution.py:103
  23.1 3.0 collective-permute-start.3
  29.5 3.6 collective-permute-start.4
  35.5 5.3 %collective-permute-done.3.rows_ref.refs_1_ = bf16[600,512]{1,0:T(8,128)(2,1)S(1)} collective-permute-done((bf16[600,512]{1,0:T(8,128)(2,1)S(1)}, bf16[600,512]{1,0:T(8,128)(2,1)S(1)}, u32[]{:S(2)}, u32[]{:S(2)}) %collective-permute-start.3) | collective-permute-done | bytes 614432 | tf_op jit(solution)/shard_map/ppermute | solution.py:430
  43.6 10.5 %collective-permute-done.4.dy_ref = bf16[600,512]{1,0:T(8,128)(2,1)} collective-permute-done((bf16[600,512]{1,0:T(8,128)(2,1)S(1)}, bf16[600,512]{1,0:T(8,128)(2,1)}, u32[]{:S(2)}, u32[]{:S(2)}) %collective-permute-start.4) | collective-permute-done | bytes 614432 | tf_op jit(solution)/shard_map/ppermute | solution.py:430
  58.3 32.2 %all_gather.3 = s32[4,2,600]{2,1,0:T(2,128)S(1)} all-gather(s32[1,2,600]{2,1,0:T(2,128)S(1)} %all_gather_reshape.3), channel_id=1, replica_groups=mesh['dp'=4,'ctx'=2,'expert'=4] {'expert'}, dimensions={0}, use_global_device_ids=true | all-gather | bytes 24000 | tf_op jit(solution)/shard_map/all_gather | solution.py:494
  93.8 11.1 %expert.5 = (bf16[600,2048]{1,0:T(8,128)(2,1)}, bf16[600,2048]{1,0:T(8,128)(2,1)}, bf16[600,512]{1,0:T(8,128)(2,1)S(1)}, bf16[600,512]{1,0:T(8,128)(2,1)S(1)}, b...) custom-call(s32[1]{0:T(128)} %bitcast.2.me_ref, bf16[600,512]{1,0:T(8,128)(2,1)S(1)} %collective-permute-done.3.rows_ref.refs_1_, ...), custom_call_target="tpu_custom_call" | custom-call | tf_op jit(solution)/shard_map/expert/pallas_call | solution.py:187
  104.9 3.2 collective-permute-start.17
  111.9 11.0 %expert.6 = (bf16[600,2048]{1,0:T(8,128)(2,1)}, bf16[600,2048]{1,0:T(8,128)(2,1)}, bf16[600,512]{1,0:T(8,128)(2,1)S(1)}, bf16[600,512]{1,0:T(8,128)(2,1)S(1)}, b...) custom-call(s32[1]{0:T(128)} %bitcast.2.me_ref, bf16[600,512]{1,0:T(8,128)(2,1)S(1)} %broadcast_select_fusion.3.rows_ref.refs_2_, ...), custom_call_target="tpu_custom_call" | custom-call | tf_op jit(solution)/shard_map/expert/pallas_call | solution.py:187
  123.0 3.6 collective-permute-start.18
  127.9 10.9 %expert.7 = (bf16[600,2048]{1,0:T(8,128)(2,1)}, bf16[600,2048]{1,0:T(8,128)(2,1)}, bf16[600,512]{1,0:T(8,128)(2,1)S(1)}, bf16[600,512]{1,0:T(8,128)(2,1)S(1)}, b...) custom-call(s32[1]{0:T(128)} %bitcast.2.me_ref, bf16[600,512]{1,0:T(8,128)(2,1)S(1)} %broadcast_select_fusion.1.rows_ref.refs_3_, ...), custom_call_target="tpu_custom_call" | custom-call | tf_op jit(solution)/shard_map/expert/pallas_call | solution.py:187
  140.5 2.6 collective-permute-start.19
  144.9 10.6 %collective-permute-done.20.gg1_ref = f32[8,600]{1,0:T(8,128)S(1)} collective-permute-done((f32[8,600]{1,0:T(8,128)S(1)}, f32[8,600]{1,0:T(8,128)S(1)}, u32[]{:S(2)}, u32[]{:S(2)}) %collective-permute-start.20) | collective-permute-done | bytes 19232 | tf_op jit(solution)/shard_map/ppermute | solution.py:430
  155.4 2.4 collective-permute-start.22
  163.1 10.7 %expert.4 = (bf16[600,2048]{1,0:T(8,128)(2,1)}, bf16[600,2048]{1,0:T(8,128)(2,1)}, bf16[600,512]{1,0:T(8,128)(2,1)S(1)}, bf16[600,512]{1,0:T(8,128)(2,1)S(1)}, b...) custom-call(s32[1]{0:T(128)} %bitcast.2.me_ref, bf16[600,512]{1,0:T(8,128)(2,1)S(1)} %copy-done.2, ...), custom_call_target="tpu_custom_call" | custom-call | tf_op jit(solution)/shard_map/expert/pallas_call | solution.py:187
  179.1 17.2 %attend_back.1 = (bf16[3,100,512]{2,1,0:T(8,128)(2,1)}, bf16[3,100,512]{2,1,0:T(8,128)(2,1)}, bf16[512,2048]{1,0:T(8,128)(2,1)}, f32[24,512]{1,0:T(8,128)}) custom-call(s32[1]{0:T(128)} %bitcast.2.me_ref, bf16[600,512]{1,0:T(8,128)(2,1)} %copy-done.25, bf16[600,512]{1,0:T(8,128)(2,1)} %collective-permute-done.17.din1_ref, ...), custom_call_target="tpu_custom_call" | custom-call | tf_op jit(solution)/shard_map/attend_back/pallas_call | solution.py:345
  196.2 2.1 convert_element_type.67
  198.4 2.0 copy-done.35
  200.6 2.6 collective-permute-done.29
  203.2 1.8 convert_add_fusion
  209.2 5.6 %collective-permute-done.30 = bf16[128,1024]{1,0:T(8,128)(2,1)} collective-permute-done((bf16[128,1024]{1,0:T(8,128)(2,1)}, bf16[128,1024]{1,0:T(8,128)(2,1)}, u32[]{:S(2)}, u32[]{:S(2)}) %collective-permute-start.30) | collective-permute-done | bytes 262176 | tf_op jit(solution)/shard_map/ppermute | solution.py:430
  220.9 2.7 collective-permute-done.33
  224.4 2.4 collective-permute-start.36
  226.8 2.1 collective-permute-start.34
  233.1 2.4 collective-permute-start.39
  240.7 17.5 %weight_grads.1 = (bf16[1,512,2048]{2,1,0:T(8,128)(2,1)}, bf16[1,2048,512]{2,1,0:T(8,128)(2,1)}) custom-call(bf16[600,512]{1,0:T(8,128)(2,1)S(1)} %copy-done.3, bf16[600,512]{1,0:T(8,128)(2,1)S(1)} %copy-done.8, bf16[600,512]{1,0:T(8,128)(2,1)S(1)} %broadcast_select_fusion.3.rows_ref.refs_2_, bf16[600,512]{1,0:T(8,128)(2,1)S(1)} %broadcast_select_fusion.1.rows_ref.refs_3_, ...), custom_call_target="tpu_custom_call" | custom-call | tf_op jit(solution)/shard_map/weight_grads/pallas_call | solution.py:243
  261.0 3.1 collective-permute-done.42
  264.5 2.7 collective-permute-done.40
  267.5 2.5 collective-permute-start.12
  270.0 1.9 collective-permute-start.15
  271.9 4.3 %collective-permute-done.43 = bf16[128,1024]{1,0:T(8,128)(2,1)S(1)} collective-permute-done((bf16[128,1024]{1,0:T(8,128)(2,1)S(1)}, bf16[128,1024]{1,0:T(8,128)(2,1)S(1)}, u32[]{:S(2)}, u32[]{:S(2)}) %collective-permute-start.43) | collective-permute-done | bytes 262176 | tf_op jit(solution)/shard_map/ppermute | solution.py:430
  276.3 3.0 collective-permute-done.41
  281.0 1.9 collective-permute-done.24
  283.6 3.5 collective-permute-done.25
  287.1 2.4 collective-permute-start.26
  289.4 2.1 collective-permute-done.26
  291.9 12.0 %collective-permute-done.27 = f32[24,512]{1,0:T(8,128)S(1)} collective-permute-done((f32[24,512]{1,0:T(8,128)S(1)}, f32[24,512]{1,0:T(8,128)S(1)}, u32[]{:S(2)}, u32[]{:S(2)}) %collective-permute-start.27) | collective-permute-done | bytes 49184 | tf_op jit(solution)/shard_map/ppermute | solution.py:430
  304.0 3.5 collective-permute-start.28
  307.4 5.2 %collective-permute-done.12.c_ref = bf16[600,512]{1,0:T(8,128)(2,1)S(1)} collective-permute-done((bf16[600,512]{1,0:T(8,128)(2,1)S(1)}, bf16[600,512]{1,0:T(8,128)(2,1)S(1)}, u32[]{:S(2)}, u32[]{:S(2)}) %collective-permute-start.12) | collective-permute-done | bytes 614432 | tf_op jit(solution)/shard_map/ppermute | solution.py:430
  314.3 3.9 %combine.1 = (bf16[3,100,512]{2,1,0:T(8,128)(2,1)}, bf16[3,100,512]{2,1,0:T(8,128)(2,1)}) custom-call(f32[600,512]{1,0:T(8,128)} %copy-done.6, bf16[600,512]{1,0:T(8,128)(2,1)} %copy-done.21, bf16[600,512]{1,0:T(8,128)(2,1)} %copy-done.40, bf16[600,512]{1,0:T(8,128)(2,1)} %copy-done.41, bf16[600,512]{1,0:T(8,128)(2,1)} %copy-done.42), custom_call_target="tpu_custom_call" | custom-call | tf_op jit(solution)/shard_map/combine/pallas_call | solution.py:395
  318.7 2.2 collective-permute-done.28
  322.9 2.1 maximum_select_fusion.1
  326.0 17.3 %all-reduce.5.cloned.1.call-done = (bf16[1,512,2048]{2,1,0:T(8,128)(2,1)}, bf16[1,2048,512]{2,1,0:T(8,128)(2,1)}) async-done(((bf16[1,512,2048]{2,1,0:T(8,128)(2,1)}, bf16[1,2048,512]{2,1,0:T(8,128)(2,1)}), (bf16[1,512,2048]{2,1,0:T(8,128)(2,1)}, bf16[1,2048,512]{2,1,0:T(8,128)(2,1)})) %all-reduce.5.cloned.1.call-update) | async-done | bytes 4194320 | tf_op jit(solution)/shard_map/psum | solution.py:538
  343.3 4.3 %convert_element_type.86 = f32[1,512,2048]{2,1,0:T(8,128)} convert(bf16[1,512,2048]{2,1,0:T(8,128)(2,1)} %get-tuple-element.87) | non-fusion elementwise | flops 1048576 | bytes 6291456 | tf_op jit(solution)/shard_map/convert_element_type | solution.py:547
  347.5 2.6 convert_element_type.87
  350.1 8.7 %fusion = f32[512,2048]{1,0:T(8,128)S(1)} fusion(bf16[256,2048]{1,0:T(8,128)(2,1)} %collective-permute-done.44, bf16[256,1024]{1,0:T(8,128)(2,1)S(1)} %maximum_select_fusion.4, bf16[256,1024]{1,0:T(8,128)(2,1)S(1)} %maximum_select_fusion.3, pred[]{:T(512)S(6)} %eq.12), kind=kLoop, calls=%fused_computation.1 | loop fusion | flops 14680064 | bytes 6291457 | tf_op jit(solution)/shard_map/convert_element_type | solution.py:469
  358.8 1.9 slice.44
  (216 shorter events, 73.5 us)
Async XLA Ops:
  7.2 336.0 %all-reduce.5.cloned.1.call-start = ((), (), s32[]{:S(2)}) async-start(), calls=%async_computation | async-start | bytes 8388608 | tf_op jit(solution)/shard_map/psum | solution.py:538
  8.4 2.7 collective-permute-start
  10.9 17.5 %collective-permute-start.1 = (bf16[3,100,512]{2,1,0:T(8,128)(2,1)}, bf16[3,100,512]{2,1,0:T(8,128)(2,1)}, u32[]{:S(2)}, u32[]{:S(2)}) collective-permute-start(bf16[3,100,512]{2,1,0:T(8,128)(2,1)} %get-tuple-element.92), channel_id=1, source_target_pairs={{0,4},{4,0},{1,5},{5,1},{2,6},{6,2},{3,7},{7,3},{8,12},{12,8},{9,1... | collective-permute-start | bytes 921608 | tf_op jit(solution)/shard_map/ppermute | solution.py:430
  11.2 82.6 %copy-start = (bf16[1,512,2048]{2,1,0:T(8,128)(2,1)S(1)}, bf16[1,512,2048]{2,1,0:T(8,128)(2,1)}, u32[]{:S(2)}) copy-start(bf16[1,512,2048]{2,1,0:T(8,128)(2,1)} %win_ref.7) | copy-start | bytes 6291460
  23.1 17.7 %collective-permute-start.3 = (bf16[600,512]{1,0:T(8,128)(2,1)S(1)}, bf16[600,512]{1,0:T(8,128)(2,1)S(1)}, u32[]{:S(2)}, u32[]{:S(2)}) collective-permute-start(bf16[600,512]{1,0:T(8,128)(2,1)S(1)} %get-tuple-element.49.rows_ref.routed_ref.refs_0_), channel_id=1, source_target_pairs={{0,1},{1,0},{2,3},{3,2},{4,5},{5,4},{6,7},{7,6},{8,9},{9,8},{10,11... | collective-permute-start | bytes 1843208 | tf_op jit(solution)/shard_map/ppermute | solution.py:430
  26.1 16.1 %collective-permute-start.7 = (bf16[600,512]{1,0:T(8,128)(2,1)S(1)}, bf16[600,512]{1,0:T(8,128)(2,1)}, u32[]{:S(2)}, u32[]{:S(2)}) collective-permute-start(bf16[600,512]{1,0:T(8,128)(2,1)S(1)} %get-tuple-element.49.rows_ref.routed_ref.refs_0_), channel_id=1, source_target_pairs={{1,2},{2,1},{5,6},{6,5},{9,10},{10,9},{13,14},{14,13},{17,18},{18,... | collective-permute-start | bytes 1843208 | tf_op jit(solution)/shard_map/ppermute | solution.py:430
  29.5 24.6 %collective-permute-start.4 = (bf16[600,512]{1,0:T(8,128)(2,1)S(1)}, bf16[600,512]{1,0:T(8,128)(2,1)}, u32[]{:S(2)}, u32[]{:S(2)}) collective-permute-start(bf16[600,512]{1,0:T(8,128)(2,1)S(1)} %bitcast.41), channel_id=1, source_target_pairs={{0,1},{1,0},{2,3},{3,2},{4,5},{5,4},{6,7},{7,6},{8,9},{9,8},{10,11... | collective-permute-start | bytes 1843208 | tf_op jit(solution)/shard_map/ppermute | solution.py:430
  33.1 22.4 %collective-permute-start.10 = (bf16[600,512]{1,0:T(8,128)(2,1)S(1)}, bf16[600,512]{1,0:T(8,128)(2,1)}, u32[]{:S(2)}, u32[]{:S(2)}) collective-permute-start(bf16[600,512]{1,0:T(8,128)(2,1)S(1)} %bitcast.42), channel_id=1, source_target_pairs={{1,2},{2,1},{5,6},{6,5},{9,10},{10,9},{13,14},{14,13},{17,18},{18,... | collective-permute-start | bytes 1843208 | tf_op jit(solution)/shard_map/ppermute | solution.py:430
  40.8 64.1 %copy-start.7 = (bf16[600,512]{1,0:T(8,128)(2,1)}, bf16[600,512]{1,0:T(8,128)(2,1)S(1)}, u32[]{:S(2)}) copy-start(bf16[600,512]{1,0:T(8,128)(2,1)S(1)} %collective-permute-done.3.rows_ref.refs_1_) | copy-start | bytes 1843204
  40.8 64.1 %collective-permute-start.6 = (bf16[600,512]{1,0:T(8,128)(2,1)S(1)}, bf16[600,512]{1,0:T(8,128)(2,1)}, u32[]{:S(2)}, u32[]{:S(2)}) collective-permute-start(bf16[600,512]{1,0:T(8,128)(2,1)S(1)} %collective-permute-done.3.rows_ref.refs_1_), channel_id=1, source_target_pairs={{1,2},{2,1},{5,6},{6,5},{9,10},{10,9},{13,14},{14,13},{17,18},{18,... | collective-permute-start | bytes 1843208 | tf_op jit(solution)/shard_map/ppermute | solution.py:430
  42.3 65.8 %collective-permute-start.8 = (bf16[600,512]{1,0:T(8,128)(2,1)}, bf16[600,512]{1,0:T(8,128)(2,1)}, u32[]{:S(2)}, u32[]{:S(2)}) collective-permute-start(bf16[600,512]{1,0:T(8,128)(2,1)} %collective-permute-done.7), channel_id=1, source_target_pairs={{1,0},{2,3},{5,4},{6,7},{9,8},{10,11},{13,12},{14,15},{17,16},{18,... | collective-permute-start | bytes 1843208 | tf_op jit(solution)/shard_map/ppermute | solution.py:430
  54.0 56.7 %collective-permute-start.9 = (bf16[600,512]{1,0:T(8,128)(2,1)}, bf16[600,512]{1,0:T(8,128)(2,1)}, u32[]{:S(2)}, u32[]{:S(2)}) collective-permute-start(bf16[600,512]{1,0:T(8,128)(2,1)} %collective-permute-done.4.dy_ref), channel_id=1, source_target_pairs={{1,2},{2,1},{5,6},{6,5},{9,10},{10,9},{13,14},{14,13},{17,18},{18,... | collective-permute-start | bytes 1843208 | tf_op jit(solution)/shard_map/ppermute | solution.py:430
  55.5 55.2 %collective-permute-start.11 = (bf16[600,512]{1,0:T(8,128)(2,1)}, bf16[600,512]{1,0:T(8,128)(2,1)}, u32[]{:S(2)}, u32[]{:S(2)}) collective-permute-start(bf16[600,512]{1,0:T(8,128)(2,1)} %collective-permute-done.10), channel_id=1, source_target_pairs={{1,0},{2,3},{5,4},{6,7},{9,8},{10,11},{13,12},{14,15},{17,16},{18,... | collective-permute-start | bytes 1843208 | tf_op jit(solution)/shard_map/ppermute | solution.py:430
  56.9 1.2 collective-permute-start.2
  90.5 36.1 %collective-permute-start.13 = (bf16[600,512]{1,0:T(8,128)(2,1)S(1)}, bf16[600,512]{1,0:T(8,128)(2,1)}, u32[]{:S(2)}, u32[]{:S(2)}) collective-permute-start(bf16[600,512]{1,0:T(8,128)(2,1)S(1)} %collective-permute-done.3.rows_ref.refs_1_), channel_id=1, source_target_pairs={{2,0},{1,3},{6,4},{5,7},{10,8},{9,11},{14,12},{13,15},{18,16},{17,... | collective-permute-start | bytes 1843208 | tf_op jit(solution)/shard_map/ppermute | solution.py:430
  104.9 72.0 %collective-permute-start.17 = (bf16[600,512]{1,0:T(8,128)(2,1)}, bf16[600,512]{1,0:T(8,128)(2,1)}, u32[]{:S(2)}, u32[]{:S(2)}) collective-permute-start(bf16[600,512]{1,0:T(8,128)(2,1)} %get-tuple-element.57), channel_id=1, source_target_pairs={{0,1},{1,0},{2,3},{3,2},{4,5},{5,4},{6,7},{7,6},{8,9},{9,8},{10,11... | collective-permute-start | bytes 1843208 | tf_op jit(solution)/shard_map/ppermute | solution.py:430
  108.1 19.6 %collective-permute-start.14 = (bf16[600,512]{1,0:T(8,128)(2,1)}, bf16[600,512]{1,0:T(8,128)(2,1)S(1)}, u32[]{:S(2)}, u32[]{:S(2)}) collective-permute-start(bf16[600,512]{1,0:T(8,128)(2,1)} %collective-permute-done.4.dy_ref), channel_id=1, source_target_pairs={{2,0},{1,3},{6,4},{5,7},{10,8},{9,11},{14,12},{13,15},{18,16},{17,... | collective-permute-start | bytes 1843208 | tf_op jit(solution)/shard_map/ppermute | solution.py:430
  123.0 55.5 %collective-permute-start.18 = (bf16[600,512]{1,0:T(8,128)(2,1)}, bf16[600,512]{1,0:T(8,128)(2,1)}, u32[]{:S(2)}, u32[]{:S(2)}) collective-permute-start(bf16[600,512]{1,0:T(8,128)(2,1)} %get-tuple-element.58), channel_id=1, source_target_pairs={{0,2},{1,3},{2,0},{3,1},{4,6},{5,7},{6,4},{7,5},{8,10},{9,11},{10,... | collective-permute-start | bytes 1843208 | tf_op jit(solution)/shard_map/ppermute | solution.py:430
  140.5 38.0 %collective-permute-start.19 = (bf16[600,512]{1,0:T(8,128)(2,1)}, bf16[600,512]{1,0:T(8,128)(2,1)}, u32[]{:S(2)}, u32[]{:S(2)}) collective-permute-start(bf16[600,512]{1,0:T(8,128)(2,1)} %get-tuple-element.59), channel_id=1, source_target_pairs={{0,3},{1,2},{2,1},{3,0},{4,7},{5,6},{6,5},{7,4},{8,11},{9,10},{10,... | collective-permute-start | bytes 1843208 | tf_op jit(solution)/shard_map/ppermute | solution.py:430
  143.1 12.3 %collective-permute-start.20 = (f32[8,600]{1,0:T(8,128)S(1)}, f32[8,600]{1,0:T(8,128)S(1)}, u32[]{:S(2)}, u32[]{:S(2)}) collective-permute-start(f32[8,600]{1,0:T(8,128)S(1)} %get-tuple-element.61), channel_id=1, source_target_pairs={{0,1},{1,0},{2,3},{3,2},{4,5},{5,4},{6,7},{7,6},{8,9},{9,8},{10,11... | collective-permute-start | bytes 57608 | tf_op jit(solution)/shard_map/ppermute | solution.py:430
  143.1 35.3 %collective-permute-start.21 = (f32[8,600]{1,0:T(8,128)S(1)}, f32[8,600]{1,0:T(8,128)S(1)}, u32[]{:S(2)}, u32[]{:S(2)}) collective-permute-start(f32[8,600]{1,0:T(8,128)S(1)} %get-tuple-element.62), channel_id=1, source_target_pairs={{0,2},{1,3},{2,0},{3,1},{4,6},{5,7},{6,4},{7,5},{8,10},{9,11},{10,... | collective-permute-start | bytes 57608 | tf_op jit(solution)/shard_map/ppermute | solution.py:430
  155.4 23.0 %collective-permute-start.22 = (f32[8,600]{1,0:T(8,128)S(1)}, f32[8,600]{1,0:T(8,128)}, u32[]{:S(2)}, u32[]{:S(2)}) collective-permute-start(f32[8,600]{1,0:T(8,128)S(1)} %get-tuple-element.63), channel_id=1, source_target_pairs={{0,3},{1,2},{2,1},{3,0},{4,7},{5,6},{6,5},{7,4},{8,11},{9,10},{10,... | collective-permute-start | bytes 57608 | tf_op jit(solution)/shard_map/ppermute | solution.py:430
  200.5 2.7 collective-permute-start.29
  206.1 8.7 %collective-permute-start.30 = (bf16[128,1024]{1,0:T(8,128)(2,1)}, bf16[128,1024]{1,0:T(8,128)(2,1)}, u32[]{:S(2)}, u32[]{:S(2)}) collective-permute-start(bf16[128,1024]{1,0:T(8,128)(2,1)} %dynamic-slice_convert_fusion.2), channel_id=1, source_target_pairs={{0,8},{8,0},{16,24},{24,16},{1,9},{9,1},{17,25},{25,17},{2,10},{10... | collective-permute-start | bytes 786440 | tf_op jit(solution)/shard_map/ppermute | solution.py:430
  207.6 9.8 %collective-permute-start.32 = (bf16[128,1024]{1,0:T(8,128)(2,1)S(1)}, bf16[128,1024]{1,0:T(8,128)(2,1)S(1)}, u32[]{:S(2)}, u32[]{:S(2)}) collective-permute-start(bf16[128,1024]{1,0:T(8,128)(2,1)S(1)} %dynamic-slice_convert_fusion.1), channel_id=1, source_target_pairs={{0,16},{8,24},{16,0},{24,8},{1,17},{9,25},{17,1},{25,9},{2,18},{10... | collective-permute-start | bytes 786440 | tf_op jit(solution)/shard_map/ppermute | solution.py:430
  215.8 5.0 %collective-permute-start.31 = (bf16[64,1024]{1,0:T(8,128)(2,1)S(1)}, bf16[64,1024]{1,0:T(8,128)(2,1)S(1)}, u32[]{:S(2)}, u32[]{:S(2)}) collective-permute-start(bf16[64,1024]{1,0:T(8,128)(2,1)S(1)} %dynamic-slice_convert_fusion.4), channel_id=1, source_target_pairs={{0,16},{8,24},{16,0},{24,8},{1,17},{9,25},{17,1},{25,9},{2,18},{10... | collective-permute-start | bytes 393224 | tf_op jit(solution)/shard_map/ppermute | solution.py:430
  218.6 5.0 %collective-permute-start.33 = (bf16[64,1024]{1,0:T(8,128)(2,1)S(1)}, bf16[64,1024]{1,0:T(8,128)(2,1)S(1)}, u32[]{:S(2)}, u32[]{:S(2)}) collective-permute-start(bf16[64,1024]{1,0:T(8,128)(2,1)S(1)} %dynamic-slice_convert_fusion.3), channel_id=1, source_target_pairs={{0,8},{8,0},{16,24},{24,16},{1,9},{9,1},{17,25},{25,17},{2,10},{10... | collective-permute-start | bytes 393224 | tf_op jit(solution)/shard_map/ppermute | solution.py:430
  224.4 6.2 %collective-permute-start.36 = (bf16[32,1024]{1,0:T(8,128)(2,1)S(1)}, bf16[32,1024]{1,0:T(8,128)(2,1)}, u32[]{:S(2)}, u32[]{:S(2)}) collective-permute-start(bf16[32,1024]{1,0:T(8,128)(2,1)S(1)} %get-tuple-element.97), channel_id=1, source_target_pairs={{0,3},{1,2},{2,1},{3,0},{4,7},{5,6},{6,5},{7,4},{8,11},{9,10},{10,... | collective-permute-start | bytes 196616 | tf_op jit(solution)/shard_map/ppermute | solution.py:430
  226.8 5.3 %collective-permute-start.35 = (bf16[32,1024]{1,0:T(8,128)(2,1)S(1)}, bf16[32,1024]{1,0:T(8,128)(2,1)}, u32[]{:S(2)}, u32[]{:S(2)}) collective-permute-start(bf16[32,1024]{1,0:T(8,128)(2,1)S(1)} %get-tuple-element.96), channel_id=1, source_target_pairs={{0,2},{1,3},{2,0},{3,1},{4,6},{5,7},{6,4},{7,5},{8,10},{9,11},{10,... | collective-permute-start | bytes 196616 | tf_op jit(solution)/shard_map/ppermute | solution.py:430
  226.8 5.3 %collective-permute-start.34 = (bf16[32,1024]{1,0:T(8,128)(2,1)S(1)}, bf16[32,1024]{1,0:T(8,128)(2,1)}, u32[]{:S(2)}, u32[]{:S(2)}) collective-permute-start(bf16[32,1024]{1,0:T(8,128)(2,1)S(1)} %get-tuple-element.95), channel_id=1, source_target_pairs={{0,1},{1,0},{2,3},{3,2},{4,5},{5,4},{6,7},{7,6},{8,9},{9,8},{10,11... | collective-permute-start | bytes 196616 | tf_op jit(solution)/shard_map/ppermute | solution.py:430
  233.1 25.2 %collective-permute-start.39 = (bf16[32,1024]{1,0:T(8,128)(2,1)S(1)}, bf16[32,1024]{1,0:T(8,128)(2,1)S(1)}, u32[]{:S(2)}, u32[]{:S(2)}) collective-permute-start(bf16[32,1024]{1,0:T(8,128)(2,1)S(1)} %fusion.7), channel_id=1, source_target_pairs={{0,3},{1,2},{2,1},{3,0},{4,7},{5,6},{6,5},{7,4},{8,11},{9,10},{10,... | collective-permute-start | bytes 196616 | tf_op jit(solution)/shard_map/ppermute | solution.py:430
  235.5 22.8 %collective-permute-start.38 = (bf16[32,1024]{1,0:T(8,128)(2,1)S(1)}, bf16[32,1024]{1,0:T(8,128)(2,1)S(1)}, u32[]{:S(2)}, u32[]{:S(2)}) collective-permute-start(bf16[32,1024]{1,0:T(8,128)(2,1)S(1)} %fusion.7), channel_id=1, source_target_pairs={{0,2},{1,3},{2,0},{3,1},{4,6},{5,7},{6,4},{7,5},{8,10},{9,11},{10,... | collective-permute-start | bytes 196616 | tf_op jit(solution)/shard_map/ppermute | solution.py:430
  235.8 22.6 %collective-permute-start.37 = (bf16[32,1024]{1,0:T(8,128)(2,1)S(1)}, bf16[32,1024]{1,0:T(8,128)(2,1)S(1)}, u32[]{:S(2)}, u32[]{:S(2)}) collective-permute-start(bf16[32,1024]{1,0:T(8,128)(2,1)S(1)} %fusion.7), channel_id=1, source_target_pairs={{0,1},{1,0},{2,3},{3,2},{4,5},{5,4},{6,7},{7,6},{8,9},{9,8},{10,11... | collective-permute-start | bytes 196616 | tf_op jit(solution)/shard_map/ppermute | solution.py:430
  258.4 5.6 %collective-permute-start.42 = (bf16[64,1024]{1,0:T(8,128)(2,1)S(1)}, bf16[64,1024]{1,0:T(8,128)(2,1)S(1)}, u32[]{:S(2)}, u32[]{:S(2)}) collective-permute-start(bf16[64,1024]{1,0:T(8,128)(2,1)S(1)} %pad_maximum_fusion.4), channel_id=1, source_target_pairs={{0,8},{8,0},{16,24},{24,16},{1,9},{9,1},{17,25},{25,17},{2,10},{10... | collective-permute-start | bytes 393224 | tf_op jit(solution)/shard_map/ppermute | solution.py:430
  260.0 7.2 %collective-permute-start.40 = (bf16[64,1024]{1,0:T(8,128)(2,1)S(1)}, bf16[64,1024]{1,0:T(8,128)(2,1)S(1)}, u32[]{:S(2)}, u32[]{:S(2)}) collective-permute-start(bf16[64,1024]{1,0:T(8,128)(2,1)S(1)} %pad_maximum_fusion.3), channel_id=1, source_target_pairs={{0,16},{8,24},{16,0},{24,8},{1,17},{9,25},{17,1},{25,9},{2,18},{10... | collective-permute-start | bytes 393224 | tf_op jit(solution)/shard_map/ppermute | solution.py:430
  264.1 12.0 %collective-permute-start.43 = (bf16[128,1024]{1,0:T(8,128)(2,1)S(1)}, bf16[128,1024]{1,0:T(8,128)(2,1)S(1)}, u32[]{:S(2)}, u32[]{:S(2)}) collective-permute-start(bf16[128,1024]{1,0:T(8,128)(2,1)S(1)} %maximum_select_fusion.6), channel_id=1, source_target_pairs={{0,16},{8,24},{16,0},{24,8},{1,17},{9,25},{17,1},{25,9},{2,18},{10... | collective-permute-start | bytes 786440 | tf_op jit(solution)/shard_map/ppermute | solution.py:430
  267.2 12.0 %collective-permute-start.41 = (bf16[128,1024]{1,0:T(8,128)(2,1)S(1)}, bf16[128,1024]{1,0:T(8,128)(2,1)S(1)}, u32[]{:S(2)}, u32[]{:S(2)}) collective-permute-start(bf16[128,1024]{1,0:T(8,128)(2,1)S(1)} %maximum_select_fusion.5), channel_id=1, source_target_pairs={{0,8},{8,0},{16,24},{24,16},{1,9},{9,1},{17,25},{25,17},{2,10},{10... | collective-permute-start | bytes 786440 | tf_op jit(solution)/shard_map/ppermute | solution.py:430
  267.5 40.0 %collective-permute-start.5 = (bf16[600,512]{1,0:T(8,128)(2,1)S(1)}, bf16[600,512]{1,0:T(8,128)(2,1)S(1)}, u32[]{:S(2)}, u32[]{:S(2)}) collective-permute-start(bf16[600,512]{1,0:T(8,128)(2,1)S(1)} %copy-done.30), channel_id=1, source_target_pairs={{0,1},{1,0},{2,3},{3,2},{4,5},{5,4},{6,7},{7,6},{8,9},{9,8},{10,11... | collective-permute-start | bytes 1843208 | tf_op jit(solution)/shard_map/ppermute | solution.py:430
  267.5 45.1 %collective-permute-start.12 = (bf16[600,512]{1,0:T(8,128)(2,1)S(1)}, bf16[600,512]{1,0:T(8,128)(2,1)S(1)}, u32[]{:S(2)}, u32[]{:S(2)}) collective-permute-start(bf16[600,512]{1,0:T(8,128)(2,1)S(1)} %copy-done.32), channel_id=1, source_target_pairs={{0,2},{1,3},{2,0},{3,1},{4,6},{5,7},{6,4},{7,5},{8,10},{9,11},{10,... | collective-permute-start | bytes 1843208 | tf_op jit(solution)/shard_map/ppermute | solution.py:430
  270.0 42.6 %collective-permute-start.15 = (bf16[600,512]{1,0:T(8,128)(2,1)S(1)}, bf16[600,512]{1,0:T(8,128)(2,1)S(1)}, u32[]{:S(2)}, u32[]{:S(2)}) collective-permute-start(bf16[600,512]{1,0:T(8,128)(2,1)S(1)} %copy-done.34), channel_id=1, source_target_pairs={{0,3},{1,2},{2,1},{3,0},{4,7},{5,6},{6,5},{7,4},{8,11},{9,10},{10,... | collective-permute-start | bytes 1843208 | tf_op jit(solution)/shard_map/ppermute | solution.py:430
  280.4 69.7 %collective-permute-start.44 = (bf16[256,2048]{1,0:T(8,128)(2,1)}, bf16[256,2048]{1,0:T(8,128)(2,1)}, u32[]{:S(2)}, u32[]{:S(2)}) collective-permute-start(bf16[256,2048]{1,0:T(8,128)(2,1)} %pad_maximum_fusion), channel_id=1, source_target_pairs={{0,4},{4,0},{1,5},{5,1},{2,6},{6,2},{3,7},{7,3},{8,12},{12,8},{9,1... | collective-permute-start | bytes 3145736 | tf_op jit(solution)/shard_map/ppermute | solution.py:430
  280.4 2.4 collective-permute-start.24
  282.9 4.2 %collective-permute-start.25 = (f32[24,512]{1,0:T(8,128)S(1)}, f32[24,512]{1,0:T(8,128)S(1)}, u32[]{:S(2)}, u32[]{:S(2)}) collective-permute-start(f32[24,512]{1,0:T(8,128)S(1)} %add.127), channel_id=1, source_target_pairs={{0,8},{8,0},{16,24},{24,16},{1,9},{9,1},{17,25},{25,17},{2,10},{10... | collective-permute-start | bytes 147464 | tf_op jit(solution)/shard_map/ppermute | solution.py:430
  287.1 4.4 %collective-permute-start.26 = (f32[24,512]{1,0:T(8,128)S(1)}, f32[24,512]{1,0:T(8,128)S(1)}, u32[]{:S(2)}, u32[]{:S(2)}) collective-permute-start(f32[24,512]{1,0:T(8,128)S(1)} %add.128), channel_id=1, source_target_pairs={{0,16},{8,24},{16,0},{24,8},{1,17},{9,25},{17,1},{25,9},{2,18},{10... | collective-permute-start | bytes 147464 | tf_op jit(solution)/shard_map/ppermute | solution.py:430
  291.5 12.5 %collective-permute-start.27 = (f32[24,512]{1,0:T(8,128)S(1)}, f32[24,512]{1,0:T(8,128)S(1)}, u32[]{:S(2)}, u32[]{:S(2)}) collective-permute-start(f32[24,512]{1,0:T(8,128)S(1)} %add.129), channel_id=1, source_target_pairs={{0,1},{1,0},{2,3},{3,2},{4,5},{5,4},{6,7},{7,6},{8,9},{9,8},{10,11... | collective-permute-start | bytes 147464 | tf_op jit(solution)/shard_map/ppermute | solution.py:430
  304.0 16.9 %collective-permute-start.28 = (f32[24,512]{1,0:T(8,128)S(1)}, f32[24,512]{1,0:T(8,128)}, u32[]{:S(2)}, u32[]{:S(2)}) collective-permute-start(f32[24,512]{1,0:T(8,128)S(1)} %add.130), channel_id=1, source_target_pairs={{0,2},{1,3},{2,0},{3,1},{4,6},{5,7},{6,4},{7,5},{8,10},{9,11},{10,... | collective-permute-start | bytes 147464 | tf_op jit(solution)/shard_map/ppermute | solution.py:430
  318.2 4.7 %collective-permute-start.16 = (bf16[3,100,512]{2,1,0:T(8,128)(2,1)}, bf16[3,100,512]{2,1,0:T(8,128)(2,1)S(1)}, u32[]{:S(2)}, u32[]{:S(2)}) collective-permute-start(bf16[3,100,512]{2,1,0:T(8,128)(2,1)} %get-tuple-element.55), channel_id=1, source_target_pairs={{0,4},{4,0},{1,5},{5,1},{2,6},{6,2},{3,7},{7,3},{8,12},{12,8},{9,1... | collective-permute-start | bytes 921608 | tf_op jit(solution)/shard_map/ppermute | solution.py:430
  318.2 6.8 %collective-permute-start.23 = (bf16[3,100,512]{2,1,0:T(8,128)(2,1)}, bf16[3,100,512]{2,1,0:T(8,128)(2,1)S(1)}, u32[]{:S(2)}, u32[]{:S(2)}) collective-permute-start(bf16[3,100,512]{2,1,0:T(8,128)(2,1)} %get-tuple-element.70), channel_id=1, source_target_pairs={{0,4},{4,0},{1,5},{5,1},{2,6},{6,2},{3,7},{7,3},{8,12},{12,8},{9,1... | collective-permute-start | bytes 921608 | tf_op jit(solution)/shard_map/ppermute | solution.py:430
  (49 other events, 378.2 us)
Sparse Core Ops, SparseCore 0:
  258.4 84.8 all-reduce.4

commit v2 on v0

--- a/solution.py
+++ b/solution.py
@@ -1,11 +1,813 @@
+import functools
 import jax
 import jax.numpy as jnp
 from jax import lax
+from jax.experimental import pallas as pl
+from jax.experimental.pallas import tpu as pltpu
 from jax.sharding import PartitionSpec as P
 
 HEADS = 8
 HEAD_DIM = 64
 TOP = 2
+EPS = 1e-06
+SCALE = HEAD_DIM ** (-0.5)
+F32 = jnp.float32
+BF16 = jnp.bfloat16
+HELD = pltpu.HBM
+BRIEF = pl.CostEstimate(flops=1, bytes_accessed=1, transcendentals=0)
+NT = (((1,), (1,)), ((), ()))
+TN = (((0,), (0,)), ((), ()))
+NN = (((1,), (0,)), ((), ()))
+
+
+def mm(a, b, dims=NN):
+    return lax.dot_general(a, b, dims, preferred_element_type=F32)
+
+
+def two_halves(a):
+    high = a.astype(BF16)
+    return high, (a - high.astype(F32)).astype(BF16)
+
+
+def stats(value):
+    center = value - jnp.mean(value, -1, keepdims=True)
+    rstd = lax.rsqrt(jnp.mean(center * center, -1, keepdims=True) + EPS)
+    return center * rstd, rstd
+
+
+def norm_vjp(d_value, unit, rstd, gain):
+    d_unit = d_value * gain
+    return rstd * (
+        d_unit
+        - jnp.mean(d_unit, -1, keepdims=True)
+        - unit * jnp.mean(d_unit * unit, -1, keepdims=True)
+    )
+
+
+def head_pair(value):
+    lane = lax.broadcasted_iota(jnp.int32, value.shape, 1)
+    first = lane < HEAD_DIM
+    return jnp.concatenate(
+        [jnp.where(first, value, 0.0), jnp.where(first, 0.0, value)], axis=0
+    ).astype(BF16)
+
+
+def join_pair(value):
+    rows = value.shape[0] // 2
+    lane = lax.broadcasted_iota(jnp.int32, (rows, value.shape[1]), 1)
+    return jnp.where(lane < HEAD_DIM, value[:rows], value[rows:])
+
+
+def natural(core, mine, theirs):
+    return jnp.where(core == 0, mine, theirs), jnp.where(core == 0, theirs, mine)
+
+
+def attend_kernel(
+    meta_ref, own_ref, other_ref, dyown_ref, dyother_ref, mask_ref, g1_ref, wqkv_ref, wout_ref, g2_ref,
+    x_ref, dy_ref, normed_ref, qkv_ref, probs_ref, mix_ref, mid_ref, routed_ref,
+    x_s, qkv_s, mix_s,
+):
+    half = own_ref.shape[1]
+    width = own_ref.shape[2]
+    pair = 2 * HEAD_DIM
+    core = meta_ref[3]
+    for mine, theirs, ref in ((dyown_ref, dyother_ref, dy_ref), (own_ref, other_ref, x_ref)):
+        first, second = natural(core, mine[0].astype(F32), theirs[0].astype(F32))
+        x_s[0:half, :] = first
+        x_s[half : 2 * half, :] = second
+        ref[...] = x_s[...].astype(BF16)
+    x = x_s[...]
+    unit, _ = stats(x)
+    normed = (unit * g1_ref[...]).astype(BF16)
+    normed_ref[...] = normed
+    qkv_s[...] = mm(normed, wqkv_ref[...])
+    qkv_ref[...] = qkv_s[...].astype(BF16)
+    image = core * pl.num_programs(0) + pl.program_id(0)
+    is_open = mask_ref[pl.ds(image, 1), :] > 0
+    for n in range(width // pair):
+        at = n * pair
+        query = head_pair(qkv_s[:, at : at + pair])
+        keys = qkv_s[:, width + at : width + at + pair].astype(BF16)
+        vals = qkv_s[:, 2 * width + at : 2 * width + at + pair].astype(BF16)
+        scores = jnp.where(is_open, mm(query, keys, NT) * SCALE, -1e9)
+        top = jnp.max(scores, -1, keepdims=True)
+        expo = jnp.where(is_open, jnp.exp(scores - top), 0.0)
+        probs = (expo / jnp.sum(expo, -1, keepdims=True)).astype(BF16)
+        probs_ref[0, n] = probs
+        mix_s[:, at : at + pair] = join_pair(mm(probs, vals))
+    mix = mix_s[...].astype(BF16)
+    mix_ref[...] = mix
+    mid = x + mm(mix, wout_ref[...])
+    mid_ref[...] = mid
+    unit, _ = stats(mid)
+    routed_ref[...] = (unit * g2_ref[...]).astype(BF16)
+
+
+def attend(meta, own, other, dy_own, dy_other, mask, g1, wqkv, wout, g2):
+    imgs, half, width = own.shape
+    imgs //= 2
+    seq = 2 * half
+    rows = imgs * seq
+    pairs = HEADS // 2
+    raw = pl.BlockSpec((1, half, width), lambda i, m: (m[3] * imgs + i, 0, 0))
+    one = lambda *s: pl.BlockSpec(s, lambda i, m: (i,) + (0,) * (len(s) - 1))
+    fix = lambda *s: pl.BlockSpec(s, lambda i, m: (0,) * len(s))
+    late = lambda *s: HELD(s, BF16)
+    return pl.pallas_call(
+        attend_kernel,
+        grid_spec=pltpu.PrefetchScalarGridSpec(
+            num_scalar_prefetch=1,
+            grid=(imgs,),
+            in_specs=[
+                raw, raw, raw, raw, fix(*mask.shape), fix(1, width),
+                fix(width, 3 * width), fix(width, width), fix(1, width),
+            ],
+            out_specs=[
+                one(seq, width), one(seq, width), one(seq, width), one(seq, 3 * width),
+                one(1, pairs, 2 * seq, seq), one(seq, width), one(seq, width), one(seq, width),
+            ],
+            scratch_shapes=[
+                pltpu.VMEM((seq, width), F32),
+                pltpu.VMEM((seq, 3 * width), F32),
+                pltpu.VMEM((seq, width), F32),
+            ],
+        ),
+        out_shape=[
+            late(rows, width),
+            jax.ShapeDtypeStruct((rows, width), BF16),
+            late(rows, width),
+            late(rows, 3 * width),
+            late(imgs, pairs, 2 * seq, seq),
+            late(rows, width),
+            HELD((rows, width), F32),
+            jax.ShapeDtypeStruct((rows, width), BF16),
+        ],
+        compiler_params=pltpu.CompilerParams(vmem_limit_bytes=22 << 20),
+        cost_estimate=BRIEF,
+        name="attend",
+    )(meta, own, other, dy_own, dy_other, mask, g1, wqkv, wout, g2)
+
+
+def assemble_kernel(meta_ref, own_ref, other_ref, out_ref, out_s):
+    half = own_ref.shape[1]
+    first, second = natural(meta_ref[3], own_ref[0].astype(F32), other_ref[0].astype(F32))
+    out_s[0:half, :] = first
+    out_s[half : 2 * half, :] = second
+    out_ref[...] = out_s[...].astype(BF16)
+
+
+def assemble(meta, own, other):
+    imgs, half, width = own.shape
+    imgs //= 2
+    raw = pl.BlockSpec((1, half, width), lambda i, m: (m[3] * imgs + i, 0, 0))
+    return pl.pallas_call(
+        assemble_kernel,
+        grid_spec=pltpu.PrefetchScalarGridSpec(
+            num_scalar_prefetch=1,
+            grid=(imgs,),
+            in_specs=[raw, raw],
+            out_specs=pl.BlockSpec((2 * half, width), lambda i, m: (i, 0)),
+            scratch_shapes=[pltpu.VMEM((2 * half, width), F32)],
+        ),
+        out_shape=jax.ShapeDtypeStruct((imgs * 2 * half, width), BF16),
+        cost_estimate=BRIEF,
+        name="assemble",
+    )(meta, own, other)
+
+
+def row_gates(rows, ids, wr):
+    logits = mm(wr, rows, NT)
+    row = lax.broadcasted_iota(jnp.int32, logits.shape, 0)
+    pick = (row.astype(F32) == ids[0:1, :]) | (row.astype(F32) == ids[1:2, :])
+    top = jnp.max(jnp.where(pick, logits, -jnp.inf), 0, keepdims=True)
+    expo = jnp.where(pick, jnp.exp(logits - top), 0.0)
+    return expo / jnp.sum(expo, 0, keepdims=True), row
+
+
+def padded(count):
+    return -(-count // 16) * 16
+
+
+def expert_kernel(add, local, meta_ref, rows_ref, dy_ref, ids_ref, wr_ref, *rest):
+    weights, rest = (rest[:4], rest[4:]) if local else (rest[:8], rest[8:])
+    if add:
+        pmade_ref, pdin_ref, *rest = rest
+    act_ref, dpre_ref, dout_ref, made_ref, din_ref, gate_s, made_s, din_s, *rest = rest
+    step = pl.program_id(0)
+    count = act_ref.shape[0]
+    width = rows_ref.shape[1]
+    rows = rows_ref[0:count, :]
+
+    @pl.when(step == 0)
+    def _():
+        if ids_ref.shape[0] == 2:
+            ids = ids_ref[...].astype(F32)
+        else:
+            at = padded(count)
+            ids = [ids_ref[at : at + 2, :], ids_ref[at + 2 : at + 4, 0 : count - width]]
+            ids = jnp.concatenate([v.astype(F32) for v in ids], axis=1)
+        gates, row = row_gates(rows, ids, wr_ref[...])
+        high, low = two_halves(jnp.where(row == meta_ref[0], gates, 0.0))
+        ones = jnp.ones((16, 128), BF16)
+        gate_s[...] = mm(high, ones, TN) + mm(low, ones, TN)
+        gate = gate_s[:, 0:1]
+        dout_ref[...] = (gate * dy_ref[...].astype(F32)).astype(BF16)
+        made_s[...] = jnp.zeros_like(made_s)
+        din_s[...] = jnp.zeros_like(din_s)
+
+    if local:
+        w_in = jnp.concatenate([ref[0] for ref in weights[:2]], axis=1)
+        w_back = jnp.concatenate([ref[0] for ref in weights[2:]], axis=0)
+    else:
+        wi_s, wb_s = rest
+        part = wi_s.shape[0] // 2
+        for side in range(2):
+
+            @pl.when((step < pl.num_programs(0) // 2) == (side == 0))
+            def _():
+                for s in range(2):
+                    for h in range(2):
+                        wi_s[h * part : (h + 1) * part, s * part : (s + 1) * part] = weights[4 * side + s][0, h]
+                        wb_s[s * part : (s + 1) * part, h * part : (h + 1) * part] = weights[4 * side + 2 + s][0, h]
+
+        w_in, w_back = wi_s[...], wb_s[...]
+    pre = mm(rows, w_in)
+    square = pre * pre
+    inner = pre * (0.7978845608 + 0.0356774081 * square)
+    up = 0.5 + 0.5 * jnp.tanh(inner)
+    value = pre * up
+    act = value.astype(BF16)
+    slope = up + value * (1.0 - up) * (1.5957691216 + 0.2140644488 * square)
+    act_ref[...] = act
+    made_s[...] += mm(act, w_back)
+    dpre = (mm(dout_ref[...], w_back, NT) * slope).astype(BF16)
+    dpre_ref[...] = dpre
+    din_s[...] += mm(dpre, w_in, NT)
+
+    @pl.when(step == pl.num_programs(0) - 1)
+    def _():
+        gate = gate_s[:, 0:1]
+        made = made_s[...].astype(BF16).astype(F32)
+        total = gate * made
+        d_in = din_s[...]
+        high, low = two_halves(made * dy_ref[...].astype(F32))
+        ones = jnp.ones((16, made.shape[1]), BF16)
+        d_gate = (mm(ones, high, NT) + mm(ones, low, NT))[0:8]
+        row = lax.broadcasted_iota(jnp.int32, d_gate.shape, 0)
+        d_gate = jnp.where(row == meta_ref[0], d_gate, 0.0)
+        tail = padded(count)
+        if add:
+            total += pmade_ref[...].astype(F32)
+            d_in += pdin_ref[0:count, :].astype(F32)
+            d_gate += read_gate(pdin_ref, count)
+        made_ref[...] = total.astype(BF16)
+        din_ref[0:count, :] = d_in.astype(BF16)
+        high = d_gate.astype(BF16).astype(F32)
+        value = jnp.concatenate([high, d_gate - high], axis=0).astype(BF16)
+        if count > d_in.shape[1]:
+            cut = d_in.shape[1]
+            din_ref[tail : tail + 16, :] = value[:, :cut]
+            din_ref[tail + 16 : tail + 32, 0 : count - cut] = value[:, cut:]
+        else:
+            din_ref[tail : tail + 16, 0:count] = value
+
+
+def read_gate(ref, count):
+    tail = padded(count)
+    width = ref.shape[1]
+    value = ref[tail : tail + 16, 0 : min(count, width)].astype(F32)
+    if count > width:
+        value = jnp.concatenate([value, ref[tail + 16 : tail + 32, 0 : count - width].astype(F32)], axis=1)
+    return value[0:8] + value[8:16]
+
+
+PIECES = 8
+
+
+def expert(meta, rows, dy, ids, wr, weights, prev=None):
+    count = dy.shape[0]
+    width = rows.shape[1]
+    local = weights[0].ndim == 3
+    piece = weights[0].shape[2] // PIECES if local else weights[0].shape[2]
+    hidden = PIECES * piece
+    steps = PIECES // 2
+    deep = padded(count) + 16 * -(-count // width)
+    fix = lambda *s: pl.BlockSpec(s, lambda q, m: (0,) * len(s))
+    if local:
+        cuts = [pl.BlockSpec((1, width, piece), lambda q, m, s=s: (0, 0, (2 * q + s) ^ m[1])) for s in (0, 1)]
+        cuts += [pl.BlockSpec((1, piece, width), lambda q, m, s=s: (0, (2 * q + s) ^ m[1], 0)) for s in (0, 1)]
+        weights = [weights[0]] * 2 + [weights[1]] * 2
+    else:
+        block = (1, 2, piece, piece)
+        near = lambda q: jnp.minimum(q, steps // 2 - 1)
+        away = lambda q: jnp.maximum(q - steps // 2, 0)
+        cuts = [
+            pl.BlockSpec(block, lambda q, m, s=s, g=g, at=at: (2 * at(q) + s, g, 0, 0))
+            for at in (near, away) for g in (0, 1) for s in (0, 1)
+        ]
+        weights = [weights[0]] * 4 + [weights[1]] * 4
+    more = [] if prev is None else [fix(count, width), fix(deep, width)]
+    return pl.pallas_call(
+        functools.partial(expert_kernel, prev is not None, local),
+        grid_spec=pltpu.PrefetchScalarGridSpec(
+            num_scalar_prefetch=1,
+            grid=(steps,),
+            in_specs=[
+                fix(*rows.shape), fix(*dy.shape), fix(*ids.shape), fix(*wr.shape), *cuts, *more,
+            ],
+            out_specs=[
+                pl.BlockSpec((count, 2 * piece), lambda q, m: (0, q)),
+                pl.BlockSpec((count, 2 * piece), lambda q, m: (0, q)),
+                fix(count, width), fix(count, width), fix(deep, width),
+            ],
+            scratch_shapes=[
+                pltpu.VMEM((count, 128), F32),
+                pltpu.VMEM((count, width), F32),
+                pltpu.VMEM((count, width), F32),
+            ] + ([] if local else [pltpu.VMEM((width, 2 * piece), BF16), pltpu.VMEM((2 * piece, width), BF16)]),
+        ),
+        out_shape=[
+            jax.ShapeDtypeStruct((count, hidden), BF16),
+            jax.ShapeDtypeStruct((count, hidden), BF16),
+            jax.ShapeDtypeStruct((count, width), BF16),
+            jax.ShapeDtypeStruct((count, width), BF16),
+            jax.ShapeDtypeStruct((deep, width), BF16),
+        ],
+        compiler_params=pltpu.CompilerParams(vmem_limit_bytes=22 << 20),
+        cost_estimate=BRIEF,
+        name="expert",
+    )(meta, rows, dy, ids, wr, *weights, *(prev or ()))
+
+
+def weight_kernel(n, *refs):
+    rows = refs[:n]
+    sides = [[refs[n + (3 * e + g) * n : n + (3 * e + g + 1) * n] for g in range(3)] for e in range(2)]
+    iown_ref, igive_ref, bown_ref, bgive_ref = refs[7 * n :]
+    side, part = pl.program_id(0), pl.program_id(1)
+    for e in range(2):
+        acts, dpres, douts = sides[e]
+
+        @pl.when(side == e)
+        def _():
+            results = []
+            for left, right in ((dpres, rows), (acts, douts)):
+                total = 0.0
+                for b in range(n):
+                    count = left[b].shape[0]
+                    total = total + mm(left[b][...], right[b][0:count, :], TN)
+                results.append(total.astype(BF16).reshape(iown_ref.shape[1:]))
+            grad_in, grad_back = results
+
+            @pl.when(part < pl.num_programs(1) // 2)
+            def _():
+                iown_ref[0] = grad_in
+                bown_ref[0] = grad_back
+
+            @pl.when(part >= pl.num_programs(1) // 2)
+            def _():
+                igive_ref[0] = grad_in
+                bgive_ref[0] = grad_back
+
+
+def weight_grads(rows, sides):
+    n = len(rows)
+    width = rows[0].shape[1]
+    hidden = sides[0][0][0].shape[1]
+    piece = hidden // PIECES
+    upper = PIECES // 2
+    steps = PIECES // 2
+    fix = lambda a: pl.BlockSpec(a.shape, lambda e, q: (0, 0))
+    cuts = [
+        lambda a: pl.BlockSpec((a.shape[0], 2 * piece), lambda e, q: (0, jnp.where(e == 0, q, steps - 1))),
+        lambda a: pl.BlockSpec((a.shape[0], 2 * piece), lambda e, q: (0, jnp.where(e == 1, q, 0))),
+    ]
+    specs = [fix(a) for a in rows]
+    args = list(rows)
+    for e, (acts, dpres, douts) in enumerate(sides):
+        specs += [cuts[e](a) for a in acts] + [cuts[e](a) for a in dpres] + [fix(a) for a in douts]
+        args += [*acts, *dpres, *douts]
+    own = pl.BlockSpec((1, 2, piece, width), lambda e, q: (e, jnp.minimum(q, steps // 2 - 1), 0, 0))
+    give = pl.BlockSpec((1, 2, piece, width), lambda e, q: (e, jnp.maximum(q - steps // 2, 0), 0, 0))
+    return pl.pallas_call(
+        functools.partial(weight_kernel, n),
+        grid=(2, steps),
+        in_specs=specs,
+        out_specs=[own, give, own, give],
+        out_shape=[jax.ShapeDtypeStruct((2, upper, piece, width), BF16)] * 4,
+        compiler_params=pltpu.CompilerParams(vmem_limit_bytes=26 << 20),
+        cost_estimate=BRIEF,
+        name="weight_grads",
+    )(*args)
+
+
+def finish_kernel(meta_ref, im_ref, ir_ref, bm_ref, br_ref, gin_ref, gback_ref):
+    mine = pl.program_id(0) < pl.num_programs(0) // 2
+    flip = meta_ref[1] % 2 == 1
+    piece, width = im_ref.shape[1:]
+    for m_ref, r_ref, out_ref in ((im_ref, ir_ref, gin_ref), (bm_ref, br_ref, gback_ref)):
+        value = jnp.where(mine, m_ref[...], r_ref[...]).astype(F32)
+        first = jnp.where(flip, value[1], value[0])
+        second = jnp.where(flip, value[0], value[1])
+        if out_ref is gin_ref:
+            out_ref[0, :, 0:piece] = jnp.transpose(first)
+            out_ref[0, :, piece : 2 * piece] = jnp.transpose(second)
+        else:
+            out_ref[0, 0:piece, :] = first
+            out_ref[0, piece : 2 * piece, :] = second
+
+
+def finish_expert(meta, in_mine, in_recv, back_mine, back_recv):
+    upper, piece, width = in_mine.shape
+    steps = upper
+    own = pl.BlockSpec((2, piece, width), lambda q, m: (jnp.minimum(q, steps // 2 - 1), 0, 0))
+    give = pl.BlockSpec((2, piece, width), lambda q, m: (jnp.maximum(q - steps // 2, 0), 0, 0))
+    return pl.pallas_call(
+        finish_kernel,
+        grid_spec=pltpu.PrefetchScalarGridSpec(
+            num_scalar_prefetch=1,
+            grid=(steps,),
+            in_specs=[own, give, own, give],
+            out_specs=[
+                pl.BlockSpec((1, width, 2 * piece), lambda q, m: (0, 0, q ^ (m[1] // 2))),
+                pl.BlockSpec((1, 2 * piece, width), lambda q, m: (0, q ^ (m[1] // 2), 0)),
+            ],
+        ),
+        out_shape=[
+            jax.ShapeDtypeStruct((1, width, PIECES * piece), F32),
+            jax.ShapeDtypeStruct((1, PIECES * piece, width), F32),
+        ],
+        compiler_params=pltpu.CompilerParams(vmem_limit_bytes=24 << 20),
+        cost_estimate=BRIEF,
+        name="finish_expert",
+    )(meta, in_mine, in_recv, back_mine, back_recv)
+
+
+def split_halves(core, whole_ref, own_ref, other_ref):
+    imgs, half, _ = own_ref.shape
+    for i in range(imgs):
+        at = 2 * half * i
+        first, second = whole_ref[at : at + half, :], whole_ref[at + half : at + 2 * half, :]
+        mine, theirs = natural(core, first, second)
+        own_ref[i] = mine.astype(BF16)
+        other_ref[i] = theirs.astype(BF16)
+
+
+def back_kernel(
+    meta_ref, din0_ref, din1_ref,
+    ids_ref, dy_ref, mid_ref, routed_ref, wr_ref, g2_ref, mix_ref, wout_ref,
+    probs_ref, qkv_ref, x_ref, normed_ref, wqkv_ref, g1_ref,
+    own_ref, other_ref, gown_ref, ggive_ref,
+    dmid_s, dmix_s, dqkv_s, tok_s, grad_s, small_s,
+):
+    step = pl.program_id(0)
+    imgs = pl.num_programs(0)
+    seq = qkv_ref.shape[0]
+    width = x_ref.shape[1]
+    half = seq // 2
+    pair = 2 * HEAD_DIM
+    rows = x_ref.shape[0]
+
+    @pl.when(step == 0)
+    def _():
+        routed = routed_ref[...]
+        wr = wr_ref[...]
+        gates, _ = row_gates(routed, ids_ref[...].astype(F32), wr)
+        d_gate = read_gate(din0_ref, rows) + read_gate(din1_ref, rows)
+        d_gate = jnp.concatenate([d_gate, jnp.zeros_like(d_gate)], axis=0)
+        d_logits = gates * (d_gate - jnp.sum(gates * d_gate, 0, keepdims=True))
+        high, low = two_halves(d_logits)
+        small_s[...] = jnp.zeros_like(small_s)
+        small_s[0:16, :] = mm(high, routed) + mm(low, routed)
+        d_routed = din0_ref[0:rows, :].astype(F32) + din1_ref[0:rows, :].astype(F32)
+        d_routed = d_routed + mm(high, wr, TN) + mm(low, wr, TN)
+        unit, rstd = stats(mid_ref[...])
+        small_s[16:17, :] = jnp.sum(d_routed * unit, 0, keepdims=True)
+        d_mid = dy_ref[...].astype(F32) + norm_vjp(d_routed, unit, rstd, g2_ref[...])
+        dmid_s[...] = d_mid
+        d_branch = d_mid.astype(BF16)
+        grad_s[:, 3 * width : 4 * width] = mm(mix_ref[...], d_branch, TN).astype(BF16)
+        dmix_s[...] = mm(d_branch, wout_ref[...], NT)
+
+    base = pl.multiple_of(step * seq, 8)
+    for n in range(width // pair):
+        at = n * pair
+        d_mix = head_pair(dmix_s[pl.ds(base, seq), at : at + pair])
+        query = head_pair(qkv_ref[:, at : at + pair].astype(F32))
+        keys = qkv_ref[:, width + at : width + at + pair]
+        vals = qkv_ref[:, 2 * width + at : 2 * width + at + pair]
+        low = probs_ref[0, n]
+        probs = low.astype(F32)
+        d_probs = mm(d_mix, vals, NT)
+        d_scores = probs * (d_probs - jnp.sum(probs * d_probs, -1, keepdims=True))
+        d_scores = d_scores.astype(BF16)
+        d_query = join_pair(mm(d_scores, keys)) * SCALE
+        d_keys = mm(d_scores, query, TN) * SCALE
+        d_vals = mm(low, d_mix, TN)
+        dqkv_s[pl.ds(base, seq), at : at + pair] = d_query.astype(BF16)
+        dqkv_s[pl.ds(base, seq), width + at : width + at + pair] = d_keys.astype(BF16)
+        dqkv_s[pl.ds(base, seq), 2 * width + at : 2 * width + at + pair] = d_vals.astype(BF16)
+
+    @pl.when(step == imgs - 1)
+    def _():
+        d_qkv = dqkv_s[...]
+        grad_s[:, : 3 * width] = mm(normed_ref[...], d_qkv, TN).astype(BF16)
+        d_normed = mm(d_qkv, wqkv_ref[...], NT)
+        unit, rstd = stats(x_ref[...].astype(F32))
+        small_s[17:18, :] = jnp.sum(d_normed * unit, 0, keepdims=True)
+        grad_s[:, 4 * width :] = jnp.transpose(small_s[...]).astype(BF16)
+        tok_s[...] = dmid_s[...] + norm_vjp(d_normed, unit, rstd, g1_ref[...])
+        split_halves(meta_ref[3], tok_s, own_ref, other_ref)
+        part = width // SHARES
+        for r in range(SHARES):
+            ref = gown_ref if r < SHARES // 2 else ggive_ref
+            to = (r % (SHARES // 2)) * part
+            there = pl.multiple_of((r ^ meta_ref[2]) * part, part)
+            ref[to : to + part, :] = grad_s[pl.ds(there, part), :]
+
+
+SHARES = 32
+
+
+def attend_back(meta, dins, ids, dy, mid, routed, wr, g2, mix, wout, probs, qkv, x, normed, wqkv, g1):
+    imgs = probs.shape[0]
+    rows, width = x.shape
+    seq = rows // imgs
+    pairs = HEADS // 2
+    wide = 4 * width + 128
+    fix = lambda *s: pl.BlockSpec(s, lambda i, m: (0,) * len(s))
+    return pl.pallas_call(
+        back_kernel,
+        grid_spec=pltpu.PrefetchScalarGridSpec(
+            num_scalar_prefetch=1,
+            grid=(imgs,),
+            in_specs=[fix(*a.shape) for a in dins] + [
+                fix(2, rows), fix(rows, width), fix(rows, width), fix(rows, width),
+                fix(16, width), fix(1, width), fix(rows, width), fix(width, width),
+                pl.BlockSpec((1, pairs, 2 * seq, seq), lambda i, m: (i, 0, 0, 0)),
+                pl.BlockSpec((seq, 3 * width), lambda i, m: (i, 0)),
+                fix(rows, width), fix(rows, width), fix(width, 3 * width), fix(1, width),
+            ],
+            out_specs=[
+                fix(imgs, seq // 2, width), fix(imgs, seq // 2, width),
+                fix(width // 2, wide), fix(width // 2, wide),
+            ],
+            scratch_shapes=[
+                pltpu.VMEM((rows, width), F32),
+                pltpu.VMEM((rows, width), F32),
+                pltpu.VMEM((rows, 3 * width), BF16),
+                pltpu.VMEM((rows, width), F32),
+                pltpu.VMEM((width, wide), BF16),
+                pltpu.VMEM((128, width), F32),
+            ],
+        ),
+        out_shape=[
+            jax.ShapeDtypeStruct((imgs, seq // 2, width), BF16),
+            jax.ShapeDtypeStruct((imgs, seq // 2, width), BF16),
+            jax.ShapeDtypeStruct((width // 2, wide), BF16),
+            jax.ShapeDtypeStruct((width // 2, wide), BF16),
+        ],
+        compiler_params=pltpu.CompilerParams(vmem_limit_bytes=32 << 20),
+        cost_estimate=BRIEF,
+        name="attend_back",
+    )(meta, *dins, ids, dy, mid, routed, wr, g2, mix, wout, probs, qkv, x, normed, wqkv, g1)
+
+
+def shared_kernel(meta_ref, mine_ref, recv_ref, gqkv_ref, gout_ref, small_ref, all_s):
+    upper, wide = mine_ref.shape
+    width = 2 * upper
+    part = width // SHARES
+    all_s[0:upper, :] = mine_ref[...]
+    all_s[upper:width, :] = recv_ref[...]
+    for i in range(SHARES):
+        there = pl.multiple_of((i ^ meta_ref[2]) * part, part)
+        value = all_s[pl.ds(there, part), :].astype(F32)
+        at = i * part
+        gqkv_ref[at : at + part, :] = value[:, : 3 * width]
+        gout_ref[at : at + part, :] = value[:, 3 * width : 4 * width]
+        small_ref[at : at + part, :] = value[:, 4 * width :]
+
+
+def finish_shared(meta, mine, recv):
+    upper, wide = mine.shape
+    width = 2 * upper
+    fix = lambda *s: pl.BlockSpec(s, lambda i, m: (0,) * len(s))
+    return pl.pallas_call(
+        shared_kernel,
+        grid_spec=pltpu.PrefetchScalarGridSpec(
+            num_scalar_prefetch=1,
+            grid=(1,),
+            in_specs=[fix(upper, wide), fix(upper, wide)],
+            out_specs=[fix(width, 3 * width), fix(width, width), fix(width, wide - 4 * width)],
+            scratch_shapes=[pltpu.VMEM((width, wide), BF16)],
+        ),
+        out_shape=[
+            jax.ShapeDtypeStruct((width, 3 * width), F32),
+            jax.ShapeDtypeStruct((width, width), F32),
+            jax.ShapeDtypeStruct((width, wide - 4 * width), F32),
+        ],
+        compiler_params=pltpu.CompilerParams(vmem_limit_bytes=16 << 20),
+        cost_estimate=BRIEF,
+        name="finish_shared",
+    )(meta, mine, recv)
+
+
+def combine_kernel(meta_ref, mid_ref, a_ref, b_ref, own_ref, other_ref, s_ref):
+    s_ref[...] = mid_ref[...] + (a_ref[...].astype(F32) + b_ref[...].astype(F32))
+    split_halves(meta_ref[3], s_ref, own_ref, other_ref)
+
+
+def combine(meta, mid, parts, imgs):
+    rows, width = mid.shape
+    seq = rows // imgs
+    spec = pl.BlockSpec((seq, width), lambda i, m: (i, 0))
+    out = pl.BlockSpec((1, seq // 2, width), lambda i, m: (i, 0, 0))
+    shape = jax.ShapeDtypeStruct((imgs, seq // 2, width), BF16)
+    return pl.pallas_call(
+        combine_kernel,
+        grid_spec=pltpu.PrefetchScalarGridSpec(
+            num_scalar_prefetch=1,
+            grid=(imgs,),
+            in_specs=[spec] * 3,
+            out_specs=[out, out],
+            scratch_shapes=[pltpu.VMEM((seq, width), F32)],
+        ),
+        out_shape=[shape, shape],
+        cost_estimate=BRIEF,
+        name="combine",
+    )(meta, mid, *parts)
+
+
+def place_kernel(meta_ref, a_own_ref, a_recv_ref, b_own_ref, b_recv_ref, a_ref, b_ref):
+    imgs = pl.num_programs(0) // 2
+    mine = pl.program_id(0) // imgs == meta_ref[3]
+    a_ref[...] = jnp.where(mine, a_own_ref[...], a_recv_ref[...])
+    b_ref[...] = jnp.where(mine, b_own_ref[...], b_recv_ref[...])
+
+
+def place(meta, *arrays):
+    imgs, half, width = arrays[0].shape
+    spec = pl.BlockSpec((1, half, width), lambda j, m: (j % imgs, 0, 0))
+    out = pl.BlockSpec((1, half, width), lambda j, m: (j, 0, 0))
+    shape = jax.ShapeDtypeStruct((2 * imgs, half, width), BF16)
+    return pl.pallas_call(
+        place_kernel,
+        grid_spec=pltpu.PrefetchScalarGridSpec(
+            num_scalar_prefetch=1, grid=(2 * imgs,), in_specs=[spec] * 4, out_specs=[out, out]
+        ),
+        out_shape=[shape, shape],
+        cost_estimate=BRIEF,
+        name="place",
+    )(meta, *arrays)
+
+
+SWAP = [(0, 1), (1, 0)]
+
+
+def xor(k, n=4):
+    return [(i, i ^ k) for i in range(n)]
+
+
+def send(value, axis, pairs):
+    return lax.ppermute(value, axis, pairs)
+
+
+def add_low(a, b):
+    return (a.astype(F32) + b.astype(F32)).astype(BF16)
+
+
+def after(value, *earlier):
+    return lax.optimization_barrier((value, *earlier))[0]
+
+
+def tie(*values):
+    return lax.optimization_barrier(values)
+
+
+def fan(value, axis):
+    rows = value.shape[0] // 4
+    return [send(value[k * rows : (k + 1) * rows], axis, xor(k)) for k in (1, 2, 3)]
+
+
+def add_fan(value, got):
+    total = value[: value.shape[0] // 4].astype(F32)
+    for v in got:
+        total = total + v.astype(F32)
+    return total.astype(BF16)
+
+
+def dense_shards(
+    tokens, gain_one, w_qkv, w_out, gain_two, w_router, w_in, w_back, route_ids, key_mask, cotangent
+):
+    nimg, half, width = tokens.shape
+    imgs = nimg // 2
+    rows = imgs * 2 * half
+    experts = w_router.shape[1]
+    piece = w_in.shape[2] // PIECES
+    core = lax.axis_index("ctx")
+    z = lax.axis_index("expert")
+    me = core * 4 + lax.axis_index("dp")
+    meta = jnp.stack([z, me, me * 4 + z, core]).astype(jnp.int32)
+    meta_pair = jnp.stack([z ^ 1, me, me * 4 + z, core]).astype(jnp.int32)
+    far = lambda v: send(v, "expert", xor(2))
+    swap = lambda v: send(v, "ctx", SWAP)
+
+    codes = route_ids.reshape(nimg, half, TOP)
+    codes = codes[..., 0] + experts * codes[..., 1]
+    tok_other, dy_other, codes_other = swap(tokens), swap(cotangent), swap(codes)
+    mine_in = lax.dynamic_slice_in_dim(w_in[0], me * piece, piece, 1)
+    mine_back = lax.dynamic_slice_in_dim(w_back[0], me * piece, piece, 0)
+    pack = jnp.stack([mine_in[:piece], mine_in[piece:], mine_back[:, :piece], mine_back[:, piece:]])
+    first = jnp.where(core == 0, codes, codes_other)
+    second = jnp.where(core == 0, codes_other, codes)
+    codes = lax.dynamic_slice_in_dim(jnp.concatenate([first, second], 1), core * imgs, imgs, 0)
+    codes = codes.reshape(1, rows)
+    ids = jnp.concatenate([codes % experts, codes // experts], 0)
+    wide = jnp.pad(ids, ((0, 0), (0, 2 * width - rows))).reshape(TOP, 2, width)
+    ids_pack = jnp.concatenate([wide[:, 0], wide[:, 1]], 0).astype(BF16)
+    ids_pack = jnp.pad(ids_pack, ((padded(rows) - rows, 12), (0, 0)))
+    wr = jnp.pad(w_router.T, ((0, 16 - experts), (0, 0)))
+    g1, g2 = gain_one[None, :], gain_two[None, :]
+
+    pack, far_raw = send(pack, "expert", xor(1)), far(cotangent)
+    x_rows, dy, normed, qkv, probs, mix, mid, routed = attend(
+        meta, tokens, tok_other, cotangent, dy_other, key_mask, g1, w_qkv, w_out, g2
+    )
+    own_one = expert(meta, routed, dy, ids, wr, (w_in, w_back))
+    far_rows = jnp.concatenate([routed, ids_pack], 0)
+    pack, far_raw, far_rows, own_din = tie(pack, far_raw, far_rows, own_one[4])
+    own_one = [*own_one[:4], own_din]
+
+    packs = [pack] + [send(pack, "dp", xor(k)) for k in (1, 2, 3)]
+    far_other = swap(far_raw)
+    *packs, far_rows, far_other = tie(*packs, far(far_rows), far_other)
+
+    packs = jnp.stack(packs)
+    far_dy = assemble(meta, far_raw, far_other)
+    far_one = expert(meta, far_rows, far_dy, far_rows, wr, (w_in, w_back))
+    packs_other, far_din = tie(swap(packs), far_one[4])
+    pair = (packs, packs_other)
+    far_two = expert(meta_pair, far_rows, far_dy, far_rows, wr, pair, [far_one[3], far_din])
+
+    far_din, far_made = tie(far_two[4], far_two[3])
+    own_two = expert(meta_pair, routed, dy, ids, wr, pair, [own_one[3], after(own_one[4], far_din)])
+    sides = [list(zip(own_one[:3], far_one[:3])), list(zip(own_two[:3], far_two[:3]))]
+    grads = weight_grads([routed, far_rows], sides)
+    din_far, *grads = tie(far(far_din), *grads)
+
+    a, a_give, b, b_give = grads
+    a, b = tie(add_low(a, swap(a_give)), add_low(b, swap(b_give)))
+
+    y_way, x_way = ("dp", xor(2)), ("dp", xor(1))
+    a_got, b_got = send(a[:, 2:], *y_way), send(b[:, 1::2], *x_way)
+    far_made = far(after(far_made, din_far))
+    tok_own, tok_give, shared, shared_give = attend_back(
+        meta, [after(own_two[4], a, b), din_far], ids, dy, mid, routed, wr, g2, mix, w_out, probs, qkv, x_rows, normed, w_qkv, g1
+    )
+    a, b, far_made, shared, shared_give, tok_give = tie(
+        add_low(a[:, :2], a_got), add_low(b[:, 0::2], b_got), far_made, shared, shared_give, tok_give
+    )
+    others = lambda v, axis: [send(v, axis, xor(k)) for k in (1, 2, 3)]
+    mix_own, mix_give = combine(meta, mid, [own_two[3], far_made], imgs)
+    a, b, shared, tok_got, mix_give = tie(
+        add_low(a[:, :1], send(a[:, 1:], *x_way)),
+        add_low(b[:, :1], send(b[:, 1:], *y_way)),
+        add_low(shared, swap(shared_give)),
+        swap(tok_give),
+        mix_give,
+    )
+    a, b, shared = tie(
+        add_low(a[0], send(a[1], "expert", xor(1))),
+        add_low(b[0], send(b[1], "expert", xor(1))),
+        add_fan(shared, fan(shared, "dp")),
+    )
+    a, b, shared = tie(
+        jnp.concatenate([a, send(a, *x_way)], 0),
+        jnp.stack([b, send(b, *y_way)], 0),
+        add_fan(shared, fan(shared, "expert")),
+    )
+    a, b, shared = tie(
+        jnp.concatenate([a, send(a, *y_way)], 0),
+        jnp.concatenate([b, send(b, *x_way)], 1).reshape(4, piece, width),
+        jnp.concatenate([shared] + others(shared, "expert"), 0),
+    )
+    a_other, b_other, shared = tie(
+        swap(a), swap(b), jnp.concatenate([shared] + others(shared, "dp"), 0)
+    )
+    shared_other, mix_got = swap(shared), swap(mix_give)
+    grad_in, grad_back = finish_expert(meta, a, a_other, b, b_other)
+    mixed, grad_tokens = place(meta, mix_own, mix_got, tok_own, tok_got)
+    grad_qkv, grad_out, small = finish_shared(meta, shared, shared_other)
+    return (
+        mixed,
+        grad_tokens,
+        small[:, 17],
+        grad_qkv,
+        grad_out,
+        small[:, 16],
+        small[:, :experts],
+        grad_in,
+        grad_back,
+    )
 
 
 def norm_rows(value, gain):
@@ -242,8 +1044,10 @@
         P(("dp", "expert"), None),
         P(("dp", "expert"), "ctx", None),
     )
+    sizes = dict(mesh.shape)
+    dense = sizes == {"dp": 4, "ctx": 2, "expert": 4}
     return jax.shard_map(
-        shards,
+        dense_shards if dense else shards,
         mesh=mesh,
         in_specs=placed,
         out_specs=(

time: 716 us -> 280 us (0.39)
  waiting for transfers between devices: 287 us -> 98.4 us
  local copies, waits for them, and re-layouts: 160 us -> 24.4 us
  matrix products: 112 us -> 0 us
  Pallas kernels: 0 us -> 105 us
  other arithmetic: 78.6 us -> 9.6 us
  blocking collectives: 39.9 us -> 0 us
  starting transfers between devices: 19.4 us -> 39.6 us
  between operations: 15.3 us -> 1.38 us
    psum x2 -> x0, waiting for transfers between devices: 163 us -> none  [the longest x1 95.4 us: shards(): lax.psum((grad_gain_one, grad_qkv, grad_out, grad_gain_two, grad_router),...]
    all_to_all x4 -> x0, waiting for transfers between devices: 121 us -> none  [the longest x1 44.2 us: forward(): lax.all_to_all(buffer, 'expert', split_axis=0, concat_axis=1, tiled=True)]
    dot_general x20 -> x0, matrix products: 105 us -> none  [the longest x1 24.4 us: forward(): jnp.einsum('erd,edf->erf', arrived, w_in, preferred_element_type=jnp.floa...]
    pallas_call x0 -> x12, Pallas kernels: none -> 105 us  [the longest x4 42.9 us: expert(): pl.pallas_call(functools.partial(expert_kernel, prev is not None, local),...]
    ppermute x0 -> x43, waiting for transfers between devices: none -> 98.4 us  [send(): return lax.ppermute(value, axis, pairs)]
    convert_element_type x16 -> x0, local copies, waits for them, and re-layouts: 71.3 us -> none  [the longest x1 21.7 us: shards(): jnp.einsum('erf,edf->erd', d_pre, w_in, preferred_element_type=jnp.float32)]
    psum x1 -> x0, blocking collectives: 39.9 us -> none  [shards(): lax.psum((grad_gain_one, grad_qkv, grad_out, grad_gain_two, grad_router),...]
    ppermute x0 -> x43, starting transfers between devices: none -> 39.6 us  [send(): return lax.ppermute(value, axis, pairs)]
  transfers between devices with their start and end apart: 9 -> 43, of which waited for: 7 -> 25; matrix products, arithmetic and copies ran while one was open for 25% -> 4% of each run, Pallas kernels for 0% -> 32%
where the time goes in v2:
time: 280 us; the launch traced here: 279 us
  Pallas kernels  105 us (38%)
  waiting for transfers between devices  98.4 us (35%)
  starting transfers between devices  39.6 us (14%)
  local copies, waits for them, and re-layouts  24.4 us (9%)
  other arithmetic  9.6 us (3%)
    ppermute x43, waiting for transfers between devices, send(): return lax.ppermute(value, axis, pairs)  98.4 us
    pallas_call x4, Pallas kernels, expert(): pl.pallas_call(functools.partial(expert_kernel, prev is not None, local),...  42.9 us
    ppermute x43, starting transfers between devices, send(): return lax.ppermute(value, axis, pairs)  39.6 us
    unnamed x106, local copies, waits for them, and re-layouts  19.4 us
    pallas_call x1, Pallas kernels, weight_grads(): pl.pallas_call(functools.partial(weight_kernel, n), grid=(2, steps), in_s...  18 us
    pallas_call x1, Pallas kernels, attend_back(): pl.pallas_call(back_kernel, grid_spec=pltpu.PrefetchScalarGridSpec(num_sc...  13.4 us
    pallas_call x1, Pallas kernels, attend(): pl.pallas_call(attend_kernel, grid_spec=pltpu.PrefetchScalarGridSpec(num_...  9.01 us
    convert_element_type x9, other arithmetic, add_low(): return (a.astype(F32) + b.astype(F32)).astype(BF16)  5.79 us
  transfers between devices with their start and end apart: 43, of which 25 were waited for; matrix products, arithmetic and copies ran while one was open for 4% of the time, Pallas kernels for 32%

profile of v2, /device:TPU:0, one launch (start us, length us, event | category | flops | bytes accessed | tf_op | source)
XLA Modules:
  0.0 278.6 jit_solution(12001244981913410071)
XLA Ops:
  1.2 3.7 %collective-permute-start.4 = (bf16[6,100,512]{2,1,0:T(8,128)(2,1)}, bf16[6,100,512]{2,1,0:T(8,128)(2,1)}, u32[]{:S(2)}, u32[]{:S(2)}) collective-permute-start(bf16[6,100,512]{2,1,0:T(8,128)(2,1)} %dyown_ref.1), channel_id=1, source_target_pairs={{0,2},{1,3},{2,0},{3,1},{4,6},{5,7},{6,4},{7,5},{8,10},{9,11},{10,... | collective-permute-start | bytes 1843208 | tf_op jit(solution)/shard_map/ppermute | solution.py:671
  8.8 1.6 collective-permute-start.3
  10.8 1.7 collective-permute-done.other_ref
  15.6 9.0 %attend.1 = (bf16[600,512]{1,0:T(8,128)(2,1)}, bf16[600,512]{1,0:T(8,128)(2,1)S(1)}, bf16[600,512]{1,0:T(8,128)(2,1)}, bf16[600,1536]{1,0:T(8,128)(2,1)}, bf16[3...) custom-call(s32[4]{0:T(128)S(1)} %get-tuple-element.229.meta_ref, ...), custom_call_target="tpu_custom_call" | custom-call | flops 1 | bytes 1 | tf_op jit(solution)/shard_map/attend/pallas_call | solution.py:116
  24.6 10.1 %expert.4 = (bf16[600,2048]{1,0:T(8,128)(2,1)S(1)}, bf16[600,2048]{1,0:T(8,128)(2,1)S(1)}, bf16[600,512]{1,0:T(8,128)(2,1)S(1)}, bf16[600,512]{1,0:T(8,128)(2,1)S(1)}, bf16[640,512]{1,0:T(8,128)(2,1)S(1)}) custom-call(s32[4]{0:T(128)S(1)} %get-tuple-element.229.meta_ref, bf16[600,512]{1,0:T(8,128)(2,1)S(1)} %get-tuple-element.102.rows_ref.refs_0_.routed_ref, ...), custom_call_target="tpu_custom_call" | custom-call | flops 1 | bytes 1 | tf_op jit(solution)/shard_map/expert/pallas_call | solution.py:310
  37.8 2.4 collective-permute-start.7
  41.3 12.4 %collective-permute-done.7 = bf16[4,256,256]{2,1,0:T(8,128)(2,1)S(1)} collective-permute-done((bf16[4,256,256]{2,1,0:T(8,128)(2,1)}, bf16[4,256,256]{2,1,0:T(8,128)(2,1)S(1)}, u32[]{:S(2)}, u32[]{:S(2)}) %collective-permute-start.7) | collective-permute-done | bytes 524320 | tf_op jit(solution)/shard_map/ppermute | solution.py:671
  53.7 10.8 %collective-permute-done.6 = bf16[4,256,256]{2,1,0:T(8,128)(2,1)S(1)} collective-permute-done((bf16[4,256,256]{2,1,0:T(8,128)(2,1)}, bf16[4,256,256]{2,1,0:T(8,128)(2,1)S(1)}, u32[]{:S(2)}, u32[]{:S(2)}) %collective-permute-start.6) | collective-permute-done | bytes 524320 | tf_op jit(solution)/shard_map/ppermute | solution.py:671
  64.6 3.7 %collective-permute-done.8.rows_ref.ids_ref.refs_1_ = bf16[624,512]{1,0:T(8,128)(2,1)S(1)} collective-permute-done((bf16[624,512]{1,0:T(8,128)(2,1)S(1)}, bf16[624,512]{1,0:T(8,128)(2,1)S(1)}, u32[]{:S(2)}, u32[]{:S(2)}) %collective-permute-start.8) | collective-permute-done | bytes 639008 | tf_op jit(solution)/shard_map/ppermute | solution.py:671
  69.7 3.6 %assemble.1.dy_ref = bf16[600,512]{1,0:T(8,128)(2,1)} custom-call(s32[4]{0:T(128)} %copy-done.39, bf16[6,100,512]{2,1,0:T(8,128)(2,1)} %collective-permute-done.4.own_ref, bf16[6,100,512]{2,1,0:T(8,128)(2,1)} %copy-done.47), custom_call_target="tpu_custom_call" | custom-call | flops 1 | bytes 1 | tf_op jit(solution)/shard_map/assemble/pallas_call | solution.py:163
  73.3 1.6 copy-done.1
  74.9 1.6 copy-done.3
  77.5 9.9 %expert.5 = (bf16[600,2048]{1,0:T(8,128)(2,1)S(1)}, bf16[600,2048]{1,0:T(8,128)(2,1)S(1)}, bf16[600,512]{1,0:T(8,128)(2,1)S(1)}, bf16[600,512]{1,0:T(8,128)(2,1)S(1)}, bf16[640,512]{1,0:T(8,128)(2,1)S(1)}) custom-call(s32[4]{0:T(128)S(1)} %copy-done.40, bf16[624,512]{1,0:T(8,128)(2,1)S(1)} %collective-permute-done.8.rows_ref.ids_ref.refs_1_, ...), custom_call_target="tpu_custom_call" | custom-call | flops 1 | bytes 1 | tf_op jit(solution)/shard_map/expert/pallas_call | solution.py:310
  87.5 11.2 %expert.6 = (bf16[600,2048]{1,0:T(8,128)(2,1)S(1)}, bf16[600,2048]{1,0:T(8,128)(2,1)S(1)}, bf16[600,512]{1,0:T(8,128)(2,1)S(1)}, bf16[600,512]{1,0:T(8,128)(2,1)S(1)}, bf16[640,512]{1,0:T(8,128)(2,1)S(1)}) custom-call(s32[4]{0:T(128)S(1)} %get-tuple-element.230.meta_ref, bf16[624,512]{1,0:T(8,128)(2,1)S(1)} %collective-permute-done.8.rows_ref.ids_ref.refs_1_, ...), custom_call_target="tpu_custom_call" | custom-call | flops 1 | bytes 1 | tf_op jit(solution)/shard_map/expert/pallas_call | solution.py:310
  98.7 1.4 copy-done.15
  100.2 11.8 %expert.7 = (bf16[600,2048]{1,0:T(8,128)(2,1)S(1)}, bf16[600,2048]{1,0:T(8,128)(2,1)S(1)}, bf16[600,512]{1,0:T(8,128)(2,1)S(1)}, bf16[600,512]{1,0:T(8,128)(2,1)S(1)}, bf16[640,512]{1,0:T(8,128)(2,1)S(1)}) custom-call(s32[4]{0:T(128)S(1)} %get-tuple-element.230.meta_ref, bf16[600,512]{1,0:T(8,128)(2,1)S(1)} %get-tuple-element.102.rows_ref.refs_0_.routed_ref, ...), custom_call_target="tpu_custom_call" | custom-call | flops 1 | bytes 1 | tf_op jit(solution)/shard_map/expert/pallas_call | solution.py:310
  112.0 1.4 copy-done.16
  114.3 18.0 %weight_grads.1 = (bf16[2,4,256,512]{3,2,1,0:T(8,128)(2,1)S(1)}, bf16[2,4,256,512]{3,2,1,0:T(8,128)(2,1)S(1)}, bf16[2,4,256,512]{3,2,1,0:T(8,128)(2,1)S(1)}, bf16[2,4,256,512]{3,2,1,0:T(8,128)(2,1)S(1)}) custom-call(bf16[600,512]{1,0:T(8,128)(2,1)S(1)} %get-tuple-element.102.rows_ref.refs_0_.routed_ref, ...), custom_call_target="tpu_custom_call" | custom-call | flops 1 | bytes 1 | tf_op jit(solution)/shard_map/weight_grads/pallas_call | solution.py:391
  132.9 3.7 %collective-permute-done.12 = bf16[2,4,256,512]{3,2,1,0:T(8,128)(2,1)S(1)} collective-permute-done((bf16[2,4,256,512]{3,2,1,0:T(8,128)(2,1)S(1)}, bf16[2,4,256,512]{3,2,1,0:T(8,128)(2,1)S(1)}, u32[]{:S(2)}, u32[]{:S(2)}) %collective-permute-start.12) | collective-permute-done | bytes 2097184 | tf_op jit(solution)/shard_map/ppermute | solution.py:671
  137.2 2.4 collective-permute-done.13
  140.4 1.6 collective-permute-start.15
  142.0 1.6 collective-permute-start.14
  143.6 2.8 %collective-permute-start.16 = (bf16[600,512]{1,0:T(8,128)(2,1)S(1)}, bf16[600,512]{1,0:T(8,128)(2,1)S(1)}, u32[]{:S(2)}, u32[]{:S(2)}) collective-permute-start(bf16[600,512]{1,0:T(8,128)(2,1)S(1)} %get-tuple-element.149), channel_id=1, source_target_pairs={{0,2},{1,3},{2,0},{3,1},{4,6},{5,7},{6,4},{7,5},{8,10},{9,11},{10,... | collective-permute-start | bytes 1843208 | tf_op jit(solution)/shard_map/ppermute | solution.py:671
  146.4 13.4 %attend_back.1 = (bf16[3,100,512]{2,1,0:T(8,128)(2,1)S(1)}, bf16[3,100,512]{2,1,0:T(8,128)(2,1)}, bf16[256,2176]{1,0:T(8,128)(2,1)S(1)}, bf16[256,2176]{1,0:T(8,128)(2,1)}) custom-call(s32[4]{0:T(128)S(1)} %copy-done.40, bf16[640,512]{1,0:T(8,128)(2,1)S(1)} %get-tuple-element.151.din0_ref, bf16[640,512]{1,0:T(8,128)(2,1)S(1)} %collective-permute-done.11.din1_ref, ...), custom_call_target="tpu_custom_call" | custom-call | flops 1 | bytes 1 | tf_op jit(solution)/shard_map/attend_back/pallas_call | solution.py:538
  159.8 6.0 %collective-permute-done.15 = bf16[2,2,256,512]{3,2,1,0:T(8,128)(2,1)S(1)} collective-permute-done((bf16[2,2,256,512]{3,2,1,0:T(8,128)(2,1)S(1)}, bf16[2,2,256,512]{3,2,1,0:T(8,128)(2,1)S(1)}, u32[]{:S(2)}, u32[]{:S(2)}) %collective-permute-start.15) | collective-permute-done | bytes 1048608 | tf_op jit(solution)/shard_map/ppermute | solution.py:671
  167.5 5.7 %collective-permute-done.16.b_ref = bf16[600,512]{1,0:T(8,128)(2,1)S(1)} collective-permute-done((bf16[600,512]{1,0:T(8,128)(2,1)S(1)}, bf16[600,512]{1,0:T(8,128)(2,1)S(1)}, u32[]{:S(2)}, u32[]{:S(2)}) %collective-permute-start.16) | collective-permute-done | bytes 614432 | tf_op jit(solution)/shard_map/ppermute | solution.py:671
  176.0 4.2 %combine.1 = (bf16[3,100,512]{2,1,0:T(8,128)(2,1)}, bf16[3,100,512]{2,1,0:T(8,128)(2,1)}) custom-call(s32[4]{0:T(128)} %copy-done.39, f32[600,512]{1,0:T(8,128)} %get-tuple-element.101.mid_ref, bf16[600,512]{1,0:T(8,128)(2,1)} %copy-done.32, bf16[600,512]{1,0:T(8,128)(2,1)} %copy-done.48), custom_call_target="tpu_custom_call" | custom-call | flops 1 | bytes 1 | tf_op jit(solution)/shard_map/combine/pallas_call | solution.py:625
  180.1 8.6 %collective-permute-done.18 = bf16[2,1,256,512]{3,2,1,0:T(8,128)(2,1)} collective-permute-done((bf16[2,1,256,512]{3,2,1,0:T(8,128)(2,1)}, bf16[2,1,256,512]{3,2,1,0:T(8,128)(2,1)}, u32[]{:S(2)}, u32[]{:S(2)}) %collective-permute-start.18) | collective-permute-done | bytes 524320 | tf_op jit(solution)/shard_map/ppermute | solution.py:671
  191.1 1.5 add_convert_fusion.2
  192.7 2.0 collective-permute-start.22
  195.4 2.3 collective-permute-start.26
  198.4 3.6 %collective-permute-done.23 = bf16[1,256,512]{2,1,0:T(8,128)(2,1)S(1)} collective-permute-done((bf16[1,256,512]{2,1,0:T(8,128)(2,1)S(1)}, bf16[1,256,512]{2,1,0:T(8,128)(2,1)S(1)}, u32[]{:S(2)}, u32[]{:S(2)}) %collective-permute-start.23) | collective-permute-done | bytes 262176 | tf_op jit(solution)/shard_map/ppermute | solution.py:671
  202.0 4.2 %collective-permute-done.22 = bf16[1,256,512]{2,1,0:T(8,128)(2,1)S(1)} collective-permute-done((bf16[1,256,512]{2,1,0:T(8,128)(2,1)S(1)}, bf16[1,256,512]{2,1,0:T(8,128)(2,1)S(1)}, u32[]{:S(2)}, u32[]{:S(2)}) %collective-permute-start.22) | collective-permute-done | bytes 262176 | tf_op jit(solution)/shard_map/ppermute | solution.py:671
  206.3 2.8 %collective-permute-done.26 = bf16[64,2176]{1,0:T(8,128)(2,1)S(1)} collective-permute-done((bf16[64,2176]{1,0:T(8,128)(2,1)S(1)}, bf16[64,2176]{1,0:T(8,128)(2,1)S(1)}, u32[]{:S(2)}, u32[]{:S(2)}) %collective-permute-start.26) | collective-permute-done | bytes 278560 | tf_op jit(solution)/shard_map/ppermute | solution.py:671
  211.8 2.4 collective-permute-start.30
  215.7 1.6 collective-permute-done.31
  217.3 1.4 collective-permute-done.30
  218.8 5.2 %collective-permute-done.28 = bf16[1,256,512]{2,1,0:T(8,128)(2,1)S(1)} collective-permute-done((bf16[1,256,512]{2,1,0:T(8,128)(2,1)S(1)}, bf16[1,256,512]{2,1,0:T(8,128)(2,1)S(1)}, u32[]{:S(2)}, u32[]{:S(2)}) %collective-permute-start.28) | collective-permute-done | bytes 262176 | tf_op jit(solution)/shard_map/ppermute | solution.py:671
  225.3 2.2 collective-permute-start.35
  227.5 1.9 collective-permute-start.34
  233.4 5.2 %collective-permute-done.33 = bf16[2,1,256,512]{3,2,1,0:T(8,128)(2,1)S(1)} collective-permute-done((bf16[2,1,256,512]{3,2,1,0:T(8,128)(2,1)S(1)}, bf16[2,1,256,512]{3,2,1,0:T(8,128)(2,1)S(1)}, u32[]{:S(2)}, u32[]{:S(2)}) %collective-permute-start.33) | collective-permute-done | bytes 524320 | tf_op jit(solution)/shard_map/ppermute | solution.py:671
  239.3 2.0 collective-permute-start.41
  242.8 7.0 %collective-permute-done.41 = bf16[64,2176]{1,0:T(8,128)(2,1)S(1)} collective-permute-done((bf16[64,2176]{1,0:T(8,128)(2,1)S(1)}, bf16[64,2176]{1,0:T(8,128)(2,1)S(1)}, u32[]{:S(2)}, u32[]{:S(2)}) %collective-permute-start.41) | collective-permute-done | bytes 278560 | tf_op jit(solution)/shard_map/ppermute | solution.py:671
  249.7 5.1 %collective-permute-done.40 = bf16[64,2176]{1,0:T(8,128)(2,1)S(1)} collective-permute-done((bf16[64,2176]{1,0:T(8,128)(2,1)S(1)}, bf16[64,2176]{1,0:T(8,128)(2,1)S(1)}, u32[]{:S(2)}, u32[]{:S(2)}) %collective-permute-start.40) | collective-permute-done | bytes 278560 | tf_op jit(solution)/shard_map/ppermute | solution.py:671
  257.3 2.3 collective-permute-done.21.a_recv_ref
  260.4 5.4 %place.1 = (bf16[6,100,512]{2,1,0:T(8,128)(2,1)}, bf16[6,100,512]{2,1,0:T(8,128)(2,1)}) custom-call(s32[4]{0:T(128)} %copy-done.39, bf16[3,100,512]{2,1,0:T(8,128)(2,1)} %get-tuple-element.161.a_own_ref, bf16[3,100,512]{2,1,0:T(8,128)(2,1)} %copy-done.49, bf16[3,100,512]{2,1,0:T(8,128)(2,1)} %copy-done.38, ...), custom_call_target="tpu_custom_call" | custom-call | flops 1 | bytes 1 | tf_op jit(solution)/shard_map/place/pallas_call | solution.py:652
  268.3 4.4 %finish_expert.1 = (f32[1,512,2048]{2,1,0:T(8,128)}, f32[1,2048,512]{2,1,0:T(8,128)}) custom-call(s32[4]{0:T(128)S(1)} %copy-done.41, bf16[4,256,512]{2,1,0:T(8,128)(2,1)S(1)} %pad_maximum_fusion.2.im_ref, bf16[4,256,512]{2,1,0:T(8,128)(2,1)S(1)} %copy-done.21, bf16[4,256,512]{2,1,0:T(8,128)(2,1)S(1)} %bitcast.46, bf16[4,256,512]{2,1,0:T(8,128)(2,1)S(1)} %copy-done.23), custom_call_target="tpu_custom_call" | custom-call | flops 1 | bytes 1 | tf_op jit(solution)/shard_map/finish_expert/pallas_call | solution.py:424
  272.7 4.2 %finish_shared.1 = (f32[512,1536]{1,0:T(8,128)}, f32[512,512]{1,0:T(8,128)}, f32[512,128]{1,0:T(8,128)S(1)}) custom-call(s32[4]{0:T(128)S(1)} %copy-done.41, bf16[256,2176]{1,0:T(8,128)(2,1)S(1)} %pad_maximum_fusion.1.mine_ref, bf16[256,2176]{1,0:T(8,128)(2,1)} %collective-permute-done.42.recv_ref), custom_call_target="tpu_custom_call" | custom-call | flops 1 | bytes 1 | tf_op jit(solution)/shard_map/finish_shared/pallas_call | solution.py:594
  (200 shorter events, 44.8 us)
Async XLA Ops:
  0.7 11.8 %collective-permute-start.1 = (bf16[6,100,512]{2,1,0:T(8,128)(2,1)}, bf16[6,100,512]{2,1,0:T(8,128)(2,1)S(1)}, u32[]{:S(2)}, u32[]{:S(2)}) collective-permute-start(bf16[6,100,512]{2,1,0:T(8,128)(2,1)} %dyown_ref.1), channel_id=1, source_target_pairs={{0,4},{4,0},{1,5},{5,1},{2,6},{6,2},{3,7},{7,3},{8,12},{12,8},{9,1... | collective-permute-start | bytes 1843208 | tf_op jit(solution)/shard_map/ppermute | solution.py:671
  1.2 36.1 %collective-permute-start.4 = (bf16[6,100,512]{2,1,0:T(8,128)(2,1)}, bf16[6,100,512]{2,1,0:T(8,128)(2,1)}, u32[]{:S(2)}, u32[]{:S(2)}) collective-permute-start(bf16[6,100,512]{2,1,0:T(8,128)(2,1)} %dyown_ref.1), channel_id=1, source_target_pairs={{0,2},{1,3},{2,0},{3,1},{4,6},{5,7},{6,4},{7,5},{8,10},{9,11},{10,... | collective-permute-start | bytes 1843208 | tf_op jit(solution)/shard_map/ppermute | solution.py:671
  5.7 4.8 %collective-permute-start.2 = (s32[6,100]{1,0:T(8,128)S(1)}, s32[6,100]{1,0:T(8,128)S(1)}, u32[]{:S(2)}, u32[]{:S(2)}) collective-permute-start(s32[6,100]{1,0:T(8,128)S(1)} %bitcast.59), channel_id=1, source_target_pairs={{0,4},{4,0},{1,5},{5,1},{2,6},{6,2},{3,7},{7,3},{8,12},{12,8},{9,1... | collective-permute-start | bytes 7208 | tf_op jit(solution)/shard_map/ppermute | solution.py:671
  8.8 28.5 %collective-permute-start.3 = (bf16[4,256,256]{2,1,0:T(8,128)(2,1)}, bf16[4,256,256]{2,1,0:T(8,128)(2,1)}, u32[]{:S(2)}, u32[]{:S(2)}) collective-permute-start(bf16[4,256,256]{2,1,0:T(8,128)(2,1)} %pad_maximum_fusion.5), channel_id=1, source_target_pairs={{0,1},{1,0},{2,3},{3,2},{4,5},{5,4},{6,7},{7,6},{8,9},{9,8},{10,11... | collective-permute-start | bytes 1572872 | tf_op jit(solution)/shard_map/ppermute | solution.py:671
  10.3 2.2 collective-permute-start
  37.2 32.4 %copy-start.11 = (bf16[600,2048]{1,0:T(8,128)(2,1)}, bf16[600,2048]{1,0:T(8,128)(2,1)S(1)}, u32[]{:S(2)}) copy-start(bf16[600,2048]{1,0:T(8,128)(2,1)S(1)} %get-tuple-element.125.refs_2_) | copy-start | bytes 7372804
  37.2 32.4 %copy-start.13 = (bf16[600,2048]{1,0:T(8,128)(2,1)}, bf16[600,2048]{1,0:T(8,128)(2,1)S(1)}, u32[]{:S(2)}) copy-start(bf16[600,2048]{1,0:T(8,128)(2,1)S(1)} %get-tuple-element.127.refs_4_) | copy-start | bytes 7372804
  37.3 31.0 %collective-permute-start.8 = (bf16[624,512]{1,0:T(8,128)(2,1)S(1)}, bf16[624,512]{1,0:T(8,128)(2,1)S(1)}, u32[]{:S(2)}, u32[]{:S(2)}) collective-permute-start(bf16[624,512]{1,0:T(8,128)(2,1)S(1)} %pad_maximum_fusion.4), channel_id=1, source_target_pairs={{0,2},{1,3},{2,0},{3,1},{4,6},{5,7},{6,4},{7,5},{8,10},{9,11},{10,... | collective-permute-start | bytes 1916936 | tf_op jit(solution)/shard_map/ppermute | solution.py:671
  37.8 26.8 %collective-permute-start.9 = (bf16[6,100,512]{2,1,0:T(8,128)(2,1)}, bf16[6,100,512]{2,1,0:T(8,128)(2,1)S(1)}, u32[]{:S(2)}, u32[]{:S(2)}) collective-permute-start(bf16[6,100,512]{2,1,0:T(8,128)(2,1)} %collective-permute-done.4.own_ref), channel_id=1, source_target_pairs={{0,4},{4,0},{1,5},{5,1},{2,6},{6,2},{3,7},{7,3},{8,12},{12,8},{9,1... | collective-permute-start | bytes 1843208 | tf_op jit(solution)/shard_map/ppermute | solution.py:671
  37.8 15.9 %collective-permute-start.7 = (bf16[4,256,256]{2,1,0:T(8,128)(2,1)}, bf16[4,256,256]{2,1,0:T(8,128)(2,1)S(1)}, u32[]{:S(2)}, u32[]{:S(2)}) collective-permute-start(bf16[4,256,256]{2,1,0:T(8,128)(2,1)} %collective-permute-done.3), channel_id=1, source_target_pairs={{0,24},{8,16},{16,8},{24,0},{1,25},{9,17},{17,9},{25,1},{2,26},{10... | collective-permute-start | bytes 1572872 | tf_op jit(solution)/shard_map/ppermute | solution.py:671
  40.3 24.2 %collective-permute-start.6 = (bf16[4,256,256]{2,1,0:T(8,128)(2,1)}, bf16[4,256,256]{2,1,0:T(8,128)(2,1)S(1)}, u32[]{:S(2)}, u32[]{:S(2)}) collective-permute-start(bf16[4,256,256]{2,1,0:T(8,128)(2,1)} %collective-permute-done.3), channel_id=1, source_target_pairs={{0,16},{8,24},{16,0},{24,8},{1,17},{9,25},{17,1},{25,9},{2,18},{10... | collective-permute-start | bytes 1572872 | tf_op jit(solution)/shard_map/ppermute | solution.py:671
  40.8 23.8 %collective-permute-start.5 = (bf16[4,256,256]{2,1,0:T(8,128)(2,1)}, bf16[4,256,256]{2,1,0:T(8,128)(2,1)S(1)}, u32[]{:S(2)}, u32[]{:S(2)}) collective-permute-start(bf16[4,256,256]{2,1,0:T(8,128)(2,1)} %collective-permute-done.3), channel_id=1, source_target_pairs={{0,8},{8,0},{16,24},{24,16},{1,9},{9,1},{17,25},{25,17},{2,10},{10... | collective-permute-start | bytes 1572872 | tf_op jit(solution)/shard_map/ppermute | solution.py:671
  69.6 17.8 %collective-permute-start.10 = (bf16[4,4,256,256]{3,2,1,0:T(8,128)(2,1)S(1)}, bf16[4,4,256,256]{3,2,1,0:T(8,128)(2,1)}, u32[]{:S(2)}, u32[]{:S(2)}) collective-permute-start(bf16[4,4,256,256]{3,2,1,0:T(8,128)(2,1)S(1)} %pad_maximum_fusion.rest_0_.rest_1_.rest_2_.rest_3_), channel_id=1, source_target_pairs={{0,4},{4,0},{1,5},{5,1},{2,6},{6,2},{3,7},{7,3},{8,12},{12,8},{9,1... | collective-permute-start | bytes 6291464 | tf_op jit(solution)/shard_map/ppermute | solution.py:671
  100.1 32.1 %collective-permute-start.11 = (bf16[640,512]{1,0:T(8,128)(2,1)S(1)}, bf16[640,512]{1,0:T(8,128)(2,1)S(1)}, u32[]{:S(2)}, u32[]{:S(2)}) collective-permute-start(bf16[640,512]{1,0:T(8,128)(2,1)S(1)} %get-tuple-element.122), channel_id=1, source_target_pairs={{0,2},{1,3},{2,0},{3,1},{4,6},{5,7},{6,4},{7,5},{8,10},{9,11},{10,... | collective-permute-start | bytes 1966088 | tf_op jit(solution)/shard_map/ppermute | solution.py:671
  132.3 4.3 %collective-permute-start.12 = (bf16[2,4,256,512]{3,2,1,0:T(8,128)(2,1)S(1)}, bf16[2,4,256,512]{3,2,1,0:T(8,128)(2,1)S(1)}, u32[]{:S(2)}, u32[]{:S(2)}) collective-permute-start(bf16[2,4,256,512]{3,2,1,0:T(8,128)(2,1)S(1)} %get-tuple-element.142), channel_id=1, source_target_pairs={{0,4},{4,0},{1,5},{5,1},{2,6},{6,2},{3,7},{7,3},{8,12},{12,8},{9,1... | collective-permute-start | bytes 6291464 | tf_op jit(solution)/shard_map/ppermute | solution.py:671
  132.8 6.8 %collective-permute-start.13 = (bf16[2,4,256,512]{3,2,1,0:T(8,128)(2,1)S(1)}, bf16[2,4,256,512]{3,2,1,0:T(8,128)(2,1)S(1)}, u32[]{:S(2)}, u32[]{:S(2)}) collective-permute-start(bf16[2,4,256,512]{3,2,1,0:T(8,128)(2,1)S(1)} %get-tuple-element.144), channel_id=1, source_target_pairs={{0,4},{4,0},{1,5},{5,1},{2,6},{6,2},{3,7},{7,3},{8,12},{12,8},{9,1... | collective-permute-start | bytes 6291464 | tf_op jit(solution)/shard_map/ppermute | solution.py:671
  140.4 25.5 %collective-permute-start.15 = (bf16[2,2,256,512]{3,2,1,0:T(8,128)(2,1)S(1)}, bf16[2,2,256,512]{3,2,1,0:T(8,128)(2,1)S(1)}, u32[]{:S(2)}, u32[]{:S(2)}) collective-permute-start(bf16[2,2,256,512]{3,2,1,0:T(8,128)(2,1)S(1)} %slice.108), channel_id=1, source_target_pairs={{0,8},{8,0},{16,24},{24,16},{1,9},{9,1},{17,25},{25,17},{2,10},{10... | collective-permute-start | bytes 3145736 | tf_op jit(solution)/shard_map/ppermute | solution.py:671
  142.0 25.2 %collective-permute-start.14 = (bf16[2,2,256,512]{3,2,1,0:T(8,128)(2,1)S(1)}, bf16[2,2,256,512]{3,2,1,0:T(8,128)(2,1)S(1)}, u32[]{:S(2)}, u32[]{:S(2)}) collective-permute-start(bf16[2,2,256,512]{3,2,1,0:T(8,128)(2,1)S(1)} %slice.106), channel_id=1, source_target_pairs={{0,16},{8,24},{16,0},{24,8},{1,17},{9,25},{17,1},{25,9},{2,18},{10... | collective-permute-start | bytes 3145736 | tf_op jit(solution)/shard_map/ppermute | solution.py:671
  143.6 29.6 %collective-permute-start.16 = (bf16[600,512]{1,0:T(8,128)(2,1)S(1)}, bf16[600,512]{1,0:T(8,128)(2,1)S(1)}, u32[]{:S(2)}, u32[]{:S(2)}) collective-permute-start(bf16[600,512]{1,0:T(8,128)(2,1)S(1)} %get-tuple-element.149), channel_id=1, source_target_pairs={{0,2},{1,3},{2,0},{3,1},{4,6},{5,7},{6,4},{7,5},{8,10},{9,11},{10,... | collective-permute-start | bytes 1843208 | tf_op jit(solution)/shard_map/ppermute | solution.py:671
  173.2 17.9 %collective-permute-start.19 = (bf16[256,2176]{1,0:T(8,128)(2,1)}, bf16[256,2176]{1,0:T(8,128)(2,1)}, u32[]{:S(2)}, u32[]{:S(2)}) collective-permute-start(bf16[256,2176]{1,0:T(8,128)(2,1)} %get-tuple-element.165), channel_id=1, source_target_pairs={{0,4},{4,0},{1,5},{5,1},{2,6},{6,2},{3,7},{7,3},{8,12},{12,8},{9,1... | collective-permute-start | bytes 3342344 | tf_op jit(solution)/shard_map/ppermute | solution.py:671
  174.1 14.6 %collective-permute-start.18 = (bf16[2,1,256,512]{3,2,1,0:T(8,128)(2,1)}, bf16[2,1,256,512]{3,2,1,0:T(8,128)(2,1)}, u32[]{:S(2)}, u32[]{:S(2)}) collective-permute-start(bf16[2,1,256,512]{3,2,1,0:T(8,128)(2,1)} %slice.112), channel_id=1, source_target_pairs={{0,16},{8,24},{16,0},{24,8},{1,17},{9,25},{17,1},{25,9},{2,18},{10... | collective-permute-start | bytes 1572872 | tf_op jit(solution)/shard_map/ppermute | solution.py:671
  175.5 14.4 %copy-start.46 = (bf16[2,2,256,512]{3,2,1,0:T(8,128)(2,1)S(1)}, bf16[2,2,256,512]{3,2,1,0:T(8,128)(2,1)}, u32[]{:S(2)}) copy-start(bf16[2,2,256,512]{3,2,1,0:T(8,128)(2,1)} %copy-done.45) | copy-start | bytes 3145732
  175.5 14.4 %collective-permute-start.17 = (bf16[2,1,256,512]{3,2,1,0:T(8,128)(2,1)}, bf16[2,1,256,512]{3,2,1,0:T(8,128)(2,1)}, u32[]{:S(2)}, u32[]{:S(2)}) collective-permute-start(bf16[2,1,256,512]{3,2,1,0:T(8,128)(2,1)} %slice.110), channel_id=1, source_target_pairs={{0,8},{8,0},{16,24},{24,16},{1,9},{9,1},{17,25},{25,17},{2,10},{10... | collective-permute-start | bytes 1572872 | tf_op jit(solution)/shard_map/ppermute | solution.py:671
  176.0 16.6 %collective-permute-start.20 = (bf16[3,100,512]{2,1,0:T(8,128)(2,1)}, bf16[3,100,512]{2,1,0:T(8,128)(2,1)}, u32[]{:S(2)}, u32[]{:S(2)}) collective-permute-start(bf16[3,100,512]{2,1,0:T(8,128)(2,1)} %get-tuple-element.166), channel_id=1, source_target_pairs={{0,4},{4,0},{1,5},{5,1},{2,6},{6,2},{3,7},{7,3},{8,12},{12,8},{9,1... | collective-permute-start | bytes 921608 | tf_op jit(solution)/shard_map/ppermute | solution.py:671
  192.7 9.3 %collective-permute-start.23 = (bf16[1,256,512]{2,1,0:T(8,128)(2,1)S(1)}, bf16[1,256,512]{2,1,0:T(8,128)(2,1)S(1)}, u32[]{:S(2)}, u32[]{:S(2)}) collective-permute-start(bf16[1,256,512]{2,1,0:T(8,128)(2,1)S(1)} %slice_bitcast_fusion), channel_id=1, source_target_pairs={{0,1},{1,0},{2,3},{3,2},{4,5},{5,4},{6,7},{7,6},{8,9},{9,8},{10,11... | collective-permute-start | bytes 786440 | tf_op jit(solution)/shard_map/ppermute | solution.py:671
  192.7 13.5 %collective-permute-start.22 = (bf16[1,256,512]{2,1,0:T(8,128)(2,1)S(1)}, bf16[1,256,512]{2,1,0:T(8,128)(2,1)S(1)}, u32[]{:S(2)}, u32[]{:S(2)}) collective-permute-start(bf16[1,256,512]{2,1,0:T(8,128)(2,1)S(1)} %slice_bitcast_fusion.1), channel_id=1, source_target_pairs={{0,1},{1,0},{2,3},{3,2},{4,5},{5,4},{6,7},{7,6},{8,9},{9,8},{10,11... | collective-permute-start | bytes 786440 | tf_op jit(solution)/shard_map/ppermute | solution.py:671
  194.8 11.5 %collective-permute-start.24 = (bf16[64,2176]{1,0:T(8,128)(2,1)S(1)}, bf16[64,2176]{1,0:T(8,128)(2,1)S(1)}, u32[]{:S(2)}, u32[]{:S(2)}) collective-permute-start(bf16[64,2176]{1,0:T(8,128)(2,1)S(1)} %get-tuple-element.217), channel_id=1, source_target_pairs={{0,8},{8,0},{16,24},{24,16},{1,9},{9,1},{17,25},{25,17},{2,10},{10... | collective-permute-start | bytes 835592 | tf_op jit(solution)/shard_map/ppermute | solution.py:671
  195.4 13.7 %collective-permute-start.26 = (bf16[64,2176]{1,0:T(8,128)(2,1)S(1)}, bf16[64,2176]{1,0:T(8,128)(2,1)S(1)}, u32[]{:S(2)}, u32[]{:S(2)}) collective-permute-start(bf16[64,2176]{1,0:T(8,128)(2,1)S(1)} %get-tuple-element.218), channel_id=1, source_target_pairs={{0,24},{8,16},{16,8},{24,0},{1,25},{9,17},{17,9},{25,1},{2,26},{10... | collective-permute-start | bytes 835592 | tf_op jit(solution)/shard_map/ppermute | solution.py:671
  197.7 12.7 %collective-permute-start.25 = (bf16[64,2176]{1,0:T(8,128)(2,1)S(1)}, bf16[64,2176]{1,0:T(8,128)(2,1)S(1)}, u32[]{:S(2)}, u32[]{:S(2)}) collective-permute-start(bf16[64,2176]{1,0:T(8,128)(2,1)S(1)} %get-tuple-element.219), channel_id=1, source_target_pairs={{0,16},{8,24},{16,0},{24,8},{1,17},{9,25},{17,1},{25,9},{2,18},{10... | collective-permute-start | bytes 835592 | tf_op jit(solution)/shard_map/ppermute | solution.py:671
  210.7 5.1 %collective-permute-start.29 = (bf16[16,2176]{1,0:T(8,128)(2,1)S(1)}, bf16[16,2176]{1,0:T(8,128)(2,1)S(1)}, u32[]{:S(2)}, u32[]{:S(2)}) collective-permute-start(bf16[16,2176]{1,0:T(8,128)(2,1)S(1)} %get-tuple-element.220), channel_id=1, source_target_pairs={{0,1},{1,0},{2,3},{3,2},{4,5},{5,4},{6,7},{7,6},{8,9},{9,8},{10,11... | collective-permute-start | bytes 208904 | tf_op jit(solution)/shard_map/ppermute | solution.py:671
  211.1 6.2 %collective-permute-start.31 = (bf16[16,2176]{1,0:T(8,128)(2,1)S(1)}, bf16[16,2176]{1,0:T(8,128)(2,1)S(1)}, u32[]{:S(2)}, u32[]{:S(2)}) collective-permute-start(bf16[16,2176]{1,0:T(8,128)(2,1)S(1)} %get-tuple-element.221), channel_id=1, source_target_pairs={{0,3},{1,2},{2,1},{3,0},{4,7},{5,6},{6,5},{7,4},{8,11},{9,10},{10,... | collective-permute-start | bytes 208904 | tf_op jit(solution)/shard_map/ppermute | solution.py:671
  211.8 6.9 %collective-permute-start.30 = (bf16[16,2176]{1,0:T(8,128)(2,1)S(1)}, bf16[16,2176]{1,0:T(8,128)(2,1)S(1)}, u32[]{:S(2)}, u32[]{:S(2)}) collective-permute-start(bf16[16,2176]{1,0:T(8,128)(2,1)S(1)} %get-tuple-element.222), channel_id=1, source_target_pairs={{0,2},{1,3},{2,0},{3,1},{4,6},{5,7},{6,4},{7,5},{8,10},{9,11},{10,... | collective-permute-start | bytes 208904 | tf_op jit(solution)/shard_map/ppermute | solution.py:671
  214.2 9.8 %collective-permute-start.27 = (bf16[1,256,512]{2,1,0:T(8,128)(2,1)S(1)}, bf16[1,256,512]{2,1,0:T(8,128)(2,1)S(1)}, u32[]{:S(2)}, u32[]{:S(2)}) collective-permute-start(bf16[1,256,512]{2,1,0:T(8,128)(2,1)S(1)} %fusion.1), channel_id=1, source_target_pairs={{0,8},{8,0},{16,24},{24,16},{1,9},{9,1},{17,25},{25,17},{2,10},{10... | collective-permute-start | bytes 786440 | tf_op jit(solution)/shard_map/ppermute | solution.py:671
  214.8 9.2 %collective-permute-start.28 = (bf16[1,256,512]{2,1,0:T(8,128)(2,1)S(1)}, bf16[1,256,512]{2,1,0:T(8,128)(2,1)S(1)}, u32[]{:S(2)}, u32[]{:S(2)}) collective-permute-start(bf16[1,256,512]{2,1,0:T(8,128)(2,1)S(1)} %fusion), channel_id=1, source_target_pairs={{0,16},{8,24},{16,0},{24,8},{1,17},{9,25},{17,1},{25,9},{2,18},{10... | collective-permute-start | bytes 786440 | tf_op jit(solution)/shard_map/ppermute | solution.py:671
  224.1 9.2 %collective-permute-start.32 = (bf16[2,256,512]{2,1,0:T(8,128)(2,1)S(1)}, bf16[2,256,512]{2,1,0:T(8,128)(2,1)S(1)}, u32[]{:S(2)}, u32[]{:S(2)}) collective-permute-start(bf16[2,256,512]{2,1,0:T(8,128)(2,1)S(1)} %pad_maximum_fusion.6), channel_id=1, source_target_pairs={{0,16},{8,24},{16,0},{24,8},{1,17},{9,25},{17,1},{25,9},{2,18},{10... | collective-permute-start | bytes 1572872 | tf_op jit(solution)/shard_map/ppermute | solution.py:671
  225.0 6.2 %collective-permute-start.36 = (bf16[16,2176]{1,0:T(8,128)(2,1)S(1)}, bf16[16,2176]{1,0:T(8,128)(2,1)S(1)}, u32[]{:S(2)}, u32[]{:S(2)}) collective-permute-start(bf16[16,2176]{1,0:T(8,128)(2,1)S(1)} %add_convert_fusion.8), channel_id=1, source_target_pairs={{0,3},{1,2},{2,1},{3,0},{4,7},{5,6},{6,5},{7,4},{8,11},{9,10},{10,... | collective-permute-start | bytes 208904 | tf_op jit(solution)/shard_map/ppermute | solution.py:671
  225.3 6.7 %collective-permute-start.35 = (bf16[16,2176]{1,0:T(8,128)(2,1)S(1)}, bf16[16,2176]{1,0:T(8,128)(2,1)S(1)}, u32[]{:S(2)}, u32[]{:S(2)}) collective-permute-start(bf16[16,2176]{1,0:T(8,128)(2,1)S(1)} %add_convert_fusion.8), channel_id=1, source_target_pairs={{0,2},{1,3},{2,0},{3,1},{4,6},{5,7},{6,4},{7,5},{8,10},{9,11},{10,... | collective-permute-start | bytes 208904 | tf_op jit(solution)/shard_map/ppermute | solution.py:671
  227.5 4.5 %collective-permute-start.34 = (bf16[16,2176]{1,0:T(8,128)(2,1)S(1)}, bf16[16,2176]{1,0:T(8,128)(2,1)S(1)}, u32[]{:S(2)}, u32[]{:S(2)}) collective-permute-start(bf16[16,2176]{1,0:T(8,128)(2,1)S(1)} %add_convert_fusion.8), channel_id=1, source_target_pairs={{0,1},{1,0},{2,3},{3,2},{4,5},{5,4},{6,7},{7,6},{8,9},{9,8},{10,11... | collective-permute-start | bytes 208904 | tf_op jit(solution)/shard_map/ppermute | solution.py:671
  229.4 9.2 %collective-permute-start.33 = (bf16[2,1,256,512]{3,2,1,0:T(8,128)(2,1)S(1)}, bf16[2,1,256,512]{3,2,1,0:T(8,128)(2,1)S(1)}, u32[]{:S(2)}, u32[]{:S(2)}) collective-permute-start(bf16[2,1,256,512]{3,2,1,0:T(8,128)(2,1)S(1)} %pad_maximum_fusion.7), channel_id=1, source_target_pairs={{0,8},{8,0},{16,24},{24,16},{1,9},{9,1},{17,25},{25,17},{2,10},{10... | collective-permute-start | bytes 1572872 | tf_op jit(solution)/shard_map/ppermute | solution.py:671
  233.4 23.4 %copy-start.51 = (bf16[3,100,512]{2,1,0:T(8,128)(2,1)S(1)}, bf16[3,100,512]{2,1,0:T(8,128)(2,1)}, u32[]{:S(2)}) copy-start(bf16[3,100,512]{2,1,0:T(8,128)(2,1)} %get-tuple-element.168) | copy-start | bytes 921604
  238.7 27.2 %copy-start.41 = (s32[4]{0:T(128)S(1)}, s32[4]{0:T(128)}, u32[]{:S(2)}) copy-start(s32[4]{0:T(128)} %copy-done.39) | copy-start | bytes 52
  238.7 16.2 %collective-permute-start.37 = (bf16[4,256,512]{2,1,0:T(8,128)(2,1)S(1)}, bf16[4,256,512]{2,1,0:T(8,128)(2,1)S(1)}, u32[]{:S(2)}, u32[]{:S(2)}) collective-permute-start(bf16[4,256,512]{2,1,0:T(8,128)(2,1)S(1)} %pad_maximum_fusion.2.im_ref), channel_id=1, source_target_pairs={{0,4},{4,0},{1,5},{5,1},{2,6},{6,2},{3,7},{7,3},{8,12},{12,8},{9,1... | collective-permute-start | bytes 3145736 | tf_op jit(solution)/shard_map/ppermute | solution.py:671
  238.8 17.1 %collective-permute-start.38 = (bf16[4,256,512]{2,1,0:T(8,128)(2,1)S(1)}, bf16[4,256,512]{2,1,0:T(8,128)(2,1)S(1)}, u32[]{:S(2)}, u32[]{:S(2)}) collective-permute-start(bf16[4,256,512]{2,1,0:T(8,128)(2,1)S(1)} %bitcast.45), channel_id=1, source_target_pairs={{0,4},{4,0},{1,5},{5,1},{2,6},{6,2},{3,7},{7,3},{8,12},{12,8},{9,1... | collective-permute-start | bytes 3145736 | tf_op jit(solution)/shard_map/ppermute | solution.py:671
  239.3 10.5 %collective-permute-start.41 = (bf16[64,2176]{1,0:T(8,128)(2,1)S(1)}, bf16[64,2176]{1,0:T(8,128)(2,1)S(1)}, u32[]{:S(2)}, u32[]{:S(2)}) collective-permute-start(bf16[64,2176]{1,0:T(8,128)(2,1)S(1)} %pad_maximum_fusion.8), channel_id=1, source_target_pairs={{0,24},{8,16},{16,8},{24,0},{1,25},{9,17},{17,9},{25,1},{2,26},{10... | collective-permute-start | bytes 835592 | tf_op jit(solution)/shard_map/ppermute | solution.py:671
  241.3 13.5 %collective-permute-start.40 = (bf16[64,2176]{1,0:T(8,128)(2,1)S(1)}, bf16[64,2176]{1,0:T(8,128)(2,1)S(1)}, u32[]{:S(2)}, u32[]{:S(2)}) collective-permute-start(bf16[64,2176]{1,0:T(8,128)(2,1)S(1)} %pad_maximum_fusion.8), channel_id=1, source_target_pairs={{0,16},{8,24},{16,0},{24,8},{1,17},{9,25},{17,1},{25,9},{2,18},{10... | collective-permute-start | bytes 835592 | tf_op jit(solution)/shard_map/ppermute | solution.py:671
  242.0 12.8 %collective-permute-start.39 = (bf16[64,2176]{1,0:T(8,128)(2,1)S(1)}, bf16[64,2176]{1,0:T(8,128)(2,1)S(1)}, u32[]{:S(2)}, u32[]{:S(2)}) collective-permute-start(bf16[64,2176]{1,0:T(8,128)(2,1)S(1)} %pad_maximum_fusion.8), channel_id=1, source_target_pairs={{0,8},{8,0},{16,24},{24,16},{1,9},{9,1},{17,25},{25,17},{2,10},{10... | collective-permute-start | bytes 835592 | tf_op jit(solution)/shard_map/ppermute | solution.py:671
  256.8 15.9 %collective-permute-start.42 = (bf16[256,2176]{1,0:T(8,128)(2,1)S(1)}, bf16[256,2176]{1,0:T(8,128)(2,1)}, u32[]{:S(2)}, u32[]{:S(2)}) collective-permute-start(bf16[256,2176]{1,0:T(8,128)(2,1)S(1)} %pad_maximum_fusion.1.mine_ref), channel_id=1, source_target_pairs={{0,4},{4,0},{1,5},{5,1},{2,6},{6,2},{3,7},{7,3},{8,12},{12,8},{9,1... | collective-permute-start | bytes 3342344 | tf_op jit(solution)/shard_map/ppermute | solution.py:671
  256.8 2.8 %collective-permute-start.21 = (bf16[3,100,512]{2,1,0:T(8,128)(2,1)S(1)}, bf16[3,100,512]{2,1,0:T(8,128)(2,1)S(1)}, u32[]{:S(2)}, u32[]{:S(2)}) collective-permute-start(bf16[3,100,512]{2,1,0:T(8,128)(2,1)S(1)} %copy-done.51), channel_id=1, source_target_pairs={{0,4},{4,0},{1,5},{5,1},{2,6},{6,2},{3,7},{7,3},{8,12},{12,8},{9,1... | collective-permute-start | bytes 921608 | tf_op jit(solution)/shard_map/ppermute | solution.py:671
  (47 other events, 301.7 us)

commit v3 on v2

--- a/solution.py
+++ b/solution.py
@@ -14,6 +14,7 @@
 F32 = jnp.float32
 BF16 = jnp.bfloat16
 HELD = pltpu.HBM
+HERE = pl.BlockSpec(memory_space=pltpu.VMEM)
 BRIEF = pl.CostEstimate(flops=1, bytes_accessed=1, transcendentals=0)
 NT = (((1,), (1,)), ((), ()))
 TN = (((0,), (0,)), ((), ()))
@@ -145,7 +146,7 @@
         compiler_params=pltpu.CompilerParams(vmem_limit_bytes=22 << 20),
         cost_estimate=BRIEF,
         name="attend",
-    )(meta, own, other, dy_own, dy_other, mask, g1, wqkv, wout, g2)
+    )(meta, *map(held, (own, other, dy_own, dy_other)), mask, g1, held(wqkv), held(wout), g2)
 
 
 def assemble_kernel(meta_ref, own_ref, other_ref, out_ref, out_s):
@@ -170,6 +171,7 @@
             scratch_shapes=[pltpu.VMEM((2 * half, width), F32)],
         ),
         out_shape=jax.ShapeDtypeStruct((imgs * 2 * half, width), BF16),
+        compiler_params=pltpu.CompilerParams(vmem_limit_bytes=6 << 20),
         cost_estimate=BRIEF,
         name="assemble",
     )(meta, own, other)
@@ -238,10 +240,11 @@
     value = pre * up
     act = value.astype(BF16)
     slope = up + value * (1.0 - up) * (1.5957691216 + 0.2140644488 * square)
-    act_ref[...] = act
+    here = pl.ds(pl.multiple_of(step * pre.shape[1], pre.shape[1]), pre.shape[1])
+    act_ref[:, here] = act
     made_s[...] += mm(act, w_back)
     dpre = (mm(dout_ref[...], w_back, NT) * slope).astype(BF16)
-    dpre_ref[...] = dpre
+    dpre_ref[:, here] = dpre
     din_s[...] += mm(dpre, w_in, NT)
 
     @pl.when(step == pl.num_programs(0) - 1)
@@ -292,11 +295,10 @@
     hidden = PIECES * piece
     steps = PIECES // 2
     deep = padded(count) + 16 * -(-count // width)
-    fix = lambda *s: pl.BlockSpec(s, lambda q, m: (0,) * len(s))
     if local:
         cuts = [pl.BlockSpec((1, width, piece), lambda q, m, s=s: (0, 0, (2 * q + s) ^ m[1])) for s in (0, 1)]
         cuts += [pl.BlockSpec((1, piece, width), lambda q, m, s=s: (0, (2 * q + s) ^ m[1], 0)) for s in (0, 1)]
-        weights = [weights[0]] * 2 + [weights[1]] * 2
+        weights = [held(weights[0])] * 2 + [held(weights[1])] * 2
     else:
         block = (1, 2, piece, piece)
         near = lambda q: jnp.minimum(q, steps // 2 - 1)
@@ -306,20 +308,14 @@
             for at in (near, away) for g in (0, 1) for s in (0, 1)
         ]
         weights = [weights[0]] * 4 + [weights[1]] * 4
-    more = [] if prev is None else [fix(count, width), fix(deep, width)]
+    more = [] if prev is None else [HERE, HERE]
     return pl.pallas_call(
         functools.partial(expert_kernel, prev is not None, local),
         grid_spec=pltpu.PrefetchScalarGridSpec(
             num_scalar_prefetch=1,
             grid=(steps,),
-            in_specs=[
-                fix(*rows.shape), fix(*dy.shape), fix(*ids.shape), fix(*wr.shape), *cuts, *more,
-            ],
-            out_specs=[
-                pl.BlockSpec((count, 2 * piece), lambda q, m: (0, q)),
-                pl.BlockSpec((count, 2 * piece), lambda q, m: (0, q)),
-                fix(count, width), fix(count, width), fix(deep, width),
-            ],
+            in_specs=[HERE] * 4 + [*cuts, *more],
+            out_specs=[HERE] * 5,
             scratch_shapes=[
                 pltpu.VMEM((count, 128), F32),
                 pltpu.VMEM((count, width), F32),
@@ -333,71 +329,55 @@
             jax.ShapeDtypeStruct((count, width), BF16),
             jax.ShapeDtypeStruct((deep, width), BF16),
         ],
-        compiler_params=pltpu.CompilerParams(vmem_limit_bytes=22 << 20),
+        compiler_params=pltpu.CompilerParams(vmem_limit_bytes=20 << 20),
         cost_estimate=BRIEF,
         name="expert",
     )(meta, rows, dy, ids, wr, *weights, *(prev or ()))
 
 
 def weight_kernel(n, *refs):
-    rows = refs[:n]
-    sides = [[refs[n + (3 * e + g) * n : n + (3 * e + g + 1) * n] for g in range(3)] for e in range(2)]
-    iown_ref, igive_ref, bown_ref, bgive_ref = refs[7 * n :]
-    side, part = pl.program_id(0), pl.program_id(1)
-    for e in range(2):
-        acts, dpres, douts = sides[e]
-
-        @pl.when(side == e)
-        def _():
-            results = []
-            for left, right in ((dpres, rows), (acts, douts)):
-                total = 0.0
-                for b in range(n):
-                    count = left[b].shape[0]
-                    total = total + mm(left[b][...], right[b][0:count, :], TN)
-                results.append(total.astype(BF16).reshape(iown_ref.shape[1:]))
-            grad_in, grad_back = results
-
-            @pl.when(part < pl.num_programs(1) // 2)
-            def _():
-                iown_ref[0] = grad_in
-                bown_ref[0] = grad_back
-
-            @pl.when(part >= pl.num_programs(1) // 2)
-            def _():
-                igive_ref[0] = grad_in
-                bgive_ref[0] = grad_back
-
-
-def weight_grads(rows, sides):
+    rows, acts, dpres, douts = (refs[g * n : (g + 1) * n] for g in range(4))
+    iown_ref, igive_ref, bown_ref, bgive_ref = refs[4 * n :]
+    wide = iown_ref.shape[0] * iown_ref.shape[1]
+    here = pl.ds(pl.multiple_of(pl.program_id(0) * wide, wide), wide)
+    results = []
+    for left, right in ((dpres, rows), (acts, douts)):
+        total = 0.0
+        for b in range(n):
+            count = left[b].shape[0]
+            total = total + mm(left[b][:, here], right[b][0:count, :], TN)
+        results.append(total.astype(BF16).reshape(iown_ref.shape))
+    grad_in, grad_back = results
+    first = pl.program_id(0) < pl.num_programs(0) // 2
+
+    @pl.when(first)
+    def _():
+        iown_ref[...] = grad_in
+        bown_ref[...] = grad_back
+
+    @pl.when(jnp.logical_not(first))
+    def _():
+        igive_ref[...] = grad_in
+        bgive_ref[...] = grad_back
+
+
+def weight_grads(rows, acts, dpres, douts, late=False):
     n = len(rows)
     width = rows[0].shape[1]
-    hidden = sides[0][0][0].shape[1]
-    piece = hidden // PIECES
-    upper = PIECES // 2
+    piece = acts[0].shape[1] // PIECES
     steps = PIECES // 2
-    fix = lambda a: pl.BlockSpec(a.shape, lambda e, q: (0, 0))
-    cuts = [
-        lambda a: pl.BlockSpec((a.shape[0], 2 * piece), lambda e, q: (0, jnp.where(e == 0, q, steps - 1))),
-        lambda a: pl.BlockSpec((a.shape[0], 2 * piece), lambda e, q: (0, jnp.where(e == 1, q, 0))),
-    ]
-    specs = [fix(a) for a in rows]
-    args = list(rows)
-    for e, (acts, dpres, douts) in enumerate(sides):
-        specs += [cuts[e](a) for a in acts] + [cuts[e](a) for a in dpres] + [fix(a) for a in douts]
-        args += [*acts, *dpres, *douts]
-    own = pl.BlockSpec((1, 2, piece, width), lambda e, q: (e, jnp.minimum(q, steps // 2 - 1), 0, 0))
-    give = pl.BlockSpec((1, 2, piece, width), lambda e, q: (e, jnp.maximum(q - steps // 2, 0), 0, 0))
+    own = pl.BlockSpec((2, piece, width), lambda q: (jnp.minimum(q, steps // 2 - 1), 0, 0))
+    give = pl.BlockSpec((2, piece, width), lambda q: (jnp.maximum(q - steps // 2, 0), 0, 0))
     return pl.pallas_call(
         functools.partial(weight_kernel, n),
-        grid=(2, steps),
-        in_specs=specs,
+        grid=(steps,),
+        in_specs=[HERE] * (4 * n),
         out_specs=[own, give, own, give],
-        out_shape=[jax.ShapeDtypeStruct((2, upper, piece, width), BF16)] * 4,
-        compiler_params=pltpu.CompilerParams(vmem_limit_bytes=26 << 20),
+        out_shape=[(HELD if late and g % 2 == 0 else jax.ShapeDtypeStruct)((PIECES // 2, piece, width), BF16) for g in range(4)],
+        compiler_params=pltpu.CompilerParams(vmem_limit_bytes=14 << 20),
         cost_estimate=BRIEF,
         name="weight_grads",
-    )(*args)
+    )(*rows, *acts, *dpres, *douts)
 
 
 def finish_kernel(meta_ref, im_ref, ir_ref, bm_ref, br_ref, gin_ref, gback_ref):
@@ -436,7 +416,7 @@
             jax.ShapeDtypeStruct((1, width, PIECES * piece), F32),
             jax.ShapeDtypeStruct((1, PIECES * piece, width), F32),
         ],
-        compiler_params=pltpu.CompilerParams(vmem_limit_bytes=24 << 20),
+        compiler_params=pltpu.CompilerParams(vmem_limit_bytes=14 << 20),
         cost_estimate=BRIEF,
         name="finish_expert",
     )(meta, in_mine, in_recv, back_mine, back_recv)
@@ -632,6 +612,7 @@
             scratch_shapes=[pltpu.VMEM((seq, width), F32)],
         ),
         out_shape=[shape, shape],
+        compiler_params=pltpu.CompilerParams(vmem_limit_bytes=8 << 20),
         cost_estimate=BRIEF,
         name="combine",
     )(meta, mid, *parts)
@@ -655,9 +636,62 @@
             num_scalar_prefetch=1, grid=(2 * imgs,), in_specs=[spec] * 4, out_specs=[out, out]
         ),
         out_shape=[shape, shape],
+        compiler_params=pltpu.CompilerParams(vmem_limit_bytes=4 << 20),
         cost_estimate=BRIEF,
         name="place",
     )(meta, *arrays)
+
+
+def merge_kernel(plan, *refs):
+    refs = list(refs)
+    takes = [[[refs.pop(0) for _ in range(n)] for n in sizes] for sizes, _, _ in plan]
+    for groups, (_, axis, cuts) in zip(takes, plan):
+        outs = [refs.pop(0) for _ in cuts]
+        if axis is not None:
+            size = groups[0][0].shape[axis]
+            for k, ref in enumerate(groups[0]):
+                at = slice(k * size, (k + 1) * size)
+                outs[0][(slice(None),) * axis + (at,)] = ref[...]
+            continue
+        for g, take in enumerate(groups):
+            total = take[0][...].astype(F32)
+            for ref in take[1:]:
+                total += ref[...].astype(F32)
+            total = total.astype(BF16)
+            for out, cut in zip(outs, cuts):
+                if len(groups) > 1:
+                    out[g] = total[cut]
+                else:
+                    out[...] = total[cut]
+
+
+def merge(*items):
+    plan, shapes, arrays = [], [], []
+    for groups, axis, cuts in items:
+        first = jax.ShapeDtypeStruct(groups[0][0].shape, BF16)
+        if axis is not None:
+            cuts = [None]
+            shape = list(first.shape)
+            shape[axis] *= len(groups[0])
+            shapes.append(jax.ShapeDtypeStruct(tuple(shape), BF16))
+        else:
+            lead = (len(groups),) if len(groups) > 1 else ()
+            shapes += [
+                jax.ShapeDtypeStruct(lead + jax.eval_shape(lambda v, c=c: v[c], first).shape, BF16) for c in cuts
+            ]
+        plan.append(([len(g) for g in groups], axis, cuts))
+        arrays += [v for g in groups for v in g]
+    return pl.pallas_call(
+        functools.partial(merge_kernel, plan),
+        out_shape=shapes,
+        compiler_params=pltpu.CompilerParams(vmem_limit_bytes=16 << 20),
+        cost_estimate=BRIEF,
+        name="merge",
+    )(*arrays)
+
+
+def held(value):
+    return pltpu.with_memory_space_constraint(value, pltpu.HBM)
 
 
 SWAP = [(0, 1), (1, 0)]
@@ -707,8 +741,8 @@
     z = lax.axis_index("expert")
     me = core * 4 + lax.axis_index("dp")
     meta = jnp.stack([z, me, me * 4 + z, core]).astype(jnp.int32)
-    meta_pair = jnp.stack([z ^ 1, me, me * 4 + z, core]).astype(jnp.int32)
-    far = lambda v: send(v, "expert", xor(2))
+    meta_pair = jnp.stack([z ^ 2, me, me * 4 + z, core]).astype(jnp.int32)
+    far = lambda v: send(v, "expert", xor(1))
     swap = lambda v: send(v, "ctx", SWAP)
 
     codes = route_ids.reshape(nimg, half, TOP)
@@ -728,75 +762,98 @@
     wr = jnp.pad(w_router.T, ((0, 16 - experts), (0, 0)))
     g1, g2 = gain_one[None, :], gain_two[None, :]
 
-    pack, far_raw = send(pack, "expert", xor(1)), far(cotangent)
+    far_raw, pack = far(after(cotangent, pack)), send(pack, "expert", xor(2))
     x_rows, dy, normed, qkv, probs, mix, mid, routed = attend(
         meta, tokens, tok_other, cotangent, dy_other, key_mask, g1, w_qkv, w_out, g2
     )
+    far_rows = jnp.concatenate([routed, ids_pack], 0)
+    pack, far_raw, far_rows, routed = tie(pack, far_raw, far_rows, routed)
+
+    packs = [pack] + [send(pack, "dp", xor(k)) for k in (1, 2, 3)]
+    far_rows = far(far_rows)
+    far_dy = assemble(meta, far_raw, swap(far_raw))
     own_one = expert(meta, routed, dy, ids, wr, (w_in, w_back))
-    far_rows = jnp.concatenate([routed, ids_pack], 0)
-    pack, far_raw, far_rows, own_din = tie(pack, far_raw, far_rows, own_one[4])
-    own_one = [*own_one[:4], own_din]
-
-    packs = [pack] + [send(pack, "dp", xor(k)) for k in (1, 2, 3)]
-    far_other = swap(far_raw)
-    *packs, far_rows, far_other = tie(*packs, far(far_rows), far_other)
+    far_one = expert(meta, after(far_rows, own_one[4]), far_dy, far_rows, wr, (w_in, w_back))
+    *packs, far_din = tie(*packs, far_one[4])
+    far_one = [*far_one[:4], far_din]
 
     packs = jnp.stack(packs)
-    far_dy = assemble(meta, far_raw, far_other)
-    far_one = expert(meta, far_rows, far_dy, far_rows, wr, (w_in, w_back))
-    packs_other, far_din = tie(swap(packs), far_one[4])
-    pair = (packs, packs_other)
-    far_two = expert(meta_pair, far_rows, far_dy, far_rows, wr, pair, [far_one[3], far_din])
-
-    far_din, far_made = tie(far_two[4], far_two[3])
+    pair = [packs, swap(packs)]
+    grads = weight_grads([routed, far_rows], *zip(own_one[:3], far_one[:3]), late=True)
+    *pair, a, a_give, b, b_give = tie(*pair, *grads)
+
+    far_two = expert(meta_pair, far_rows, far_dy, far_rows, wr, pair, far_one[3:])
+    head, tail = slice(0, 2), slice(2, 4)
+    even, odd = [(slice(None), slice(k, k + 1)) for k in (0, 1)]
+    square = lambda v: v.reshape(2, 2, piece, width)
+
+    def across(a, a_give, b, b_give):
+        return merge(([[a, swap(a_give)]], None, [head, tail]), ([[square(b), square(swap(b_give))]], None, [even, odd]))
+
+    *one, far_din, far_made = tie(*across(a, a_give, b, b_give), far_two[4], far_two[3])
+
+    y_way, x_way = ("dp", xor(2)), ("dp", xor(1))
     own_two = expert(meta_pair, routed, dy, ids, wr, pair, [own_one[3], after(own_one[4], far_din)])
-    sides = [list(zip(own_one[:3], far_one[:3])), list(zip(own_two[:3], far_two[:3]))]
-    grads = weight_grads([routed, far_rows], sides)
-    din_far, *grads = tie(far(far_din), *grads)
-
-    a, a_give, b, b_give = grads
-    a, b = tie(add_low(a, swap(a_give)), add_low(b, swap(b_give)))
-
-    y_way, x_way = ("dp", xor(2)), ("dp", xor(1))
-    a_got, b_got = send(a[:, 2:], *y_way), send(b[:, 1::2], *x_way)
+    grads = weight_grads([routed, far_rows], *zip(own_two[:3], far_two[:3]))
+    din_far, a_got, b_got, *grads = tie(far(far_din), send(one[1], *y_way), send(one[3], *x_way), *grads)
+    a_one, b_one = [one[0], a_got], [one[2], b_got]
+
+    two = tie(*across(*grads))
+
+    a_two, b_two = [two[0], send(two[1], *y_way)], [two[2], send(two[3], *x_way)]
     far_made = far(after(far_made, din_far))
     tok_own, tok_give, shared, shared_give = attend_back(
-        meta, [after(own_two[4], a, b), din_far], ids, dy, mid, routed, wr, g2, mix, w_out, probs, qkv, x_rows, normed, w_qkv, g1
-    )
-    a, b, far_made, shared, shared_give, tok_give = tie(
-        add_low(a[:, :2], a_got), add_low(b[:, 0::2], b_got), far_made, shared, shared_give, tok_give
-    )
-    others = lambda v, axis: [send(v, axis, xor(k)) for k in (1, 2, 3)]
+        meta, [after(own_two[4], *two), din_far], ids, dy, mid, routed, wr, g2, mix, w_out, probs, qkv, x_rows, normed, w_qkv, g1
+    )
+    halves = [slice(0, 1), slice(1, 2)]
+    a, a_give, b, b_give, far_made, shared, shared_give, tok_give = tie(
+        *merge(([a_one, a_two], None, halves), ([b_one, b_two], None, halves)),
+        far_made,
+        shared,
+        shared_give,
+        tok_give,
+    )
     mix_own, mix_give = combine(meta, mid, [own_two[3], far_made], imgs)
-    a, b, shared, tok_got, mix_give = tie(
-        add_low(a[:, :1], send(a[:, 1:], *x_way)),
-        add_low(b[:, :1], send(b[:, 1:], *y_way)),
-        add_low(shared, swap(shared_give)),
+    quarters = lambda n: [slice(k * n, (k + 1) * n) for k in range(4)]
+    a, a_give, b, b_give, *shared, tok_got, mix_got = tie(
+        *merge(
+            ([[a, send(a_give, *x_way)]], None, [0, 1]),
+            ([[b, send(b_give, *y_way)]], None, [0, 1]),
+            ([[shared, swap(shared_give)]], None, quarters(width // 8)),
+        ),
         swap(tok_give),
-        mix_give,
+        swap(mix_give),
+    )
+    spread = lambda parts, axis: [send(v, axis, xor(k)) for k, v in zip((1, 2, 3), parts)]
+    everything = [slice(None)]
+    mixed, grad_tokens = place(meta, mix_own, mix_got, tok_own, tok_got)
+    a, b, *shared, mixed, grad_tokens = tie(
+        *merge(
+            ([[a, send(a_give, "expert", xor(2))]], None, everything),
+            ([[b, send(b_give, "expert", xor(2))]], None, everything),
+            ([[shared[0], *spread(shared[1:], "dp")]], None, quarters(width // 32)),
+        ),
+        mixed,
+        grad_tokens,
     )
     a, b, shared = tie(
-        add_low(a[0], send(a[1], "expert", xor(1))),
-        add_low(b[0], send(b[1], "expert", xor(1))),
-        add_fan(shared, fan(shared, "dp")),
+        *merge(
+            ([[a, send(a, *x_way)]], 0, None),
+            ([[b, send(b, *y_way)]], 0, None),
+            ([[shared[0], *spread(shared[1:], "expert")]], None, everything),
+        )
     )
     a, b, shared = tie(
-        jnp.concatenate([a, send(a, *x_way)], 0),
-        jnp.stack([b, send(b, *y_way)], 0),
-        add_fan(shared, fan(shared, "expert")),
-    )
-    a, b, shared = tie(
-        jnp.concatenate([a, send(a, *y_way)], 0),
-        jnp.concatenate([b, send(b, *x_way)], 1).reshape(4, piece, width),
-        jnp.concatenate([shared] + others(shared, "expert"), 0),
-    )
-    a_other, b_other, shared = tie(
-        swap(a), swap(b), jnp.concatenate([shared] + others(shared, "dp"), 0)
-    )
-    shared_other, mix_got = swap(shared), swap(mix_give)
-    grad_in, grad_back = finish_expert(meta, a, a_other, b, b_other)
-    mixed, grad_tokens = place(meta, mix_own, mix_got, tok_own, tok_got)
-    grad_qkv, grad_out, small = finish_shared(meta, shared, shared_other)
+        *merge(
+            ([[a, send(a, *y_way)]], 0, None),
+            ([[b, send(b, *x_way)]], 1, None),
+            ([[shared, *spread([shared] * 3, "expert")]], 0, None),
+        )
+    )
+    b = b.reshape(a.shape)
+    grad_in, grad_back = finish_expert(meta, a, swap(a), b, swap(b))
+    (shared,) = merge(([[after(shared, grad_in, grad_back), *spread([shared] * 3, "dp")]], 0, None))
+    grad_qkv, grad_out, small = finish_shared(meta, shared, swap(shared))
     return (
         mixed,
         grad_tokens,

time: 280 us -> 226 us (0.81)
  waiting for transfers between devices: 98.4 us -> 68.3 us
  local copies, waits for them, and re-layouts: 24.4 us -> 12.4 us
  Pallas kernels: 105 us -> 96 us
  other arithmetic: 9.6 us -> 3.32 us
  starting transfers between devices: 39.6 us -> 44.6 us
    ppermute x43 -> x47, waiting for transfers between devices: 98.4 us -> 68.3 us  [send(): return lax.ppermute(value, axis, pairs)]
    unnamed x106 -> x68, local copies, waits for them, and re-layouts: 19.4 us -> 9.34 us
    convert_element_type x11 -> x0, other arithmetic: 5.98 us -> none  [the longest x9 5.79 us: add_low(): return (a.astype(F32) + b.astype(F32)).astype(BF16)]
    ppermute x43 -> x47, starting transfers between devices: 39.6 us -> 44.6 us  [send(): return lax.ppermute(value, axis, pairs)]
    pallas_call x1 -> x10, Pallas kernels: 18 us -> 21.3 us  [the longest x2 17.1 us: weight_grads(): pl.pallas_call(functools.partial(weight_kernel, n), grid=(steps,), in_spe...]
    pallas_call x1, Pallas kernels: 4.15 us -> 1.14 us  [combine(): pl.pallas_call(combine_kernel, grid_spec=pltpu.PrefetchScalarGridSpec(num...]
  transfers between devices with their start and end apart: 43 -> 47, of which waited for: 25 -> 23; matrix products, arithmetic and copies ran while one was open for 4% -> 1% of each run, Pallas kernels for 32% -> 40%
where the time goes in v3:
time: 226 us
  Pallas kernels  96 us (42%)
  waiting for transfers between devices  68.3 us (30%)
  starting transfers between devices  44.6 us (20%)
  local copies, waits for them, and re-layouts  12.4 us (5%)
  other arithmetic  3.32 us (1%)
    ppermute x47, waiting for transfers between devices, send(): return lax.ppermute(value, axis, pairs)  68.3 us
    ppermute x47, starting transfers between devices, send(): return lax.ppermute(value, axis, pairs)  44.6 us
    pallas_call x4, Pallas kernels, expert(): pl.pallas_call(functools.partial(expert_kernel, prev is not None, local),...  40.2 us
    pallas_call x2, Pallas kernels, weight_grads(): pl.pallas_call(functools.partial(weight_kernel, n), grid=(steps,), in_spe...  17.1 us
    pallas_call x1, Pallas kernels, attend_back(): pl.pallas_call(back_kernel, grid_spec=pltpu.PrefetchScalarGridSpec(num_sc...  12.3 us
    pallas_call x1, Pallas kernels, attend(): pl.pallas_call(attend_kernel, grid_spec=pltpu.PrefetchScalarGridSpec(num_...  10 us
    unnamed x68, local copies, waits for them, and re-layouts  9.34 us
  transfers between devices with their start and end apart: 47, of which 23 were waited for; matrix products, arithmetic and copies ran while one was open for 1% of the time, Pallas kernels for 40%

profile of v3, /device:TPU:0, one launch (start us, length us, event | category | flops | bytes accessed | tf_op | source)
XLA Modules:
  0.0 225.9 jit_solution(11640267392000640710)
XLA Ops:
  4.9 3.6 %collective-permute-start = (bf16[4,256,256]{2,1,0:T(8,128)(2,1)}, bf16[4,256,256]{2,1,0:T(8,128)(2,1)}, u32[]{:S(2)}, u32[]{:S(2)}) collective-permute-start(bf16[4,256,256]{2,1,0:T(8,128)(2,1)} %pad_maximum_fusion.2), channel_id=1, source_target_pairs={{0,2},{1,3},{2,0},{3,1},{4,6},{5,7},{6,4},{7,5},{8,10},{9,11},{10,... | collective-permute-start | bytes 1572872 | tf_op jit(solution)/shard_map/ppermute | solution.py:705
  8.7 1.6 collective-permute-start.1
  10.7 1.7 collective-permute-done.2.other_ref
  13.4 10.0 %attend.1 = (bf16[600,512]{1,0:T(8,128)(2,1)}, bf16[600,512]{1,0:T(8,128)(2,1)S(1)}, bf16[600,512]{1,0:T(8,128)(2,1)}, bf16[600,1536]{1,0:T(8,128)(2,1)}, bf16[3...) custom-call(s32[4]{0:T(128)S(1)} %add_add_fusion.meta_ref, ...), custom_call_target="tpu_custom_call" | custom-call | flops 1 | bytes 1 | tf_op jit(solution)/shard_map/attend/pallas_call | solution.py:117
  23.5 9.2 %collective-permute-done = bf16[4,256,256]{2,1,0:T(8,128)(2,1)} collective-permute-done((bf16[4,256,256]{2,1,0:T(8,128)(2,1)}, bf16[4,256,256]{2,1,0:T(8,128)(2,1)}, u32[]{:S(2)}, u32[]{:S(2)}) %collective-permute-start) | collective-permute-done | bytes 524320 | tf_op jit(solution)/shard_map/ppermute | solution.py:705
  32.7 2.6 %collective-permute-done.1.own_ref = bf16[6,100,512]{2,1,0:T(8,128)(2,1)S(1)} collective-permute-done((bf16[6,100,512]{2,1,0:T(8,128)(2,1)S(1)}, bf16[6,100,512]{2,1,0:T(8,128)(2,1)S(1)}, u32[]{:S(2)}, u32[]{:S(2)}) %collective-permute-start.1) | collective-permute-done | bytes 614432 | tf_op jit(solution)/shard_map/ppermute | solution.py:705
  35.4 1.4 collective-permute-start.8
  36.8 2.4 %collective-permute-start.7 = (bf16[4,256,256]{2,1,0:T(8,128)(2,1)}, bf16[4,256,256]{2,1,0:T(8,128)(2,1)S(1)}, u32[]{:S(2)}, u32[]{:S(2)}) collective-permute-start(bf16[4,256,256]{2,1,0:T(8,128)(2,1)} %collective-permute-done), channel_id=1, source_target_pairs={{0,24},{8,16},{16,8},{24,0},{1,25},{9,17},{17,9},{25,1},{2,26},{10... | collective-permute-start | bytes 1572872 | tf_op jit(solution)/shard_map/ppermute | solution.py:705
  40.3 10.4 %expert.4 = (bf16[600,2048]{1,0:T(8,128)(2,1)S(1)}, bf16[600,2048]{1,0:T(8,128)(2,1)S(1)}, bf16[600,512]{1,0:T(8,128)(2,1)S(1)}, bf16[600,512]{1,0:T(8,128)(2,1)S(1)}, bf16[640,512]{1,0:T(8,128)(2,1)S(1)}) custom-call(s32[4]{0:T(128)S(1)} %add_add_fusion.meta_ref, bf16[600,512]{1,0:T(8,128)(2,1)S(1)} %get-tuple-element.154.rows_ref.refs_0_.routed_ref, ...), custom_call_target="tpu_custom_call" | custom-call | flops 1 | bytes 1 | tf_op jit(solution)/shard_map/expert/pallas_call | solution.py:312
  51.7 10.3 %expert.5 = (bf16[600,2048]{1,0:T(8,128)(2,1)S(1)}, bf16[600,2048]{1,0:T(8,128)(2,1)S(1)}, bf16[600,512]{1,0:T(8,128)(2,1)S(1)}, bf16[600,512]{1,0:T(8,128)(2,1)S(1)}, bf16[640,512]{1,0:T(8,128)(2,1)S(1)}) custom-call(s32[4]{0:T(128)S(1)} %add_add_fusion.meta_ref, bf16[624,512]{1,0:T(8,128)(2,1)S(1)} %collective-permute-done.8.rows_ref.ids_ref.refs_1_, ...), custom_call_target="tpu_custom_call" | custom-call | flops 1 | bytes 1 | tf_op jit(solution)/shard_map/expert/pallas_call | solution.py:312
  63.5 1.3 pad_maximum_fusion.rest_0_.rest_1_.rest_2_.rest_3_
  64.9 9.2 %weight_grads.2 = (bf16[4,256,512]{2,1,0:T(8,128)(2,1)}, bf16[4,256,512]{2,1,0:T(8,128)(2,1)}, bf16[4,256,512]{2,1,0:T(8,128)(2,1)}, bf16[4,256,512]{2,1,0:T(8,128)(2,1)}) custom-call(bf16[600,512]{1,0:T(8,128)(2,1)S(1)} %get-tuple-element.154.rows_ref.refs_0_.routed_ref, bf16[624,512]{1,0:T(8,128)(2,1)S(1)} %collective-permute-done.8.rows_ref.ids_ref.refs_1_, ...), custom_call_target="tpu_custom_call" | custom-call | flops 1 | bytes 1 | tf_op jit(solution)/shard_map/weight_grads/pallas_call | solution.py:371
  74.2 1.3 copy-done
  76.1 1.6 copy-done.1
  80.9 9.8 %expert.6 = (bf16[600,2048]{1,0:T(8,128)(2,1)S(1)}, bf16[600,2048]{1,0:T(8,128)(2,1)S(1)}, bf16[600,512]{1,0:T(8,128)(2,1)S(1)}, bf16[600,512]{1,0:T(8,128)(2,1)S(1)}, bf16[640,512]{1,0:T(8,128)(2,1)S(1)}) custom-call(s32[4]{0:T(128)S(1)} %add_add_fusion.1.meta_ref, bf16[624,512]{1,0:T(8,128)(2,1)S(1)} %collective-permute-done.8.rows_ref.ids_ref.refs_1_, ...), custom_call_target="tpu_custom_call" | custom-call | flops 1 | bytes 1 | tf_op jit(solution)/shard_map/expert/pallas_call | solution.py:312
  90.9 2.2 merge.8
  93.8 1.4 collective-permute-start.14
  95.3 1.5 collective-permute-start.15
  96.8 9.7 %expert.7 = (bf16[600,2048]{1,0:T(8,128)(2,1)S(1)}, bf16[600,2048]{1,0:T(8,128)(2,1)S(1)}, bf16[600,512]{1,0:T(8,128)(2,1)S(1)}, bf16[600,512]{1,0:T(8,128)(2,1)S(1)}, bf16[640,512]{1,0:T(8,128)(2,1)S(1)}) custom-call(s32[4]{0:T(128)S(1)} %add_add_fusion.1.meta_ref, bf16[600,512]{1,0:T(8,128)(2,1)S(1)} %get-tuple-element.154.rows_ref.refs_0_.routed_ref, ...), custom_call_target="tpu_custom_call" | custom-call | flops 1 | bytes 1 | tf_op jit(solution)/shard_map/expert/pallas_call | solution.py:312
  106.5 7.8 %weight_grads.3 = (bf16[4,256,512]{2,1,0:T(8,128)(2,1)S(1)}, bf16[4,256,512]{2,1,0:T(8,128)(2,1)S(1)}, bf16[4,256,512]{2,1,0:T(8,128)(2,1)S(1)}, bf16[4,256,512]{2,1,0:T(8,128)(2,1)S(1)}) custom-call(bf16[600,512]{1,0:T(8,128)(2,1)S(1)} %get-tuple-element.154.rows_ref.refs_0_.routed_ref, ...), custom_call_target="tpu_custom_call" | custom-call | flops 1 | bytes 1 | tf_op jit(solution)/shard_map/weight_grads/pallas_call | solution.py:371
  117.1 1.5 collective-permute-done.17
  120.7 12.3 %attend_back.1 = (bf16[3,100,512]{2,1,0:T(8,128)(2,1)S(1)}, bf16[3,100,512]{2,1,0:T(8,128)(2,1)S(1)}, bf16[256,2176]{1,0:T(8,128)(2,1)S(1)}, bf16[256,2176]{1,0:T(8,128)(2,1)S(1)}) custom-call(s32[4]{0:T(128)S(1)} %add_add_fusion.meta_ref, bf16[640,512]{1,0:T(8,128)(2,1)S(1)} %get-tuple-element.223.din0_ref, ...), custom_call_target="tpu_custom_call" | custom-call | flops 1 | bytes 1 | tf_op jit(solution)/shard_map/attend_back/pallas_call | solution.py:518
  134.8 1.5 collective-permute-start.22
  138.0 10.3 %collective-permute-done.21.refs_1_ = bf16[2,1,256,512]{3,2,1,0:T(8,128)(2,1)S(1)} collective-permute-done((bf16[2,1,256,512]{3,2,1,0:T(8,128)(2,1)S(1)}, bf16[2,1,256,512]{3,2,1,0:T(8,128)(2,1)S(1)}, u32[]{:S(2)}, u32[]{:S(2)}) %collective-permute-start.21) | collective-permute-done | bytes 524320 | tf_op jit(solution)/shard_map/ppermute | solution.py:705
  149.3 1.3 collective-permute-start.28
  150.6 1.5 collective-permute-start.29
  152.9 1.5 collective-permute-start.26
  154.3 1.5 collective-permute-start.27
  155.8 2.8 %place.1 = (bf16[6,100,512]{2,1,0:T(8,128)(2,1)}, bf16[6,100,512]{2,1,0:T(8,128)(2,1)}) custom-call(s32[4]{0:T(128)S(1)} %add_add_fusion.meta_ref, bf16[3,100,512]{2,1,0:T(8,128)(2,1)S(1)} %get-tuple-element.265.a_own_ref, bf16[3,100,512]{2,1,0:T(8,128)(2,1)S(1)} %collective-permute-done.25.a_recv_ref, ...), custom_call_target="tpu_custom_call" | custom-call | flops 1 | bytes 1 | tf_op jit(solution)/shard_map/place/pallas_call | solution.py:633
  158.5 14.1 %collective-permute-done.26.refs_1_ = bf16[1,256,512]{2,1,0:T(8,128)(2,1)S(1)} collective-permute-done((bf16[1,256,512]{2,1,0:T(8,128)(2,1)S(1)}, bf16[1,256,512]{2,1,0:T(8,128)(2,1)S(1)}, u32[]{:S(2)}, u32[]{:S(2)}) %collective-permute-start.26) | collective-permute-done | bytes 262176 | tf_op jit(solution)/shard_map/ppermute | solution.py:705
  172.6 4.7 %collective-permute-done.27.refs_3_ = bf16[1,1,256,512]{3,2,1,0:T(8,128)(2,1)S(1)} collective-permute-done((bf16[1,1,256,512]{3,2,1,0:T(8,128)(2,1)S(1)}, bf16[1,1,256,512]{3,2,1,0:T(8,128)(2,1)S(1)}, u32[]{:S(2)}, u32[]{:S(2)}) %collective-permute-start.27) | collective-permute-done | bytes 262176 | tf_op jit(solution)/shard_map/ppermute | solution.py:705
  177.6 1.3 collective-permute-start.31
  178.9 1.5 collective-permute-start.32
  180.4 2.6 %collective-permute-start.34 = (bf16[16,2176]{1,0:T(8,128)(2,1)S(1)}, bf16[16,2176]{1,0:T(8,128)(2,1)S(1)}, u32[]{:S(2)}, u32[]{:S(2)}) collective-permute-start(bf16[16,2176]{1,0:T(8,128)(2,1)S(1)} %get-tuple-element.277), channel_id=1, source_target_pairs={{0,2},{1,3},{2,0},{3,1},{4,6},{5,7},{6,4},{7,5},{8,10},{9,11},{10,... | collective-permute-start | bytes 208904 | tf_op jit(solution)/shard_map/ppermute | solution.py:705
  183.1 1.8 collective-permute-start.35
  184.8 2.8 %collective-permute-done.34.refs_6_ = bf16[16,2176]{1,0:T(8,128)(2,1)S(1)} collective-permute-done((bf16[16,2176]{1,0:T(8,128)(2,1)S(1)}, bf16[16,2176]{1,0:T(8,128)(2,1)S(1)}, u32[]{:S(2)}, u32[]{:S(2)}) %collective-permute-start.34) | collective-permute-done | bytes 69664 | tf_op jit(solution)/shard_map/ppermute | solution.py:705
  187.6 1.6 collective-permute-done.35.refs_7_
  191.0 1.6 collective-permute-start.40
  192.5 2.8 %collective-permute-start.38 = (bf16[16,2176]{1,0:T(8,128)(2,1)S(1)}, bf16[16,2176]{1,0:T(8,128)(2,1)S(1)}, u32[]{:S(2)}, u32[]{:S(2)}) collective-permute-start(bf16[16,2176]{1,0:T(8,128)(2,1)S(1)} %get-tuple-element.281.refs_4_), channel_id=1, source_target_pairs={{0,1},{1,0},{2,3},{3,2},{4,5},{5,4},{6,7},{7,6},{8,9},{9,8},{10,11... | collective-permute-start | bytes 208904 | tf_op jit(solution)/shard_map/ppermute | solution.py:705
  195.3 1.7 collective-permute-done.40.refs_7_
  197.1 1.5 collective-permute-done.39.refs_6_
  198.6 2.4 %collective-permute-done.36.refs_1_ = bf16[2,256,512]{2,1,0:T(8,128)(2,1)S(1)} collective-permute-done((bf16[2,256,512]{2,1,0:T(8,128)(2,1)S(1)}, bf16[2,256,512]{2,1,0:T(8,128)(2,1)S(1)}, u32[]{:S(2)}, u32[]{:S(2)}) %collective-permute-start.36) | collective-permute-done | bytes 524320 | tf_op jit(solution)/shard_map/ppermute | solution.py:705
  202.8 1.6 collective-permute-start.45
  206.4 4.4 %finish_expert.1 = (f32[1,512,2048]{2,1,0:T(8,128)}, f32[1,2048,512]{2,1,0:T(8,128)}) custom-call(s32[4]{0:T(128)S(1)} %add_add_fusion.meta_ref, bf16[4,256,512]{2,1,0:T(8,128)(2,1)S(1)} %get-tuple-element.283.im_ref, bf16[4,256,512]{2,1,0:T(8,128)(2,1)S(1)} %collective-permute-done.41.ir_ref, bf16[4,256,512]{2,1,0:T(8,128)(2,1)S(1)} %bitcast.39, ...), custom_call_target="tpu_custom_call" | custom-call | flops 1 | bytes 1 | tf_op jit(solution)/shard_map/finish_expert/pallas_call | solution.py:404
  210.9 2.4 %collective-permute-done.45.refs_3_ = bf16[64,2176]{1,0:T(8,128)(2,1)S(1)} collective-permute-done((bf16[64,2176]{1,0:T(8,128)(2,1)S(1)}, bf16[64,2176]{1,0:T(8,128)(2,1)S(1)}, u32[]{:S(2)}, u32[]{:S(2)}) %collective-permute-start.45) | collective-permute-done | bytes 278560 | tf_op jit(solution)/shard_map/ppermute | solution.py:705
  213.2 5.1 %collective-permute-done.44.refs_2_ = bf16[64,2176]{1,0:T(8,128)(2,1)S(1)} collective-permute-done((bf16[64,2176]{1,0:T(8,128)(2,1)S(1)}, bf16[64,2176]{1,0:T(8,128)(2,1)S(1)}, u32[]{:S(2)}, u32[]{:S(2)}) %collective-permute-start.44) | collective-permute-done | bytes 278560 | tf_op jit(solution)/shard_map/ppermute | solution.py:705
  218.5 2.7 %collective-permute-done.46.recv_ref = bf16[256,2176]{1,0:T(8,128)(2,1)S(1)} collective-permute-done((bf16[256,2176]{1,0:T(8,128)(2,1)S(1)}, bf16[256,2176]{1,0:T(8,128)(2,1)S(1)}, u32[]{:S(2)}, u32[]{:S(2)}) %collective-permute-start.46) | collective-permute-done | bytes 1114144 | tf_op jit(solution)/shard_map/ppermute | solution.py:705
  221.2 3.0 %finish_shared.1 = (f32[512,1536]{1,0:T(8,128)}, f32[512,512]{1,0:T(8,128)}, f32[512,128]{1,0:T(8,128)S(1)}) custom-call(s32[4]{0:T(128)S(1)} %add_add_fusion.meta_ref, bf16[256,2176]{1,0:T(8,128)(2,1)S(1)} %merge.15.mine_ref, bf16[256,2176]{1,0:T(8,128)(2,1)S(1)} %collective-permute-done.46.recv_ref), custom_call_target="tpu_custom_call" | custom-call | flops 1 | bytes 1 | tf_op jit(solution)/shard_map/finish_shared/pallas_call | solution.py:574
  (155 shorter events, 31.8 us)
Async XLA Ops:
  1.5 8.9 %collective-permute-start.4 = (s32[6,100]{1,0:T(8,128)S(1)}, s32[6,100]{1,0:T(8,128)S(1)}, u32[]{:S(2)}, u32[]{:S(2)}) collective-permute-start(s32[6,100]{1,0:T(8,128)S(1)} %bitcast.52), channel_id=1, source_target_pairs={{0,4},{4,0},{1,5},{5,1},{2,6},{6,2},{3,7},{7,3},{8,12},{12,8},{9,1... | collective-permute-start | bytes 7208 | tf_op jit(solution)/shard_map/ppermute | solution.py:705
  4.9 27.8 %collective-permute-start = (bf16[4,256,256]{2,1,0:T(8,128)(2,1)}, bf16[4,256,256]{2,1,0:T(8,128)(2,1)}, u32[]{:S(2)}, u32[]{:S(2)}) collective-permute-start(bf16[4,256,256]{2,1,0:T(8,128)(2,1)} %pad_maximum_fusion.2), channel_id=1, source_target_pairs={{0,2},{1,3},{2,0},{3,1},{4,6},{5,7},{6,4},{7,5},{8,10},{9,11},{10,... | collective-permute-start | bytes 1572872 | tf_op jit(solution)/shard_map/ppermute | solution.py:705
  8.5 3.9 %collective-permute-start.3 = (bf16[6,100,512]{2,1,0:T(8,128)(2,1)S(1)}, bf16[6,100,512]{2,1,0:T(8,128)(2,1)S(1)}, u32[]{:S(2)}, u32[]{:S(2)}) collective-permute-start(bf16[6,100,512]{2,1,0:T(8,128)(2,1)S(1)} %copy-done.29), channel_id=1, source_target_pairs={{0,4},{4,0},{1,5},{5,1},{2,6},{6,2},{3,7},{7,3},{8,12},{12,8},{9,1... | collective-permute-start | bytes 1843208 | tf_op jit(solution)/shard_map/ppermute | solution.py:705
  8.7 26.7 %collective-permute-start.1 = (bf16[6,100,512]{2,1,0:T(8,128)(2,1)S(1)}, bf16[6,100,512]{2,1,0:T(8,128)(2,1)S(1)}, u32[]{:S(2)}, u32[]{:S(2)}) collective-permute-start(bf16[6,100,512]{2,1,0:T(8,128)(2,1)S(1)} %copy-done.29), channel_id=1, source_target_pairs={{0,1},{1,0},{2,3},{3,2},{4,5},{5,4},{6,7},{7,6},{8,9},{9,8},{10,11... | collective-permute-start | bytes 1843208 | tf_op jit(solution)/shard_map/ppermute | solution.py:705
  10.3 2.1 collective-permute-start.2
  23.5 27.2 %copy-start.4 = (bf16[600,512]{1,0:T(8,128)(2,1)}, bf16[600,512]{1,0:T(8,128)(2,1)S(1)}, u32[]{:S(2)}) copy-start(bf16[600,512]{1,0:T(8,128)(2,1)S(1)} %get-tuple-element.155.dy_ref) | copy-start | bytes 1843204
  35.4 16.2 %collective-permute-start.8 = (bf16[624,512]{1,0:T(8,128)(2,1)S(1)}, bf16[624,512]{1,0:T(8,128)(2,1)S(1)}, u32[]{:S(2)}, u32[]{:S(2)}) collective-permute-start(bf16[624,512]{1,0:T(8,128)(2,1)S(1)} %pad_maximum_fusion.1), channel_id=1, source_target_pairs={{0,1},{1,0},{2,3},{3,2},{4,5},{5,4},{6,7},{7,6},{8,9},{9,8},{10,11... | collective-permute-start | bytes 1916936 | tf_op jit(solution)/shard_map/ppermute | solution.py:705
  36.8 13.9 %collective-permute-start.9 = (bf16[6,100,512]{2,1,0:T(8,128)(2,1)S(1)}, bf16[6,100,512]{2,1,0:T(8,128)(2,1)S(1)}, u32[]{:S(2)}, u32[]{:S(2)}) collective-permute-start(bf16[6,100,512]{2,1,0:T(8,128)(2,1)S(1)} %collective-permute-done.1.own_ref), channel_id=1, source_target_pairs={{0,4},{4,0},{1,5},{5,1},{2,6},{6,2},{3,7},{7,3},{8,12},{12,8},{9,1... | collective-permute-start | bytes 1843208 | tf_op jit(solution)/shard_map/ppermute | solution.py:705
  36.8 26.1 %collective-permute-start.7 = (bf16[4,256,256]{2,1,0:T(8,128)(2,1)}, bf16[4,256,256]{2,1,0:T(8,128)(2,1)S(1)}, u32[]{:S(2)}, u32[]{:S(2)}) collective-permute-start(bf16[4,256,256]{2,1,0:T(8,128)(2,1)} %collective-permute-done), channel_id=1, source_target_pairs={{0,24},{8,16},{16,8},{24,0},{1,25},{9,17},{17,9},{25,1},{2,26},{10... | collective-permute-start | bytes 1572872 | tf_op jit(solution)/shard_map/ppermute | solution.py:705
  39.2 24.2 %collective-permute-start.6 = (bf16[4,256,256]{2,1,0:T(8,128)(2,1)}, bf16[4,256,256]{2,1,0:T(8,128)(2,1)S(1)}, u32[]{:S(2)}, u32[]{:S(2)}) collective-permute-start(bf16[4,256,256]{2,1,0:T(8,128)(2,1)} %collective-permute-done), channel_id=1, source_target_pairs={{0,16},{8,24},{16,0},{24,8},{1,17},{9,25},{17,1},{25,9},{2,18},{10... | collective-permute-start | bytes 1572872 | tf_op jit(solution)/shard_map/ppermute | solution.py:705
  39.7 23.8 %collective-permute-start.5 = (bf16[4,256,256]{2,1,0:T(8,128)(2,1)}, bf16[4,256,256]{2,1,0:T(8,128)(2,1)S(1)}, u32[]{:S(2)}, u32[]{:S(2)}) collective-permute-start(bf16[4,256,256]{2,1,0:T(8,128)(2,1)} %collective-permute-done), channel_id=1, source_target_pairs={{0,8},{8,0},{16,24},{24,16},{1,9},{9,1},{17,25},{25,17},{2,10},{10... | collective-permute-start | bytes 1572872 | tf_op jit(solution)/shard_map/ppermute | solution.py:705
  64.9 9.3 %collective-permute-start.10 = (bf16[4,4,256,256]{3,2,1,0:T(8,128)(2,1)S(1)}, bf16[4,4,256,256]{3,2,1,0:T(8,128)(2,1)S(1)}, u32[]{:S(2)}, u32[]{:S(2)}) collective-permute-start(bf16[4,4,256,256]{3,2,1,0:T(8,128)(2,1)S(1)} %pad_maximum_fusion.rest_0_.rest_1_.rest_2_.rest_3_), channel_id=1, source_target_pairs={{0,4},{4,0},{1,5},{5,1},{2,6},{6,2},{3,7},{7,3},{8,12},{12,8},{9,1... | collective-permute-start | bytes 6291464 | tf_op jit(solution)/shard_map/ppermute | solution.py:705
  75.5 15.3 %collective-permute-start.11 = (bf16[4,256,512]{2,1,0:T(8,128)(2,1)}, bf16[4,256,512]{2,1,0:T(8,128)(2,1)}, u32[]{:S(2)}, u32[]{:S(2)}) collective-permute-start(bf16[4,256,512]{2,1,0:T(8,128)(2,1)} %get-tuple-element.175), channel_id=1, source_target_pairs={{0,4},{4,0},{1,5},{5,1},{2,6},{6,2},{3,7},{7,3},{8,12},{12,8},{9,1... | collective-permute-start | bytes 3145736 | tf_op jit(solution)/shard_map/ppermute | solution.py:705
  75.9 14.9 %collective-permute-start.12 = (bf16[4,256,512]{2,1,0:T(8,128)(2,1)}, bf16[4,256,512]{2,1,0:T(8,128)(2,1)}, u32[]{:S(2)}, u32[]{:S(2)}) collective-permute-start(bf16[4,256,512]{2,1,0:T(8,128)(2,1)} %get-tuple-element.177), channel_id=1, source_target_pairs={{0,4},{4,0},{1,5},{5,1},{2,6},{6,2},{3,7},{7,3},{8,12},{12,8},{9,1... | collective-permute-start | bytes 3145736 | tf_op jit(solution)/shard_map/ppermute | solution.py:705
  93.0 21.3 %collective-permute-start.13 = (bf16[640,512]{1,0:T(8,128)(2,1)S(1)}, bf16[640,512]{1,0:T(8,128)(2,1)S(1)}, u32[]{:S(2)}, u32[]{:S(2)}) collective-permute-start(bf16[640,512]{1,0:T(8,128)(2,1)S(1)} %get-tuple-element.189), channel_id=1, source_target_pairs={{0,1},{1,0},{2,3},{3,2},{4,5},{5,4},{6,7},{7,6},{8,9},{9,8},{10,11... | collective-permute-start | bytes 1966088 | tf_op jit(solution)/shard_map/ppermute | solution.py:705
  93.8 20.5 %collective-permute-start.14 = (bf16[2,256,512]{2,1,0:T(8,128)(2,1)S(1)}, bf16[2,256,512]{2,1,0:T(8,128)(2,1)S(1)}, u32[]{:S(2)}, u32[]{:S(2)}) collective-permute-start(bf16[2,256,512]{2,1,0:T(8,128)(2,1)S(1)} %get-tuple-element.190), channel_id=1, source_target_pairs={{0,16},{8,24},{16,0},{24,8},{1,17},{9,25},{17,1},{25,9},{2,18},{10... | collective-permute-start | bytes 1572872 | tf_op jit(solution)/shard_map/ppermute | solution.py:705
  95.3 19.1 %collective-permute-start.15 = (bf16[2,1,256,512]{3,2,1,0:T(8,128)(2,1)S(1)}, bf16[2,1,256,512]{3,2,1,0:T(8,128)(2,1)S(1)}, u32[]{:S(2)}, u32[]{:S(2)}) collective-permute-start(bf16[2,1,256,512]{3,2,1,0:T(8,128)(2,1)S(1)} %get-tuple-element.191), channel_id=1, source_target_pairs={{0,8},{8,0},{16,24},{24,16},{1,9},{9,1},{17,25},{25,17},{2,10},{10... | collective-permute-start | bytes 1572872 | tf_op jit(solution)/shard_map/ppermute | solution.py:705
  114.4 2.7 %collective-permute-start.16 = (bf16[4,256,512]{2,1,0:T(8,128)(2,1)S(1)}, bf16[4,256,512]{2,1,0:T(8,128)(2,1)S(1)}, u32[]{:S(2)}, u32[]{:S(2)}) collective-permute-start(bf16[4,256,512]{2,1,0:T(8,128)(2,1)S(1)} %get-tuple-element.206), channel_id=1, source_target_pairs={{0,4},{4,0},{1,5},{5,1},{2,6},{6,2},{3,7},{7,3},{8,12},{12,8},{9,1... | collective-permute-start | bytes 3145736 | tf_op jit(solution)/shard_map/ppermute | solution.py:705
  114.5 4.1 %collective-permute-start.17 = (bf16[4,256,512]{2,1,0:T(8,128)(2,1)S(1)}, bf16[4,256,512]{2,1,0:T(8,128)(2,1)S(1)}, u32[]{:S(2)}, u32[]{:S(2)}) collective-permute-start(bf16[4,256,512]{2,1,0:T(8,128)(2,1)S(1)} %get-tuple-element.208), channel_id=1, source_target_pairs={{0,4},{4,0},{1,5},{5,1},{2,6},{6,2},{3,7},{7,3},{8,12},{12,8},{9,1... | collective-permute-start | bytes 3145736 | tf_op jit(solution)/shard_map/ppermute | solution.py:705
  115.0 18.9 %collective-permute-start.20 = (bf16[600,512]{1,0:T(8,128)(2,1)S(1)}, bf16[600,512]{1,0:T(8,128)(2,1)S(1)}, u32[]{:S(2)}, u32[]{:S(2)}) collective-permute-start(bf16[600,512]{1,0:T(8,128)(2,1)S(1)} %get-tuple-element.221), channel_id=1, source_target_pairs={{0,1},{1,0},{2,3},{3,2},{4,5},{5,4},{6,7},{7,6},{8,9},{9,8},{10,11... | collective-permute-start | bytes 1843208 | tf_op jit(solution)/shard_map/ppermute | solution.py:705
  119.1 14.0 %collective-permute-start.18 = (bf16[2,256,512]{2,1,0:T(8,128)(2,1)S(1)}, bf16[2,256,512]{2,1,0:T(8,128)(2,1)S(1)}, u32[]{:S(2)}, u32[]{:S(2)}) collective-permute-start(bf16[2,256,512]{2,1,0:T(8,128)(2,1)S(1)} %get-tuple-element.210), channel_id=1, source_target_pairs={{0,16},{8,24},{16,0},{24,8},{1,17},{9,25},{17,1},{25,9},{2,18},{10... | collective-permute-start | bytes 1572872 | tf_op jit(solution)/shard_map/ppermute | solution.py:705
  119.7 13.7 %collective-permute-start.19 = (bf16[2,1,256,512]{3,2,1,0:T(8,128)(2,1)S(1)}, bf16[2,1,256,512]{3,2,1,0:T(8,128)(2,1)S(1)}, u32[]{:S(2)}, u32[]{:S(2)}) collective-permute-start(bf16[2,1,256,512]{3,2,1,0:T(8,128)(2,1)S(1)} %get-tuple-element.214), channel_id=1, source_target_pairs={{0,8},{8,0},{16,24},{24,16},{1,9},{9,1},{17,25},{25,17},{2,10},{10... | collective-permute-start | bytes 1572872 | tf_op jit(solution)/shard_map/ppermute | solution.py:705
  133.9 14.9 %collective-permute-start.23 = (bf16[256,2176]{1,0:T(8,128)(2,1)S(1)}, bf16[256,2176]{1,0:T(8,128)(2,1)S(1)}, u32[]{:S(2)}, u32[]{:S(2)}) collective-permute-start(bf16[256,2176]{1,0:T(8,128)(2,1)S(1)} %get-tuple-element.238), channel_id=1, source_target_pairs={{0,4},{4,0},{1,5},{5,1},{2,6},{6,2},{3,7},{7,3},{8,12},{12,8},{9,1... | collective-permute-start | bytes 3342344 | tf_op jit(solution)/shard_map/ppermute | solution.py:705
  134.0 14.3 %collective-permute-start.21 = (bf16[2,1,256,512]{3,2,1,0:T(8,128)(2,1)S(1)}, bf16[2,1,256,512]{3,2,1,0:T(8,128)(2,1)S(1)}, u32[]{:S(2)}, u32[]{:S(2)}) collective-permute-start(bf16[2,1,256,512]{3,2,1,0:T(8,128)(2,1)S(1)} %get-tuple-element.234), channel_id=1, source_target_pairs={{0,8},{8,0},{16,24},{24,16},{1,9},{9,1},{17,25},{25,17},{2,10},{10... | collective-permute-start | bytes 1572872 | tf_op jit(solution)/shard_map/ppermute | solution.py:705
  134.8 14.0 %collective-permute-start.22 = (bf16[2,1,1,256,512]{4,3,2,1,0:T(8,128)(2,1)S(1)}, bf16[2,1,1,256,512]{4,3,2,1,0:T(8,128)(2,1)S(1)}, u32[]{:S(2)}, u32[]{:S(2)}) collective-permute-start(bf16[2,1,1,256,512]{4,3,2,1,0:T(8,128)(2,1)S(1)} %get-tuple-element.236), channel_id=1, source_target_pairs={{0,16},{8,24},{16,0},{24,8},{1,17},{9,25},{17,1},{25,9},{2,18},{10... | collective-permute-start | bytes 1572872 | tf_op jit(solution)/shard_map/ppermute | solution.py:705
  136.3 13.0 %collective-permute-start.24 = (bf16[3,100,512]{2,1,0:T(8,128)(2,1)S(1)}, bf16[3,100,512]{2,1,0:T(8,128)(2,1)S(1)}, u32[]{:S(2)}, u32[]{:S(2)}) collective-permute-start(bf16[3,100,512]{2,1,0:T(8,128)(2,1)S(1)} %get-tuple-element.247), channel_id=1, source_target_pairs={{0,4},{4,0},{1,5},{5,1},{2,6},{6,2},{3,7},{7,3},{8,12},{12,8},{9,1... | collective-permute-start | bytes 921608 | tf_op jit(solution)/shard_map/ppermute | solution.py:705
  137.4 11.9 %collective-permute-start.25 = (bf16[3,100,512]{2,1,0:T(8,128)(2,1)S(1)}, bf16[3,100,512]{2,1,0:T(8,128)(2,1)S(1)}, u32[]{:S(2)}, u32[]{:S(2)}) collective-permute-start(bf16[3,100,512]{2,1,0:T(8,128)(2,1)S(1)} %get-tuple-element.250), channel_id=1, source_target_pairs={{0,4},{4,0},{1,5},{5,1},{2,6},{6,2},{3,7},{7,3},{8,12},{12,8},{9,1... | collective-permute-start | bytes 921608 | tf_op jit(solution)/shard_map/ppermute | solution.py:705
  149.3 28.0 %collective-permute-start.28 = (bf16[64,2176]{1,0:T(8,128)(2,1)S(1)}, bf16[64,2176]{1,0:T(8,128)(2,1)S(1)}, u32[]{:S(2)}, u32[]{:S(2)}) collective-permute-start(bf16[64,2176]{1,0:T(8,128)(2,1)S(1)} %get-tuple-element.256), channel_id=1, source_target_pairs={{0,8},{8,0},{16,24},{24,16},{1,9},{9,1},{17,25},{25,17},{2,10},{10... | collective-permute-start | bytes 835592 | tf_op jit(solution)/shard_map/ppermute | solution.py:705
  150.6 26.7 %collective-permute-start.29 = (bf16[64,2176]{1,0:T(8,128)(2,1)S(1)}, bf16[64,2176]{1,0:T(8,128)(2,1)S(1)}, u32[]{:S(2)}, u32[]{:S(2)}) collective-permute-start(bf16[64,2176]{1,0:T(8,128)(2,1)S(1)} %get-tuple-element.257), channel_id=1, source_target_pairs={{0,16},{8,24},{16,0},{24,8},{1,17},{9,25},{17,1},{25,9},{2,18},{10... | collective-permute-start | bytes 835592 | tf_op jit(solution)/shard_map/ppermute | solution.py:705
  152.1 25.2 %collective-permute-start.30 = (bf16[64,2176]{1,0:T(8,128)(2,1)S(1)}, bf16[64,2176]{1,0:T(8,128)(2,1)S(1)}, u32[]{:S(2)}, u32[]{:S(2)}) collective-permute-start(bf16[64,2176]{1,0:T(8,128)(2,1)S(1)} %get-tuple-element.258), channel_id=1, source_target_pairs={{0,24},{8,16},{16,8},{24,0},{1,25},{9,17},{17,9},{25,1},{2,26},{10... | collective-permute-start | bytes 835592 | tf_op jit(solution)/shard_map/ppermute | solution.py:705
  152.9 19.8 %collective-permute-start.26 = (bf16[1,256,512]{2,1,0:T(8,128)(2,1)S(1)}, bf16[1,256,512]{2,1,0:T(8,128)(2,1)S(1)}, u32[]{:S(2)}, u32[]{:S(2)}) collective-permute-start(bf16[1,256,512]{2,1,0:T(8,128)(2,1)S(1)} %get-tuple-element.252), channel_id=1, source_target_pairs={{0,2},{1,3},{2,0},{3,1},{4,6},{5,7},{6,4},{7,5},{8,10},{9,11},{10,... | collective-permute-start | bytes 786440 | tf_op jit(solution)/shard_map/ppermute | solution.py:705
  154.3 23.0 %collective-permute-start.27 = (bf16[1,1,256,512]{3,2,1,0:T(8,128)(2,1)S(1)}, bf16[1,1,256,512]{3,2,1,0:T(8,128)(2,1)S(1)}, u32[]{:S(2)}, u32[]{:S(2)}) collective-permute-start(bf16[1,1,256,512]{3,2,1,0:T(8,128)(2,1)S(1)} %get-tuple-element.254), channel_id=1, source_target_pairs={{0,2},{1,3},{2,0},{3,1},{4,6},{5,7},{6,4},{7,5},{8,10},{9,11},{10,... | collective-permute-start | bytes 786440 | tf_op jit(solution)/shard_map/ppermute | solution.py:705
  177.6 11.6 %collective-permute-start.31 = (bf16[1,256,512]{2,1,0:T(8,128)(2,1)S(1)}, bf16[1,256,512]{2,1,0:T(8,128)(2,1)S(1)}, u32[]{:S(2)}, u32[]{:S(2)}) collective-permute-start(bf16[1,256,512]{2,1,0:T(8,128)(2,1)S(1)} %get-tuple-element.273.refs_0_), channel_id=1, source_target_pairs={{0,8},{8,0},{16,24},{24,16},{1,9},{9,1},{17,25},{25,17},{2,10},{10... | collective-permute-start | bytes 786440 | tf_op jit(solution)/shard_map/ppermute | solution.py:705
  178.9 10.2 %collective-permute-start.32 = (bf16[1,1,256,512]{3,2,1,0:T(8,128)(2,1)S(1)}, bf16[1,1,256,512]{3,2,1,0:T(8,128)(2,1)S(1)}, u32[]{:S(2)}, u32[]{:S(2)}) collective-permute-start(bf16[1,1,256,512]{3,2,1,0:T(8,128)(2,1)S(1)} %get-tuple-element.274.refs_2_), channel_id=1, source_target_pairs={{0,16},{8,24},{16,0},{24,8},{1,17},{9,25},{17,1},{25,9},{2,18},{10... | collective-permute-start | bytes 786440 | tf_op jit(solution)/shard_map/ppermute | solution.py:705
  180.4 4.4 %collective-permute-start.33 = (bf16[16,2176]{1,0:T(8,128)(2,1)S(1)}, bf16[16,2176]{1,0:T(8,128)(2,1)S(1)}, u32[]{:S(2)}, u32[]{:S(2)}) collective-permute-start(bf16[16,2176]{1,0:T(8,128)(2,1)S(1)} %get-tuple-element.276), channel_id=1, source_target_pairs={{0,1},{1,0},{2,3},{3,2},{4,5},{5,4},{6,7},{7,6},{8,9},{9,8},{10,11... | collective-permute-start | bytes 208904 | tf_op jit(solution)/shard_map/ppermute | solution.py:705
  180.4 7.2 %collective-permute-start.34 = (bf16[16,2176]{1,0:T(8,128)(2,1)S(1)}, bf16[16,2176]{1,0:T(8,128)(2,1)S(1)}, u32[]{:S(2)}, u32[]{:S(2)}) collective-permute-start(bf16[16,2176]{1,0:T(8,128)(2,1)S(1)} %get-tuple-element.277), channel_id=1, source_target_pairs={{0,2},{1,3},{2,0},{3,1},{4,6},{5,7},{6,4},{7,5},{8,10},{9,11},{10,... | collective-permute-start | bytes 208904 | tf_op jit(solution)/shard_map/ppermute | solution.py:705
  183.1 6.1 %collective-permute-start.35 = (bf16[16,2176]{1,0:T(8,128)(2,1)S(1)}, bf16[16,2176]{1,0:T(8,128)(2,1)S(1)}, u32[]{:S(2)}, u32[]{:S(2)}) collective-permute-start(bf16[16,2176]{1,0:T(8,128)(2,1)S(1)} %get-tuple-element.278), channel_id=1, source_target_pairs={{0,3},{1,2},{2,1},{3,0},{4,7},{5,6},{6,5},{7,4},{8,11},{9,10},{10,... | collective-permute-start | bytes 208904 | tf_op jit(solution)/shard_map/ppermute | solution.py:705
  189.3 11.7 %collective-permute-start.36 = (bf16[2,256,512]{2,1,0:T(8,128)(2,1)S(1)}, bf16[2,256,512]{2,1,0:T(8,128)(2,1)S(1)}, u32[]{:S(2)}, u32[]{:S(2)}) collective-permute-start(bf16[2,256,512]{2,1,0:T(8,128)(2,1)S(1)} %get-tuple-element.279.refs_0_), channel_id=1, source_target_pairs={{0,16},{8,24},{16,0},{24,8},{1,17},{9,25},{17,1},{25,9},{2,18},{10... | collective-permute-start | bytes 1572872 | tf_op jit(solution)/shard_map/ppermute | solution.py:705
  190.2 11.9 %collective-permute-start.37 = (bf16[2,1,256,512]{3,2,1,0:T(8,128)(2,1)S(1)}, bf16[2,1,256,512]{3,2,1,0:T(8,128)(2,1)S(1)}, u32[]{:S(2)}, u32[]{:S(2)}) collective-permute-start(bf16[2,1,256,512]{3,2,1,0:T(8,128)(2,1)S(1)} %get-tuple-element.280.refs_2_), channel_id=1, source_target_pairs={{0,8},{8,0},{16,24},{24,16},{1,9},{9,1},{17,25},{25,17},{2,10},{10... | collective-permute-start | bytes 1572872 | tf_op jit(solution)/shard_map/ppermute | solution.py:705
  191.0 6.1 %collective-permute-start.40 = (bf16[16,2176]{1,0:T(8,128)(2,1)S(1)}, bf16[16,2176]{1,0:T(8,128)(2,1)S(1)}, u32[]{:S(2)}, u32[]{:S(2)}) collective-permute-start(bf16[16,2176]{1,0:T(8,128)(2,1)S(1)} %get-tuple-element.281.refs_4_), channel_id=1, source_target_pairs={{0,3},{1,2},{2,1},{3,0},{4,7},{5,6},{6,5},{7,4},{8,11},{9,10},{10,... | collective-permute-start | bytes 208904 | tf_op jit(solution)/shard_map/ppermute | solution.py:705
  192.5 6.0 %collective-permute-start.39 = (bf16[16,2176]{1,0:T(8,128)(2,1)S(1)}, bf16[16,2176]{1,0:T(8,128)(2,1)S(1)}, u32[]{:S(2)}, u32[]{:S(2)}) collective-permute-start(bf16[16,2176]{1,0:T(8,128)(2,1)S(1)} %get-tuple-element.281.refs_4_), channel_id=1, source_target_pairs={{0,2},{1,3},{2,0},{3,1},{4,6},{5,7},{6,4},{7,5},{8,10},{9,11},{10,... | collective-permute-start | bytes 208904 | tf_op jit(solution)/shard_map/ppermute | solution.py:705
  192.5 6.0 %collective-permute-start.38 = (bf16[16,2176]{1,0:T(8,128)(2,1)S(1)}, bf16[16,2176]{1,0:T(8,128)(2,1)S(1)}, u32[]{:S(2)}, u32[]{:S(2)}) collective-permute-start(bf16[16,2176]{1,0:T(8,128)(2,1)S(1)} %get-tuple-element.281.refs_4_), channel_id=1, source_target_pairs={{0,1},{1,0},{2,3},{3,2},{4,5},{5,4},{6,7},{7,6},{8,9},{9,8},{10,11... | collective-permute-start | bytes 208904 | tf_op jit(solution)/shard_map/ppermute | solution.py:705
  202.2 4.1 %collective-permute-start.42 = (bf16[4,256,512]{2,1,0:T(8,128)(2,1)S(1)}, bf16[4,256,512]{2,1,0:T(8,128)(2,1)S(1)}, u32[]{:S(2)}, u32[]{:S(2)}) collective-permute-start(bf16[4,256,512]{2,1,0:T(8,128)(2,1)S(1)} %bitcast.38), channel_id=1, source_target_pairs={{0,4},{4,0},{1,5},{5,1},{2,6},{6,2},{3,7},{7,3},{8,12},{12,8},{9,1... | collective-permute-start | bytes 3145736 | tf_op jit(solution)/shard_map/ppermute | solution.py:705
  202.3 4.1 %collective-permute-start.41 = (bf16[4,256,512]{2,1,0:T(8,128)(2,1)S(1)}, bf16[4,256,512]{2,1,0:T(8,128)(2,1)S(1)}, u32[]{:S(2)}, u32[]{:S(2)}) collective-permute-start(bf16[4,256,512]{2,1,0:T(8,128)(2,1)S(1)} %get-tuple-element.283.im_ref), channel_id=1, source_target_pairs={{0,4},{4,0},{1,5},{5,1},{2,6},{6,2},{3,7},{7,3},{8,12},{12,8},{9,1... | collective-permute-start | bytes 3145736 | tf_op jit(solution)/shard_map/ppermute | solution.py:705
  202.8 10.5 %collective-permute-start.45 = (bf16[64,2176]{1,0:T(8,128)(2,1)S(1)}, bf16[64,2176]{1,0:T(8,128)(2,1)S(1)}, u32[]{:S(2)}, u32[]{:S(2)}) collective-permute-start(bf16[64,2176]{1,0:T(8,128)(2,1)S(1)} %get-tuple-element.287.refs_0_), channel_id=1, source_target_pairs={{0,24},{8,16},{16,8},{24,0},{1,25},{9,17},{17,9},{25,1},{2,26},{10... | collective-permute-start | bytes 835592 | tf_op jit(solution)/shard_map/ppermute | solution.py:705
  204.4 13.9 %collective-permute-start.44 = (bf16[64,2176]{1,0:T(8,128)(2,1)S(1)}, bf16[64,2176]{1,0:T(8,128)(2,1)S(1)}, u32[]{:S(2)}, u32[]{:S(2)}) collective-permute-start(bf16[64,2176]{1,0:T(8,128)(2,1)S(1)} %get-tuple-element.287.refs_0_), channel_id=1, source_target_pairs={{0,16},{8,24},{16,0},{24,8},{1,17},{9,25},{17,1},{25,9},{2,18},{10... | collective-permute-start | bytes 835592 | tf_op jit(solution)/shard_map/ppermute | solution.py:705
  205.0 13.3 %collective-permute-start.43 = (bf16[64,2176]{1,0:T(8,128)(2,1)S(1)}, bf16[64,2176]{1,0:T(8,128)(2,1)S(1)}, u32[]{:S(2)}, u32[]{:S(2)}) collective-permute-start(bf16[64,2176]{1,0:T(8,128)(2,1)S(1)} %get-tuple-element.287.refs_0_), channel_id=1, source_target_pairs={{0,8},{8,0},{16,24},{24,16},{1,9},{9,1},{17,25},{25,17},{2,10},{10... | collective-permute-start | bytes 835592 | tf_op jit(solution)/shard_map/ppermute | solution.py:705
  218.4 2.8 %collective-permute-start.46 = (bf16[256,2176]{1,0:T(8,128)(2,1)S(1)}, bf16[256,2176]{1,0:T(8,128)(2,1)S(1)}, u32[]{:S(2)}, u32[]{:S(2)}) collective-permute-start(bf16[256,2176]{1,0:T(8,128)(2,1)S(1)} %merge.15.mine_ref), channel_id=1, source_target_pairs={{0,4},{4,0},{1,5},{5,1},{2,6},{6,2},{3,7},{7,3},{8,12},{12,8},{9,1... | collective-permute-start | bytes 3342344 | tf_op jit(solution)/shard_map/ppermute | solution.py:705
  (32 other events, 211.9 us)

commit v4 on v3

--- a/solution.py
+++ b/solution.py
@@ -191,17 +191,31 @@
 
 
 def expert_kernel(add, local, meta_ref, rows_ref, dy_ref, ids_ref, wr_ref, *rest):
-    weights, rest = (rest[:4], rest[4:]) if local else (rest[:8], rest[8:])
+    wi_ref, wb_ref, *rest = rest
+    sources = [] if local else [wb_ref]
     if add:
-        pmade_ref, pdin_ref, *rest = rest
+        sources += rest[:2]
+        rest = rest[2:]
     act_ref, dpre_ref, dout_ref, made_ref, din_ref, gate_s, made_s, din_s, *rest = rest
     step = pl.program_id(0)
+    copies = []
+    if sources:
+        *rest, sems = rest
+        landings = rest[len(rest) - len(sources) :]
+        rest = rest[: len(rest) - len(sources)]
+        copies = [pltpu.make_async_copy(v, w, sems.at[n]) for n, (v, w) in enumerate(zip(sources, landings))]
+    if not local:
+        wb_ref = landings[0]
+    if add:
+        pmade_ref, pdin_ref = landings[-2:]
     count = act_ref.shape[0]
     width = rows_ref.shape[1]
     rows = rows_ref[0:count, :]
 
     @pl.when(step == 0)
     def _():
+        for copy in copies:
+            copy.start()
         if ids_ref.shape[0] == 2:
             ids = ids_ref[...].astype(F32)
         else:
@@ -218,19 +232,28 @@
         din_s[...] = jnp.zeros_like(din_s)
 
     if local:
-        w_in = jnp.concatenate([ref[0] for ref in weights[:2]], axis=1)
-        w_back = jnp.concatenate([ref[0] for ref in weights[2:]], axis=0)
+        part = wi_ref.shape[2] // PIECES
+        at = [pl.multiple_of(((2 * step + s) ^ meta_ref[1]) * part, part) for s in range(2)]
+        w_in = jnp.concatenate([wi_ref[0, :, pl.ds(v, part)] for v in at], axis=1)
+        w_back = jnp.concatenate([wb_ref[0, pl.ds(v, part), :] for v in at], axis=0)
     else:
         wi_s, wb_s = rest
         part = wi_s.shape[0] // 2
-        for side in range(2):
-
-            @pl.when((step < pl.num_programs(0) // 2) == (side == 0))
+        upper = pl.num_programs(0) // 2
+
+        @pl.when(step == upper)
+        def _():
+            copies[0].wait()
+
+        for ref, first in ((wi_ref, 0), (wb_ref, upper)):
+
+            @pl.when((step < upper) == (first == 0))
             def _():
                 for s in range(2):
                     for h in range(2):
-                        wi_s[h * part : (h + 1) * part, s * part : (s + 1) * part] = weights[4 * side + s][0, h]
-                        wb_s[s * part : (s + 1) * part, h * part : (h + 1) * part] = weights[4 * side + 2 + s][0, h]
+                        at = 2 * (step - first) + s
+                        wi_s[h * part : (h + 1) * part, s * part : (s + 1) * part] = ref[at, h]
+                        wb_s[s * part : (s + 1) * part, h * part : (h + 1) * part] = ref[at, 2 + h]
 
         w_in, w_back = wi_s[...], wb_s[...]
     pre = mm(rows, w_in)
@@ -259,6 +282,8 @@
         row = lax.broadcasted_iota(jnp.int32, d_gate.shape, 0)
         d_gate = jnp.where(row == meta_ref[0], d_gate, 0.0)
         tail = padded(count)
+        for copy in copies[0 if local else 1 :]:
+            copy.wait()
         if add:
             total += pmade_ref[...].astype(F32)
             d_in += pdin_ref[0:count, :].astype(F32)
@@ -295,44 +320,44 @@
     hidden = PIECES * piece
     steps = PIECES // 2
     deep = padded(count) + 16 * -(-count // width)
-    if local:
-        cuts = [pl.BlockSpec((1, width, piece), lambda q, m, s=s: (0, 0, (2 * q + s) ^ m[1])) for s in (0, 1)]
-        cuts += [pl.BlockSpec((1, piece, width), lambda q, m, s=s: (0, (2 * q + s) ^ m[1], 0)) for s in (0, 1)]
-        weights = [held(weights[0])] * 2 + [held(weights[1])] * 2
-    else:
-        block = (1, 2, piece, piece)
-        near = lambda q: jnp.minimum(q, steps // 2 - 1)
-        away = lambda q: jnp.maximum(q - steps // 2, 0)
-        cuts = [
-            pl.BlockSpec(block, lambda q, m, s=s, g=g, at=at: (2 * at(q) + s, g, 0, 0))
-            for at in (near, away) for g in (0, 1) for s in (0, 1)
-        ]
-        weights = [weights[0]] * 4 + [weights[1]] * 4
-    more = [] if prev is None else [HERE, HERE]
+    fix = lambda *s: pl.BlockSpec(s, lambda q, m: (0,) * len(s))
+    first = prev is None
+    away = pl.BlockSpec(memory_space=pl.ANY)
+    more = [] if first else [away, away]
+    landings = [] if local else [pltpu.VMEM(weights[1].shape, BF16)]
+    if not first:
+        landings += [pltpu.VMEM((count, width), BF16), pltpu.VMEM((deep, width), BF16)]
+    if landings:
+        landings.append(pltpu.SemaphoreType.DMA((len(landings),)))
+    given = [] if first else [held(v) for v in prev]
+    ends = [fix(count, width), fix(deep, width)] if first else [HERE, HERE]
+    kept = HELD if first else jax.ShapeDtypeStruct
     return pl.pallas_call(
         functools.partial(expert_kernel, prev is not None, local),
         grid_spec=pltpu.PrefetchScalarGridSpec(
             num_scalar_prefetch=1,
             grid=(steps,),
-            in_specs=[HERE] * 4 + [*cuts, *more],
-            out_specs=[HERE] * 5,
+            in_specs=[HERE, fix(*dy.shape), HERE, HERE, HERE, HERE if local else away, *more],
+            out_specs=[HERE] * 3 + ends,
             scratch_shapes=[
                 pltpu.VMEM((count, 128), F32),
                 pltpu.VMEM((count, width), F32),
                 pltpu.VMEM((count, width), F32),
-            ] + ([] if local else [pltpu.VMEM((width, 2 * piece), BF16), pltpu.VMEM((2 * piece, width), BF16)]),
+            ]
+            + ([] if local else [pltpu.VMEM((width, 2 * piece), BF16), pltpu.VMEM((2 * piece, width), BF16)])
+            + landings,
         ),
         out_shape=[
             jax.ShapeDtypeStruct((count, hidden), BF16),
             jax.ShapeDtypeStruct((count, hidden), BF16),
             jax.ShapeDtypeStruct((count, width), BF16),
-            jax.ShapeDtypeStruct((count, width), BF16),
-            jax.ShapeDtypeStruct((deep, width), BF16),
+            kept((count, width), BF16),
+            kept((deep, width), BF16),
         ],
         compiler_params=pltpu.CompilerParams(vmem_limit_bytes=20 << 20),
         cost_estimate=BRIEF,
         name="expert",
-    )(meta, rows, dy, ids, wr, *weights, *(prev or ()))
+    )(meta, rows, dy if first else held(dy), ids, wr, weights[0], weights[1] if local else held(weights[1]), *given)
 
 
 def weight_kernel(n, *refs):
@@ -642,22 +667,48 @@
     )(meta, *arrays)
 
 
+def pack_kernel(meta_ref, wi_ref, wb_ref, out_ref):
+    part = out_ref.shape[1]
+    for h in range(2):
+        at = slice(h * part, (h + 1) * part)
+        out_ref[h] = wi_ref[0, at, :]
+        out_ref[2 + h] = wb_ref[0, :, at]
+
+
+def pack_piece(meta, w_in, w_back):
+    width, hidden = w_in.shape[1:]
+    piece = hidden // PIECES
+    return pl.pallas_call(
+        pack_kernel,
+        grid_spec=pltpu.PrefetchScalarGridSpec(
+            num_scalar_prefetch=1,
+            grid=(1,),
+            in_specs=[
+                pl.BlockSpec((1, width, piece), lambda i, m: (0, 0, m[1])),
+                pl.BlockSpec((1, piece, width), lambda i, m: (0, m[1], 0)),
+            ],
+            out_specs=pl.BlockSpec((4, piece, piece), lambda i, m: (0, 0, 0)),
+        ),
+        out_shape=jax.ShapeDtypeStruct((4, piece, piece), BF16),
+        compiler_params=pltpu.CompilerParams(vmem_limit_bytes=4 << 20),
+        cost_estimate=BRIEF,
+        name="pack_piece",
+    )(meta, held(w_in), held(w_back))
+
+
 def merge_kernel(plan, *refs):
     refs = list(refs)
-    takes = [[[refs.pop(0) for _ in range(n)] for n in sizes] for sizes, _, _ in plan]
+    takes = [[[(refs.pop(0), at) for at in views] for views in groups] for groups, _, _ in plan]
     for groups, (_, axis, cuts) in zip(takes, plan):
         outs = [refs.pop(0) for _ in cuts]
         if axis is not None:
-            size = groups[0][0].shape[axis]
-            for k, ref in enumerate(groups[0]):
+            size = groups[0][0][0].shape[axis]
+            for k, (ref, _) in enumerate(groups[0]):
                 at = slice(k * size, (k + 1) * size)
                 outs[0][(slice(None),) * axis + (at,)] = ref[...]
             continue
         for g, take in enumerate(groups):
-            total = take[0][...].astype(F32)
-            for ref in take[1:]:
-                total += ref[...].astype(F32)
-            total = total.astype(BF16)
+            total = sum(ref[at].astype(F32) for ref, at in take).astype(BF16)
             for out, cut in zip(outs, cuts):
                 if len(groups) > 1:
                     out[g] = total[cut]
@@ -668,7 +719,9 @@
 def merge(*items):
     plan, shapes, arrays = [], [], []
     for groups, axis, cuts in items:
-        first = jax.ShapeDtypeStruct(groups[0][0].shape, BF16)
+        head = groups[0][0]
+        shape = jax.eval_shape(lambda v: v[head[1]], head[0]).shape if isinstance(head, tuple) else head.shape
+        first = jax.ShapeDtypeStruct(shape, BF16)
         if axis is not None:
             cuts = [None]
             shape = list(first.shape)
@@ -679,8 +732,9 @@
             shapes += [
                 jax.ShapeDtypeStruct(lead + jax.eval_shape(lambda v, c=c: v[c], first).shape, BF16) for c in cuts
             ]
-        plan.append(([len(g) for g in groups], axis, cuts))
-        arrays += [v for g in groups for v in g]
+        pairs = [[v if isinstance(v, tuple) else (v, ...) for v in g] for g in groups]
+        plan.append(([[at for _, at in g] for g in pairs], axis, cuts))
+        arrays += [v for g in pairs for v, _ in g]
     return pl.pallas_call(
         functools.partial(merge_kernel, plan),
         out_shape=shapes,
@@ -745,12 +799,10 @@
     far = lambda v: send(v, "expert", xor(1))
     swap = lambda v: send(v, "ctx", SWAP)
 
-    codes = route_ids.reshape(nimg, half, TOP)
+    pack = pack_piece(meta, w_in, w_back)
+    codes = after(route_ids, pack).reshape(nimg, half, TOP)
     codes = codes[..., 0] + experts * codes[..., 1]
     tok_other, dy_other, codes_other = swap(tokens), swap(cotangent), swap(codes)
-    mine_in = lax.dynamic_slice_in_dim(w_in[0], me * piece, piece, 1)
-    mine_back = lax.dynamic_slice_in_dim(w_back[0], me * piece, piece, 0)
-    pack = jnp.stack([mine_in[:piece], mine_in[piece:], mine_back[:, :piece], mine_back[:, piece:]])
     first = jnp.where(core == 0, codes, codes_other)
     second = jnp.where(core == 0, codes_other, codes)
     codes = lax.dynamic_slice_in_dim(jnp.concatenate([first, second], 1), core * imgs, imgs, 0)
@@ -766,34 +818,37 @@
     x_rows, dy, normed, qkv, probs, mix, mid, routed = attend(
         meta, tokens, tok_other, cotangent, dy_other, key_mask, g1, w_qkv, w_out, g2
     )
+    own_one = expert(meta, routed, dy, ids, wr, (w_in, w_back))
     far_rows = jnp.concatenate([routed, ids_pack], 0)
-    pack, far_raw, far_rows, routed = tie(pack, far_raw, far_rows, routed)
+    pack, wr_far = after(pack, routed), after(wr, own_one[2])
 
     packs = [pack] + [send(pack, "dp", xor(k)) for k in (1, 2, 3)]
     far_rows = far(far_rows)
+    far_raw = after(far_raw, own_one[2])
     far_dy = assemble(meta, far_raw, swap(far_raw))
-    own_one = expert(meta, routed, dy, ids, wr, (w_in, w_back))
-    far_one = expert(meta, after(far_rows, own_one[4]), far_dy, far_rows, wr, (w_in, w_back))
-    *packs, far_din = tie(*packs, far_one[4])
-    far_one = [*far_one[:4], far_din]
-
+    far_one = expert(meta, far_rows, far_dy, far_rows, wr_far, (w_in, w_back))
+    *packs, wr_far = tie(*packs, after(wr, far_one[2]))
     packs = jnp.stack(packs)
     pair = [packs, swap(packs)]
     grads = weight_grads([routed, far_rows], *zip(own_one[:3], far_one[:3]), late=True)
-    *pair, a, a_give, b, b_give = tie(*pair, *grads)
-
-    far_two = expert(meta_pair, far_rows, far_dy, far_rows, wr, pair, far_one[3:])
+    wr_far = after(wr_far, grads[0])
+
+    far_two = expert(meta_pair, far_rows, far_dy, far_rows, wr_far, pair, far_one[3:])
     head, tail = slice(0, 2), slice(2, 4)
     even, odd = [(slice(None), slice(k, k + 1)) for k in (0, 1)]
     square = lambda v: v.reshape(2, 2, piece, width)
 
     def across(a, a_give, b, b_give):
-        return merge(([[a, swap(a_give)]], None, [head, tail]), ([[square(b), square(swap(b_give))]], None, [even, odd]))
-
-    *one, far_din, far_made = tie(*across(a, a_give, b, b_give), far_two[4], far_two[3])
+        return merge(
+            ([[a, swap(a_give)]], None, [head, tail]), ([[square(b), square(swap(b_give))]], None, [even, odd])
+        )
+
+    one = across(*grads)
+    wr_own, *one = tie(after(wr, far_two[2]), *one)
+    far_din, far_made = far_two[4], far_two[3]
 
     y_way, x_way = ("dp", xor(2)), ("dp", xor(1))
-    own_two = expert(meta_pair, routed, dy, ids, wr, pair, [own_one[3], after(own_one[4], far_din)])
+    own_two = expert(meta_pair, routed, dy, ids, wr_own, pair, own_one[3:])
     grads = weight_grads([routed, far_rows], *zip(own_two[:3], far_two[:3]))
     din_far, a_got, b_got, *grads = tie(far(far_din), send(one[1], *y_way), send(one[3], *x_way), *grads)
     a_one, b_one = [one[0], a_got], [one[2], b_got]
@@ -806,8 +861,10 @@
         meta, [after(own_two[4], *two), din_far], ids, dy, mid, routed, wr, g2, mix, w_out, probs, qkv, x_rows, normed, w_qkv, g1
     )
     halves = [slice(0, 1), slice(1, 2)]
-    a, a_give, b, b_give, far_made, shared, shared_give, tok_give = tie(
-        *merge(([a_one, a_two], None, halves), ([b_one, b_two], None, halves)),
+    line = lambda v: v.reshape(2, piece, width)
+    flat = lambda group: [line(v) for v in group]
+    one, one_give, two, two_give, far_made, shared, shared_give, tok_give = tie(
+        *merge(([a_one, flat(b_one)], None, halves), ([a_two, flat(b_two)], None, halves)),
         far_made,
         shared,
         shared_give,
@@ -815,27 +872,30 @@
     )
     mix_own, mix_give = combine(meta, mid, [own_two[3], far_made], imgs)
     quarters = lambda n: [slice(k * n, (k + 1) * n) for k in range(4)]
-    a, a_give, b, b_give, *shared, tok_got, mix_got = tie(
+    everything = [slice(None)]
+    second = lambda give: [send(give[0], *x_way), send(give[1], *y_way)]
+    got = second(two_give)
+    two, *shared, tok_got, mix_got = tie(
         *merge(
-            ([[a, send(a_give, *x_way)]], None, [0, 1]),
-            ([[b, send(b_give, *y_way)]], None, [0, 1]),
+            ([[(two, 0), got[0]], [(two, 1), got[1]]], None, everything),
             ([[shared, swap(shared_give)]], None, quarters(width // 8)),
         ),
         swap(tok_give),
         swap(mix_give),
     )
     spread = lambda parts, axis: [send(v, axis, xor(k)) for k, v in zip((1, 2, 3), parts)]
-    everything = [slice(None)]
     mixed, grad_tokens = place(meta, mix_own, mix_got, tok_own, tok_got)
+    got, cross = second(one_give), send(two, "expert", xor(2))
     a, b, *shared, mixed, grad_tokens = tie(
         *merge(
-            ([[a, send(a_give, "expert", xor(2))]], None, everything),
-            ([[b, send(b_give, "expert", xor(2))]], None, everything),
+            ([[(one, 0), got[0], (cross, 0)]], None, everything),
+            ([[(one, 1), got[1], (cross, 1)]], None, everything),
             ([[shared[0], *spread(shared[1:], "dp")]], None, quarters(width // 32)),
         ),
         mixed,
         grad_tokens,
     )
+    b = b[None]
     a, b, shared = tie(
         *merge(
             ([[a, send(a, *x_way)]], 0, None),

time: 226 us -> 212 us (0.938)
  local copies, waits for them, and re-layouts: 12.4 us -> 2.76 us
  waiting for transfers between devices: 68.3 us -> 60.8 us
  Pallas kernels: 96 us -> 99.9 us
    unnamed x68 -> x46, local copies, waits for them, and re-layouts: 9.34 us -> 1.64 us
    ppermute x47 -> x48, waiting for transfers between devices: 68.3 us -> 60.8 us  [send(): return lax.ppermute(value, axis, pairs)]
    ppermute x47 -> x48, starting transfers between devices: 44.6 us -> 45 us  [send(): return lax.ppermute(value, axis, pairs)]
  transfers between devices with their start and end apart: 47 -> 48, of which waited for: 23 -> 22; matrix products, arithmetic and copies ran while one was open for 1% -> 0% of each run, Pallas kernels for 40% -> 45%
where the time goes in v4:
time: 212 us; the launch traced here: 211 us
  Pallas kernels  99.9 us (47%)
  waiting for transfers between devices  60.8 us (29%)
  starting transfers between devices  45 us (21%)
  local copies, waits for them, and re-layouts  2.76 us (1%)
    ppermute x48, waiting for transfers between devices, send(): return lax.ppermute(value, axis, pairs)  60.8 us
    ppermute x48, starting transfers between devices, send(): return lax.ppermute(value, axis, pairs)  45 us
    pallas_call x4, Pallas kernels, expert(): pl.pallas_call(functools.partial(expert_kernel, prev is not None, local),...  42.3 us
    pallas_call x2, Pallas kernels, weight_grads(): pl.pallas_call(functools.partial(weight_kernel, n), grid=(steps,), in_spe...  17 us
    pallas_call x1, Pallas kernels, attend_back(): pl.pallas_call(back_kernel, grid_spec=pltpu.PrefetchScalarGridSpec(num_sc...  12.3 us
    pallas_call x1, Pallas kernels, attend(): pl.pallas_call(attend_kernel, grid_spec=pltpu.PrefetchScalarGridSpec(num_...  10.4 us
    pallas_call x1, Pallas kernels, finish_expert(): pl.pallas_call(finish_kernel, grid_spec=pltpu.PrefetchScalarGridSpec(num_...  4.43 us
  transfers between devices with their start and end apart: 48, of which 22 were waited for; matrix products, arithmetic and copies ran while one was open for 0% of the time, Pallas kernels for 45%

profile of v4, /device:TPU:0, one launch (start us, length us, event | category | flops | bytes accessed | tf_op | source)
XLA Modules:
  0.0 211.3 jit_solution(5904072339512056691)
XLA Ops:
  0.8 1.6 pack_piece.1
  2.9 3.7 %collective-permute-start.6 = (bf16[4,256,256]{2,1,0:T(8,128)(2,1)S(1)}, bf16[4,256,256]{2,1,0:T(8,128)(2,1)}, u32[]{:S(2)}, u32[]{:S(2)}) collective-permute-start(bf16[4,256,256]{2,1,0:T(8,128)(2,1)S(1)} %pack_piece.1), channel_id=1, source_target_pairs={{0,2},{1,3},{2,0},{3,1},{4,6},{5,7},{6,4},{7,5},{8,10},{9,11},{10,... | collective-permute-start | bytes 1572872 | tf_op jit(solution)/shard_map/ppermute | solution.py:759
  6.8 1.6 collective-permute-start.4
  8.7 1.9 collective-permute-done.other_ref
  11.4 10.4 %attend.1 = (bf16[600,512]{1,0:T(8,128)(2,1)}, bf16[600,512]{1,0:T(8,128)(2,1)S(1)}, bf16[600,512]{1,0:T(8,128)(2,1)}, bf16[600,1536]{1,0:T(8,128)(2,1)}, bf16[3...) custom-call(s32[4]{0:T(128)S(1)} %add_add_fusion.1.meta_ref, ...), custom_call_target="tpu_custom_call" | custom-call | flops 1 | bytes 1 | tf_op jit(solution)/shard_map/attend/pallas_call | solution.py:117
  22.7 10.2 %expert.4 = (bf16[600,2048]{1,0:T(8,128)(2,1)S(1)}, bf16[600,2048]{1,0:T(8,128)(2,1)S(1)}, bf16[600,512]{1,0:T(8,128)(2,1)S(1)}, bf16[600,512]{1,0:T(8,128)(2,1)}, bf16[640,512]{1,0:T(8,128)(2,1)}) custom-call(s32[4]{0:T(128)S(1)} %add_add_fusion.1.meta_ref, bf16[600,512]{1,0:T(8,128)(2,1)S(1)} %get-tuple-element.138.rows_ref.refs_0_.routed_ref, ...), custom_call_target="tpu_custom_call" | custom-call | flops 1 | bytes 1 | tf_op jit(solution)/shard_map/expert/pallas_call | solution.py:335
  32.9 1.3 collective-permute-done.4.own_ref
  34.2 2.5 %collective-permute-start.9 = (bf16[4,256,256]{2,1,0:T(8,128)(2,1)}, bf16[4,256,256]{2,1,0:T(8,128)(2,1)S(1)}, u32[]{:S(2)}, u32[]{:S(2)}) collective-permute-start(bf16[4,256,256]{2,1,0:T(8,128)(2,1)} %collective-permute-done.6), channel_id=1, source_target_pairs={{0,24},{8,16},{16,8},{24,0},{1,25},{9,17},{17,9},{25,1},{2,26},{10... | collective-permute-start | bytes 1572872 | tf_op jit(solution)/shard_map/ppermute | solution.py:759
  38.6 8.8 %collective-permute-done.3.rows_ref.ids_ref.refs_1_ = bf16[624,512]{1,0:T(8,128)(2,1)S(1)} collective-permute-done((bf16[624,512]{1,0:T(8,128)(2,1)S(1)}, bf16[624,512]{1,0:T(8,128)(2,1)S(1)}, u32[]{:S(2)}, u32[]{:S(2)}) %collective-permute-start.3) | collective-permute-done | bytes 639008 | tf_op jit(solution)/shard_map/ppermute | solution.py:759
  47.3 10.3 %expert.5 = (bf16[600,2048]{1,0:T(8,128)(2,1)S(1)}, bf16[600,2048]{1,0:T(8,128)(2,1)S(1)}, bf16[600,512]{1,0:T(8,128)(2,1)S(1)}, bf16[600,512]{1,0:T(8,128)(2,1)}, bf16[640,512]{1,0:T(8,128)(2,1)}) custom-call(s32[4]{0:T(128)S(1)} %add_add_fusion.1.meta_ref, bf16[624,512]{1,0:T(8,128)(2,1)S(1)} %collective-permute-done.3.rows_ref.ids_ref.refs_1_, ...), custom_call_target="tpu_custom_call" | custom-call | flops 1 | bytes 1 | tf_op jit(solution)/shard_map/expert/pallas_call | solution.py:335
  57.7 3.2 %collective-permute-done.8 = bf16[4,256,256]{2,1,0:T(8,128)(2,1)S(1)} collective-permute-done((bf16[4,256,256]{2,1,0:T(8,128)(2,1)}, bf16[4,256,256]{2,1,0:T(8,128)(2,1)S(1)}, u32[]{:S(2)}, u32[]{:S(2)}) %collective-permute-start.8) | collective-permute-done | bytes 524320 | tf_op jit(solution)/shard_map/ppermute | solution.py:759
  61.1 1.3 pad_maximum_fusion.rest_0_
  62.5 9.3 %weight_grads.2 = (bf16[4,256,512]{2,1,0:T(8,128)(2,1)}, bf16[4,256,512]{2,1,0:T(8,128)(2,1)}, bf16[4,256,512]{2,1,0:T(8,128)(2,1)}, bf16[4,256,512]{2,1,0:T(8,128)(2,1)}) custom-call(bf16[600,512]{1,0:T(8,128)(2,1)S(1)} %get-tuple-element.138.rows_ref.refs_0_.routed_ref, bf16[624,512]{1,0:T(8,128)(2,1)S(1)} %collective-permute-done.3.rows_ref.ids_ref.refs_1_, ...), custom_call_target="tpu_custom_call" | custom-call | flops 1 | bytes 1 | tf_op jit(solution)/shard_map/weight_grads/pallas_call | solution.py:396
  72.3 11.0 %expert.6 = (bf16[600,2048]{1,0:T(8,128)(2,1)S(1)}, bf16[600,2048]{1,0:T(8,128)(2,1)S(1)}, bf16[600,512]{1,0:T(8,128)(2,1)S(1)}, bf16[600,512]{1,0:T(8,128)(2,1)S(1)}, bf16[640,512]{1,0:T(8,128)(2,1)S(1)}) custom-call(s32[4]{0:T(128)S(1)} %add_add_fusion.meta_ref, bf16[624,512]{1,0:T(8,128)(2,1)S(1)} %collective-permute-done.3.rows_ref.ids_ref.refs_1_, ...), custom_call_target="tpu_custom_call" | custom-call | flops 1 | bytes 1 | tf_op jit(solution)/shard_map/expert/pallas_call | solution.py:335
  84.2 2.0 merge.8
  86.3 1.5 collective-permute-start.14
  88.5 10.7 %expert.7 = (bf16[600,2048]{1,0:T(8,128)(2,1)S(1)}, bf16[600,2048]{1,0:T(8,128)(2,1)S(1)}, bf16[600,512]{1,0:T(8,128)(2,1)S(1)}, bf16[600,512]{1,0:T(8,128)(2,1)S(1)}, bf16[640,512]{1,0:T(8,128)(2,1)S(1)}) custom-call(s32[4]{0:T(128)S(1)} %add_add_fusion.meta_ref, bf16[600,512]{1,0:T(8,128)(2,1)S(1)} %get-tuple-element.138.rows_ref.refs_0_.routed_ref, ...), custom_call_target="tpu_custom_call" | custom-call | flops 1 | bytes 1 | tf_op jit(solution)/shard_map/expert/pallas_call | solution.py:335
  99.3 7.8 %weight_grads.3 = (bf16[4,256,512]{2,1,0:T(8,128)(2,1)S(1)}, bf16[4,256,512]{2,1,0:T(8,128)(2,1)S(1)}, bf16[4,256,512]{2,1,0:T(8,128)(2,1)S(1)}, bf16[4,256,512]{2,1,0:T(8,128)(2,1)S(1)}) custom-call(bf16[600,512]{1,0:T(8,128)(2,1)S(1)} %get-tuple-element.138.rows_ref.refs_0_.routed_ref, ...), custom_call_target="tpu_custom_call" | custom-call | flops 1 | bytes 1 | tf_op jit(solution)/shard_map/weight_grads/pallas_call | solution.py:396
  109.9 1.5 collective-permute-done.17
  111.9 1.3 collective-permute-start.19
  113.8 12.3 %attend_back.1 = (bf16[3,100,512]{2,1,0:T(8,128)(2,1)S(1)}, bf16[3,100,512]{2,1,0:T(8,128)(2,1)S(1)}, bf16[256,2176]{1,0:T(8,128)(2,1)S(1)}, bf16[256,2176]{1,0:T(8,128)(2,1)S(1)}) custom-call(s32[4]{0:T(128)S(1)} %add_add_fusion.1.meta_ref, bf16[640,512]{1,0:T(8,128)(2,1)S(1)} %get-tuple-element.205.din0_ref, ...), custom_call_target="tpu_custom_call" | custom-call | flops 1 | bytes 1 | tf_op jit(solution)/shard_map/attend_back/pallas_call | solution.py:543
  130.1 1.4 collective-permute-start.22
  131.4 6.5 %collective-permute-done.23.refs_3_ = bf16[1,256,512]{2,1,0:T(8,128)(2,1)S(1)} collective-permute-done((bf16[1,256,512]{2,1,0:T(8,128)(2,1)S(1)}, bf16[1,256,512]{2,1,0:T(8,128)(2,1)S(1)}, u32[]{:S(2)}, u32[]{:S(2)}) %collective-permute-start.23) | collective-permute-done | bytes 262176 | tf_op jit(solution)/shard_map/ppermute | solution.py:759
  139.1 2.3 %collective-permute-start.27 = (bf16[2,1,256,512]{3,2,1,0:T(8,128)(2,1)S(1)}, bf16[2,1,256,512]{3,2,1,0:T(8,128)(2,1)S(1)}, u32[]{:S(2)}, u32[]{:S(2)}) collective-permute-start(bf16[2,1,256,512]{3,2,1,0:T(8,128)(2,1)S(1)} %get-tuple-element.230), channel_id=1, source_target_pairs={{0,2},{1,3},{2,0},{3,1},{4,6},{5,7},{6,4},{7,5},{8,10},{9,11},{10,... | collective-permute-start | bytes 1572872 | tf_op jit(solution)/shard_map/ppermute | solution.py:759
  141.4 1.4 collective-permute-start.29
  143.5 1.4 collective-permute-start.31
  144.9 2.2 %collective-permute-done.28.refs_4_ = bf16[1,256,512]{2,1,0:T(8,128)(2,1)S(1)} collective-permute-done((bf16[1,256,512]{2,1,0:T(8,128)(2,1)S(1)}, bf16[1,256,512]{2,1,0:T(8,128)(2,1)S(1)}, u32[]{:S(2)}, u32[]{:S(2)}) %collective-permute-start.28) | collective-permute-done | bytes 262176 | tf_op jit(solution)/shard_map/ppermute | solution.py:759
  148.0 2.8 %place.1 = (bf16[6,100,512]{2,1,0:T(8,128)(2,1)}, bf16[6,100,512]{2,1,0:T(8,128)(2,1)}) custom-call(s32[4]{0:T(128)S(1)} %add_add_fusion.1.meta_ref, bf16[3,100,512]{2,1,0:T(8,128)(2,1)S(1)} %get-tuple-element.241.a_own_ref, bf16[3,100,512]{2,1,0:T(8,128)(2,1)S(1)} %collective-permute-done.26.a_recv_ref, ...), custom_call_target="tpu_custom_call" | custom-call | flops 1 | bytes 1 | tf_op jit(solution)/shard_map/place/pallas_call | solution.py:658
  150.8 10.0 %collective-permute-done.21.refs_1_ = bf16[1,256,512]{2,1,0:T(8,128)(2,1)S(1)} collective-permute-done((bf16[1,256,512]{2,1,0:T(8,128)(2,1)S(1)}, bf16[1,256,512]{2,1,0:T(8,128)(2,1)S(1)}, u32[]{:S(2)}, u32[]{:S(2)}) %collective-permute-start.21) | collective-permute-done | bytes 262176 | tf_op jit(solution)/shard_map/ppermute | solution.py:759
  160.7 3.8 %collective-permute-done.27.refs_2_.refs_5_ = bf16[2,1,256,512]{3,2,1,0:T(8,128)(2,1)S(1)} collective-permute-done((bf16[2,1,256,512]{3,2,1,0:T(8,128)(2,1)S(1)}, bf16[2,1,256,512]{3,2,1,0:T(8,128)(2,1)S(1)}, u32[]{:S(2)}, u32[]{:S(2)}) %collective-permute-start.27) | collective-permute-done | bytes 524320 | tf_op jit(solution)/shard_map/ppermute | solution.py:759
  164.9 1.3 collective-permute-start.33
  167.0 2.3 %collective-permute-start.35 = (bf16[16,2176]{1,0:T(8,128)(2,1)S(1)}, bf16[16,2176]{1,0:T(8,128)(2,1)S(1)}, u32[]{:S(2)}, u32[]{:S(2)}) collective-permute-start(bf16[16,2176]{1,0:T(8,128)(2,1)S(1)} %get-tuple-element.253), channel_id=1, source_target_pairs={{0,2},{1,3},{2,0},{3,1},{4,6},{5,7},{6,4},{7,5},{8,10},{9,11},{10,... | collective-permute-start | bytes 208904 | tf_op jit(solution)/shard_map/ppermute | solution.py:759
  169.3 2.1 collective-permute-start.36
  171.4 2.5 %collective-permute-done.35.refs_6_ = bf16[16,2176]{1,0:T(8,128)(2,1)S(1)} collective-permute-done((bf16[16,2176]{1,0:T(8,128)(2,1)S(1)}, bf16[16,2176]{1,0:T(8,128)(2,1)S(1)}, u32[]{:S(2)}, u32[]{:S(2)}) %collective-permute-start.35) | collective-permute-done | bytes 69664 | tf_op jit(solution)/shard_map/ppermute | solution.py:759
  173.9 1.5 collective-permute-done.36.refs_7_
  175.5 1.3 collective-permute-start.37
  177.6 2.1 %collective-permute-start.41 = (bf16[16,2176]{1,0:T(8,128)(2,1)S(1)}, bf16[16,2176]{1,0:T(8,128)(2,1)S(1)}, u32[]{:S(2)}, u32[]{:S(2)}) collective-permute-start(bf16[16,2176]{1,0:T(8,128)(2,1)S(1)} %get-tuple-element.257.refs_4_), channel_id=1, source_target_pairs={{0,3},{1,2},{2,1},{3,0},{4,7},{5,6},{6,5},{7,4},{8,11},{9,10},{10,... | collective-permute-start | bytes 208904 | tf_op jit(solution)/shard_map/ppermute | solution.py:759
  179.7 2.3 %collective-permute-start.39 = (bf16[16,2176]{1,0:T(8,128)(2,1)S(1)}, bf16[16,2176]{1,0:T(8,128)(2,1)S(1)}, u32[]{:S(2)}, u32[]{:S(2)}) collective-permute-start(bf16[16,2176]{1,0:T(8,128)(2,1)S(1)} %get-tuple-element.257.refs_4_), channel_id=1, source_target_pairs={{0,1},{1,0},{2,3},{3,2},{4,5},{5,4},{6,7},{7,6},{8,9},{9,8},{10,11... | collective-permute-start | bytes 208904 | tf_op jit(solution)/shard_map/ppermute | solution.py:759
  181.9 1.7 collective-permute-done.41.refs_7_
  183.7 1.5 collective-permute-done.40.refs_6_
  185.2 1.3 collective-permute-done.37.refs_1_
  188.2 1.4 collective-permute-start.46
  190.3 1.3 collective-permute-start.44
  191.8 4.4 %finish_expert.1 = (f32[1,512,2048]{2,1,0:T(8,128)}, f32[1,2048,512]{2,1,0:T(8,128)}) custom-call(s32[4]{0:T(128)S(1)} %add_add_fusion.1.meta_ref, bf16[4,256,512]{2,1,0:T(8,128)(2,1)S(1)} %get-tuple-element.259.im_ref, bf16[4,256,512]{2,1,0:T(8,128)(2,1)S(1)} %collective-permute-done.42.ir_ref, bf16[4,256,512]{2,1,0:T(8,128)(2,1)S(1)} %bitcast.48, ...), custom_call_target="tpu_custom_call" | custom-call | flops 1 | bytes 1 | tf_op jit(solution)/shard_map/finish_expert/pallas_call | solution.py:429
  196.3 2.4 %collective-permute-done.46.refs_3_ = bf16[64,2176]{1,0:T(8,128)(2,1)S(1)} collective-permute-done((bf16[64,2176]{1,0:T(8,128)(2,1)S(1)}, bf16[64,2176]{1,0:T(8,128)(2,1)S(1)}, u32[]{:S(2)}, u32[]{:S(2)}) %collective-permute-start.46) | collective-permute-done | bytes 278560 | tf_op jit(solution)/shard_map/ppermute | solution.py:759
  198.6 5.1 %collective-permute-done.45.refs_2_ = bf16[64,2176]{1,0:T(8,128)(2,1)S(1)} collective-permute-done((bf16[64,2176]{1,0:T(8,128)(2,1)S(1)}, bf16[64,2176]{1,0:T(8,128)(2,1)S(1)}, u32[]{:S(2)}, u32[]{:S(2)}) %collective-permute-start.45) | collective-permute-done | bytes 278560 | tf_op jit(solution)/shard_map/ppermute | solution.py:759
  203.9 2.7 %collective-permute-done.47.recv_ref = bf16[256,2176]{1,0:T(8,128)(2,1)S(1)} collective-permute-done((bf16[256,2176]{1,0:T(8,128)(2,1)S(1)}, bf16[256,2176]{1,0:T(8,128)(2,1)S(1)}, u32[]{:S(2)}, u32[]{:S(2)}) %collective-permute-start.47) | collective-permute-done | bytes 1114144 | tf_op jit(solution)/shard_map/ppermute | solution.py:759
  206.6 3.0 %finish_shared.1 = (f32[512,1536]{1,0:T(8,128)}, f32[512,512]{1,0:T(8,128)}, f32[512,128]{1,0:T(8,128)S(1)}) custom-call(s32[4]{0:T(128)S(1)} %add_add_fusion.1.meta_ref, bf16[256,2176]{1,0:T(8,128)(2,1)S(1)} %merge.15.mine_ref, bf16[256,2176]{1,0:T(8,128)(2,1)S(1)} %collective-permute-done.47.recv_ref), custom_call_target="tpu_custom_call" | custom-call | flops 1 | bytes 1 | tf_op jit(solution)/shard_map/finish_shared/pallas_call | solution.py:599
  (134 shorter events, 24.0 us)
Async XLA Ops:
  2.4 6.0 %collective-permute-start.2 = (s32[6,100]{1,0:T(8,128)S(1)}, s32[6,100]{1,0:T(8,128)S(1)}, u32[]{:S(2)}, u32[]{:S(2)}) collective-permute-start(s32[6,100]{1,0:T(8,128)S(1)} %bitcast.69), channel_id=1, source_target_pairs={{0,4},{4,0},{1,5},{5,1},{2,6},{6,2},{3,7},{7,3},{8,12},{12,8},{9,1... | collective-permute-start | bytes 7208 | tf_op jit(solution)/shard_map/ppermute | solution.py:759
  2.9 31.3 %collective-permute-start.6 = (bf16[4,256,256]{2,1,0:T(8,128)(2,1)S(1)}, bf16[4,256,256]{2,1,0:T(8,128)(2,1)}, u32[]{:S(2)}, u32[]{:S(2)}) collective-permute-start(bf16[4,256,256]{2,1,0:T(8,128)(2,1)S(1)} %pack_piece.1), channel_id=1, source_target_pairs={{0,2},{1,3},{2,0},{3,1},{4,6},{5,7},{6,4},{7,5},{8,10},{9,11},{10,... | collective-permute-start | bytes 1572872 | tf_op jit(solution)/shard_map/ppermute | solution.py:759
  6.6 4.0 %collective-permute-start.1 = (bf16[6,100,512]{2,1,0:T(8,128)(2,1)}, bf16[6,100,512]{2,1,0:T(8,128)(2,1)S(1)}, u32[]{:S(2)}, u32[]{:S(2)}) collective-permute-start(bf16[6,100,512]{2,1,0:T(8,128)(2,1)} %dyown_ref.1), channel_id=1, source_target_pairs={{0,4},{4,0},{1,5},{5,1},{2,6},{6,2},{3,7},{7,3},{8,12},{12,8},{9,1... | collective-permute-start | bytes 1843208 | tf_op jit(solution)/shard_map/ppermute | solution.py:759
  6.8 27.5 %collective-permute-start.4 = (bf16[6,100,512]{2,1,0:T(8,128)(2,1)}, bf16[6,100,512]{2,1,0:T(8,128)(2,1)S(1)}, u32[]{:S(2)}, u32[]{:S(2)}) collective-permute-start(bf16[6,100,512]{2,1,0:T(8,128)(2,1)} %dyown_ref.1), channel_id=1, source_target_pairs={{0,1},{1,0},{2,3},{3,2},{4,5},{5,4},{6,7},{7,6},{8,9},{9,8},{10,11... | collective-permute-start | bytes 1843208 | tf_op jit(solution)/shard_map/ppermute | solution.py:759
  8.3 2.2 %collective-permute-start = (bf16[6,100,512]{2,1,0:T(8,128)(2,1)S(1)}, bf16[6,100,512]{2,1,0:T(8,128)(2,1)}, u32[]{:S(2)}, u32[]{:S(2)}) collective-permute-start(bf16[6,100,512]{2,1,0:T(8,128)(2,1)S(1)} %copy-done.18), channel_id=1, source_target_pairs={{0,4},{4,0},{1,5},{5,1},{2,6},{6,2},{3,7},{7,3},{8,12},{12,8},{9,1... | collective-permute-start | bytes 1843208 | tf_op jit(solution)/shard_map/ppermute | solution.py:759
  21.9 25.5 %collective-permute-start.3 = (bf16[624,512]{1,0:T(8,128)(2,1)S(1)}, bf16[624,512]{1,0:T(8,128)(2,1)S(1)}, u32[]{:S(2)}, u32[]{:S(2)}) collective-permute-start(bf16[624,512]{1,0:T(8,128)(2,1)S(1)} %pad_maximum_fusion.1), channel_id=1, source_target_pairs={{0,1},{1,0},{2,3},{3,2},{4,5},{5,4},{6,7},{7,6},{8,9},{9,8},{10,11... | collective-permute-start | bytes 1916936 | tf_op jit(solution)/shard_map/ppermute | solution.py:759
  34.2 3.5 %collective-permute-start.5 = (bf16[6,100,512]{2,1,0:T(8,128)(2,1)S(1)}, bf16[6,100,512]{2,1,0:T(8,128)(2,1)S(1)}, u32[]{:S(2)}, u32[]{:S(2)}) collective-permute-start(bf16[6,100,512]{2,1,0:T(8,128)(2,1)S(1)} %collective-permute-done.4.own_ref), channel_id=1, source_target_pairs={{0,4},{4,0},{1,5},{5,1},{2,6},{6,2},{3,7},{7,3},{8,12},{12,8},{9,1... | collective-permute-start | bytes 1843208 | tf_op jit(solution)/shard_map/ppermute | solution.py:759
  34.2 23.4 %collective-permute-start.9 = (bf16[4,256,256]{2,1,0:T(8,128)(2,1)}, bf16[4,256,256]{2,1,0:T(8,128)(2,1)S(1)}, u32[]{:S(2)}, u32[]{:S(2)}) collective-permute-start(bf16[4,256,256]{2,1,0:T(8,128)(2,1)} %collective-permute-done.6), channel_id=1, source_target_pairs={{0,24},{8,16},{16,8},{24,0},{1,25},{9,17},{17,9},{25,1},{2,26},{10... | collective-permute-start | bytes 1572872 | tf_op jit(solution)/shard_map/ppermute | solution.py:759
  36.7 24.2 %collective-permute-start.8 = (bf16[4,256,256]{2,1,0:T(8,128)(2,1)}, bf16[4,256,256]{2,1,0:T(8,128)(2,1)S(1)}, u32[]{:S(2)}, u32[]{:S(2)}) collective-permute-start(bf16[4,256,256]{2,1,0:T(8,128)(2,1)} %collective-permute-done.6), channel_id=1, source_target_pairs={{0,16},{8,24},{16,0},{24,8},{1,17},{9,25},{17,1},{25,9},{2,18},{10... | collective-permute-start | bytes 1572872 | tf_op jit(solution)/shard_map/ppermute | solution.py:759
  37.3 23.8 %collective-permute-start.7 = (bf16[4,256,256]{2,1,0:T(8,128)(2,1)}, bf16[4,256,256]{2,1,0:T(8,128)(2,1)S(1)}, u32[]{:S(2)}, u32[]{:S(2)}) collective-permute-start(bf16[4,256,256]{2,1,0:T(8,128)(2,1)} %collective-permute-done.6), channel_id=1, source_target_pairs={{0,8},{8,0},{16,24},{24,16},{1,9},{9,1},{17,25},{25,17},{2,10},{10... | collective-permute-start | bytes 1572872 | tf_op jit(solution)/shard_map/ppermute | solution.py:759
  62.4 9.9 %collective-permute-start.10 = (bf16[4,4,256,256]{3,2,1,0:T(8,128)(2,1)S(1)}, bf16[4,4,256,256]{3,2,1,0:T(8,128)(2,1)}, u32[]{:S(2)}, u32[]{:S(2)}) collective-permute-start(bf16[4,4,256,256]{3,2,1,0:T(8,128)(2,1)S(1)} %pad_maximum_fusion.rest_0_), channel_id=1, source_target_pairs={{0,4},{4,0},{1,5},{5,1},{2,6},{6,2},{3,7},{7,3},{8,12},{12,8},{9,1... | collective-permute-start | bytes 6291464 | tf_op jit(solution)/shard_map/ppermute | solution.py:759
  71.7 12.5 %collective-permute-start.11 = (bf16[4,256,512]{2,1,0:T(8,128)(2,1)}, bf16[4,256,512]{2,1,0:T(8,128)(2,1)}, u32[]{:S(2)}, u32[]{:S(2)}) collective-permute-start(bf16[4,256,512]{2,1,0:T(8,128)(2,1)} %get-tuple-element.163), channel_id=1, source_target_pairs={{0,4},{4,0},{1,5},{5,1},{2,6},{6,2},{3,7},{7,3},{8,12},{12,8},{9,1... | collective-permute-start | bytes 3145736 | tf_op jit(solution)/shard_map/ppermute | solution.py:759
  72.2 12.1 %collective-permute-start.12 = (bf16[4,256,512]{2,1,0:T(8,128)(2,1)}, bf16[4,256,512]{2,1,0:T(8,128)(2,1)}, u32[]{:S(2)}, u32[]{:S(2)}) collective-permute-start(bf16[4,256,512]{2,1,0:T(8,128)(2,1)} %get-tuple-element.165), channel_id=1, source_target_pairs={{0,4},{4,0},{1,5},{5,1},{2,6},{6,2},{3,7},{7,3},{8,12},{12,8},{9,1... | collective-permute-start | bytes 3145736 | tf_op jit(solution)/shard_map/ppermute | solution.py:759
  83.4 23.8 %collective-permute-start.13 = (bf16[640,512]{1,0:T(8,128)(2,1)S(1)}, bf16[640,512]{1,0:T(8,128)(2,1)S(1)}, u32[]{:S(2)}, u32[]{:S(2)}) collective-permute-start(bf16[640,512]{1,0:T(8,128)(2,1)S(1)} %get-tuple-element.171), channel_id=1, source_target_pairs={{0,1},{1,0},{2,3},{3,2},{4,5},{5,4},{6,7},{7,6},{8,9},{9,8},{10,11... | collective-permute-start | bytes 1966088 | tf_op jit(solution)/shard_map/ppermute | solution.py:759
  86.3 20.9 %collective-permute-start.14 = (bf16[2,256,512]{2,1,0:T(8,128)(2,1)S(1)}, bf16[2,256,512]{2,1,0:T(8,128)(2,1)S(1)}, u32[]{:S(2)}, u32[]{:S(2)}) collective-permute-start(bf16[2,256,512]{2,1,0:T(8,128)(2,1)S(1)} %get-tuple-element.172), channel_id=1, source_target_pairs={{0,16},{8,24},{16,0},{24,8},{1,17},{9,25},{17,1},{25,9},{2,18},{10... | collective-permute-start | bytes 1572872 | tf_op jit(solution)/shard_map/ppermute | solution.py:759
  87.7 19.4 %collective-permute-start.15 = (bf16[2,1,256,512]{3,2,0,1:T(8,128)(2,1)S(1)}, bf16[2,1,256,512]{3,2,0,1:T(8,128)(2,1)S(1)}, u32[]{:S(2)}, u32[]{:S(2)}) collective-permute-start(bf16[2,1,256,512]{3,2,0,1:T(8,128)(2,1)S(1)} %bitcast.62), channel_id=1, source_target_pairs={{0,8},{8,0},{16,24},{24,16},{1,9},{9,1},{17,25},{25,17},{2,10},{10... | collective-permute-start | bytes 1572872 | tf_op jit(solution)/shard_map/ppermute | solution.py:759
  107.2 2.7 %collective-permute-start.16 = (bf16[4,256,512]{2,1,0:T(8,128)(2,1)S(1)}, bf16[4,256,512]{2,1,0:T(8,128)(2,1)S(1)}, u32[]{:S(2)}, u32[]{:S(2)}) collective-permute-start(bf16[4,256,512]{2,1,0:T(8,128)(2,1)S(1)} %get-tuple-element.190), channel_id=1, source_target_pairs={{0,4},{4,0},{1,5},{5,1},{2,6},{6,2},{3,7},{7,3},{8,12},{12,8},{9,1... | collective-permute-start | bytes 3145736 | tf_op jit(solution)/shard_map/ppermute | solution.py:759
  107.2 4.1 %collective-permute-start.17 = (bf16[4,256,512]{2,1,0:T(8,128)(2,1)S(1)}, bf16[4,256,512]{2,1,0:T(8,128)(2,1)S(1)}, u32[]{:S(2)}, u32[]{:S(2)}) collective-permute-start(bf16[4,256,512]{2,1,0:T(8,128)(2,1)S(1)} %get-tuple-element.192), channel_id=1, source_target_pairs={{0,4},{4,0},{1,5},{5,1},{2,6},{6,2},{3,7},{7,3},{8,12},{12,8},{9,1... | collective-permute-start | bytes 3145736 | tf_op jit(solution)/shard_map/ppermute | solution.py:759
  107.7 19.6 %collective-permute-start.20 = (bf16[600,512]{1,0:T(8,128)(2,1)S(1)}, bf16[600,512]{1,0:T(8,128)(2,1)S(1)}, u32[]{:S(2)}, u32[]{:S(2)}) collective-permute-start(bf16[600,512]{1,0:T(8,128)(2,1)S(1)} %get-tuple-element.203), channel_id=1, source_target_pairs={{0,1},{1,0},{2,3},{3,2},{4,5},{5,4},{6,7},{7,6},{8,9},{9,8},{10,11... | collective-permute-start | bytes 1843208 | tf_op jit(solution)/shard_map/ppermute | solution.py:759
  111.9 14.3 %collective-permute-start.19 = (bf16[2,1,256,512]{3,2,0,1:T(8,128)(2,1)S(1)}, bf16[2,1,256,512]{3,2,0,1:T(8,128)(2,1)S(1)}, u32[]{:S(2)}, u32[]{:S(2)}) collective-permute-start(bf16[2,1,256,512]{3,2,0,1:T(8,128)(2,1)S(1)} %bitcast.63), channel_id=1, source_target_pairs={{0,8},{8,0},{16,24},{24,16},{1,9},{9,1},{17,25},{25,17},{2,10},{10... | collective-permute-start | bytes 1572872 | tf_op jit(solution)/shard_map/ppermute | solution.py:759
  113.1 13.7 %collective-permute-start.18 = (bf16[2,256,512]{2,1,0:T(8,128)(2,1)S(1)}, bf16[2,256,512]{2,1,0:T(8,128)(2,1)S(1)}, u32[]{:S(2)}, u32[]{:S(2)}) collective-permute-start(bf16[2,256,512]{2,1,0:T(8,128)(2,1)S(1)} %get-tuple-element.194), channel_id=1, source_target_pairs={{0,16},{8,24},{16,0},{24,8},{1,17},{9,25},{17,1},{25,9},{2,18},{10... | collective-permute-start | bytes 1572872 | tf_op jit(solution)/shard_map/ppermute | solution.py:759
  127.3 11.4 %collective-permute-start.24 = (bf16[256,2176]{1,0:T(8,128)(2,1)S(1)}, bf16[256,2176]{1,0:T(8,128)(2,1)S(1)}, u32[]{:S(2)}, u32[]{:S(2)}) collective-permute-start(bf16[256,2176]{1,0:T(8,128)(2,1)S(1)} %get-tuple-element.220), channel_id=1, source_target_pairs={{0,4},{4,0},{1,5},{5,1},{2,6},{6,2},{3,7},{7,3},{8,12},{12,8},{9,1... | collective-permute-start | bytes 3342344 | tf_op jit(solution)/shard_map/ppermute | solution.py:759
  127.4 11.7 %collective-permute-start.25 = (bf16[3,100,512]{2,1,0:T(8,128)(2,1)S(1)}, bf16[3,100,512]{2,1,0:T(8,128)(2,1)S(1)}, u32[]{:S(2)}, u32[]{:S(2)}) collective-permute-start(bf16[3,100,512]{2,1,0:T(8,128)(2,1)S(1)} %get-tuple-element.226), channel_id=1, source_target_pairs={{0,4},{4,0},{1,5},{5,1},{2,6},{6,2},{3,7},{7,3},{8,12},{12,8},{9,1... | collective-permute-start | bytes 921608 | tf_op jit(solution)/shard_map/ppermute | solution.py:759
  129.0 10.1 %collective-permute-start.26 = (bf16[3,100,512]{2,1,0:T(8,128)(2,1)S(1)}, bf16[3,100,512]{2,1,0:T(8,128)(2,1)S(1)}, u32[]{:S(2)}, u32[]{:S(2)}) collective-permute-start(bf16[3,100,512]{2,1,0:T(8,128)(2,1)S(1)} %get-tuple-element.229), channel_id=1, source_target_pairs={{0,4},{4,0},{1,5},{5,1},{2,6},{6,2},{3,7},{7,3},{8,12},{12,8},{9,1... | collective-permute-start | bytes 921608 | tf_op jit(solution)/shard_map/ppermute | solution.py:759
  129.2 8.7 %collective-permute-start.23 = (bf16[1,256,512]{2,1,0:T(8,128)(2,1)S(1)}, bf16[1,256,512]{2,1,0:T(8,128)(2,1)S(1)}, u32[]{:S(2)}, u32[]{:S(2)}) collective-permute-start(bf16[1,256,512]{2,1,0:T(8,128)(2,1)S(1)} %get-tuple-element.291), channel_id=1, source_target_pairs={{0,16},{8,24},{16,0},{24,8},{1,17},{9,25},{17,1},{25,9},{2,18},{10... | collective-permute-start | bytes 786440 | tf_op jit(solution)/shard_map/ppermute | solution.py:759
  130.1 8.7 %collective-permute-start.22 = (bf16[1,256,512]{2,1,0:T(8,128)(2,1)S(1)}, bf16[1,256,512]{2,1,0:T(8,128)(2,1)S(1)}, u32[]{:S(2)}, u32[]{:S(2)}) collective-permute-start(bf16[1,256,512]{2,1,0:T(8,128)(2,1)S(1)} %get-tuple-element.292), channel_id=1, source_target_pairs={{0,8},{8,0},{16,24},{24,16},{1,9},{9,1},{17,25},{25,17},{2,10},{10... | collective-permute-start | bytes 786440 | tf_op jit(solution)/shard_map/ppermute | solution.py:759
  138.0 9.2 %collective-permute-start.28 = (bf16[1,256,512]{2,1,0:T(8,128)(2,1)S(1)}, bf16[1,256,512]{2,1,0:T(8,128)(2,1)S(1)}, u32[]{:S(2)}, u32[]{:S(2)}) collective-permute-start(bf16[1,256,512]{2,1,0:T(8,128)(2,1)S(1)} %get-tuple-element.289), channel_id=1, source_target_pairs={{0,16},{8,24},{16,0},{24,8},{1,17},{9,25},{17,1},{25,9},{2,18},{10... | collective-permute-start | bytes 786440 | tf_op jit(solution)/shard_map/ppermute | solution.py:759
  139.1 25.4 %collective-permute-start.27 = (bf16[2,1,256,512]{3,2,1,0:T(8,128)(2,1)S(1)}, bf16[2,1,256,512]{3,2,1,0:T(8,128)(2,1)S(1)}, u32[]{:S(2)}, u32[]{:S(2)}) collective-permute-start(bf16[2,1,256,512]{3,2,1,0:T(8,128)(2,1)S(1)} %get-tuple-element.230), channel_id=1, source_target_pairs={{0,2},{1,3},{2,0},{3,1},{4,6},{5,7},{6,4},{7,5},{8,10},{9,11},{10,... | collective-permute-start | bytes 1572872 | tf_op jit(solution)/shard_map/ppermute | solution.py:759
  141.4 19.3 %collective-permute-start.29 = (bf16[64,2176]{1,0:T(8,128)(2,1)S(1)}, bf16[64,2176]{1,0:T(8,128)(2,1)S(1)}, u32[]{:S(2)}, u32[]{:S(2)}) collective-permute-start(bf16[64,2176]{1,0:T(8,128)(2,1)S(1)} %get-tuple-element.232), channel_id=1, source_target_pairs={{0,8},{8,0},{16,24},{24,16},{1,9},{9,1},{17,25},{25,17},{2,10},{10... | collective-permute-start | bytes 835592 | tf_op jit(solution)/shard_map/ppermute | solution.py:759
  142.8 17.9 %collective-permute-start.30 = (bf16[64,2176]{1,0:T(8,128)(2,1)S(1)}, bf16[64,2176]{1,0:T(8,128)(2,1)S(1)}, u32[]{:S(2)}, u32[]{:S(2)}) collective-permute-start(bf16[64,2176]{1,0:T(8,128)(2,1)S(1)} %get-tuple-element.233), channel_id=1, source_target_pairs={{0,16},{8,24},{16,0},{24,8},{1,17},{9,25},{17,1},{25,9},{2,18},{10... | collective-permute-start | bytes 835592 | tf_op jit(solution)/shard_map/ppermute | solution.py:759
  143.5 17.2 %collective-permute-start.31 = (bf16[64,2176]{1,0:T(8,128)(2,1)S(1)}, bf16[64,2176]{1,0:T(8,128)(2,1)S(1)}, u32[]{:S(2)}, u32[]{:S(2)}) collective-permute-start(bf16[64,2176]{1,0:T(8,128)(2,1)S(1)} %get-tuple-element.234), channel_id=1, source_target_pairs={{0,24},{8,16},{16,8},{24,0},{1,25},{9,17},{17,9},{25,1},{2,26},{10... | collective-permute-start | bytes 835592 | tf_op jit(solution)/shard_map/ppermute | solution.py:759
  147.2 13.6 %collective-permute-start.21 = (bf16[1,256,512]{2,1,0:T(8,128)(2,1)S(1)}, bf16[1,256,512]{2,1,0:T(8,128)(2,1)S(1)}, u32[]{:S(2)}, u32[]{:S(2)}) collective-permute-start(bf16[1,256,512]{2,1,0:T(8,128)(2,1)S(1)} %get-tuple-element.290), channel_id=1, source_target_pairs={{0,8},{8,0},{16,24},{24,16},{1,9},{9,1},{17,25},{25,17},{2,10},{10... | collective-permute-start | bytes 786440 | tf_op jit(solution)/shard_map/ppermute | solution.py:759
  164.9 10.6 %collective-permute-start.33 = (bf16[1,1,256,512]{3,2,1,0:T(8,128)(2,1)S(1)}, bf16[1,1,256,512]{3,2,1,0:T(8,128)(2,1)S(1)}, u32[]{:S(2)}, u32[]{:S(2)}) collective-permute-start(bf16[1,1,256,512]{3,2,1,0:T(8,128)(2,1)S(1)} %bitcast.56), channel_id=1, source_target_pairs={{0,16},{8,24},{16,0},{24,8},{1,17},{9,25},{17,1},{25,9},{2,18},{10... | collective-permute-start | bytes 786440 | tf_op jit(solution)/shard_map/ppermute | solution.py:759
  166.2 9.2 %collective-permute-start.32 = (bf16[1,256,512]{2,1,0:T(8,128)(2,1)S(1)}, bf16[1,256,512]{2,1,0:T(8,128)(2,1)S(1)}, u32[]{:S(2)}, u32[]{:S(2)}) collective-permute-start(bf16[1,256,512]{2,1,0:T(8,128)(2,1)S(1)} %get-tuple-element.249.refs_0_), channel_id=1, source_target_pairs={{0,8},{8,0},{16,24},{24,16},{1,9},{9,1},{17,25},{25,17},{2,10},{10... | collective-permute-start | bytes 786440 | tf_op jit(solution)/shard_map/ppermute | solution.py:759
  167.0 4.4 %collective-permute-start.34 = (bf16[16,2176]{1,0:T(8,128)(2,1)S(1)}, bf16[16,2176]{1,0:T(8,128)(2,1)S(1)}, u32[]{:S(2)}, u32[]{:S(2)}) collective-permute-start(bf16[16,2176]{1,0:T(8,128)(2,1)S(1)} %get-tuple-element.252), channel_id=1, source_target_pairs={{0,1},{1,0},{2,3},{3,2},{4,5},{5,4},{6,7},{7,6},{8,9},{9,8},{10,11... | collective-permute-start | bytes 208904 | tf_op jit(solution)/shard_map/ppermute | solution.py:759
  167.0 6.9 %collective-permute-start.35 = (bf16[16,2176]{1,0:T(8,128)(2,1)S(1)}, bf16[16,2176]{1,0:T(8,128)(2,1)S(1)}, u32[]{:S(2)}, u32[]{:S(2)}) collective-permute-start(bf16[16,2176]{1,0:T(8,128)(2,1)S(1)} %get-tuple-element.253), channel_id=1, source_target_pairs={{0,2},{1,3},{2,0},{3,1},{4,6},{5,7},{6,4},{7,5},{8,10},{9,11},{10,... | collective-permute-start | bytes 208904 | tf_op jit(solution)/shard_map/ppermute | solution.py:759
  169.3 6.1 %collective-permute-start.36 = (bf16[16,2176]{1,0:T(8,128)(2,1)S(1)}, bf16[16,2176]{1,0:T(8,128)(2,1)S(1)}, u32[]{:S(2)}, u32[]{:S(2)}) collective-permute-start(bf16[16,2176]{1,0:T(8,128)(2,1)S(1)} %get-tuple-element.254), channel_id=1, source_target_pairs={{0,3},{1,2},{2,1},{3,0},{4,7},{5,6},{6,5},{7,4},{8,11},{9,10},{10,... | collective-permute-start | bytes 208904 | tf_op jit(solution)/shard_map/ppermute | solution.py:759
  175.5 10.9 %collective-permute-start.37 = (bf16[2,256,512]{2,1,0:T(8,128)(2,1)S(1)}, bf16[2,256,512]{2,1,0:T(8,128)(2,1)S(1)}, u32[]{:S(2)}, u32[]{:S(2)}) collective-permute-start(bf16[2,256,512]{2,1,0:T(8,128)(2,1)S(1)} %get-tuple-element.255.refs_0_), channel_id=1, source_target_pairs={{0,16},{8,24},{16,0},{24,8},{1,17},{9,25},{17,1},{25,9},{2,18},{10... | collective-permute-start | bytes 1572872 | tf_op jit(solution)/shard_map/ppermute | solution.py:759
  176.9 10.6 %collective-permute-start.38 = (bf16[2,1,256,512]{3,2,1,0:T(8,128)(2,1)S(1)}, bf16[2,1,256,512]{3,2,1,0:T(8,128)(2,1)S(1)}, u32[]{:S(2)}, u32[]{:S(2)}) collective-permute-start(bf16[2,1,256,512]{3,2,1,0:T(8,128)(2,1)S(1)} %get-tuple-element.256.refs_2_), channel_id=1, source_target_pairs={{0,8},{8,0},{16,24},{24,16},{1,9},{9,1},{17,25},{25,17},{2,10},{10... | collective-permute-start | bytes 1572872 | tf_op jit(solution)/shard_map/ppermute | solution.py:759
  177.6 6.1 %collective-permute-start.41 = (bf16[16,2176]{1,0:T(8,128)(2,1)S(1)}, bf16[16,2176]{1,0:T(8,128)(2,1)S(1)}, u32[]{:S(2)}, u32[]{:S(2)}) collective-permute-start(bf16[16,2176]{1,0:T(8,128)(2,1)S(1)} %get-tuple-element.257.refs_4_), channel_id=1, source_target_pairs={{0,3},{1,2},{2,1},{3,0},{4,7},{5,6},{6,5},{7,4},{8,11},{9,10},{10,... | collective-permute-start | bytes 208904 | tf_op jit(solution)/shard_map/ppermute | solution.py:759
  179.7 5.5 %collective-permute-start.40 = (bf16[16,2176]{1,0:T(8,128)(2,1)S(1)}, bf16[16,2176]{1,0:T(8,128)(2,1)S(1)}, u32[]{:S(2)}, u32[]{:S(2)}) collective-permute-start(bf16[16,2176]{1,0:T(8,128)(2,1)S(1)} %get-tuple-element.257.refs_4_), channel_id=1, source_target_pairs={{0,2},{1,3},{2,0},{3,1},{4,6},{5,7},{6,4},{7,5},{8,10},{9,11},{10,... | collective-permute-start | bytes 208904 | tf_op jit(solution)/shard_map/ppermute | solution.py:759
  179.7 5.5 %collective-permute-start.39 = (bf16[16,2176]{1,0:T(8,128)(2,1)S(1)}, bf16[16,2176]{1,0:T(8,128)(2,1)S(1)}, u32[]{:S(2)}, u32[]{:S(2)}) collective-permute-start(bf16[16,2176]{1,0:T(8,128)(2,1)S(1)} %get-tuple-element.257.refs_4_), channel_id=1, source_target_pairs={{0,1},{1,0},{2,3},{3,2},{4,5},{5,4},{6,7},{7,6},{8,9},{9,8},{10,11... | collective-permute-start | bytes 208904 | tf_op jit(solution)/shard_map/ppermute | solution.py:759
  187.6 4.1 %collective-permute-start.43 = (bf16[4,256,512]{2,1,0:T(8,128)(2,1)S(1)}, bf16[4,256,512]{2,1,0:T(8,128)(2,1)S(1)}, u32[]{:S(2)}, u32[]{:S(2)}) collective-permute-start(bf16[4,256,512]{2,1,0:T(8,128)(2,1)S(1)} %bitcast.47), channel_id=1, source_target_pairs={{0,4},{4,0},{1,5},{5,1},{2,6},{6,2},{3,7},{7,3},{8,12},{12,8},{9,1... | collective-permute-start | bytes 3145736 | tf_op jit(solution)/shard_map/ppermute | solution.py:759
  187.7 4.1 %collective-permute-start.42 = (bf16[4,256,512]{2,1,0:T(8,128)(2,1)S(1)}, bf16[4,256,512]{2,1,0:T(8,128)(2,1)S(1)}, u32[]{:S(2)}, u32[]{:S(2)}) collective-permute-start(bf16[4,256,512]{2,1,0:T(8,128)(2,1)S(1)} %get-tuple-element.259.im_ref), channel_id=1, source_target_pairs={{0,4},{4,0},{1,5},{5,1},{2,6},{6,2},{3,7},{7,3},{8,12},{12,8},{9,1... | collective-permute-start | bytes 3145736 | tf_op jit(solution)/shard_map/ppermute | solution.py:759
  188.2 10.5 %collective-permute-start.46 = (bf16[64,2176]{1,0:T(8,128)(2,1)S(1)}, bf16[64,2176]{1,0:T(8,128)(2,1)S(1)}, u32[]{:S(2)}, u32[]{:S(2)}) collective-permute-start(bf16[64,2176]{1,0:T(8,128)(2,1)S(1)} %get-tuple-element.263.refs_0_), channel_id=1, source_target_pairs={{0,24},{8,16},{16,8},{24,0},{1,25},{9,17},{17,9},{25,1},{2,26},{10... | collective-permute-start | bytes 835592 | tf_op jit(solution)/shard_map/ppermute | solution.py:759
  189.6 14.1 %collective-permute-start.45 = (bf16[64,2176]{1,0:T(8,128)(2,1)S(1)}, bf16[64,2176]{1,0:T(8,128)(2,1)S(1)}, u32[]{:S(2)}, u32[]{:S(2)}) collective-permute-start(bf16[64,2176]{1,0:T(8,128)(2,1)S(1)} %get-tuple-element.263.refs_0_), channel_id=1, source_target_pairs={{0,16},{8,24},{16,0},{24,8},{1,17},{9,25},{17,1},{25,9},{2,18},{10... | collective-permute-start | bytes 835592 | tf_op jit(solution)/shard_map/ppermute | solution.py:759
  190.3 13.4 %collective-permute-start.44 = (bf16[64,2176]{1,0:T(8,128)(2,1)S(1)}, bf16[64,2176]{1,0:T(8,128)(2,1)S(1)}, u32[]{:S(2)}, u32[]{:S(2)}) collective-permute-start(bf16[64,2176]{1,0:T(8,128)(2,1)S(1)} %get-tuple-element.263.refs_0_), channel_id=1, source_target_pairs={{0,8},{8,0},{16,24},{24,16},{1,9},{9,1},{17,25},{25,17},{2,10},{10... | collective-permute-start | bytes 835592 | tf_op jit(solution)/shard_map/ppermute | solution.py:759
  203.8 2.8 %collective-permute-start.47 = (bf16[256,2176]{1,0:T(8,128)(2,1)S(1)}, bf16[256,2176]{1,0:T(8,128)(2,1)S(1)}, u32[]{:S(2)}, u32[]{:S(2)}) collective-permute-start(bf16[256,2176]{1,0:T(8,128)(2,1)S(1)} %merge.15.mine_ref), channel_id=1, source_target_pairs={{0,4},{4,0},{1,5},{5,1},{2,6},{6,2},{3,7},{7,3},{8,12},{12,8},{9,1... | collective-permute-start | bytes 3342344 | tf_op jit(solution)/shard_map/ppermute | solution.py:759
  (22 other events, 212.1 us)

commit v5 on v4

--- a/solution.py
+++ b/solution.py
@@ -190,7 +190,132 @@
     return -(-count // 16) * 16
 
 
-def expert_kernel(add, local, meta_ref, rows_ref, dy_ref, ids_ref, wr_ref, *rest):
+def expert_kernel(add, local, meta_ref, rows_ref, dy_ref, ids_ref, wr_ref, wi_ref, wb_ref, *rest):
+    sources = [] if local else [wb_ref]
+    if add:
+        sources += rest[:2]
+        rest = rest[2:]
+    act_ref, dpre_ref, dout_ref, made_ref, din_ref, wi_s, wb_s, *rest = rest
+    if sources:
+        *landings, sems = rest
+        copies = [pltpu.make_async_copy(v, w, sems.at[n]) for n, (v, w) in enumerate(zip(sources, landings))]
+        for copy in copies:
+            copy.start()
+    count = act_ref.shape[0]
+    width = rows_ref.shape[1]
+    rows = rows_ref[0:count, :]
+    part = wi_s.shape[1] // PIECES
+    if local:
+        for n in range(PIECES):
+            at = pl.ds(pl.multiple_of((n ^ meta_ref[1]) * part, part), part)
+            wi_s[:, n * part : (n + 1) * part] = wi_ref[0, :, at]
+            wb_s[n * part : (n + 1) * part, :] = wb_ref[0, at, :]
+
+    if ids_ref.shape[0] == 2:
+        ids = ids_ref[...].astype(F32)
+    else:
+        at = padded(count)
+        ids = [ids_ref[at : at + 2, :], ids_ref[at + 2 : at + 4, 0 : count - width]]
+        ids = jnp.concatenate([v.astype(F32) for v in ids], axis=1)
+    gates, row = row_gates(rows, ids, wr_ref[...])
+    high, low = two_halves(jnp.where(row == meta_ref[0], gates, 0.0))
+    ones = jnp.ones((16, 128), BF16)
+    gate = (mm(high, ones, TN) + mm(low, ones, TN))[:, 0:1]
+    dout_ref[...] = (gate * dy_ref[...].astype(F32)).astype(BF16)
+    wide = wi_s.shape[1] // CHUNKS
+    for q in range(CHUNKS):
+        if not local and q % (CHUNKS // 2) == 0:
+            ref, first = (landings[0], PIECES // 2) if q else (wi_ref, 0)
+            if q:
+                copies[0].wait()
+            for n in range(PIECES // 2):
+                to = slice((first + n) * part, (first + n + 1) * part)
+                for h in range(2):
+                    side = slice(h * part, (h + 1) * part)
+                    wi_s[side, to] = ref[n, h]
+                    wb_s[to, side] = ref[n, 2 + h]
+        here = slice(q * wide, (q + 1) * wide)
+        pre = mm(rows, wi_s[:, here])
+        square = pre * pre
+        inner = pre * (0.7978845608 + 0.0356774081 * square)
+        up = 0.5 + 0.5 * jnp.tanh(inner)
+        value = pre * up
+        act_ref[:, here] = value.astype(BF16)
+        slope = up + value * (1.0 - up) * (1.5957691216 + 0.2140644488 * square)
+        dpre_ref[:, here] = (mm(dout_ref[...], wb_s[here, :], NT) * slope).astype(BF16)
+    made = mm(act_ref[...], wb_s[...]).astype(BF16).astype(F32)
+    d_in = mm(dpre_ref[...], wi_s[...], NT)
+    total = gate * made
+    high, low = two_halves(made * dy_ref[...].astype(F32))
+    ones = jnp.ones((16, width), BF16)
+    d_gate = (mm(ones, high, NT) + mm(ones, low, NT))[0:8]
+    row = lax.broadcasted_iota(jnp.int32, d_gate.shape, 0)
+    d_gate = jnp.where(row == meta_ref[0], d_gate, 0.0)
+    tail = padded(count)
+    if add:
+        for copy in copies[-2:]:
+            copy.wait()
+        pmade_ref, pdin_ref = landings[-2:]
+        total += pmade_ref[...].astype(F32)
+        d_in += pdin_ref[0:count, :].astype(F32)
+        d_gate += read_gate(pdin_ref, count)
+    made_ref[...] = total.astype(BF16)
+    din_ref[0:count, :] = d_in.astype(BF16)
+    high = d_gate.astype(BF16).astype(F32)
+    value = jnp.concatenate([high, d_gate - high], axis=0).astype(BF16)
+    din_ref[tail : tail + 16, :] = value[:, :width]
+    din_ref[tail + 16 : tail + 32, 0 : count - width] = value[:, width:]
+
+
+CHUNKS = 4
+
+
+def read_gate(ref, count):
+    tail = padded(count)
+    width = ref.shape[1]
+    value = ref[tail : tail + 16, 0 : min(count, width)].astype(F32)
+    if count > width:
+        value = jnp.concatenate([value, ref[tail + 16 : tail + 32, 0 : count - width].astype(F32)], axis=1)
+    return value[0:8] + value[8:16]
+
+
+PIECES = 8
+
+
+def expert(meta, rows, dy, ids, wr, weights, prev=None):
+    count, width = dy.shape
+    local = weights[0].ndim == 3
+    hidden = weights[0].shape[2] if local else PIECES * weights[0].shape[2]
+    deep = padded(count) + 32
+    first = prev is None
+    away = pl.BlockSpec(memory_space=pl.ANY)
+    more = [] if first else [away, away]
+    landings = [] if local else [pltpu.VMEM(weights[1].shape, BF16)]
+    if not first:
+        landings += [pltpu.VMEM((count, width), BF16), pltpu.VMEM((deep, width), BF16)]
+    if landings:
+        landings.append(pltpu.SemaphoreType.DMA((len(landings),)))
+    shape = lambda *s: jax.ShapeDtypeStruct(s, BF16)
+    return pl.pallas_call(
+        functools.partial(expert_kernel, not first, local),
+        grid_spec=pltpu.PrefetchScalarGridSpec(
+            num_scalar_prefetch=1,
+            grid=(1,),
+            in_specs=[HERE] * 5 + [HERE if local else away, *more],
+            out_specs=[HERE] * 5,
+            scratch_shapes=[pltpu.VMEM((width, hidden), BF16), pltpu.VMEM((hidden, width), BF16), *landings],
+        ),
+        out_shape=[shape(count, hidden), shape(count, hidden), shape(count, width), shape(count, width), shape(deep, width)],
+        compiler_params=pltpu.CompilerParams(vmem_limit_bytes=LIMIT << 20),
+        cost_estimate=BRIEF,
+        name="expert",
+    )(meta, rows, dy, ids, wr, weights[0], weights[1] if local else held(weights[1]), *[held(v) for v in prev or ()])
+
+
+LIMIT = 26
+
+
+def expert_steps_kernel(add, local, meta_ref, rows_ref, dy_ref, ids_ref, wr_ref, *rest):
     wi_ref, wb_ref, *rest = rest
     sources = [] if local else [wb_ref]
     if add:
@@ -300,19 +425,7 @@
             din_ref[tail : tail + 16, 0:count] = value
 
 
-def read_gate(ref, count):
-    tail = padded(count)
-    width = ref.shape[1]
-    value = ref[tail : tail + 16, 0 : min(count, width)].astype(F32)
-    if count > width:
-        value = jnp.concatenate([value, ref[tail + 16 : tail + 32, 0 : count - width].astype(F32)], axis=1)
-    return value[0:8] + value[8:16]
-
-
-PIECES = 8
-
-
-def expert(meta, rows, dy, ids, wr, weights, prev=None):
+def expert_steps(meta, rows, dy, ids, wr, weights, prev=None):
     count = dy.shape[0]
     width = rows.shape[1]
     local = weights[0].ndim == 3
@@ -333,7 +446,7 @@
     ends = [fix(count, width), fix(deep, width)] if first else [HERE, HERE]
     kept = HELD if first else jax.ShapeDtypeStruct
     return pl.pallas_call(
-        functools.partial(expert_kernel, prev is not None, local),
+        functools.partial(expert_steps_kernel, prev is not None, local),
         grid_spec=pltpu.PrefetchScalarGridSpec(
             num_scalar_prefetch=1,
             grid=(steps,),
@@ -356,7 +469,7 @@
         ],
         compiler_params=pltpu.CompilerParams(vmem_limit_bytes=20 << 20),
         cost_estimate=BRIEF,
-        name="expert",
+        name="expert_steps",
     )(meta, rows, dy if first else held(dy), ids, wr, weights[0], weights[1] if local else held(weights[1]), *given)
 
 
@@ -523,11 +636,13 @@
         tok_s[...] = dmid_s[...] + norm_vjp(d_normed, unit, rstd, g1_ref[...])
         split_halves(meta_ref[3], tok_s, own_ref, other_ref)
         part = width // SHARES
-        for r in range(SHARES):
-            ref = gown_ref if r < SHARES // 2 else ggive_ref
-            to = (r % (SHARES // 2)) * part
-            there = pl.multiple_of((r ^ meta_ref[2]) * part, part)
-            ref[to : to + part, :] = grad_s[pl.ds(there, part), :]
+
+        @pl.loop(0, SHARES // 2)
+        def _(r):
+            to = pl.ds(pl.multiple_of(r * part, part), part)
+            for ref, first in ((gown_ref, 0), (ggive_ref, SHARES // 2)):
+                there = pl.multiple_of(((r + first) ^ meta_ref[2]) * part, part)
+                ref[to, :] = grad_s[pl.ds(there, part), :]
 
 
 SHARES = 32
@@ -583,13 +698,15 @@
     part = width // SHARES
     all_s[0:upper, :] = mine_ref[...]
     all_s[upper:width, :] = recv_ref[...]
-    for i in range(SHARES):
+
+    @pl.loop(0, SHARES)
+    def _(i):
         there = pl.multiple_of((i ^ meta_ref[2]) * part, part)
         value = all_s[pl.ds(there, part), :].astype(F32)
-        at = i * part
-        gqkv_ref[at : at + part, :] = value[:, : 3 * width]
-        gout_ref[at : at + part, :] = value[:, 3 * width : 4 * width]
-        small_ref[at : at + part, :] = value[:, 4 * width :]
+        at = pl.ds(pl.multiple_of(i * part, part), part)
+        gqkv_ref[at, :] = value[:, : 3 * width]
+        gout_ref[at, :] = value[:, 3 * width : 4 * width]
+        small_ref[at, :] = value[:, 4 * width :]
 
 
 def finish_shared(meta, mine, recv):
@@ -696,24 +813,58 @@
     )(meta, held(w_in), held(w_back))
 
 
+def by_rows(count, step, body):
+    @pl.loop(0, count // step)
+    def _(n):
+        body(n * step if isinstance(n, int) else pl.multiple_of(n * step, step))
+
+
 def merge_kernel(plan, *refs):
     refs = list(refs)
     takes = [[[(refs.pop(0), at) for at in views] for views in groups] for groups, _, _ in plan]
+    full = lambda n: (slice(None),) * n
+
+    def rows_of(ref, lead, at, size):
+        return lead + full(len(ref.shape) - 2 - len(lead)) + (pl.ds(at, size), slice(None))
+
     for groups, (_, axis, cuts) in zip(takes, plan):
         outs = [refs.pop(0) for _ in cuts]
+        head = groups[0][0][0]
+        count = head.shape[-2]
+        step = 16 if len(head.shape) == 2 else 64
         if axis is not None:
-            size = groups[0][0][0].shape[axis]
+            size = head.shape[axis]
             for k, (ref, _) in enumerate(groups[0]):
-                at = slice(k * size, (k + 1) * size)
-                outs[0][(slice(None),) * axis + (at,)] = ref[...]
+
+                def copy(at, k=k, ref=ref):
+                    if len(ref.shape) == 2:
+                        outs[0][pl.ds(k * size + at, step), :] = ref[pl.ds(at, step), :]
+                    else:
+                        lead = full(axis) + (slice(k * size, (k + 1) * size),)
+                        outs[0][rows_of(outs[0], lead, at, step)] = ref[rows_of(ref, (), at, step)]
+
+                by_rows(count, step, copy)
             continue
         for g, take in enumerate(groups):
-            total = sum(ref[at].astype(F32) for ref, at in take).astype(BF16)
-            for out, cut in zip(outs, cuts):
-                if len(groups) > 1:
-                    out[g] = total[cut]
-                else:
-                    out[...] = total[cut]
+            place = (g,) if len(groups) > 1 else ()
+            if len(head.shape) == 2:
+                for out, cut in zip(outs, cuts):
+                    start = cut.start or 0
+
+                    def add(at, out=out, start=start):
+                        total = sum(ref[pl.ds(start + at, step), :].astype(F32) for ref, _ in take)
+                        out[pl.ds(at, step), :] = total.astype(BF16)
+
+                    by_rows(out.shape[0], step, add)
+                continue
+
+            def add(at, take=take, place=place):
+                parts = [ref[rows_of(ref, () if view is ... else (view,), at, step)] for ref, view in take]
+                total = sum(v.astype(F32) for v in parts).astype(BF16)
+                for out, cut in zip(outs, cuts):
+                    out[rows_of(out, place, at, step)] = total[cut]
+
+            by_rows(count, step, add)
 
 
 def merge(*items):
@@ -818,7 +969,7 @@
     x_rows, dy, normed, qkv, probs, mix, mid, routed = attend(
         meta, tokens, tok_other, cotangent, dy_other, key_mask, g1, w_qkv, w_out, g2
     )
-    own_one = expert(meta, routed, dy, ids, wr, (w_in, w_back))
+    own_one = expert_steps(meta, routed, dy, ids, wr, (w_in, w_back))
     far_rows = jnp.concatenate([routed, ids_pack], 0)
     pack, wr_far = after(pack, routed), after(wr, own_one[2])
 
@@ -826,7 +977,7 @@
     far_rows = far(far_rows)
     far_raw = after(far_raw, own_one[2])
     far_dy = assemble(meta, far_raw, swap(far_raw))
-    far_one = expert(meta, far_rows, far_dy, far_rows, wr_far, (w_in, w_back))
+    far_one = expert_steps(meta, far_rows, far_dy, far_rows, wr_far, (w_in, w_back))
     *packs, wr_far = tie(*packs, after(wr, far_one[2]))
     packs = jnp.stack(packs)
     pair = [packs, swap(packs)]

time: 212 us -> 209 us (0.986)
  Pallas kernels: 99.9 us -> 96.5 us
    pallas_call x4, Pallas kernels: 42.3 us -> 37.6 us  [the longest x2 20.5 us: expert_steps(): pl.pallas_call(functools.partial(expert_steps_kernel, prev is not None, l...]
  transfers between devices with their start and end apart: 48 -> 48, of which waited for: 22 -> 22; matrix products, arithmetic and copies ran while one was open for 0% -> 0% of each run, Pallas kernels for 45% -> 43%
where the time goes in v5:
time: 209 us
  Pallas kernels  96.5 us (46%)
  waiting for transfers between devices  60.2 us (29%)
  starting transfers between devices  45.4 us (22%)
  local copies, waits for them, and re-layouts  3.83 us (2%)
    ppermute x48, waiting for transfers between devices, send(): return lax.ppermute(value, axis, pairs)  60.2 us
    ppermute x48, starting transfers between devices, send(): return lax.ppermute(value, axis, pairs)  45.4 us
    pallas_call x2, Pallas kernels, expert_steps(): pl.pallas_call(functools.partial(expert_steps_kernel, prev is not None, l...  20.5 us
    pallas_call x2, Pallas kernels, weight_grads(): pl.pallas_call(functools.partial(weight_kernel, n), grid=(steps,), in_spe...  17.1 us
    pallas_call x2, Pallas kernels, expert(): pl.pallas_call(functools.partial(expert_kernel, not first, local), grid_s...  17.1 us
    pallas_call x1, Pallas kernels, attend_back(): pl.pallas_call(back_kernel, grid_spec=pltpu.PrefetchScalarGridSpec(num_sc...  12.5 us
    pallas_call x1, Pallas kernels, attend(): pl.pallas_call(attend_kernel, grid_spec=pltpu.PrefetchScalarGridSpec(num_...  10.4 us
    pallas_call x8, Pallas kernels, merge(): pl.pallas_call(functools.partial(merge_kernel, plan), out_shape=shapes, c...  4.8 us
  transfers between devices with their start and end apart: 48, of which 22 were waited for; matrix products, arithmetic and copies ran while one was open for 0% of the time, Pallas kernels for 43%

profile of v5, /device:TPU:0, one launch (start us, length us, event | category | flops | bytes accessed | tf_op | source)
XLA Modules:
  0.0 208.7 jit_solution(16462852952204865900)
XLA Ops:
  0.8 1.6 pack_piece.1
  2.9 3.7 %collective-permute-start.6 = (bf16[4,256,256]{2,1,0:T(8,128)(2,1)S(1)}, bf16[4,256,256]{2,1,0:T(8,128)(2,1)}, u32[]{:S(2)}, u32[]{:S(2)}) collective-permute-start(bf16[4,256,256]{2,1,0:T(8,128)(2,1)S(1)} %pack_piece.1), channel_id=1, source_target_pairs={{0,2},{1,3},{2,0},{3,1},{4,6},{5,7},{6,4},{7,5},{8,10},{9,11},{10,... | collective-permute-start | bytes 1572872 | tf_op jit(solution)/shard_map/ppermute | solution.py:910
  6.8 1.6 collective-permute-start.4
  8.7 1.9 collective-permute-done.other_ref
  11.4 10.4 %attend.1 = (bf16[600,512]{1,0:T(8,128)(2,1)}, bf16[600,512]{1,0:T(8,128)(2,1)S(1)}, bf16[600,512]{1,0:T(8,128)(2,1)}, bf16[600,1536]{1,0:T(8,128)(2,1)}, bf16[3...) custom-call(s32[4]{0:T(128)S(1)} %add_add_fusion.1.meta_ref, ...), custom_call_target="tpu_custom_call" | custom-call | flops 1 | bytes 1 | tf_op jit(solution)/shard_map/attend/pallas_call | solution.py:117
  22.7 10.2 %expert_steps.2 = (bf16[600,2048]{1,0:T(8,128)(2,1)S(1)}, bf16[600,2048]{1,0:T(8,128)(2,1)S(1)}, bf16[600,512]{1,0:T(8,128)(2,1)S(1)}, bf16[600,512]{1,0:T(8,128)(2,1)}, bf16[640,512]{1,0:T(8,128)(2,1)}) custom-call(s32[4]{0:T(128)S(1)} %add_add_fusion.1.meta_ref, bf16[600,512]{1,0:T(8,128)(2,1)S(1)} %get-tuple-element.138.rows_ref.refs_0_.routed_ref, ...), custom_call_target="tpu_custom_call" | custom-call | flops 1 | bytes 1 | tf_op jit(solution)/shard_map/expert_steps/pallas_call | solution.py:448
  32.9 1.3 collective-permute-done.4.own_ref
  34.2 2.5 %collective-permute-start.9 = (bf16[4,256,256]{2,1,0:T(8,128)(2,1)}, bf16[4,256,256]{2,1,0:T(8,128)(2,1)S(1)}, u32[]{:S(2)}, u32[]{:S(2)}) collective-permute-start(bf16[4,256,256]{2,1,0:T(8,128)(2,1)} %collective-permute-done.6), channel_id=1, source_target_pairs={{0,24},{8,16},{16,8},{24,0},{1,25},{9,17},{17,9},{25,1},{2,26},{10... | collective-permute-start | bytes 1572872 | tf_op jit(solution)/shard_map/ppermute | solution.py:910
  38.6 8.8 %collective-permute-done.3.rows_ref.ids_ref.refs_1_ = bf16[624,512]{1,0:T(8,128)(2,1)S(1)} collective-permute-done((bf16[624,512]{1,0:T(8,128)(2,1)S(1)}, bf16[624,512]{1,0:T(8,128)(2,1)S(1)}, u32[]{:S(2)}, u32[]{:S(2)}) %collective-permute-start.3) | collective-permute-done | bytes 639008 | tf_op jit(solution)/shard_map/ppermute | solution.py:910
  47.3 10.3 %expert_steps.3 = (bf16[600,2048]{1,0:T(8,128)(2,1)S(1)}, bf16[600,2048]{1,0:T(8,128)(2,1)S(1)}, bf16[600,512]{1,0:T(8,128)(2,1)S(1)}, bf16[600,512]{1,0:T(8,128)(2,1)}, bf16[640,512]{1,0:T(8,128)(2,1)}) custom-call(s32[4]{0:T(128)S(1)} %add_add_fusion.1.meta_ref, bf16[624,512]{1,0:T(8,128)(2,1)S(1)} %collective-permute-done.3.rows_ref.ids_ref.refs_1_, ...), custom_call_target="tpu_custom_call" | custom-call | flops 1 | bytes 1 | tf_op jit(solution)/shard_map/expert_steps/pallas_call | solution.py:448
  57.7 3.2 %collective-permute-done.8 = bf16[4,256,256]{2,1,0:T(8,128)(2,1)S(1)} collective-permute-done((bf16[4,256,256]{2,1,0:T(8,128)(2,1)}, bf16[4,256,256]{2,1,0:T(8,128)(2,1)S(1)}, u32[]{:S(2)}, u32[]{:S(2)}) %collective-permute-start.8) | collective-permute-done | bytes 524320 | tf_op jit(solution)/shard_map/ppermute | solution.py:910
  61.1 1.3 pad_maximum_fusion.wi_ref
  62.5 9.3 %weight_grads.2 = (bf16[4,256,512]{2,1,0:T(8,128)(2,1)}, bf16[4,256,512]{2,1,0:T(8,128)(2,1)}, bf16[4,256,512]{2,1,0:T(8,128)(2,1)}, bf16[4,256,512]{2,1,0:T(8,128)(2,1)}) custom-call(bf16[600,512]{1,0:T(8,128)(2,1)S(1)} %get-tuple-element.138.rows_ref.refs_0_.routed_ref, bf16[624,512]{1,0:T(8,128)(2,1)S(1)} %collective-permute-done.3.rows_ref.ids_ref.refs_1_, ...), custom_call_target="tpu_custom_call" | custom-call | flops 1 | bytes 1 | tf_op jit(solution)/shard_map/weight_grads/pallas_call | solution.py:509
  73.4 8.5 %expert.2 = (bf16[600,2048]{1,0:T(8,128)(2,1)S(1)}, bf16[600,2048]{1,0:T(8,128)(2,1)S(1)}, bf16[600,512]{1,0:T(8,128)(2,1)S(1)}, bf16[600,512]{1,0:T(8,128)(2,1)S(1)}, bf16[640,512]{1,0:T(8,128)(2,1)S(1)}) custom-call(s32[4]{0:T(128)S(1)} %add_add_fusion.meta_ref, bf16[624,512]{1,0:T(8,128)(2,1)S(1)} %collective-permute-done.3.rows_ref.ids_ref.refs_1_, ...), custom_call_target="tpu_custom_call" | custom-call | flops 1 | bytes 1 | tf_op jit(solution)/shard_map/expert/pallas_call | solution.py:299
  82.8 2.4 %merge.8 = (bf16[2,256,512]{2,1,0:T(8,128)(2,1)S(1)}, bf16[2,256,512]{2,1,0:T(8,128)(2,1)S(1)}, bf16[2,1,256,512]{3,2,1,0:T(8,128)(2,1)S(1)}, bf16[2,1,256,512]{3,2,1,0:T(8,128)(2,1)S(1)}) custom-call(bf16[4,256,512]{2,1,0:T(8,128)(2,1)S(1)} %copy-done.11, bf16[4,256,512]{2,1,0:T(8,128)(2,1)} %collective-permute-done.11.refs_1_, ...), custom_call_target="tpu_custom_call" | custom-call | flops 1 | bytes 1 | tf_op jit(solution)/shard_map/merge/pallas_call | solution.py:889
  85.2 1.5 collective-permute-start.14
  87.5 8.5 %expert.3 = (bf16[600,2048]{1,0:T(8,128)(2,1)S(1)}, bf16[600,2048]{1,0:T(8,128)(2,1)S(1)}, bf16[600,512]{1,0:T(8,128)(2,1)S(1)}, bf16[600,512]{1,0:T(8,128)(2,1)S(1)}, bf16[640,512]{1,0:T(8,128)(2,1)S(1)}) custom-call(s32[4]{0:T(128)S(1)} %add_add_fusion.meta_ref, bf16[600,512]{1,0:T(8,128)(2,1)S(1)} %get-tuple-element.138.rows_ref.refs_0_.routed_ref, ...), custom_call_target="tpu_custom_call" | custom-call | flops 1 | bytes 1 | tf_op jit(solution)/shard_map/expert/pallas_call | solution.py:299
  96.1 7.8 %weight_grads.3 = (bf16[4,256,512]{2,1,0:T(8,128)(2,1)S(1)}, bf16[4,256,512]{2,1,0:T(8,128)(2,1)S(1)}, bf16[4,256,512]{2,1,0:T(8,128)(2,1)S(1)}, bf16[4,256,512]{2,1,0:T(8,128)(2,1)S(1)}) custom-call(bf16[600,512]{1,0:T(8,128)(2,1)S(1)} %get-tuple-element.138.rows_ref.refs_0_.routed_ref, ...), custom_call_target="tpu_custom_call" | custom-call | flops 1 | bytes 1 | tf_op jit(solution)/shard_map/weight_grads/pallas_call | solution.py:509
  104.5 1.2 collective-permute-start.20
  106.7 1.5 collective-permute-done.17
  108.7 1.3 collective-permute-start.19
  110.7 12.5 %attend_back.1 = (bf16[3,100,512]{2,1,0:T(8,128)(2,1)S(1)}, bf16[3,100,512]{2,1,0:T(8,128)(2,1)S(1)}, bf16[256,2176]{1,0:T(8,128)(2,1)S(1)}, bf16[256,2176]{1,0:T(8,128)(2,1)S(1)}) custom-call(s32[4]{0:T(128)S(1)} %add_add_fusion.1.meta_ref, bf16[640,512]{1,0:T(8,128)(2,1)S(1)} %get-tuple-element.205.din0_ref, ...), custom_call_target="tpu_custom_call" | custom-call | flops 1 | bytes 1 | tf_op jit(solution)/shard_map/attend_back/pallas_call | solution.py:658
  127.2 1.1 collective-permute-start.22
  128.4 6.5 %collective-permute-done.23.refs_3_ = bf16[1,256,512]{2,1,0:T(8,128)(2,1)S(1)} collective-permute-done((bf16[1,256,512]{2,1,0:T(8,128)(2,1)S(1)}, bf16[1,256,512]{2,1,0:T(8,128)(2,1)S(1)}, u32[]{:S(2)}, u32[]{:S(2)}) %collective-permute-start.23) | collective-permute-done | bytes 262176 | tf_op jit(solution)/shard_map/ppermute | solution.py:910
  136.4 2.3 %collective-permute-start.27 = (bf16[2,1,256,512]{3,2,1,0:T(8,128)(2,1)S(1)}, bf16[2,1,256,512]{3,2,1,0:T(8,128)(2,1)S(1)}, u32[]{:S(2)}, u32[]{:S(2)}) collective-permute-start(bf16[2,1,256,512]{3,2,1,0:T(8,128)(2,1)S(1)} %get-tuple-element.230), channel_id=1, source_target_pairs={{0,2},{1,3},{2,0},{3,1},{4,6},{5,7},{6,4},{7,5},{8,10},{9,11},{10,... | collective-permute-start | bytes 1572872 | tf_op jit(solution)/shard_map/ppermute | solution.py:910
  138.7 1.2 collective-permute-start.29
  140.8 1.4 collective-permute-start.31
  142.2 1.9 collective-permute-done.28.refs_4_
  145.1 2.8 %place.1 = (bf16[6,100,512]{2,1,0:T(8,128)(2,1)}, bf16[6,100,512]{2,1,0:T(8,128)(2,1)}) custom-call(s32[4]{0:T(128)S(1)} %add_add_fusion.1.meta_ref, bf16[3,100,512]{2,1,0:T(8,128)(2,1)S(1)} %get-tuple-element.241.a_own_ref, bf16[3,100,512]{2,1,0:T(8,128)(2,1)S(1)} %collective-permute-done.26.a_recv_ref, ...), custom_call_target="tpu_custom_call" | custom-call | flops 1 | bytes 1 | tf_op jit(solution)/shard_map/place/pallas_call | solution.py:775
  147.9 10.1 %collective-permute-done.21.refs_1_ = bf16[1,256,512]{2,1,0:T(8,128)(2,1)S(1)} collective-permute-done((bf16[1,256,512]{2,1,0:T(8,128)(2,1)S(1)}, bf16[1,256,512]{2,1,0:T(8,128)(2,1)S(1)}, u32[]{:S(2)}, u32[]{:S(2)}) %collective-permute-start.21) | collective-permute-done | bytes 262176 | tf_op jit(solution)/shard_map/ppermute | solution.py:910
  158.0 3.8 %collective-permute-done.27.refs_2_.refs_5_ = bf16[2,1,256,512]{3,2,1,0:T(8,128)(2,1)S(1)} collective-permute-done((bf16[2,1,256,512]{3,2,1,0:T(8,128)(2,1)S(1)}, bf16[2,1,256,512]{3,2,1,0:T(8,128)(2,1)S(1)}, u32[]{:S(2)}, u32[]{:S(2)}) %collective-permute-start.27) | collective-permute-done | bytes 524320 | tf_op jit(solution)/shard_map/ppermute | solution.py:910
  162.2 1.1 collective-permute-start.33
  164.3 2.3 %collective-permute-start.35 = (bf16[16,2176]{1,0:T(8,128)(2,1)S(1)}, bf16[16,2176]{1,0:T(8,128)(2,1)S(1)}, u32[]{:S(2)}, u32[]{:S(2)}) collective-permute-start(bf16[16,2176]{1,0:T(8,128)(2,1)S(1)} %get-tuple-element.253), channel_id=1, source_target_pairs={{0,2},{1,3},{2,0},{3,1},{4,6},{5,7},{6,4},{7,5},{8,10},{9,11},{10,... | collective-permute-start | bytes 208904 | tf_op jit(solution)/shard_map/ppermute | solution.py:910
  166.6 2.1 %collective-permute-start.36 = (bf16[16,2176]{1,0:T(8,128)(2,1)S(1)}, bf16[16,2176]{1,0:T(8,128)(2,1)S(1)}, u32[]{:S(2)}, u32[]{:S(2)}) collective-permute-start(bf16[16,2176]{1,0:T(8,128)(2,1)S(1)} %get-tuple-element.254), channel_id=1, source_target_pairs={{0,3},{1,2},{2,1},{3,0},{4,7},{5,6},{6,5},{7,4},{8,11},{9,10},{10,... | collective-permute-start | bytes 208904 | tf_op jit(solution)/shard_map/ppermute | solution.py:910
  168.7 2.5 %collective-permute-done.35.refs_6_ = bf16[16,2176]{1,0:T(8,128)(2,1)S(1)} collective-permute-done((bf16[16,2176]{1,0:T(8,128)(2,1)S(1)}, bf16[16,2176]{1,0:T(8,128)(2,1)S(1)}, u32[]{:S(2)}, u32[]{:S(2)}) %collective-permute-start.35) | collective-permute-done | bytes 69664 | tf_op jit(solution)/shard_map/ppermute | solution.py:910
  171.2 1.5 collective-permute-done.36.refs_7_
  174.9 2.1 %collective-permute-start.41 = (bf16[16,2176]{1,0:T(8,128)(2,1)S(1)}, bf16[16,2176]{1,0:T(8,128)(2,1)S(1)}, u32[]{:S(2)}, u32[]{:S(2)}) collective-permute-start(bf16[16,2176]{1,0:T(8,128)(2,1)S(1)} %get-tuple-element.257.refs_4_), channel_id=1, source_target_pairs={{0,3},{1,2},{2,1},{3,0},{4,7},{5,6},{6,5},{7,4},{8,11},{9,10},{10,... | collective-permute-start | bytes 208904 | tf_op jit(solution)/shard_map/ppermute | solution.py:910
  177.0 2.3 %collective-permute-start.39 = (bf16[16,2176]{1,0:T(8,128)(2,1)S(1)}, bf16[16,2176]{1,0:T(8,128)(2,1)S(1)}, u32[]{:S(2)}, u32[]{:S(2)}) collective-permute-start(bf16[16,2176]{1,0:T(8,128)(2,1)S(1)} %get-tuple-element.257.refs_4_), channel_id=1, source_target_pairs={{0,1},{1,0},{2,3},{3,2},{4,5},{5,4},{6,7},{7,6},{8,9},{9,8},{10,11... | collective-permute-start | bytes 208904 | tf_op jit(solution)/shard_map/ppermute | solution.py:910
  179.3 1.7 collective-permute-done.41.refs_7_
  181.0 1.5 collective-permute-done.40.refs_6_
  182.5 1.3 collective-permute-done.37.refs_1_
  185.4 1.4 collective-permute-start.46
  187.7 1.1 collective-permute-start.44
  189.0 4.4 %finish_expert.1 = (f32[1,512,2048]{2,1,0:T(8,128)}, f32[1,2048,512]{2,1,0:T(8,128)}) custom-call(s32[4]{0:T(128)S(1)} %add_add_fusion.1.meta_ref, bf16[4,256,512]{2,1,0:T(8,128)(2,1)S(1)} %get-tuple-element.259.im_ref, bf16[4,256,512]{2,1,0:T(8,128)(2,1)S(1)} %collective-permute-done.42.ir_ref, bf16[4,256,512]{2,1,0:T(8,128)(2,1)S(1)} %bitcast.48, ...), custom_call_target="tpu_custom_call" | custom-call | flops 1 | bytes 1 | tf_op jit(solution)/shard_map/finish_expert/pallas_call | solution.py:542
  193.4 2.4 %collective-permute-done.46.refs_3_ = bf16[64,2176]{1,0:T(8,128)(2,1)S(1)} collective-permute-done((bf16[64,2176]{1,0:T(8,128)(2,1)S(1)}, bf16[64,2176]{1,0:T(8,128)(2,1)S(1)}, u32[]{:S(2)}, u32[]{:S(2)}) %collective-permute-start.46) | collective-permute-done | bytes 278560 | tf_op jit(solution)/shard_map/ppermute | solution.py:910
  195.8 5.1 %collective-permute-done.45.refs_2_ = bf16[64,2176]{1,0:T(8,128)(2,1)S(1)} collective-permute-done((bf16[64,2176]{1,0:T(8,128)(2,1)S(1)}, bf16[64,2176]{1,0:T(8,128)(2,1)S(1)}, u32[]{:S(2)}, u32[]{:S(2)}) %collective-permute-start.45) | collective-permute-done | bytes 278560 | tf_op jit(solution)/shard_map/ppermute | solution.py:910
  201.1 2.7 %collective-permute-done.47.recv_ref = bf16[256,2176]{1,0:T(8,128)(2,1)S(1)} collective-permute-done((bf16[256,2176]{1,0:T(8,128)(2,1)S(1)}, bf16[256,2176]{1,0:T(8,128)(2,1)S(1)}, u32[]{:S(2)}, u32[]{:S(2)}) %collective-permute-start.47) | collective-permute-done | bytes 1114144 | tf_op jit(solution)/shard_map/ppermute | solution.py:910
  203.8 3.3 %finish_shared.1 = (f32[512,1536]{1,0:T(8,128)}, f32[512,512]{1,0:T(8,128)}, f32[512,128]{1,0:T(8,128)S(1)}) custom-call(s32[4]{0:T(128)S(1)} %add_add_fusion.1.meta_ref, bf16[256,2176]{1,0:T(8,128)(2,1)S(1)} %merge.15.mine_ref, bf16[256,2176]{1,0:T(8,128)(2,1)S(1)} %collective-permute-done.47.recv_ref), custom_call_target="tpu_custom_call" | custom-call | flops 1 | bytes 1 | tf_op jit(solution)/shard_map/finish_shared/pallas_call | solution.py:716
  (136 shorter events, 26.5 us)
Async XLA Ops:
  2.4 6.0 %collective-permute-start.2 = (s32[6,100]{1,0:T(8,128)S(1)}, s32[6,100]{1,0:T(8,128)S(1)}, u32[]{:S(2)}, u32[]{:S(2)}) collective-permute-start(s32[6,100]{1,0:T(8,128)S(1)} %bitcast.69), channel_id=1, source_target_pairs={{0,4},{4,0},{1,5},{5,1},{2,6},{6,2},{3,7},{7,3},{8,12},{12,8},{9,1... | collective-permute-start | bytes 7208 | tf_op jit(solution)/shard_map/ppermute | solution.py:910
  2.9 31.3 %collective-permute-start.6 = (bf16[4,256,256]{2,1,0:T(8,128)(2,1)S(1)}, bf16[4,256,256]{2,1,0:T(8,128)(2,1)}, u32[]{:S(2)}, u32[]{:S(2)}) collective-permute-start(bf16[4,256,256]{2,1,0:T(8,128)(2,1)S(1)} %pack_piece.1), channel_id=1, source_target_pairs={{0,2},{1,3},{2,0},{3,1},{4,6},{5,7},{6,4},{7,5},{8,10},{9,11},{10,... | collective-permute-start | bytes 1572872 | tf_op jit(solution)/shard_map/ppermute | solution.py:910
  6.6 4.0 %collective-permute-start.1 = (bf16[6,100,512]{2,1,0:T(8,128)(2,1)}, bf16[6,100,512]{2,1,0:T(8,128)(2,1)S(1)}, u32[]{:S(2)}, u32[]{:S(2)}) collective-permute-start(bf16[6,100,512]{2,1,0:T(8,128)(2,1)} %dyown_ref.1), channel_id=1, source_target_pairs={{0,4},{4,0},{1,5},{5,1},{2,6},{6,2},{3,7},{7,3},{8,12},{12,8},{9,1... | collective-permute-start | bytes 1843208 | tf_op jit(solution)/shard_map/ppermute | solution.py:910
  6.8 27.5 %collective-permute-start.4 = (bf16[6,100,512]{2,1,0:T(8,128)(2,1)}, bf16[6,100,512]{2,1,0:T(8,128)(2,1)S(1)}, u32[]{:S(2)}, u32[]{:S(2)}) collective-permute-start(bf16[6,100,512]{2,1,0:T(8,128)(2,1)} %dyown_ref.1), channel_id=1, source_target_pairs={{0,1},{1,0},{2,3},{3,2},{4,5},{5,4},{6,7},{7,6},{8,9},{9,8},{10,11... | collective-permute-start | bytes 1843208 | tf_op jit(solution)/shard_map/ppermute | solution.py:910
  8.3 2.2 %collective-permute-start = (bf16[6,100,512]{2,1,0:T(8,128)(2,1)S(1)}, bf16[6,100,512]{2,1,0:T(8,128)(2,1)}, u32[]{:S(2)}, u32[]{:S(2)}) collective-permute-start(bf16[6,100,512]{2,1,0:T(8,128)(2,1)S(1)} %copy-done.19), channel_id=1, source_target_pairs={{0,4},{4,0},{1,5},{5,1},{2,6},{6,2},{3,7},{7,3},{8,12},{12,8},{9,1... | collective-permute-start | bytes 1843208 | tf_op jit(solution)/shard_map/ppermute | solution.py:910
  21.9 25.5 %collective-permute-start.3 = (bf16[624,512]{1,0:T(8,128)(2,1)S(1)}, bf16[624,512]{1,0:T(8,128)(2,1)S(1)}, u32[]{:S(2)}, u32[]{:S(2)}) collective-permute-start(bf16[624,512]{1,0:T(8,128)(2,1)S(1)} %pad_maximum_fusion.1), channel_id=1, source_target_pairs={{0,1},{1,0},{2,3},{3,2},{4,5},{5,4},{6,7},{7,6},{8,9},{9,8},{10,11... | collective-permute-start | bytes 1916936 | tf_op jit(solution)/shard_map/ppermute | solution.py:910
  34.2 3.5 %collective-permute-start.5 = (bf16[6,100,512]{2,1,0:T(8,128)(2,1)S(1)}, bf16[6,100,512]{2,1,0:T(8,128)(2,1)S(1)}, u32[]{:S(2)}, u32[]{:S(2)}) collective-permute-start(bf16[6,100,512]{2,1,0:T(8,128)(2,1)S(1)} %collective-permute-done.4.own_ref), channel_id=1, source_target_pairs={{0,4},{4,0},{1,5},{5,1},{2,6},{6,2},{3,7},{7,3},{8,12},{12,8},{9,1... | collective-permute-start | bytes 1843208 | tf_op jit(solution)/shard_map/ppermute | solution.py:910
  34.2 23.5 %collective-permute-start.9 = (bf16[4,256,256]{2,1,0:T(8,128)(2,1)}, bf16[4,256,256]{2,1,0:T(8,128)(2,1)S(1)}, u32[]{:S(2)}, u32[]{:S(2)}) collective-permute-start(bf16[4,256,256]{2,1,0:T(8,128)(2,1)} %collective-permute-done.6), channel_id=1, source_target_pairs={{0,24},{8,16},{16,8},{24,0},{1,25},{9,17},{17,9},{25,1},{2,26},{10... | collective-permute-start | bytes 1572872 | tf_op jit(solution)/shard_map/ppermute | solution.py:910
  36.7 24.2 %collective-permute-start.8 = (bf16[4,256,256]{2,1,0:T(8,128)(2,1)}, bf16[4,256,256]{2,1,0:T(8,128)(2,1)S(1)}, u32[]{:S(2)}, u32[]{:S(2)}) collective-permute-start(bf16[4,256,256]{2,1,0:T(8,128)(2,1)} %collective-permute-done.6), channel_id=1, source_target_pairs={{0,16},{8,24},{16,0},{24,8},{1,17},{9,25},{17,1},{25,9},{2,18},{10... | collective-permute-start | bytes 1572872 | tf_op jit(solution)/shard_map/ppermute | solution.py:910
  37.3 23.8 %collective-permute-start.7 = (bf16[4,256,256]{2,1,0:T(8,128)(2,1)}, bf16[4,256,256]{2,1,0:T(8,128)(2,1)S(1)}, u32[]{:S(2)}, u32[]{:S(2)}) collective-permute-start(bf16[4,256,256]{2,1,0:T(8,128)(2,1)} %collective-permute-done.6), channel_id=1, source_target_pairs={{0,8},{8,0},{16,24},{24,16},{1,9},{9,1},{17,25},{25,17},{2,10},{10... | collective-permute-start | bytes 1572872 | tf_op jit(solution)/shard_map/ppermute | solution.py:910
  62.4 9.9 %collective-permute-start.10 = (bf16[4,4,256,256]{3,2,1,0:T(8,128)(2,1)S(1)}, bf16[4,4,256,256]{3,2,1,0:T(8,128)(2,1)}, u32[]{:S(2)}, u32[]{:S(2)}) collective-permute-start(bf16[4,4,256,256]{3,2,1,0:T(8,128)(2,1)S(1)} %pad_maximum_fusion.wi_ref), channel_id=1, source_target_pairs={{0,4},{4,0},{1,5},{5,1},{2,6},{6,2},{3,7},{7,3},{8,12},{12,8},{9,1... | collective-permute-start | bytes 6291464 | tf_op jit(solution)/shard_map/ppermute | solution.py:910
  71.7 11.1 %collective-permute-start.11 = (bf16[4,256,512]{2,1,0:T(8,128)(2,1)}, bf16[4,256,512]{2,1,0:T(8,128)(2,1)}, u32[]{:S(2)}, u32[]{:S(2)}) collective-permute-start(bf16[4,256,512]{2,1,0:T(8,128)(2,1)} %get-tuple-element.163), channel_id=1, source_target_pairs={{0,4},{4,0},{1,5},{5,1},{2,6},{6,2},{3,7},{7,3},{8,12},{12,8},{9,1... | collective-permute-start | bytes 3145736 | tf_op jit(solution)/shard_map/ppermute | solution.py:910
  72.2 10.6 %collective-permute-start.12 = (bf16[4,256,512]{2,1,0:T(8,128)(2,1)}, bf16[4,256,512]{2,1,0:T(8,128)(2,1)}, u32[]{:S(2)}, u32[]{:S(2)}) collective-permute-start(bf16[4,256,512]{2,1,0:T(8,128)(2,1)} %get-tuple-element.165), channel_id=1, source_target_pairs={{0,4},{4,0},{1,5},{5,1},{2,6},{6,2},{3,7},{7,3},{8,12},{12,8},{9,1... | collective-permute-start | bytes 3145736 | tf_op jit(solution)/shard_map/ppermute | solution.py:910
  81.9 22.0 %collective-permute-start.13 = (bf16[640,512]{1,0:T(8,128)(2,1)S(1)}, bf16[640,512]{1,0:T(8,128)(2,1)S(1)}, u32[]{:S(2)}, u32[]{:S(2)}) collective-permute-start(bf16[640,512]{1,0:T(8,128)(2,1)S(1)} %get-tuple-element.171), channel_id=1, source_target_pairs={{0,1},{1,0},{2,3},{3,2},{4,5},{5,4},{6,7},{7,6},{8,9},{9,8},{10,11... | collective-permute-start | bytes 1966088 | tf_op jit(solution)/shard_map/ppermute | solution.py:910
  85.2 18.7 %collective-permute-start.14 = (bf16[2,256,512]{2,1,0:T(8,128)(2,1)S(1)}, bf16[2,256,512]{2,1,0:T(8,128)(2,1)S(1)}, u32[]{:S(2)}, u32[]{:S(2)}) collective-permute-start(bf16[2,256,512]{2,1,0:T(8,128)(2,1)S(1)} %get-tuple-element.172), channel_id=1, source_target_pairs={{0,16},{8,24},{16,0},{24,8},{1,17},{9,25},{17,1},{25,9},{2,18},{10... | collective-permute-start | bytes 1572872 | tf_op jit(solution)/shard_map/ppermute | solution.py:910
  86.7 17.3 %collective-permute-start.15 = (bf16[2,1,256,512]{3,2,0,1:T(8,128)(2,1)S(1)}, bf16[2,1,256,512]{3,2,0,1:T(8,128)(2,1)S(1)}, u32[]{:S(2)}, u32[]{:S(2)}) collective-permute-start(bf16[2,1,256,512]{3,2,0,1:T(8,128)(2,1)S(1)} %bitcast.62), channel_id=1, source_target_pairs={{0,8},{8,0},{16,24},{24,16},{1,9},{9,1},{17,25},{25,17},{2,10},{10... | collective-permute-start | bytes 1572872 | tf_op jit(solution)/shard_map/ppermute | solution.py:910
  103.9 2.7 %collective-permute-start.16 = (bf16[4,256,512]{2,1,0:T(8,128)(2,1)S(1)}, bf16[4,256,512]{2,1,0:T(8,128)(2,1)S(1)}, u32[]{:S(2)}, u32[]{:S(2)}) collective-permute-start(bf16[4,256,512]{2,1,0:T(8,128)(2,1)S(1)} %get-tuple-element.190), channel_id=1, source_target_pairs={{0,4},{4,0},{1,5},{5,1},{2,6},{6,2},{3,7},{7,3},{8,12},{12,8},{9,1... | collective-permute-start | bytes 3145736 | tf_op jit(solution)/shard_map/ppermute | solution.py:910
  104.0 4.1 %collective-permute-start.17 = (bf16[4,256,512]{2,1,0:T(8,128)(2,1)S(1)}, bf16[4,256,512]{2,1,0:T(8,128)(2,1)S(1)}, u32[]{:S(2)}, u32[]{:S(2)}) collective-permute-start(bf16[4,256,512]{2,1,0:T(8,128)(2,1)S(1)} %get-tuple-element.192), channel_id=1, source_target_pairs={{0,4},{4,0},{1,5},{5,1},{2,6},{6,2},{3,7},{7,3},{8,12},{12,8},{9,1... | collective-permute-start | bytes 3145736 | tf_op jit(solution)/shard_map/ppermute | solution.py:910
  104.5 19.7 %collective-permute-start.20 = (bf16[600,512]{1,0:T(8,128)(2,1)S(1)}, bf16[600,512]{1,0:T(8,128)(2,1)S(1)}, u32[]{:S(2)}, u32[]{:S(2)}) collective-permute-start(bf16[600,512]{1,0:T(8,128)(2,1)S(1)} %get-tuple-element.203), channel_id=1, source_target_pairs={{0,1},{1,0},{2,3},{3,2},{4,5},{5,4},{6,7},{7,6},{8,9},{9,8},{10,11... | collective-permute-start | bytes 1843208 | tf_op jit(solution)/shard_map/ppermute | solution.py:910
  108.7 14.5 %collective-permute-start.19 = (bf16[2,1,256,512]{3,2,0,1:T(8,128)(2,1)S(1)}, bf16[2,1,256,512]{3,2,0,1:T(8,128)(2,1)S(1)}, u32[]{:S(2)}, u32[]{:S(2)}) collective-permute-start(bf16[2,1,256,512]{3,2,0,1:T(8,128)(2,1)S(1)} %bitcast.63), channel_id=1, source_target_pairs={{0,8},{8,0},{16,24},{24,16},{1,9},{9,1},{17,25},{25,17},{2,10},{10... | collective-permute-start | bytes 1572872 | tf_op jit(solution)/shard_map/ppermute | solution.py:910
  110.0 13.7 %collective-permute-start.18 = (bf16[2,256,512]{2,1,0:T(8,128)(2,1)S(1)}, bf16[2,256,512]{2,1,0:T(8,128)(2,1)S(1)}, u32[]{:S(2)}, u32[]{:S(2)}) collective-permute-start(bf16[2,256,512]{2,1,0:T(8,128)(2,1)S(1)} %get-tuple-element.194), channel_id=1, source_target_pairs={{0,16},{8,24},{16,0},{24,8},{1,17},{9,25},{17,1},{25,9},{2,18},{10... | collective-permute-start | bytes 1572872 | tf_op jit(solution)/shard_map/ppermute | solution.py:910
  124.3 11.6 %collective-permute-start.24 = (bf16[256,2176]{1,0:T(8,128)(2,1)S(1)}, bf16[256,2176]{1,0:T(8,128)(2,1)S(1)}, u32[]{:S(2)}, u32[]{:S(2)}) collective-permute-start(bf16[256,2176]{1,0:T(8,128)(2,1)S(1)} %get-tuple-element.220), channel_id=1, source_target_pairs={{0,4},{4,0},{1,5},{5,1},{2,6},{6,2},{3,7},{7,3},{8,12},{12,8},{9,1... | collective-permute-start | bytes 3342344 | tf_op jit(solution)/shard_map/ppermute | solution.py:910
  124.3 12.0 %collective-permute-start.25 = (bf16[3,100,512]{2,1,0:T(8,128)(2,1)S(1)}, bf16[3,100,512]{2,1,0:T(8,128)(2,1)S(1)}, u32[]{:S(2)}, u32[]{:S(2)}) collective-permute-start(bf16[3,100,512]{2,1,0:T(8,128)(2,1)S(1)} %get-tuple-element.226), channel_id=1, source_target_pairs={{0,4},{4,0},{1,5},{5,1},{2,6},{6,2},{3,7},{7,3},{8,12},{12,8},{9,1... | collective-permute-start | bytes 921608 | tf_op jit(solution)/shard_map/ppermute | solution.py:910
  126.0 10.4 %collective-permute-start.26 = (bf16[3,100,512]{2,1,0:T(8,128)(2,1)S(1)}, bf16[3,100,512]{2,1,0:T(8,128)(2,1)S(1)}, u32[]{:S(2)}, u32[]{:S(2)}) collective-permute-start(bf16[3,100,512]{2,1,0:T(8,128)(2,1)S(1)} %get-tuple-element.229), channel_id=1, source_target_pairs={{0,4},{4,0},{1,5},{5,1},{2,6},{6,2},{3,7},{7,3},{8,12},{12,8},{9,1... | collective-permute-start | bytes 921608 | tf_op jit(solution)/shard_map/ppermute | solution.py:910
  126.2 8.7 %collective-permute-start.23 = (bf16[1,256,512]{2,1,0:T(8,128)(2,1)S(1)}, bf16[1,256,512]{2,1,0:T(8,128)(2,1)S(1)}, u32[]{:S(2)}, u32[]{:S(2)}) collective-permute-start(bf16[1,256,512]{2,1,0:T(8,128)(2,1)S(1)} %get-tuple-element.291), channel_id=1, source_target_pairs={{0,16},{8,24},{16,0},{24,8},{1,17},{9,25},{17,1},{25,9},{2,18},{10... | collective-permute-start | bytes 786440 | tf_op jit(solution)/shard_map/ppermute | solution.py:910
  127.2 8.7 %collective-permute-start.22 = (bf16[1,256,512]{2,1,0:T(8,128)(2,1)S(1)}, bf16[1,256,512]{2,1,0:T(8,128)(2,1)S(1)}, u32[]{:S(2)}, u32[]{:S(2)}) collective-permute-start(bf16[1,256,512]{2,1,0:T(8,128)(2,1)S(1)} %get-tuple-element.292), channel_id=1, source_target_pairs={{0,8},{8,0},{16,24},{24,16},{1,9},{9,1},{17,25},{25,17},{2,10},{10... | collective-permute-start | bytes 786440 | tf_op jit(solution)/shard_map/ppermute | solution.py:910
  134.9 9.2 %collective-permute-start.28 = (bf16[1,256,512]{2,1,0:T(8,128)(2,1)S(1)}, bf16[1,256,512]{2,1,0:T(8,128)(2,1)S(1)}, u32[]{:S(2)}, u32[]{:S(2)}) collective-permute-start(bf16[1,256,512]{2,1,0:T(8,128)(2,1)S(1)} %get-tuple-element.289), channel_id=1, source_target_pairs={{0,16},{8,24},{16,0},{24,8},{1,17},{9,25},{17,1},{25,9},{2,18},{10... | collective-permute-start | bytes 786440 | tf_op jit(solution)/shard_map/ppermute | solution.py:910
  136.4 25.4 %collective-permute-start.27 = (bf16[2,1,256,512]{3,2,1,0:T(8,128)(2,1)S(1)}, bf16[2,1,256,512]{3,2,1,0:T(8,128)(2,1)S(1)}, u32[]{:S(2)}, u32[]{:S(2)}) collective-permute-start(bf16[2,1,256,512]{3,2,1,0:T(8,128)(2,1)S(1)} %get-tuple-element.230), channel_id=1, source_target_pairs={{0,2},{1,3},{2,0},{3,1},{4,6},{5,7},{6,4},{7,5},{8,10},{9,11},{10,... | collective-permute-start | bytes 1572872 | tf_op jit(solution)/shard_map/ppermute | solution.py:910
  138.7 19.3 %collective-permute-start.29 = (bf16[64,2176]{1,0:T(8,128)(2,1)S(1)}, bf16[64,2176]{1,0:T(8,128)(2,1)S(1)}, u32[]{:S(2)}, u32[]{:S(2)}) collective-permute-start(bf16[64,2176]{1,0:T(8,128)(2,1)S(1)} %get-tuple-element.232), channel_id=1, source_target_pairs={{0,8},{8,0},{16,24},{24,16},{1,9},{9,1},{17,25},{25,17},{2,10},{10... | collective-permute-start | bytes 835592 | tf_op jit(solution)/shard_map/ppermute | solution.py:910
  139.9 18.1 %collective-permute-start.30 = (bf16[64,2176]{1,0:T(8,128)(2,1)S(1)}, bf16[64,2176]{1,0:T(8,128)(2,1)S(1)}, u32[]{:S(2)}, u32[]{:S(2)}) collective-permute-start(bf16[64,2176]{1,0:T(8,128)(2,1)S(1)} %get-tuple-element.233), channel_id=1, source_target_pairs={{0,16},{8,24},{16,0},{24,8},{1,17},{9,25},{17,1},{25,9},{2,18},{10... | collective-permute-start | bytes 835592 | tf_op jit(solution)/shard_map/ppermute | solution.py:910
  140.8 17.2 %collective-permute-start.31 = (bf16[64,2176]{1,0:T(8,128)(2,1)S(1)}, bf16[64,2176]{1,0:T(8,128)(2,1)S(1)}, u32[]{:S(2)}, u32[]{:S(2)}) collective-permute-start(bf16[64,2176]{1,0:T(8,128)(2,1)S(1)} %get-tuple-element.234), channel_id=1, source_target_pairs={{0,24},{8,16},{16,8},{24,0},{1,25},{9,17},{17,9},{25,1},{2,26},{10... | collective-permute-start | bytes 835592 | tf_op jit(solution)/shard_map/ppermute | solution.py:910
  144.1 13.9 %collective-permute-start.21 = (bf16[1,256,512]{2,1,0:T(8,128)(2,1)S(1)}, bf16[1,256,512]{2,1,0:T(8,128)(2,1)S(1)}, u32[]{:S(2)}, u32[]{:S(2)}) collective-permute-start(bf16[1,256,512]{2,1,0:T(8,128)(2,1)S(1)} %get-tuple-element.290), channel_id=1, source_target_pairs={{0,8},{8,0},{16,24},{24,16},{1,9},{9,1},{17,25},{25,17},{2,10},{10... | collective-permute-start | bytes 786440 | tf_op jit(solution)/shard_map/ppermute | solution.py:910
  162.2 10.6 %collective-permute-start.33 = (bf16[1,1,256,512]{3,2,1,0:T(8,128)(2,1)S(1)}, bf16[1,1,256,512]{3,2,1,0:T(8,128)(2,1)S(1)}, u32[]{:S(2)}, u32[]{:S(2)}) collective-permute-start(bf16[1,1,256,512]{3,2,1,0:T(8,128)(2,1)S(1)} %bitcast.56), channel_id=1, source_target_pairs={{0,16},{8,24},{16,0},{24,8},{1,17},{9,25},{17,1},{25,9},{2,18},{10... | collective-permute-start | bytes 786440 | tf_op jit(solution)/shard_map/ppermute | solution.py:910
  163.3 9.4 %collective-permute-start.32 = (bf16[1,256,512]{2,1,0:T(8,128)(2,1)S(1)}, bf16[1,256,512]{2,1,0:T(8,128)(2,1)S(1)}, u32[]{:S(2)}, u32[]{:S(2)}) collective-permute-start(bf16[1,256,512]{2,1,0:T(8,128)(2,1)S(1)} %get-tuple-element.249.refs_0_), channel_id=1, source_target_pairs={{0,8},{8,0},{16,24},{24,16},{1,9},{9,1},{17,25},{25,17},{2,10},{10... | collective-permute-start | bytes 786440 | tf_op jit(solution)/shard_map/ppermute | solution.py:910
  164.3 4.4 %collective-permute-start.34 = (bf16[16,2176]{1,0:T(8,128)(2,1)S(1)}, bf16[16,2176]{1,0:T(8,128)(2,1)S(1)}, u32[]{:S(2)}, u32[]{:S(2)}) collective-permute-start(bf16[16,2176]{1,0:T(8,128)(2,1)S(1)} %get-tuple-element.252), channel_id=1, source_target_pairs={{0,1},{1,0},{2,3},{3,2},{4,5},{5,4},{6,7},{7,6},{8,9},{9,8},{10,11... | collective-permute-start | bytes 208904 | tf_op jit(solution)/shard_map/ppermute | solution.py:910
  164.3 6.9 %collective-permute-start.35 = (bf16[16,2176]{1,0:T(8,128)(2,1)S(1)}, bf16[16,2176]{1,0:T(8,128)(2,1)S(1)}, u32[]{:S(2)}, u32[]{:S(2)}) collective-permute-start(bf16[16,2176]{1,0:T(8,128)(2,1)S(1)} %get-tuple-element.253), channel_id=1, source_target_pairs={{0,2},{1,3},{2,0},{3,1},{4,6},{5,7},{6,4},{7,5},{8,10},{9,11},{10,... | collective-permute-start | bytes 208904 | tf_op jit(solution)/shard_map/ppermute | solution.py:910
  166.6 6.1 %collective-permute-start.36 = (bf16[16,2176]{1,0:T(8,128)(2,1)S(1)}, bf16[16,2176]{1,0:T(8,128)(2,1)S(1)}, u32[]{:S(2)}, u32[]{:S(2)}) collective-permute-start(bf16[16,2176]{1,0:T(8,128)(2,1)S(1)} %get-tuple-element.254), channel_id=1, source_target_pairs={{0,3},{1,2},{2,1},{3,0},{4,7},{5,6},{6,5},{7,4},{8,11},{9,10},{10,... | collective-permute-start | bytes 208904 | tf_op jit(solution)/shard_map/ppermute | solution.py:910
  172.9 10.9 %collective-permute-start.37 = (bf16[2,256,512]{2,1,0:T(8,128)(2,1)S(1)}, bf16[2,256,512]{2,1,0:T(8,128)(2,1)S(1)}, u32[]{:S(2)}, u32[]{:S(2)}) collective-permute-start(bf16[2,256,512]{2,1,0:T(8,128)(2,1)S(1)} %get-tuple-element.255.refs_0_), channel_id=1, source_target_pairs={{0,16},{8,24},{16,0},{24,8},{1,17},{9,25},{17,1},{25,9},{2,18},{10... | collective-permute-start | bytes 1572872 | tf_op jit(solution)/shard_map/ppermute | solution.py:910
  174.0 10.6 %collective-permute-start.38 = (bf16[2,1,256,512]{3,2,1,0:T(8,128)(2,1)S(1)}, bf16[2,1,256,512]{3,2,1,0:T(8,128)(2,1)S(1)}, u32[]{:S(2)}, u32[]{:S(2)}) collective-permute-start(bf16[2,1,256,512]{3,2,1,0:T(8,128)(2,1)S(1)} %get-tuple-element.256.refs_2_), channel_id=1, source_target_pairs={{0,8},{8,0},{16,24},{24,16},{1,9},{9,1},{17,25},{25,17},{2,10},{10... | collective-permute-start | bytes 1572872 | tf_op jit(solution)/shard_map/ppermute | solution.py:910
  174.9 6.1 %collective-permute-start.41 = (bf16[16,2176]{1,0:T(8,128)(2,1)S(1)}, bf16[16,2176]{1,0:T(8,128)(2,1)S(1)}, u32[]{:S(2)}, u32[]{:S(2)}) collective-permute-start(bf16[16,2176]{1,0:T(8,128)(2,1)S(1)} %get-tuple-element.257.refs_4_), channel_id=1, source_target_pairs={{0,3},{1,2},{2,1},{3,0},{4,7},{5,6},{6,5},{7,4},{8,11},{9,10},{10,... | collective-permute-start | bytes 208904 | tf_op jit(solution)/shard_map/ppermute | solution.py:910
  177.0 5.5 %collective-permute-start.40 = (bf16[16,2176]{1,0:T(8,128)(2,1)S(1)}, bf16[16,2176]{1,0:T(8,128)(2,1)S(1)}, u32[]{:S(2)}, u32[]{:S(2)}) collective-permute-start(bf16[16,2176]{1,0:T(8,128)(2,1)S(1)} %get-tuple-element.257.refs_4_), channel_id=1, source_target_pairs={{0,2},{1,3},{2,0},{3,1},{4,6},{5,7},{6,4},{7,5},{8,10},{9,11},{10,... | collective-permute-start | bytes 208904 | tf_op jit(solution)/shard_map/ppermute | solution.py:910
  177.0 5.5 %collective-permute-start.39 = (bf16[16,2176]{1,0:T(8,128)(2,1)S(1)}, bf16[16,2176]{1,0:T(8,128)(2,1)S(1)}, u32[]{:S(2)}, u32[]{:S(2)}) collective-permute-start(bf16[16,2176]{1,0:T(8,128)(2,1)S(1)} %get-tuple-element.257.refs_4_), channel_id=1, source_target_pairs={{0,1},{1,0},{2,3},{3,2},{4,5},{5,4},{6,7},{7,6},{8,9},{9,8},{10,11... | collective-permute-start | bytes 208904 | tf_op jit(solution)/shard_map/ppermute | solution.py:910
  184.8 4.1 %collective-permute-start.43 = (bf16[4,256,512]{2,1,0:T(8,128)(2,1)S(1)}, bf16[4,256,512]{2,1,0:T(8,128)(2,1)S(1)}, u32[]{:S(2)}, u32[]{:S(2)}) collective-permute-start(bf16[4,256,512]{2,1,0:T(8,128)(2,1)S(1)} %bitcast.47), channel_id=1, source_target_pairs={{0,4},{4,0},{1,5},{5,1},{2,6},{6,2},{3,7},{7,3},{8,12},{12,8},{9,1... | collective-permute-start | bytes 3145736 | tf_op jit(solution)/shard_map/ppermute | solution.py:910
  184.9 4.1 %collective-permute-start.42 = (bf16[4,256,512]{2,1,0:T(8,128)(2,1)S(1)}, bf16[4,256,512]{2,1,0:T(8,128)(2,1)S(1)}, u32[]{:S(2)}, u32[]{:S(2)}) collective-permute-start(bf16[4,256,512]{2,1,0:T(8,128)(2,1)S(1)} %get-tuple-element.259.im_ref), channel_id=1, source_target_pairs={{0,4},{4,0},{1,5},{5,1},{2,6},{6,2},{3,7},{7,3},{8,12},{12,8},{9,1... | collective-permute-start | bytes 3145736 | tf_op jit(solution)/shard_map/ppermute | solution.py:910
  185.4 10.5 %collective-permute-start.46 = (bf16[64,2176]{1,0:T(8,128)(2,1)S(1)}, bf16[64,2176]{1,0:T(8,128)(2,1)S(1)}, u32[]{:S(2)}, u32[]{:S(2)}) collective-permute-start(bf16[64,2176]{1,0:T(8,128)(2,1)S(1)} %get-tuple-element.263.refs_0_), channel_id=1, source_target_pairs={{0,24},{8,16},{16,8},{24,0},{1,25},{9,17},{17,9},{25,1},{2,26},{10... | collective-permute-start | bytes 835592 | tf_op jit(solution)/shard_map/ppermute | solution.py:910
  186.7 14.1 %collective-permute-start.45 = (bf16[64,2176]{1,0:T(8,128)(2,1)S(1)}, bf16[64,2176]{1,0:T(8,128)(2,1)S(1)}, u32[]{:S(2)}, u32[]{:S(2)}) collective-permute-start(bf16[64,2176]{1,0:T(8,128)(2,1)S(1)} %get-tuple-element.263.refs_0_), channel_id=1, source_target_pairs={{0,16},{8,24},{16,0},{24,8},{1,17},{9,25},{17,1},{25,9},{2,18},{10... | collective-permute-start | bytes 835592 | tf_op jit(solution)/shard_map/ppermute | solution.py:910
  187.7 13.2 %collective-permute-start.44 = (bf16[64,2176]{1,0:T(8,128)(2,1)S(1)}, bf16[64,2176]{1,0:T(8,128)(2,1)S(1)}, u32[]{:S(2)}, u32[]{:S(2)}) collective-permute-start(bf16[64,2176]{1,0:T(8,128)(2,1)S(1)} %get-tuple-element.263.refs_0_), channel_id=1, source_target_pairs={{0,8},{8,0},{16,24},{24,16},{1,9},{9,1},{17,25},{25,17},{2,10},{10... | collective-permute-start | bytes 835592 | tf_op jit(solution)/shard_map/ppermute | solution.py:910
  201.0 2.8 %collective-permute-start.47 = (bf16[256,2176]{1,0:T(8,128)(2,1)S(1)}, bf16[256,2176]{1,0:T(8,128)(2,1)S(1)}, u32[]{:S(2)}, u32[]{:S(2)}) collective-permute-start(bf16[256,2176]{1,0:T(8,128)(2,1)S(1)} %merge.15.mine_ref), channel_id=1, source_target_pairs={{0,4},{4,0},{1,5},{5,1},{2,6},{6,2},{3,7},{7,3},{8,12},{12,8},{9,1... | collective-permute-start | bytes 3342344 | tf_op jit(solution)/shard_map/ppermute | solution.py:910
  (23 other events, 198.9 us)

commit v6 on v5

--- a/solution.py
+++ b/solution.py
@@ -692,45 +692,41 @@
     )(meta, *dins, ids, dy, mid, routed, wr, g2, mix, wout, probs, qkv, x, normed, wqkv, g1)
 
 
-def shared_kernel(meta_ref, mine_ref, recv_ref, gqkv_ref, gout_ref, small_ref, all_s):
-    upper, wide = mine_ref.shape
+def shared_kernel(meta_ref, half_ref, *refs):
+    gqkv_ref, gout_ref, small_ref = refs[-3:]
+    upper = half_ref.shape[0]
     width = 2 * upper
     part = width // SHARES
-    all_s[0:upper, :] = mine_ref[...]
-    all_s[upper:width, :] = recv_ref[...]
-
-    @pl.loop(0, SHARES)
+
+    @pl.loop(0, SHARES // 2)
     def _(i):
-        there = pl.multiple_of((i ^ meta_ref[2]) * part, part)
-        value = all_s[pl.ds(there, part), :].astype(F32)
+        there = pl.multiple_of((i ^ (meta_ref[2] % (SHARES // 2))) * part, part)
+        value = half_ref[pl.ds(there, part), :].astype(F32)
         at = pl.ds(pl.multiple_of(i * part, part), part)
         gqkv_ref[at, :] = value[:, : 3 * width]
         gout_ref[at, :] = value[:, 3 * width : 4 * width]
         small_ref[at, :] = value[:, 4 * width :]
 
 
-def finish_shared(meta, mine, recv):
-    upper, wide = mine.shape
+def finish_shared(meta, half, earlier=()):
+    upper, wide = half.shape
     width = 2 * upper
-    fix = lambda *s: pl.BlockSpec(s, lambda i, m: (0,) * len(s))
+    at = (lambda i, m: (1 - m[3], 0)) if earlier else (lambda i, m: (m[3], 0))
+    columns = (3 * width, width, wide - 4 * width)
     return pl.pallas_call(
         shared_kernel,
         grid_spec=pltpu.PrefetchScalarGridSpec(
             num_scalar_prefetch=1,
             grid=(1,),
-            in_specs=[fix(upper, wide), fix(upper, wide)],
-            out_specs=[fix(width, 3 * width), fix(width, width), fix(width, wide - 4 * width)],
-            scratch_shapes=[pltpu.VMEM((width, wide), BF16)],
+            in_specs=[pl.BlockSpec((upper, wide), lambda i, m: (0, 0))] + [pl.BlockSpec(memory_space=pl.ANY)] * len(earlier),
+            out_specs=[pl.BlockSpec((upper, c), at) for c in columns],
         ),
-        out_shape=[
-            jax.ShapeDtypeStruct((width, 3 * width), F32),
-            jax.ShapeDtypeStruct((width, width), F32),
-            jax.ShapeDtypeStruct((width, wide - 4 * width), F32),
-        ],
-        compiler_params=pltpu.CompilerParams(vmem_limit_bytes=16 << 20),
+        out_shape=[jax.ShapeDtypeStruct((width, c), F32) for c in columns],
+        input_output_aliases={2 + n: n for n in range(len(earlier))},
+        compiler_params=pltpu.CompilerParams(vmem_limit_bytes=12 << 20),
         cost_estimate=BRIEF,
         name="finish_shared",
-    )(meta, mine, recv)
+    )(meta, half, *earlier)
 
 
 def combine_kernel(meta_ref, mid_ref, a_ref, b_ref, own_ref, other_ref, s_ref):
@@ -1064,7 +1060,8 @@
     b = b.reshape(a.shape)
     grad_in, grad_back = finish_expert(meta, a, swap(a), b, swap(b))
     (shared,) = merge(([[after(shared, grad_in, grad_back), *spread([shared] * 3, "dp")]], 0, None))
-    grad_qkv, grad_out, small = finish_shared(meta, shared, swap(shared))
+    earlier = finish_shared(meta, shared)
+    grad_qkv, grad_out, small = finish_shared(meta, swap(shared), earlier)
     return (
         mixed,
         grad_tokens,

time: 209 us -> 208 us (level)
  waiting for transfers between devices: 60.2 us -> 58 us
    ppermute x48, waiting for transfers between devices: 60.2 us -> 58 us  [send(): return lax.ppermute(value, axis, pairs)]
    pallas_call x1 -> x2, Pallas kernels: 3.25 us -> 4.4 us  [finish_shared(): pl.pallas_call(shared_kernel, grid_spec=pltpu.PrefetchScalarGridSpec(num_...]
  transfers between devices with their start and end apart: 48 -> 48, of which waited for: 22 -> 22; matrix products, arithmetic and copies ran while one was open for 0% -> 0% of each run, Pallas kernels for 43% -> 45%
where the time goes in v6:
time: 208 us
  Pallas kernels  97.6 us (47%)
  waiting for transfers between devices  58 us (28%)
  starting transfers between devices  45.4 us (22%)
  local copies, waits for them, and re-layouts  3.83 us (2%)
    ppermute x48, waiting for transfers between devices, send(): return lax.ppermute(value, axis, pairs)  58 us
    ppermute x48, starting transfers between devices, send(): return lax.ppermute(value, axis, pairs)  45.4 us
    pallas_call x2, Pallas kernels, expert_steps(): pl.pallas_call(functools.partial(expert_steps_kernel, prev is not None, l...  20.5 us
    pallas_call x2, Pallas kernels, weight_grads(): pl.pallas_call(functools.partial(weight_kernel, n), grid=(steps,), in_spe...  17.1 us
    pallas_call x2, Pallas kernels, expert(): pl.pallas_call(functools.partial(expert_kernel, not first, local), grid_s...  17.1 us
    pallas_call x1, Pallas kernels, attend_back(): pl.pallas_call(back_kernel, grid_spec=pltpu.PrefetchScalarGridSpec(num_sc...  12.5 us
    pallas_call x1, Pallas kernels, attend(): pl.pallas_call(attend_kernel, grid_spec=pltpu.PrefetchScalarGridSpec(num_...  10.4 us
    pallas_call x8, Pallas kernels, merge(): pl.pallas_call(functools.partial(merge_kernel, plan), out_shape=shapes, c...  4.8 us
  transfers between devices with their start and end apart: 48, of which 22 were waited for; matrix products, arithmetic and copies ran while one was open for 0% of the time, Pallas kernels for 45%

profile of v6, /device:TPU:0, one launch (start us, length us, event | category | flops | bytes accessed | tf_op | source)
XLA Modules:
  0.0 207.7 jit_solution(7126437385329194578)
XLA Ops:
  0.8 1.6 pack_piece.1
  2.9 3.7 %collective-permute-start.6 = (bf16[4,256,256]{2,1,0:T(8,128)(2,1)S(1)}, bf16[4,256,256]{2,1,0:T(8,128)(2,1)}, u32[]{:S(2)}, u32[]{:S(2)}) collective-permute-start(bf16[4,256,256]{2,1,0:T(8,128)(2,1)S(1)} %pack_piece.1), channel_id=1, source_target_pairs={{0,2},{1,3},{2,0},{3,1},{4,6},{5,7},{6,4},{7,5},{8,10},{9,11},{10,... | collective-permute-start | bytes 1572872 | tf_op jit(solution)/shard_map/ppermute | solution.py:906
  6.8 1.6 collective-permute-start.4
  8.7 1.9 collective-permute-done.other_ref
  11.4 10.4 %attend.1 = (bf16[600,512]{1,0:T(8,128)(2,1)}, bf16[600,512]{1,0:T(8,128)(2,1)S(1)}, bf16[600,512]{1,0:T(8,128)(2,1)}, bf16[600,1536]{1,0:T(8,128)(2,1)}, bf16[3...) custom-call(s32[4]{0:T(128)S(1)} %add_add_fusion.1.meta_ref, ...), custom_call_target="tpu_custom_call" | custom-call | flops 1 | bytes 1 | tf_op jit(solution)/shard_map/attend/pallas_call | solution.py:117
  22.7 10.2 %expert_steps.2 = (bf16[600,2048]{1,0:T(8,128)(2,1)S(1)}, bf16[600,2048]{1,0:T(8,128)(2,1)S(1)}, bf16[600,512]{1,0:T(8,128)(2,1)S(1)}, bf16[600,512]{1,0:T(8,128)(2,1)}, bf16[640,512]{1,0:T(8,128)(2,1)}) custom-call(s32[4]{0:T(128)S(1)} %add_add_fusion.1.meta_ref, bf16[600,512]{1,0:T(8,128)(2,1)S(1)} %get-tuple-element.141.rows_ref.refs_0_.routed_ref, ...), custom_call_target="tpu_custom_call" | custom-call | flops 1 | bytes 1 | tf_op jit(solution)/shard_map/expert_steps/pallas_call | solution.py:448
  32.9 1.3 collective-permute-done.4.own_ref
  34.2 2.5 %collective-permute-start.9 = (bf16[4,256,256]{2,1,0:T(8,128)(2,1)}, bf16[4,256,256]{2,1,0:T(8,128)(2,1)S(1)}, u32[]{:S(2)}, u32[]{:S(2)}) collective-permute-start(bf16[4,256,256]{2,1,0:T(8,128)(2,1)} %collective-permute-done.6), channel_id=1, source_target_pairs={{0,24},{8,16},{16,8},{24,0},{1,25},{9,17},{17,9},{25,1},{2,26},{10... | collective-permute-start | bytes 1572872 | tf_op jit(solution)/shard_map/ppermute | solution.py:906
  38.6 8.8 %collective-permute-done.3.rows_ref.ids_ref.refs_1_ = bf16[624,512]{1,0:T(8,128)(2,1)S(1)} collective-permute-done((bf16[624,512]{1,0:T(8,128)(2,1)S(1)}, bf16[624,512]{1,0:T(8,128)(2,1)S(1)}, u32[]{:S(2)}, u32[]{:S(2)}) %collective-permute-start.3) | collective-permute-done | bytes 639008 | tf_op jit(solution)/shard_map/ppermute | solution.py:906
  47.3 10.3 %expert_steps.3 = (bf16[600,2048]{1,0:T(8,128)(2,1)S(1)}, bf16[600,2048]{1,0:T(8,128)(2,1)S(1)}, bf16[600,512]{1,0:T(8,128)(2,1)S(1)}, bf16[600,512]{1,0:T(8,128)(2,1)}, bf16[640,512]{1,0:T(8,128)(2,1)}) custom-call(s32[4]{0:T(128)S(1)} %add_add_fusion.1.meta_ref, bf16[624,512]{1,0:T(8,128)(2,1)S(1)} %collective-permute-done.3.rows_ref.ids_ref.refs_1_, ...), custom_call_target="tpu_custom_call" | custom-call | flops 1 | bytes 1 | tf_op jit(solution)/shard_map/expert_steps/pallas_call | solution.py:448
  57.7 3.2 %collective-permute-done.8 = bf16[4,256,256]{2,1,0:T(8,128)(2,1)S(1)} collective-permute-done((bf16[4,256,256]{2,1,0:T(8,128)(2,1)}, bf16[4,256,256]{2,1,0:T(8,128)(2,1)S(1)}, u32[]{:S(2)}, u32[]{:S(2)}) %collective-permute-start.8) | collective-permute-done | bytes 524320 | tf_op jit(solution)/shard_map/ppermute | solution.py:906
  61.1 1.3 pad_maximum_fusion.wi_ref
  62.5 9.2 %weight_grads.2 = (bf16[4,256,512]{2,1,0:T(8,128)(2,1)}, bf16[4,256,512]{2,1,0:T(8,128)(2,1)}, bf16[4,256,512]{2,1,0:T(8,128)(2,1)}, bf16[4,256,512]{2,1,0:T(8,128)(2,1)}) custom-call(bf16[600,512]{1,0:T(8,128)(2,1)S(1)} %get-tuple-element.141.rows_ref.refs_0_.routed_ref, bf16[624,512]{1,0:T(8,128)(2,1)S(1)} %collective-permute-done.3.rows_ref.ids_ref.refs_1_, ...), custom_call_target="tpu_custom_call" | custom-call | flops 1 | bytes 1 | tf_op jit(solution)/shard_map/weight_grads/pallas_call | solution.py:509
  73.4 8.5 %expert.2 = (bf16[600,2048]{1,0:T(8,128)(2,1)S(1)}, bf16[600,2048]{1,0:T(8,128)(2,1)S(1)}, bf16[600,512]{1,0:T(8,128)(2,1)S(1)}, bf16[600,512]{1,0:T(8,128)(2,1)S(1)}, bf16[640,512]{1,0:T(8,128)(2,1)S(1)}) custom-call(s32[4]{0:T(128)S(1)} %add_add_fusion.meta_ref, bf16[624,512]{1,0:T(8,128)(2,1)S(1)} %collective-permute-done.3.rows_ref.ids_ref.refs_1_, ...), custom_call_target="tpu_custom_call" | custom-call | flops 1 | bytes 1 | tf_op jit(solution)/shard_map/expert/pallas_call | solution.py:299
  82.8 2.4 %merge.8 = (bf16[2,256,512]{2,1,0:T(8,128)(2,1)S(1)}, bf16[2,256,512]{2,1,0:T(8,128)(2,1)S(1)}, bf16[2,1,256,512]{3,2,1,0:T(8,128)(2,1)S(1)}, bf16[2,1,256,512]{3,2,1,0:T(8,128)(2,1)S(1)}) custom-call(bf16[4,256,512]{2,1,0:T(8,128)(2,1)S(1)} %copy-done.11, bf16[4,256,512]{2,1,0:T(8,128)(2,1)} %collective-permute-done.11.refs_1_, ...), custom_call_target="tpu_custom_call" | custom-call | flops 1 | bytes 1 | tf_op jit(solution)/shard_map/merge/pallas_call | solution.py:885
  85.2 1.5 collective-permute-start.14
  87.5 8.5 %expert.3 = (bf16[600,2048]{1,0:T(8,128)(2,1)S(1)}, bf16[600,2048]{1,0:T(8,128)(2,1)S(1)}, bf16[600,512]{1,0:T(8,128)(2,1)S(1)}, bf16[600,512]{1,0:T(8,128)(2,1)S(1)}, bf16[640,512]{1,0:T(8,128)(2,1)S(1)}) custom-call(s32[4]{0:T(128)S(1)} %add_add_fusion.meta_ref, bf16[600,512]{1,0:T(8,128)(2,1)S(1)} %get-tuple-element.141.rows_ref.refs_0_.routed_ref, ...), custom_call_target="tpu_custom_call" | custom-call | flops 1 | bytes 1 | tf_op jit(solution)/shard_map/expert/pallas_call | solution.py:299
  96.1 7.8 %weight_grads.3 = (bf16[4,256,512]{2,1,0:T(8,128)(2,1)S(1)}, bf16[4,256,512]{2,1,0:T(8,128)(2,1)S(1)}, bf16[4,256,512]{2,1,0:T(8,128)(2,1)S(1)}, bf16[4,256,512]{2,1,0:T(8,128)(2,1)S(1)}) custom-call(bf16[600,512]{1,0:T(8,128)(2,1)S(1)} %get-tuple-element.141.rows_ref.refs_0_.routed_ref, ...), custom_call_target="tpu_custom_call" | custom-call | flops 1 | bytes 1 | tf_op jit(solution)/shard_map/weight_grads/pallas_call | solution.py:509
  104.5 1.2 collective-permute-start.20
  106.7 1.5 collective-permute-done.17
  108.7 1.3 collective-permute-start.19
  110.7 12.5 %attend_back.1 = (bf16[3,100,512]{2,1,0:T(8,128)(2,1)S(1)}, bf16[3,100,512]{2,1,0:T(8,128)(2,1)S(1)}, bf16[256,2176]{1,0:T(8,128)(2,1)S(1)}, bf16[256,2176]{1,0:T(8,128)(2,1)S(1)}) custom-call(s32[4]{0:T(128)S(1)} %add_add_fusion.1.meta_ref, bf16[640,512]{1,0:T(8,128)(2,1)S(1)} %get-tuple-element.208.din0_ref, ...), custom_call_target="tpu_custom_call" | custom-call | flops 1 | bytes 1 | tf_op jit(solution)/shard_map/attend_back/pallas_call | solution.py:658
  127.2 1.2 collective-permute-start.22
  128.4 6.5 %collective-permute-done.23.refs_3_ = bf16[1,256,512]{2,1,0:T(8,128)(2,1)S(1)} collective-permute-done((bf16[1,256,512]{2,1,0:T(8,128)(2,1)S(1)}, bf16[1,256,512]{2,1,0:T(8,128)(2,1)S(1)}, u32[]{:S(2)}, u32[]{:S(2)}) %collective-permute-start.23) | collective-permute-done | bytes 262176 | tf_op jit(solution)/shard_map/ppermute | solution.py:906
  136.4 2.3 %collective-permute-start.27 = (bf16[2,1,256,512]{3,2,1,0:T(8,128)(2,1)S(1)}, bf16[2,1,256,512]{3,2,1,0:T(8,128)(2,1)S(1)}, u32[]{:S(2)}, u32[]{:S(2)}) collective-permute-start(bf16[2,1,256,512]{3,2,1,0:T(8,128)(2,1)S(1)} %get-tuple-element.233), channel_id=1, source_target_pairs={{0,2},{1,3},{2,0},{3,1},{4,6},{5,7},{6,4},{7,5},{8,10},{9,11},{10,... | collective-permute-start | bytes 1572872 | tf_op jit(solution)/shard_map/ppermute | solution.py:906
  138.7 1.1 collective-permute-start.29
  140.8 1.4 collective-permute-start.31
  142.2 1.9 collective-permute-done.28.refs_4_
  145.1 2.8 %place.1 = (bf16[6,100,512]{2,1,0:T(8,128)(2,1)}, bf16[6,100,512]{2,1,0:T(8,128)(2,1)}) custom-call(s32[4]{0:T(128)S(1)} %add_add_fusion.1.meta_ref, bf16[3,100,512]{2,1,0:T(8,128)(2,1)S(1)} %get-tuple-element.244.a_own_ref, bf16[3,100,512]{2,1,0:T(8,128)(2,1)S(1)} %collective-permute-done.26.a_recv_ref, ...), custom_call_target="tpu_custom_call" | custom-call | flops 1 | bytes 1 | tf_op jit(solution)/shard_map/place/pallas_call | solution.py:771
  147.9 10.1 %collective-permute-done.21.refs_1_ = bf16[1,256,512]{2,1,0:T(8,128)(2,1)S(1)} collective-permute-done((bf16[1,256,512]{2,1,0:T(8,128)(2,1)S(1)}, bf16[1,256,512]{2,1,0:T(8,128)(2,1)S(1)}, u32[]{:S(2)}, u32[]{:S(2)}) %collective-permute-start.21) | collective-permute-done | bytes 262176 | tf_op jit(solution)/shard_map/ppermute | solution.py:906
  158.0 3.8 %collective-permute-done.27.refs_2_.refs_5_ = bf16[2,1,256,512]{3,2,1,0:T(8,128)(2,1)S(1)} collective-permute-done((bf16[2,1,256,512]{3,2,1,0:T(8,128)(2,1)S(1)}, bf16[2,1,256,512]{3,2,1,0:T(8,128)(2,1)S(1)}, u32[]{:S(2)}, u32[]{:S(2)}) %collective-permute-start.27) | collective-permute-done | bytes 524320 | tf_op jit(solution)/shard_map/ppermute | solution.py:906
  162.2 1.1 collective-permute-start.33
  164.3 2.2 %collective-permute-start.35 = (bf16[16,2176]{1,0:T(8,128)(2,1)S(1)}, bf16[16,2176]{1,0:T(8,128)(2,1)S(1)}, u32[]{:S(2)}, u32[]{:S(2)}) collective-permute-start(bf16[16,2176]{1,0:T(8,128)(2,1)S(1)} %get-tuple-element.256), channel_id=1, source_target_pairs={{0,2},{1,3},{2,0},{3,1},{4,6},{5,7},{6,4},{7,5},{8,10},{9,11},{10,... | collective-permute-start | bytes 208904 | tf_op jit(solution)/shard_map/ppermute | solution.py:906
  166.6 2.1 %collective-permute-start.36 = (bf16[16,2176]{1,0:T(8,128)(2,1)S(1)}, bf16[16,2176]{1,0:T(8,128)(2,1)S(1)}, u32[]{:S(2)}, u32[]{:S(2)}) collective-permute-start(bf16[16,2176]{1,0:T(8,128)(2,1)S(1)} %get-tuple-element.257), channel_id=1, source_target_pairs={{0,3},{1,2},{2,1},{3,0},{4,7},{5,6},{6,5},{7,4},{8,11},{9,10},{10,... | collective-permute-start | bytes 208904 | tf_op jit(solution)/shard_map/ppermute | solution.py:906
  168.7 2.5 %collective-permute-done.35.refs_6_ = bf16[16,2176]{1,0:T(8,128)(2,1)S(1)} collective-permute-done((bf16[16,2176]{1,0:T(8,128)(2,1)S(1)}, bf16[16,2176]{1,0:T(8,128)(2,1)S(1)}, u32[]{:S(2)}, u32[]{:S(2)}) %collective-permute-start.35) | collective-permute-done | bytes 69664 | tf_op jit(solution)/shard_map/ppermute | solution.py:906
  171.2 1.5 collective-permute-done.36.refs_7_
  174.9 2.1 %collective-permute-start.41 = (bf16[16,2176]{1,0:T(8,128)(2,1)S(1)}, bf16[16,2176]{1,0:T(8,128)(2,1)S(1)}, u32[]{:S(2)}, u32[]{:S(2)}) collective-permute-start(bf16[16,2176]{1,0:T(8,128)(2,1)S(1)} %get-tuple-element.260.refs_4_), channel_id=1, source_target_pairs={{0,3},{1,2},{2,1},{3,0},{4,7},{5,6},{6,5},{7,4},{8,11},{9,10},{10,... | collective-permute-start | bytes 208904 | tf_op jit(solution)/shard_map/ppermute | solution.py:906
  177.0 2.3 %collective-permute-start.39 = (bf16[16,2176]{1,0:T(8,128)(2,1)S(1)}, bf16[16,2176]{1,0:T(8,128)(2,1)S(1)}, u32[]{:S(2)}, u32[]{:S(2)}) collective-permute-start(bf16[16,2176]{1,0:T(8,128)(2,1)S(1)} %get-tuple-element.260.refs_4_), channel_id=1, source_target_pairs={{0,1},{1,0},{2,3},{3,2},{4,5},{5,4},{6,7},{7,6},{8,9},{9,8},{10,11... | collective-permute-start | bytes 208904 | tf_op jit(solution)/shard_map/ppermute | solution.py:906
  179.3 1.7 collective-permute-done.41.refs_7_
  181.0 1.5 collective-permute-done.40.refs_6_
  182.5 1.3 collective-permute-done.37.refs_1_
  185.3 1.4 collective-permute-start.46
  187.7 1.1 collective-permute-start.44
  189.0 4.4 %finish_expert.1 = (f32[1,512,2048]{2,1,0:T(8,128)}, f32[1,2048,512]{2,1,0:T(8,128)}) custom-call(s32[4]{0:T(128)S(1)} %add_add_fusion.1.meta_ref, bf16[4,256,512]{2,1,0:T(8,128)(2,1)S(1)} %get-tuple-element.262.im_ref, bf16[4,256,512]{2,1,0:T(8,128)(2,1)S(1)} %collective-permute-done.42.ir_ref, bf16[4,256,512]{2,1,0:T(8,128)(2,1)S(1)} %bitcast.48, ...), custom_call_target="tpu_custom_call" | custom-call | flops 1 | bytes 1 | tf_op jit(solution)/shard_map/finish_expert/pallas_call | solution.py:542
  193.4 2.4 %collective-permute-done.46.refs_3_ = bf16[64,2176]{1,0:T(8,128)(2,1)S(1)} collective-permute-done((bf16[64,2176]{1,0:T(8,128)(2,1)S(1)}, bf16[64,2176]{1,0:T(8,128)(2,1)S(1)}, u32[]{:S(2)}, u32[]{:S(2)}) %collective-permute-start.46) | collective-permute-done | bytes 278560 | tf_op jit(solution)/shard_map/ppermute | solution.py:906
  195.8 5.1 %collective-permute-done.45.refs_2_ = bf16[64,2176]{1,0:T(8,128)(2,1)S(1)} collective-permute-done((bf16[64,2176]{1,0:T(8,128)(2,1)S(1)}, bf16[64,2176]{1,0:T(8,128)(2,1)S(1)}, u32[]{:S(2)}, u32[]{:S(2)}) %collective-permute-start.45) | collective-permute-done | bytes 278560 | tf_op jit(solution)/shard_map/ppermute | solution.py:906
  201.1 2.2 %finish_shared.2 = (f32[512,1536]{1,0:T(8,128)}, f32[512,512]{1,0:T(8,128)}, f32[512,128]{1,0:T(8,128)S(1)}) custom-call(s32[4]{0:T(128)S(1)} %add_add_fusion.1.meta_ref, bf16[256,2176]{1,0:T(8,128)(2,1)S(1)} %merge.15.half_ref), custom_call_target="tpu_custom_call" | custom-call | flops 1 | bytes 1 | tf_op jit(solution)/shard_map/finish_shared/pallas_call | solution.py:716
  203.8 2.2 %finish_shared.3 = (f32[512,1536]{1,0:T(8,128)}, f32[512,512]{1,0:T(8,128)}, f32[512,128]{1,0:T(8,128)S(1)}) custom-call(s32[4]{0:T(128)S(1)} %add_add_fusion.1.meta_ref, bf16[256,2176]{1,0:T(8,128)(2,1)S(1)} %collective-permute-done.47.half_ref, f32[512,1536]{1,0:T(8,128)} %get-tuple-element.267.refs_0_, ...), custom_call_target="tpu_custom_call", output_to_operand_aliasing={{0}: (2, {}), {1}: (3, {}), {2}: (4, {})} | custom-call | flops 1 | bytes 1 | tf_op jit(solution)/shard_map/finish_shared/pallas_call | solution.py:716
  (137 shorter events, 27.0 us)
Async XLA Ops:
  2.4 6.0 %collective-permute-start.2 = (s32[6,100]{1,0:T(8,128)S(1)}, s32[6,100]{1,0:T(8,128)S(1)}, u32[]{:S(2)}, u32[]{:S(2)}) collective-permute-start(s32[6,100]{1,0:T(8,128)S(1)} %bitcast.69), channel_id=1, source_target_pairs={{0,4},{4,0},{1,5},{5,1},{2,6},{6,2},{3,7},{7,3},{8,12},{12,8},{9,1... | collective-permute-start | bytes 7208 | tf_op jit(solution)/shard_map/ppermute | solution.py:906
  2.9 31.3 %collective-permute-start.6 = (bf16[4,256,256]{2,1,0:T(8,128)(2,1)S(1)}, bf16[4,256,256]{2,1,0:T(8,128)(2,1)}, u32[]{:S(2)}, u32[]{:S(2)}) collective-permute-start(bf16[4,256,256]{2,1,0:T(8,128)(2,1)S(1)} %pack_piece.1), channel_id=1, source_target_pairs={{0,2},{1,3},{2,0},{3,1},{4,6},{5,7},{6,4},{7,5},{8,10},{9,11},{10,... | collective-permute-start | bytes 1572872 | tf_op jit(solution)/shard_map/ppermute | solution.py:906
  6.6 4.0 %collective-permute-start.1 = (bf16[6,100,512]{2,1,0:T(8,128)(2,1)}, bf16[6,100,512]{2,1,0:T(8,128)(2,1)S(1)}, u32[]{:S(2)}, u32[]{:S(2)}) collective-permute-start(bf16[6,100,512]{2,1,0:T(8,128)(2,1)} %dyown_ref.1), channel_id=1, source_target_pairs={{0,4},{4,0},{1,5},{5,1},{2,6},{6,2},{3,7},{7,3},{8,12},{12,8},{9,1... | collective-permute-start | bytes 1843208 | tf_op jit(solution)/shard_map/ppermute | solution.py:906
  6.8 27.5 %collective-permute-start.4 = (bf16[6,100,512]{2,1,0:T(8,128)(2,1)}, bf16[6,100,512]{2,1,0:T(8,128)(2,1)S(1)}, u32[]{:S(2)}, u32[]{:S(2)}) collective-permute-start(bf16[6,100,512]{2,1,0:T(8,128)(2,1)} %dyown_ref.1), channel_id=1, source_target_pairs={{0,1},{1,0},{2,3},{3,2},{4,5},{5,4},{6,7},{7,6},{8,9},{9,8},{10,11... | collective-permute-start | bytes 1843208 | tf_op jit(solution)/shard_map/ppermute | solution.py:906
  8.3 2.2 %collective-permute-start = (bf16[6,100,512]{2,1,0:T(8,128)(2,1)S(1)}, bf16[6,100,512]{2,1,0:T(8,128)(2,1)}, u32[]{:S(2)}, u32[]{:S(2)}) collective-permute-start(bf16[6,100,512]{2,1,0:T(8,128)(2,1)S(1)} %copy-done.19), channel_id=1, source_target_pairs={{0,4},{4,0},{1,5},{5,1},{2,6},{6,2},{3,7},{7,3},{8,12},{12,8},{9,1... | collective-permute-start | bytes 1843208 | tf_op jit(solution)/shard_map/ppermute | solution.py:906
  21.9 25.5 %collective-permute-start.3 = (bf16[624,512]{1,0:T(8,128)(2,1)S(1)}, bf16[624,512]{1,0:T(8,128)(2,1)S(1)}, u32[]{:S(2)}, u32[]{:S(2)}) collective-permute-start(bf16[624,512]{1,0:T(8,128)(2,1)S(1)} %pad_maximum_fusion.1), channel_id=1, source_target_pairs={{0,1},{1,0},{2,3},{3,2},{4,5},{5,4},{6,7},{7,6},{8,9},{9,8},{10,11... | collective-permute-start | bytes 1916936 | tf_op jit(solution)/shard_map/ppermute | solution.py:906
  34.2 3.5 %collective-permute-start.5 = (bf16[6,100,512]{2,1,0:T(8,128)(2,1)S(1)}, bf16[6,100,512]{2,1,0:T(8,128)(2,1)S(1)}, u32[]{:S(2)}, u32[]{:S(2)}) collective-permute-start(bf16[6,100,512]{2,1,0:T(8,128)(2,1)S(1)} %collective-permute-done.4.own_ref), channel_id=1, source_target_pairs={{0,4},{4,0},{1,5},{5,1},{2,6},{6,2},{3,7},{7,3},{8,12},{12,8},{9,1... | collective-permute-start | bytes 1843208 | tf_op jit(solution)/shard_map/ppermute | solution.py:906
  34.2 23.4 %collective-permute-start.9 = (bf16[4,256,256]{2,1,0:T(8,128)(2,1)}, bf16[4,256,256]{2,1,0:T(8,128)(2,1)S(1)}, u32[]{:S(2)}, u32[]{:S(2)}) collective-permute-start(bf16[4,256,256]{2,1,0:T(8,128)(2,1)} %collective-permute-done.6), channel_id=1, source_target_pairs={{0,24},{8,16},{16,8},{24,0},{1,25},{9,17},{17,9},{25,1},{2,26},{10... | collective-permute-start | bytes 1572872 | tf_op jit(solution)/shard_map/ppermute | solution.py:906
  36.7 24.2 %collective-permute-start.8 = (bf16[4,256,256]{2,1,0:T(8,128)(2,1)}, bf16[4,256,256]{2,1,0:T(8,128)(2,1)S(1)}, u32[]{:S(2)}, u32[]{:S(2)}) collective-permute-start(bf16[4,256,256]{2,1,0:T(8,128)(2,1)} %collective-permute-done.6), channel_id=1, source_target_pairs={{0,16},{8,24},{16,0},{24,8},{1,17},{9,25},{17,1},{25,9},{2,18},{10... | collective-permute-start | bytes 1572872 | tf_op jit(solution)/shard_map/ppermute | solution.py:906
  37.3 23.8 %collective-permute-start.7 = (bf16[4,256,256]{2,1,0:T(8,128)(2,1)}, bf16[4,256,256]{2,1,0:T(8,128)(2,1)S(1)}, u32[]{:S(2)}, u32[]{:S(2)}) collective-permute-start(bf16[4,256,256]{2,1,0:T(8,128)(2,1)} %collective-permute-done.6), channel_id=1, source_target_pairs={{0,8},{8,0},{16,24},{24,16},{1,9},{9,1},{17,25},{25,17},{2,10},{10... | collective-permute-start | bytes 1572872 | tf_op jit(solution)/shard_map/ppermute | solution.py:906
  62.4 9.9 %collective-permute-start.10 = (bf16[4,4,256,256]{3,2,1,0:T(8,128)(2,1)S(1)}, bf16[4,4,256,256]{3,2,1,0:T(8,128)(2,1)}, u32[]{:S(2)}, u32[]{:S(2)}) collective-permute-start(bf16[4,4,256,256]{3,2,1,0:T(8,128)(2,1)S(1)} %pad_maximum_fusion.wi_ref), channel_id=1, source_target_pairs={{0,4},{4,0},{1,5},{5,1},{2,6},{6,2},{3,7},{7,3},{8,12},{12,8},{9,1... | collective-permute-start | bytes 6291464 | tf_op jit(solution)/shard_map/ppermute | solution.py:906
  71.7 11.1 %collective-permute-start.11 = (bf16[4,256,512]{2,1,0:T(8,128)(2,1)}, bf16[4,256,512]{2,1,0:T(8,128)(2,1)}, u32[]{:S(2)}, u32[]{:S(2)}) collective-permute-start(bf16[4,256,512]{2,1,0:T(8,128)(2,1)} %get-tuple-element.166), channel_id=1, source_target_pairs={{0,4},{4,0},{1,5},{5,1},{2,6},{6,2},{3,7},{7,3},{8,12},{12,8},{9,1... | collective-permute-start | bytes 3145736 | tf_op jit(solution)/shard_map/ppermute | solution.py:906
  72.2 10.6 %collective-permute-start.12 = (bf16[4,256,512]{2,1,0:T(8,128)(2,1)}, bf16[4,256,512]{2,1,0:T(8,128)(2,1)}, u32[]{:S(2)}, u32[]{:S(2)}) collective-permute-start(bf16[4,256,512]{2,1,0:T(8,128)(2,1)} %get-tuple-element.168), channel_id=1, source_target_pairs={{0,4},{4,0},{1,5},{5,1},{2,6},{6,2},{3,7},{7,3},{8,12},{12,8},{9,1... | collective-permute-start | bytes 3145736 | tf_op jit(solution)/shard_map/ppermute | solution.py:906
  81.9 22.0 %collective-permute-start.13 = (bf16[640,512]{1,0:T(8,128)(2,1)S(1)}, bf16[640,512]{1,0:T(8,128)(2,1)S(1)}, u32[]{:S(2)}, u32[]{:S(2)}) collective-permute-start(bf16[640,512]{1,0:T(8,128)(2,1)S(1)} %get-tuple-element.174), channel_id=1, source_target_pairs={{0,1},{1,0},{2,3},{3,2},{4,5},{5,4},{6,7},{7,6},{8,9},{9,8},{10,11... | collective-permute-start | bytes 1966088 | tf_op jit(solution)/shard_map/ppermute | solution.py:906
  85.2 18.7 %collective-permute-start.14 = (bf16[2,256,512]{2,1,0:T(8,128)(2,1)S(1)}, bf16[2,256,512]{2,1,0:T(8,128)(2,1)S(1)}, u32[]{:S(2)}, u32[]{:S(2)}) collective-permute-start(bf16[2,256,512]{2,1,0:T(8,128)(2,1)S(1)} %get-tuple-element.175), channel_id=1, source_target_pairs={{0,16},{8,24},{16,0},{24,8},{1,17},{9,25},{17,1},{25,9},{2,18},{10... | collective-permute-start | bytes 1572872 | tf_op jit(solution)/shard_map/ppermute | solution.py:906
  86.6 17.3 %collective-permute-start.15 = (bf16[2,1,256,512]{3,2,0,1:T(8,128)(2,1)S(1)}, bf16[2,1,256,512]{3,2,0,1:T(8,128)(2,1)S(1)}, u32[]{:S(2)}, u32[]{:S(2)}) collective-permute-start(bf16[2,1,256,512]{3,2,0,1:T(8,128)(2,1)S(1)} %bitcast.62), channel_id=1, source_target_pairs={{0,8},{8,0},{16,24},{24,16},{1,9},{9,1},{17,25},{25,17},{2,10},{10... | collective-permute-start | bytes 1572872 | tf_op jit(solution)/shard_map/ppermute | solution.py:906
  103.9 2.7 %collective-permute-start.16 = (bf16[4,256,512]{2,1,0:T(8,128)(2,1)S(1)}, bf16[4,256,512]{2,1,0:T(8,128)(2,1)S(1)}, u32[]{:S(2)}, u32[]{:S(2)}) collective-permute-start(bf16[4,256,512]{2,1,0:T(8,128)(2,1)S(1)} %get-tuple-element.193), channel_id=1, source_target_pairs={{0,4},{4,0},{1,5},{5,1},{2,6},{6,2},{3,7},{7,3},{8,12},{12,8},{9,1... | collective-permute-start | bytes 3145736 | tf_op jit(solution)/shard_map/ppermute | solution.py:906
  104.0 4.1 %collective-permute-start.17 = (bf16[4,256,512]{2,1,0:T(8,128)(2,1)S(1)}, bf16[4,256,512]{2,1,0:T(8,128)(2,1)S(1)}, u32[]{:S(2)}, u32[]{:S(2)}) collective-permute-start(bf16[4,256,512]{2,1,0:T(8,128)(2,1)S(1)} %get-tuple-element.195), channel_id=1, source_target_pairs={{0,4},{4,0},{1,5},{5,1},{2,6},{6,2},{3,7},{7,3},{8,12},{12,8},{9,1... | collective-permute-start | bytes 3145736 | tf_op jit(solution)/shard_map/ppermute | solution.py:906
  104.5 19.7 %collective-permute-start.20 = (bf16[600,512]{1,0:T(8,128)(2,1)S(1)}, bf16[600,512]{1,0:T(8,128)(2,1)S(1)}, u32[]{:S(2)}, u32[]{:S(2)}) collective-permute-start(bf16[600,512]{1,0:T(8,128)(2,1)S(1)} %get-tuple-element.206), channel_id=1, source_target_pairs={{0,1},{1,0},{2,3},{3,2},{4,5},{5,4},{6,7},{7,6},{8,9},{9,8},{10,11... | collective-permute-start | bytes 1843208 | tf_op jit(solution)/shard_map/ppermute | solution.py:906
  108.7 14.5 %collective-permute-start.19 = (bf16[2,1,256,512]{3,2,0,1:T(8,128)(2,1)S(1)}, bf16[2,1,256,512]{3,2,0,1:T(8,128)(2,1)S(1)}, u32[]{:S(2)}, u32[]{:S(2)}) collective-permute-start(bf16[2,1,256,512]{3,2,0,1:T(8,128)(2,1)S(1)} %bitcast.63), channel_id=1, source_target_pairs={{0,8},{8,0},{16,24},{24,16},{1,9},{9,1},{17,25},{25,17},{2,10},{10... | collective-permute-start | bytes 1572872 | tf_op jit(solution)/shard_map/ppermute | solution.py:906
  110.0 13.7 %collective-permute-start.18 = (bf16[2,256,512]{2,1,0:T(8,128)(2,1)S(1)}, bf16[2,256,512]{2,1,0:T(8,128)(2,1)S(1)}, u32[]{:S(2)}, u32[]{:S(2)}) collective-permute-start(bf16[2,256,512]{2,1,0:T(8,128)(2,1)S(1)} %get-tuple-element.197), channel_id=1, source_target_pairs={{0,16},{8,24},{16,0},{24,8},{1,17},{9,25},{17,1},{25,9},{2,18},{10... | collective-permute-start | bytes 1572872 | tf_op jit(solution)/shard_map/ppermute | solution.py:906
  124.3 11.6 %collective-permute-start.24 = (bf16[256,2176]{1,0:T(8,128)(2,1)S(1)}, bf16[256,2176]{1,0:T(8,128)(2,1)S(1)}, u32[]{:S(2)}, u32[]{:S(2)}) collective-permute-start(bf16[256,2176]{1,0:T(8,128)(2,1)S(1)} %get-tuple-element.223), channel_id=1, source_target_pairs={{0,4},{4,0},{1,5},{5,1},{2,6},{6,2},{3,7},{7,3},{8,12},{12,8},{9,1... | collective-permute-start | bytes 3342344 | tf_op jit(solution)/shard_map/ppermute | solution.py:906
  124.3 12.0 %collective-permute-start.25 = (bf16[3,100,512]{2,1,0:T(8,128)(2,1)S(1)}, bf16[3,100,512]{2,1,0:T(8,128)(2,1)S(1)}, u32[]{:S(2)}, u32[]{:S(2)}) collective-permute-start(bf16[3,100,512]{2,1,0:T(8,128)(2,1)S(1)} %get-tuple-element.229), channel_id=1, source_target_pairs={{0,4},{4,0},{1,5},{5,1},{2,6},{6,2},{3,7},{7,3},{8,12},{12,8},{9,1... | collective-permute-start | bytes 921608 | tf_op jit(solution)/shard_map/ppermute | solution.py:906
  126.0 10.4 %collective-permute-start.26 = (bf16[3,100,512]{2,1,0:T(8,128)(2,1)S(1)}, bf16[3,100,512]{2,1,0:T(8,128)(2,1)S(1)}, u32[]{:S(2)}, u32[]{:S(2)}) collective-permute-start(bf16[3,100,512]{2,1,0:T(8,128)(2,1)S(1)} %get-tuple-element.232), channel_id=1, source_target_pairs={{0,4},{4,0},{1,5},{5,1},{2,6},{6,2},{3,7},{7,3},{8,12},{12,8},{9,1... | collective-permute-start | bytes 921608 | tf_op jit(solution)/shard_map/ppermute | solution.py:906
  126.2 8.7 %collective-permute-start.23 = (bf16[1,256,512]{2,1,0:T(8,128)(2,1)S(1)}, bf16[1,256,512]{2,1,0:T(8,128)(2,1)S(1)}, u32[]{:S(2)}, u32[]{:S(2)}) collective-permute-start(bf16[1,256,512]{2,1,0:T(8,128)(2,1)S(1)} %get-tuple-element.297), channel_id=1, source_target_pairs={{0,16},{8,24},{16,0},{24,8},{1,17},{9,25},{17,1},{25,9},{2,18},{10... | collective-permute-start | bytes 786440 | tf_op jit(solution)/shard_map/ppermute | solution.py:906
  127.2 8.7 %collective-permute-start.22 = (bf16[1,256,512]{2,1,0:T(8,128)(2,1)S(1)}, bf16[1,256,512]{2,1,0:T(8,128)(2,1)S(1)}, u32[]{:S(2)}, u32[]{:S(2)}) collective-permute-start(bf16[1,256,512]{2,1,0:T(8,128)(2,1)S(1)} %get-tuple-element.298), channel_id=1, source_target_pairs={{0,8},{8,0},{16,24},{24,16},{1,9},{9,1},{17,25},{25,17},{2,10},{10... | collective-permute-start | bytes 786440 | tf_op jit(solution)/shard_map/ppermute | solution.py:906
  134.9 9.2 %collective-permute-start.28 = (bf16[1,256,512]{2,1,0:T(8,128)(2,1)S(1)}, bf16[1,256,512]{2,1,0:T(8,128)(2,1)S(1)}, u32[]{:S(2)}, u32[]{:S(2)}) collective-permute-start(bf16[1,256,512]{2,1,0:T(8,128)(2,1)S(1)} %get-tuple-element.295), channel_id=1, source_target_pairs={{0,16},{8,24},{16,0},{24,8},{1,17},{9,25},{17,1},{25,9},{2,18},{10... | collective-permute-start | bytes 786440 | tf_op jit(solution)/shard_map/ppermute | solution.py:906
  136.4 25.4 %collective-permute-start.27 = (bf16[2,1,256,512]{3,2,1,0:T(8,128)(2,1)S(1)}, bf16[2,1,256,512]{3,2,1,0:T(8,128)(2,1)S(1)}, u32[]{:S(2)}, u32[]{:S(2)}) collective-permute-start(bf16[2,1,256,512]{3,2,1,0:T(8,128)(2,1)S(1)} %get-tuple-element.233), channel_id=1, source_target_pairs={{0,2},{1,3},{2,0},{3,1},{4,6},{5,7},{6,4},{7,5},{8,10},{9,11},{10,... | collective-permute-start | bytes 1572872 | tf_op jit(solution)/shard_map/ppermute | solution.py:906
  138.7 19.3 %collective-permute-start.29 = (bf16[64,2176]{1,0:T(8,128)(2,1)S(1)}, bf16[64,2176]{1,0:T(8,128)(2,1)S(1)}, u32[]{:S(2)}, u32[]{:S(2)}) collective-permute-start(bf16[64,2176]{1,0:T(8,128)(2,1)S(1)} %get-tuple-element.235), channel_id=1, source_target_pairs={{0,8},{8,0},{16,24},{24,16},{1,9},{9,1},{17,25},{25,17},{2,10},{10... | collective-permute-start | bytes 835592 | tf_op jit(solution)/shard_map/ppermute | solution.py:906
  139.8 18.2 %collective-permute-start.30 = (bf16[64,2176]{1,0:T(8,128)(2,1)S(1)}, bf16[64,2176]{1,0:T(8,128)(2,1)S(1)}, u32[]{:S(2)}, u32[]{:S(2)}) collective-permute-start(bf16[64,2176]{1,0:T(8,128)(2,1)S(1)} %get-tuple-element.236), channel_id=1, source_target_pairs={{0,16},{8,24},{16,0},{24,8},{1,17},{9,25},{17,1},{25,9},{2,18},{10... | collective-permute-start | bytes 835592 | tf_op jit(solution)/shard_map/ppermute | solution.py:906
  140.8 17.2 %collective-permute-start.31 = (bf16[64,2176]{1,0:T(8,128)(2,1)S(1)}, bf16[64,2176]{1,0:T(8,128)(2,1)S(1)}, u32[]{:S(2)}, u32[]{:S(2)}) collective-permute-start(bf16[64,2176]{1,0:T(8,128)(2,1)S(1)} %get-tuple-element.237), channel_id=1, source_target_pairs={{0,24},{8,16},{16,8},{24,0},{1,25},{9,17},{17,9},{25,1},{2,26},{10... | collective-permute-start | bytes 835592 | tf_op jit(solution)/shard_map/ppermute | solution.py:906
  144.1 13.9 %collective-permute-start.21 = (bf16[1,256,512]{2,1,0:T(8,128)(2,1)S(1)}, bf16[1,256,512]{2,1,0:T(8,128)(2,1)S(1)}, u32[]{:S(2)}, u32[]{:S(2)}) collective-permute-start(bf16[1,256,512]{2,1,0:T(8,128)(2,1)S(1)} %get-tuple-element.296), channel_id=1, source_target_pairs={{0,8},{8,0},{16,24},{24,16},{1,9},{9,1},{17,25},{25,17},{2,10},{10... | collective-permute-start | bytes 786440 | tf_op jit(solution)/shard_map/ppermute | solution.py:906
  162.2 10.6 %collective-permute-start.33 = (bf16[1,1,256,512]{3,2,1,0:T(8,128)(2,1)S(1)}, bf16[1,1,256,512]{3,2,1,0:T(8,128)(2,1)S(1)}, u32[]{:S(2)}, u32[]{:S(2)}) collective-permute-start(bf16[1,1,256,512]{3,2,1,0:T(8,128)(2,1)S(1)} %bitcast.56), channel_id=1, source_target_pairs={{0,16},{8,24},{16,0},{24,8},{1,17},{9,25},{17,1},{25,9},{2,18},{10... | collective-permute-start | bytes 786440 | tf_op jit(solution)/shard_map/ppermute | solution.py:906
  163.3 9.4 %collective-permute-start.32 = (bf16[1,256,512]{2,1,0:T(8,128)(2,1)S(1)}, bf16[1,256,512]{2,1,0:T(8,128)(2,1)S(1)}, u32[]{:S(2)}, u32[]{:S(2)}) collective-permute-start(bf16[1,256,512]{2,1,0:T(8,128)(2,1)S(1)} %get-tuple-element.252.refs_0_), channel_id=1, source_target_pairs={{0,8},{8,0},{16,24},{24,16},{1,9},{9,1},{17,25},{25,17},{2,10},{10... | collective-permute-start | bytes 786440 | tf_op jit(solution)/shard_map/ppermute | solution.py:906
  164.3 4.4 %collective-permute-start.34 = (bf16[16,2176]{1,0:T(8,128)(2,1)S(1)}, bf16[16,2176]{1,0:T(8,128)(2,1)S(1)}, u32[]{:S(2)}, u32[]{:S(2)}) collective-permute-start(bf16[16,2176]{1,0:T(8,128)(2,1)S(1)} %get-tuple-element.255), channel_id=1, source_target_pairs={{0,1},{1,0},{2,3},{3,2},{4,5},{5,4},{6,7},{7,6},{8,9},{9,8},{10,11... | collective-permute-start | bytes 208904 | tf_op jit(solution)/shard_map/ppermute | solution.py:906
  164.3 6.9 %collective-permute-start.35 = (bf16[16,2176]{1,0:T(8,128)(2,1)S(1)}, bf16[16,2176]{1,0:T(8,128)(2,1)S(1)}, u32[]{:S(2)}, u32[]{:S(2)}) collective-permute-start(bf16[16,2176]{1,0:T(8,128)(2,1)S(1)} %get-tuple-element.256), channel_id=1, source_target_pairs={{0,2},{1,3},{2,0},{3,1},{4,6},{5,7},{6,4},{7,5},{8,10},{9,11},{10,... | collective-permute-start | bytes 208904 | tf_op jit(solution)/shard_map/ppermute | solution.py:906
  166.6 6.1 %collective-permute-start.36 = (bf16[16,2176]{1,0:T(8,128)(2,1)S(1)}, bf16[16,2176]{1,0:T(8,128)(2,1)S(1)}, u32[]{:S(2)}, u32[]{:S(2)}) collective-permute-start(bf16[16,2176]{1,0:T(8,128)(2,1)S(1)} %get-tuple-element.257), channel_id=1, source_target_pairs={{0,3},{1,2},{2,1},{3,0},{4,7},{5,6},{6,5},{7,4},{8,11},{9,10},{10,... | collective-permute-start | bytes 208904 | tf_op jit(solution)/shard_map/ppermute | solution.py:906
  172.9 10.9 %collective-permute-start.37 = (bf16[2,256,512]{2,1,0:T(8,128)(2,1)S(1)}, bf16[2,256,512]{2,1,0:T(8,128)(2,1)S(1)}, u32[]{:S(2)}, u32[]{:S(2)}) collective-permute-start(bf16[2,256,512]{2,1,0:T(8,128)(2,1)S(1)} %get-tuple-element.258.refs_0_), channel_id=1, source_target_pairs={{0,16},{8,24},{16,0},{24,8},{1,17},{9,25},{17,1},{25,9},{2,18},{10... | collective-permute-start | bytes 1572872 | tf_op jit(solution)/shard_map/ppermute | solution.py:906
  174.0 10.5 %collective-permute-start.38 = (bf16[2,1,256,512]{3,2,1,0:T(8,128)(2,1)S(1)}, bf16[2,1,256,512]{3,2,1,0:T(8,128)(2,1)S(1)}, u32[]{:S(2)}, u32[]{:S(2)}) collective-permute-start(bf16[2,1,256,512]{3,2,1,0:T(8,128)(2,1)S(1)} %get-tuple-element.259.refs_2_), channel_id=1, source_target_pairs={{0,8},{8,0},{16,24},{24,16},{1,9},{9,1},{17,25},{25,17},{2,10},{10... | collective-permute-start | bytes 1572872 | tf_op jit(solution)/shard_map/ppermute | solution.py:906
  174.9 6.1 %collective-permute-start.41 = (bf16[16,2176]{1,0:T(8,128)(2,1)S(1)}, bf16[16,2176]{1,0:T(8,128)(2,1)S(1)}, u32[]{:S(2)}, u32[]{:S(2)}) collective-permute-start(bf16[16,2176]{1,0:T(8,128)(2,1)S(1)} %get-tuple-element.260.refs_4_), channel_id=1, source_target_pairs={{0,3},{1,2},{2,1},{3,0},{4,7},{5,6},{6,5},{7,4},{8,11},{9,10},{10,... | collective-permute-start | bytes 208904 | tf_op jit(solution)/shard_map/ppermute | solution.py:906
  177.0 5.5 %collective-permute-start.40 = (bf16[16,2176]{1,0:T(8,128)(2,1)S(1)}, bf16[16,2176]{1,0:T(8,128)(2,1)S(1)}, u32[]{:S(2)}, u32[]{:S(2)}) collective-permute-start(bf16[16,2176]{1,0:T(8,128)(2,1)S(1)} %get-tuple-element.260.refs_4_), channel_id=1, source_target_pairs={{0,2},{1,3},{2,0},{3,1},{4,6},{5,7},{6,4},{7,5},{8,10},{9,11},{10,... | collective-permute-start | bytes 208904 | tf_op jit(solution)/shard_map/ppermute | solution.py:906
  177.0 5.5 %collective-permute-start.39 = (bf16[16,2176]{1,0:T(8,128)(2,1)S(1)}, bf16[16,2176]{1,0:T(8,128)(2,1)S(1)}, u32[]{:S(2)}, u32[]{:S(2)}) collective-permute-start(bf16[16,2176]{1,0:T(8,128)(2,1)S(1)} %get-tuple-element.260.refs_4_), channel_id=1, source_target_pairs={{0,1},{1,0},{2,3},{3,2},{4,5},{5,4},{6,7},{7,6},{8,9},{9,8},{10,11... | collective-permute-start | bytes 208904 | tf_op jit(solution)/shard_map/ppermute | solution.py:906
  184.8 4.1 %collective-permute-start.43 = (bf16[4,256,512]{2,1,0:T(8,128)(2,1)S(1)}, bf16[4,256,512]{2,1,0:T(8,128)(2,1)S(1)}, u32[]{:S(2)}, u32[]{:S(2)}) collective-permute-start(bf16[4,256,512]{2,1,0:T(8,128)(2,1)S(1)} %bitcast.47), channel_id=1, source_target_pairs={{0,4},{4,0},{1,5},{5,1},{2,6},{6,2},{3,7},{7,3},{8,12},{12,8},{9,1... | collective-permute-start | bytes 3145736 | tf_op jit(solution)/shard_map/ppermute | solution.py:906
  184.8 4.1 %collective-permute-start.42 = (bf16[4,256,512]{2,1,0:T(8,128)(2,1)S(1)}, bf16[4,256,512]{2,1,0:T(8,128)(2,1)S(1)}, u32[]{:S(2)}, u32[]{:S(2)}) collective-permute-start(bf16[4,256,512]{2,1,0:T(8,128)(2,1)S(1)} %get-tuple-element.262.im_ref), channel_id=1, source_target_pairs={{0,4},{4,0},{1,5},{5,1},{2,6},{6,2},{3,7},{7,3},{8,12},{12,8},{9,1... | collective-permute-start | bytes 3145736 | tf_op jit(solution)/shard_map/ppermute | solution.py:906
  185.3 10.5 %collective-permute-start.46 = (bf16[64,2176]{1,0:T(8,128)(2,1)S(1)}, bf16[64,2176]{1,0:T(8,128)(2,1)S(1)}, u32[]{:S(2)}, u32[]{:S(2)}) collective-permute-start(bf16[64,2176]{1,0:T(8,128)(2,1)S(1)} %get-tuple-element.266.refs_0_), channel_id=1, source_target_pairs={{0,24},{8,16},{16,8},{24,0},{1,25},{9,17},{17,9},{25,1},{2,26},{10... | collective-permute-start | bytes 835592 | tf_op jit(solution)/shard_map/ppermute | solution.py:906
  186.7 14.1 %collective-permute-start.45 = (bf16[64,2176]{1,0:T(8,128)(2,1)S(1)}, bf16[64,2176]{1,0:T(8,128)(2,1)S(1)}, u32[]{:S(2)}, u32[]{:S(2)}) collective-permute-start(bf16[64,2176]{1,0:T(8,128)(2,1)S(1)} %get-tuple-element.266.refs_0_), channel_id=1, source_target_pairs={{0,16},{8,24},{16,0},{24,8},{1,17},{9,25},{17,1},{25,9},{2,18},{10... | collective-permute-start | bytes 835592 | tf_op jit(solution)/shard_map/ppermute | solution.py:906
  187.7 13.2 %collective-permute-start.44 = (bf16[64,2176]{1,0:T(8,128)(2,1)S(1)}, bf16[64,2176]{1,0:T(8,128)(2,1)S(1)}, u32[]{:S(2)}, u32[]{:S(2)}) collective-permute-start(bf16[64,2176]{1,0:T(8,128)(2,1)S(1)} %get-tuple-element.266.refs_0_), channel_id=1, source_target_pairs={{0,8},{8,0},{16,24},{24,16},{1,9},{9,1},{17,25},{25,17},{2,10},{10... | collective-permute-start | bytes 835592 | tf_op jit(solution)/shard_map/ppermute | solution.py:906
  201.0 2.8 %collective-permute-start.47 = (bf16[256,2176]{1,0:T(8,128)(2,1)S(1)}, bf16[256,2176]{1,0:T(8,128)(2,1)S(1)}, u32[]{:S(2)}, u32[]{:S(2)}) collective-permute-start(bf16[256,2176]{1,0:T(8,128)(2,1)S(1)} %merge.15.half_ref), channel_id=1, source_target_pairs={{0,4},{4,0},{1,5},{5,1},{2,6},{6,2},{3,7},{7,3},{8,12},{12,8},{9,1... | collective-permute-start | bytes 3342344 | tf_op jit(solution)/shard_map/ppermute | solution.py:906
  (23 other events, 198.9 us)

commit v7 on v6

--- a/solution.py
+++ b/solution.py
@@ -997,7 +997,8 @@
     y_way, x_way = ("dp", xor(2)), ("dp", xor(1))
     own_two = expert(meta_pair, routed, dy, ids, wr_own, pair, own_one[3:])
     grads = weight_grads([routed, far_rows], *zip(own_two[:3], far_two[:3]))
-    din_far, a_got, b_got, *grads = tie(far(far_din), send(one[1], *y_way), send(one[3], *x_way), *grads)
+    din_far, a_got, b_got, give_a = tie(far(far_din), send(one[1], *y_way), send(one[3], *x_way), grads[1])
+    grads = [grads[0], give_a, *grads[2:]]
     a_one, b_one = [one[0], a_got], [one[2], b_got]
 
     two = tie(*across(*grads))

time: 208 us -> 208 us (level)
  no operation moved by 1% of the time
where the time goes in v7:
time: 208 us
  Pallas kernels  97.6 us (47%)
  waiting for transfers between devices  58 us (28%)
  starting transfers between devices  45.5 us (22%)
  local copies, waits for them, and re-layouts  3.83 us (2%)
    ppermute x48, waiting for transfers between devices, send(): return lax.ppermute(value, axis, pairs)  58 us
    ppermute x48, starting transfers between devices, send(): return lax.ppermute(value, axis, pairs)  45.5 us
    pallas_call x2, Pallas kernels, expert_steps(): pl.pallas_call(functools.partial(expert_steps_kernel, prev is not None, l...  20.5 us
    pallas_call x2, Pallas kernels, weight_grads(): pl.pallas_call(functools.partial(weight_kernel, n), grid=(steps,), in_spe...  17.1 us
    pallas_call x2, Pallas kernels, expert(): pl.pallas_call(functools.partial(expert_kernel, not first, local), grid_s...  17.1 us
    pallas_call x1, Pallas kernels, attend_back(): pl.pallas_call(back_kernel, grid_spec=pltpu.PrefetchScalarGridSpec(num_sc...  12.5 us
    pallas_call x1, Pallas kernels, attend(): pl.pallas_call(attend_kernel, grid_spec=pltpu.PrefetchScalarGridSpec(num_...  10.4 us
    pallas_call x8, Pallas kernels, merge(): pl.pallas_call(functools.partial(merge_kernel, plan), out_shape=shapes, c...  4.8 us
  transfers between devices with their start and end apart: 48, of which 22 were waited for; matrix products, arithmetic and copies ran while one was open for 0% of the time, Pallas kernels for 45%

profile of v7, /device:TPU:0, one launch (start us, length us, event | category | flops | bytes accessed | tf_op | source)
XLA Modules:
  0.0 207.6 jit_solution(3937912770015276127)
XLA Ops:
  0.8 1.6 pack_piece.1
  2.9 3.7 %collective-permute-start.6 = (bf16[4,256,256]{2,1,0:T(8,128)(2,1)S(1)}, bf16[4,256,256]{2,1,0:T(8,128)(2,1)}, u32[]{:S(2)}, u32[]{:S(2)}) collective-permute-start(bf16[4,256,256]{2,1,0:T(8,128)(2,1)S(1)} %pack_piece.1), channel_id=1, source_target_pairs={{0,2},{1,3},{2,0},{3,1},{4,6},{5,7},{6,4},{7,5},{8,10},{9,11},{10,... | collective-permute-start | bytes 1572872 | tf_op jit(solution)/shard_map/ppermute | solution.py:906
  6.8 1.6 collective-permute-start.4
  8.7 1.9 collective-permute-done.other_ref
  11.4 10.4 %attend.1 = (bf16[600,512]{1,0:T(8,128)(2,1)}, bf16[600,512]{1,0:T(8,128)(2,1)S(1)}, bf16[600,512]{1,0:T(8,128)(2,1)}, bf16[600,1536]{1,0:T(8,128)(2,1)}, bf16[3...) custom-call(s32[4]{0:T(128)S(1)} %add_add_fusion.1.meta_ref, ...), custom_call_target="tpu_custom_call" | custom-call | flops 1 | bytes 1 | tf_op jit(solution)/shard_map/attend/pallas_call | solution.py:117
  22.7 10.2 %expert_steps.2 = (bf16[600,2048]{1,0:T(8,128)(2,1)S(1)}, bf16[600,2048]{1,0:T(8,128)(2,1)S(1)}, bf16[600,512]{1,0:T(8,128)(2,1)S(1)}, bf16[600,512]{1,0:T(8,128)(2,1)}, bf16[640,512]{1,0:T(8,128)(2,1)}) custom-call(s32[4]{0:T(128)S(1)} %add_add_fusion.1.meta_ref, bf16[600,512]{1,0:T(8,128)(2,1)S(1)} %get-tuple-element.138.rows_ref.refs_0_.routed_ref, ...), custom_call_target="tpu_custom_call" | custom-call | flops 1 | bytes 1 | tf_op jit(solution)/shard_map/expert_steps/pallas_call | solution.py:448
  32.9 1.3 collective-permute-done.4.own_ref
  34.2 2.5 %collective-permute-start.9 = (bf16[4,256,256]{2,1,0:T(8,128)(2,1)}, bf16[4,256,256]{2,1,0:T(8,128)(2,1)S(1)}, u32[]{:S(2)}, u32[]{:S(2)}) collective-permute-start(bf16[4,256,256]{2,1,0:T(8,128)(2,1)} %collective-permute-done.6), channel_id=1, source_target_pairs={{0,24},{8,16},{16,8},{24,0},{1,25},{9,17},{17,9},{25,1},{2,26},{10... | collective-permute-start | bytes 1572872 | tf_op jit(solution)/shard_map/ppermute | solution.py:906
  38.6 8.8 %collective-permute-done.3.rows_ref.ids_ref.refs_1_ = bf16[624,512]{1,0:T(8,128)(2,1)S(1)} collective-permute-done((bf16[624,512]{1,0:T(8,128)(2,1)S(1)}, bf16[624,512]{1,0:T(8,128)(2,1)S(1)}, u32[]{:S(2)}, u32[]{:S(2)}) %collective-permute-start.3) | collective-permute-done | bytes 639008 | tf_op jit(solution)/shard_map/ppermute | solution.py:906
  47.3 10.3 %expert_steps.3 = (bf16[600,2048]{1,0:T(8,128)(2,1)S(1)}, bf16[600,2048]{1,0:T(8,128)(2,1)S(1)}, bf16[600,512]{1,0:T(8,128)(2,1)S(1)}, bf16[600,512]{1,0:T(8,128)(2,1)}, bf16[640,512]{1,0:T(8,128)(2,1)}) custom-call(s32[4]{0:T(128)S(1)} %add_add_fusion.1.meta_ref, bf16[624,512]{1,0:T(8,128)(2,1)S(1)} %collective-permute-done.3.rows_ref.ids_ref.refs_1_, ...), custom_call_target="tpu_custom_call" | custom-call | flops 1 | bytes 1 | tf_op jit(solution)/shard_map/expert_steps/pallas_call | solution.py:448
  57.7 3.2 %collective-permute-done.8 = bf16[4,256,256]{2,1,0:T(8,128)(2,1)S(1)} collective-permute-done((bf16[4,256,256]{2,1,0:T(8,128)(2,1)}, bf16[4,256,256]{2,1,0:T(8,128)(2,1)S(1)}, u32[]{:S(2)}, u32[]{:S(2)}) %collective-permute-start.8) | collective-permute-done | bytes 524320 | tf_op jit(solution)/shard_map/ppermute | solution.py:906
  61.1 1.3 pad_maximum_fusion.wi_ref
  62.5 9.2 %weight_grads.2 = (bf16[4,256,512]{2,1,0:T(8,128)(2,1)}, bf16[4,256,512]{2,1,0:T(8,128)(2,1)}, bf16[4,256,512]{2,1,0:T(8,128)(2,1)}, bf16[4,256,512]{2,1,0:T(8,128)(2,1)}) custom-call(bf16[600,512]{1,0:T(8,128)(2,1)S(1)} %get-tuple-element.138.rows_ref.refs_0_.routed_ref, bf16[624,512]{1,0:T(8,128)(2,1)S(1)} %collective-permute-done.3.rows_ref.ids_ref.refs_1_, ...), custom_call_target="tpu_custom_call" | custom-call | flops 1 | bytes 1 | tf_op jit(solution)/shard_map/weight_grads/pallas_call | solution.py:509
  73.4 8.5 %expert.2 = (bf16[600,2048]{1,0:T(8,128)(2,1)S(1)}, bf16[600,2048]{1,0:T(8,128)(2,1)S(1)}, bf16[600,512]{1,0:T(8,128)(2,1)S(1)}, bf16[600,512]{1,0:T(8,128)(2,1)S(1)}, bf16[640,512]{1,0:T(8,128)(2,1)S(1)}) custom-call(s32[4]{0:T(128)S(1)} %add_add_fusion.meta_ref, bf16[624,512]{1,0:T(8,128)(2,1)S(1)} %collective-permute-done.3.rows_ref.ids_ref.refs_1_, ...), custom_call_target="tpu_custom_call" | custom-call | flops 1 | bytes 1 | tf_op jit(solution)/shard_map/expert/pallas_call | solution.py:299
  82.8 2.4 %merge.8 = (bf16[2,256,512]{2,1,0:T(8,128)(2,1)S(1)}, bf16[2,256,512]{2,1,0:T(8,128)(2,1)S(1)}, bf16[2,1,256,512]{3,2,1,0:T(8,128)(2,1)S(1)}, bf16[2,1,256,512]{3,2,1,0:T(8,128)(2,1)S(1)}) custom-call(bf16[4,256,512]{2,1,0:T(8,128)(2,1)S(1)} %copy-done.11, bf16[4,256,512]{2,1,0:T(8,128)(2,1)} %collective-permute-done.11.refs_1_, ...), custom_call_target="tpu_custom_call" | custom-call | flops 1 | bytes 1 | tf_op jit(solution)/shard_map/merge/pallas_call | solution.py:885
  85.2 1.5 collective-permute-start.14
  87.5 8.5 %expert.3 = (bf16[600,2048]{1,0:T(8,128)(2,1)S(1)}, bf16[600,2048]{1,0:T(8,128)(2,1)S(1)}, bf16[600,512]{1,0:T(8,128)(2,1)S(1)}, bf16[600,512]{1,0:T(8,128)(2,1)S(1)}, bf16[640,512]{1,0:T(8,128)(2,1)S(1)}) custom-call(s32[4]{0:T(128)S(1)} %add_add_fusion.meta_ref, bf16[600,512]{1,0:T(8,128)(2,1)S(1)} %get-tuple-element.138.rows_ref.refs_0_.routed_ref, ...), custom_call_target="tpu_custom_call" | custom-call | flops 1 | bytes 1 | tf_op jit(solution)/shard_map/expert/pallas_call | solution.py:299
  96.1 7.8 %weight_grads.3 = (bf16[4,256,512]{2,1,0:T(8,128)(2,1)S(1)}, bf16[4,256,512]{2,1,0:T(8,128)(2,1)S(1)}, bf16[4,256,512]{2,1,0:T(8,128)(2,1)S(1)}, bf16[4,256,512]{2,1,0:T(8,128)(2,1)S(1)}) custom-call(bf16[600,512]{1,0:T(8,128)(2,1)S(1)} %get-tuple-element.138.rows_ref.refs_0_.routed_ref, ...), custom_call_target="tpu_custom_call" | custom-call | flops 1 | bytes 1 | tf_op jit(solution)/shard_map/weight_grads/pallas_call | solution.py:509
  104.6 1.2 collective-permute-start.20
  106.6 1.5 collective-permute-done.16.refs_1_
  108.7 1.3 collective-permute-start.19
  110.6 12.5 %attend_back.1 = (bf16[3,100,512]{2,1,0:T(8,128)(2,1)S(1)}, bf16[3,100,512]{2,1,0:T(8,128)(2,1)S(1)}, bf16[256,2176]{1,0:T(8,128)(2,1)S(1)}, bf16[256,2176]{1,0:T(8,128)(2,1)S(1)}) custom-call(s32[4]{0:T(128)S(1)} %add_add_fusion.1.meta_ref, bf16[640,512]{1,0:T(8,128)(2,1)S(1)} %get-tuple-element.202.din0_ref, ...), custom_call_target="tpu_custom_call" | custom-call | flops 1 | bytes 1 | tf_op jit(solution)/shard_map/attend_back/pallas_call | solution.py:658
  127.1 1.2 collective-permute-start.22
  128.3 6.5 %collective-permute-done.23.refs_3_ = bf16[1,256,512]{2,1,0:T(8,128)(2,1)S(1)} collective-permute-done((bf16[1,256,512]{2,1,0:T(8,128)(2,1)S(1)}, bf16[1,256,512]{2,1,0:T(8,128)(2,1)S(1)}, u32[]{:S(2)}, u32[]{:S(2)}) %collective-permute-start.23) | collective-permute-done | bytes 262176 | tf_op jit(solution)/shard_map/ppermute | solution.py:906
  136.3 2.3 %collective-permute-start.27 = (bf16[2,1,256,512]{3,2,1,0:T(8,128)(2,1)S(1)}, bf16[2,1,256,512]{3,2,1,0:T(8,128)(2,1)S(1)}, u32[]{:S(2)}, u32[]{:S(2)}) collective-permute-start(bf16[2,1,256,512]{3,2,1,0:T(8,128)(2,1)S(1)} %get-tuple-element.227), channel_id=1, source_target_pairs={{0,2},{1,3},{2,0},{3,1},{4,6},{5,7},{6,4},{7,5},{8,10},{9,11},{10,... | collective-permute-start | bytes 1572872 | tf_op jit(solution)/shard_map/ppermute | solution.py:906
  138.7 1.2 collective-permute-start.29
  140.8 1.4 collective-permute-start.31
  142.1 1.9 collective-permute-done.28.refs_4_
  145.1 2.8 %place.1 = (bf16[6,100,512]{2,1,0:T(8,128)(2,1)}, bf16[6,100,512]{2,1,0:T(8,128)(2,1)}) custom-call(s32[4]{0:T(128)S(1)} %add_add_fusion.1.meta_ref, bf16[3,100,512]{2,1,0:T(8,128)(2,1)S(1)} %get-tuple-element.238.a_own_ref, bf16[3,100,512]{2,1,0:T(8,128)(2,1)S(1)} %collective-permute-done.26.a_recv_ref, ...), custom_call_target="tpu_custom_call" | custom-call | flops 1 | bytes 1 | tf_op jit(solution)/shard_map/place/pallas_call | solution.py:771
  147.8 10.1 %collective-permute-done.21.refs_1_ = bf16[1,256,512]{2,1,0:T(8,128)(2,1)S(1)} collective-permute-done((bf16[1,256,512]{2,1,0:T(8,128)(2,1)S(1)}, bf16[1,256,512]{2,1,0:T(8,128)(2,1)S(1)}, u32[]{:S(2)}, u32[]{:S(2)}) %collective-permute-start.21) | collective-permute-done | bytes 262176 | tf_op jit(solution)/shard_map/ppermute | solution.py:906
  158.0 3.8 %collective-permute-done.27.refs_2_.refs_5_ = bf16[2,1,256,512]{3,2,1,0:T(8,128)(2,1)S(1)} collective-permute-done((bf16[2,1,256,512]{3,2,1,0:T(8,128)(2,1)S(1)}, bf16[2,1,256,512]{3,2,1,0:T(8,128)(2,1)S(1)}, u32[]{:S(2)}, u32[]{:S(2)}) %collective-permute-start.27) | collective-permute-done | bytes 524320 | tf_op jit(solution)/shard_map/ppermute | solution.py:906
  162.1 1.1 collective-permute-start.33
  164.3 2.2 %collective-permute-start.35 = (bf16[16,2176]{1,0:T(8,128)(2,1)S(1)}, bf16[16,2176]{1,0:T(8,128)(2,1)S(1)}, u32[]{:S(2)}, u32[]{:S(2)}) collective-permute-start(bf16[16,2176]{1,0:T(8,128)(2,1)S(1)} %get-tuple-element.250), channel_id=1, source_target_pairs={{0,2},{1,3},{2,0},{3,1},{4,6},{5,7},{6,4},{7,5},{8,10},{9,11},{10,... | collective-permute-start | bytes 208904 | tf_op jit(solution)/shard_map/ppermute | solution.py:906
  166.5 2.1 %collective-permute-start.36 = (bf16[16,2176]{1,0:T(8,128)(2,1)S(1)}, bf16[16,2176]{1,0:T(8,128)(2,1)S(1)}, u32[]{:S(2)}, u32[]{:S(2)}) collective-permute-start(bf16[16,2176]{1,0:T(8,128)(2,1)S(1)} %get-tuple-element.251), channel_id=1, source_target_pairs={{0,3},{1,2},{2,1},{3,0},{4,7},{5,6},{6,5},{7,4},{8,11},{9,10},{10,... | collective-permute-start | bytes 208904 | tf_op jit(solution)/shard_map/ppermute | solution.py:906
  168.7 2.5 %collective-permute-done.35.refs_6_ = bf16[16,2176]{1,0:T(8,128)(2,1)S(1)} collective-permute-done((bf16[16,2176]{1,0:T(8,128)(2,1)S(1)}, bf16[16,2176]{1,0:T(8,128)(2,1)S(1)}, u32[]{:S(2)}, u32[]{:S(2)}) %collective-permute-start.35) | collective-permute-done | bytes 69664 | tf_op jit(solution)/shard_map/ppermute | solution.py:906
  171.2 1.5 collective-permute-done.36.refs_7_
  174.9 2.1 %collective-permute-start.41 = (bf16[16,2176]{1,0:T(8,128)(2,1)S(1)}, bf16[16,2176]{1,0:T(8,128)(2,1)S(1)}, u32[]{:S(2)}, u32[]{:S(2)}) collective-permute-start(bf16[16,2176]{1,0:T(8,128)(2,1)S(1)} %get-tuple-element.254.refs_4_), channel_id=1, source_target_pairs={{0,3},{1,2},{2,1},{3,0},{4,7},{5,6},{6,5},{7,4},{8,11},{9,10},{10,... | collective-permute-start | bytes 208904 | tf_op jit(solution)/shard_map/ppermute | solution.py:906
  177.0 2.3 %collective-permute-start.39 = (bf16[16,2176]{1,0:T(8,128)(2,1)S(1)}, bf16[16,2176]{1,0:T(8,128)(2,1)S(1)}, u32[]{:S(2)}, u32[]{:S(2)}) collective-permute-start(bf16[16,2176]{1,0:T(8,128)(2,1)S(1)} %get-tuple-element.254.refs_4_), channel_id=1, source_target_pairs={{0,1},{1,0},{2,3},{3,2},{4,5},{5,4},{6,7},{7,6},{8,9},{9,8},{10,11... | collective-permute-start | bytes 208904 | tf_op jit(solution)/shard_map/ppermute | solution.py:906
  179.2 1.7 collective-permute-done.41.refs_7_
  181.0 1.5 collective-permute-done.40.refs_6_
  182.5 1.3 collective-permute-done.37.refs_1_
  185.3 1.4 collective-permute-start.46
  187.7 1.2 collective-permute-start.44
  189.0 4.4 %finish_expert.1 = (f32[1,512,2048]{2,1,0:T(8,128)}, f32[1,2048,512]{2,1,0:T(8,128)}) custom-call(s32[4]{0:T(128)S(1)} %add_add_fusion.1.meta_ref, bf16[4,256,512]{2,1,0:T(8,128)(2,1)S(1)} %get-tuple-element.256.im_ref, bf16[4,256,512]{2,1,0:T(8,128)(2,1)S(1)} %collective-permute-done.42.ir_ref, bf16[4,256,512]{2,1,0:T(8,128)(2,1)S(1)} %bitcast.48, ...), custom_call_target="tpu_custom_call" | custom-call | flops 1 | bytes 1 | tf_op jit(solution)/shard_map/finish_expert/pallas_call | solution.py:542
  193.4 2.4 %collective-permute-done.46.refs_3_ = bf16[64,2176]{1,0:T(8,128)(2,1)S(1)} collective-permute-done((bf16[64,2176]{1,0:T(8,128)(2,1)S(1)}, bf16[64,2176]{1,0:T(8,128)(2,1)S(1)}, u32[]{:S(2)}, u32[]{:S(2)}) %collective-permute-start.46) | collective-permute-done | bytes 278560 | tf_op jit(solution)/shard_map/ppermute | solution.py:906
  195.8 5.1 %collective-permute-done.45.refs_2_ = bf16[64,2176]{1,0:T(8,128)(2,1)S(1)} collective-permute-done((bf16[64,2176]{1,0:T(8,128)(2,1)S(1)}, bf16[64,2176]{1,0:T(8,128)(2,1)S(1)}, u32[]{:S(2)}, u32[]{:S(2)}) %collective-permute-start.45) | collective-permute-done | bytes 278560 | tf_op jit(solution)/shard_map/ppermute | solution.py:906
  201.0 2.2 %finish_shared.2 = (f32[512,1536]{1,0:T(8,128)}, f32[512,512]{1,0:T(8,128)}, f32[512,128]{1,0:T(8,128)S(1)}) custom-call(s32[4]{0:T(128)S(1)} %add_add_fusion.1.meta_ref, bf16[256,2176]{1,0:T(8,128)(2,1)S(1)} %merge.15.half_ref), custom_call_target="tpu_custom_call" | custom-call | flops 1 | bytes 1 | tf_op jit(solution)/shard_map/finish_shared/pallas_call | solution.py:716
  203.8 2.2 %finish_shared.3 = (f32[512,1536]{1,0:T(8,128)}, f32[512,512]{1,0:T(8,128)}, f32[512,128]{1,0:T(8,128)S(1)}) custom-call(s32[4]{0:T(128)S(1)} %add_add_fusion.1.meta_ref, bf16[256,2176]{1,0:T(8,128)(2,1)S(1)} %collective-permute-done.47.half_ref, f32[512,1536]{1,0:T(8,128)} %get-tuple-element.261.refs_0_, ...), custom_call_target="tpu_custom_call", output_to_operand_aliasing={{0}: (2, {}), {1}: (3, {}), {2}: (4, {})} | custom-call | flops 1 | bytes 1 | tf_op jit(solution)/shard_map/finish_shared/pallas_call | solution.py:716
  (137 shorter events, 26.9 us)
Async XLA Ops:
  2.4 6.0 %collective-permute-start.2 = (s32[6,100]{1,0:T(8,128)S(1)}, s32[6,100]{1,0:T(8,128)S(1)}, u32[]{:S(2)}, u32[]{:S(2)}) collective-permute-start(s32[6,100]{1,0:T(8,128)S(1)} %bitcast.69), channel_id=1, source_target_pairs={{0,4},{4,0},{1,5},{5,1},{2,6},{6,2},{3,7},{7,3},{8,12},{12,8},{9,1... | collective-permute-start | bytes 7208 | tf_op jit(solution)/shard_map/ppermute | solution.py:906
  2.9 31.3 %collective-permute-start.6 = (bf16[4,256,256]{2,1,0:T(8,128)(2,1)S(1)}, bf16[4,256,256]{2,1,0:T(8,128)(2,1)}, u32[]{:S(2)}, u32[]{:S(2)}) collective-permute-start(bf16[4,256,256]{2,1,0:T(8,128)(2,1)S(1)} %pack_piece.1), channel_id=1, source_target_pairs={{0,2},{1,3},{2,0},{3,1},{4,6},{5,7},{6,4},{7,5},{8,10},{9,11},{10,... | collective-permute-start | bytes 1572872 | tf_op jit(solution)/shard_map/ppermute | solution.py:906
  6.6 4.0 %collective-permute-start.1 = (bf16[6,100,512]{2,1,0:T(8,128)(2,1)}, bf16[6,100,512]{2,1,0:T(8,128)(2,1)S(1)}, u32[]{:S(2)}, u32[]{:S(2)}) collective-permute-start(bf16[6,100,512]{2,1,0:T(8,128)(2,1)} %dyown_ref.1), channel_id=1, source_target_pairs={{0,4},{4,0},{1,5},{5,1},{2,6},{6,2},{3,7},{7,3},{8,12},{12,8},{9,1... | collective-permute-start | bytes 1843208 | tf_op jit(solution)/shard_map/ppermute | solution.py:906
  6.8 27.5 %collective-permute-start.4 = (bf16[6,100,512]{2,1,0:T(8,128)(2,1)}, bf16[6,100,512]{2,1,0:T(8,128)(2,1)S(1)}, u32[]{:S(2)}, u32[]{:S(2)}) collective-permute-start(bf16[6,100,512]{2,1,0:T(8,128)(2,1)} %dyown_ref.1), channel_id=1, source_target_pairs={{0,1},{1,0},{2,3},{3,2},{4,5},{5,4},{6,7},{7,6},{8,9},{9,8},{10,11... | collective-permute-start | bytes 1843208 | tf_op jit(solution)/shard_map/ppermute | solution.py:906
  8.3 2.2 %collective-permute-start = (bf16[6,100,512]{2,1,0:T(8,128)(2,1)S(1)}, bf16[6,100,512]{2,1,0:T(8,128)(2,1)}, u32[]{:S(2)}, u32[]{:S(2)}) collective-permute-start(bf16[6,100,512]{2,1,0:T(8,128)(2,1)S(1)} %copy-done.19), channel_id=1, source_target_pairs={{0,4},{4,0},{1,5},{5,1},{2,6},{6,2},{3,7},{7,3},{8,12},{12,8},{9,1... | collective-permute-start | bytes 1843208 | tf_op jit(solution)/shard_map/ppermute | solution.py:906
  21.9 25.5 %collective-permute-start.3 = (bf16[624,512]{1,0:T(8,128)(2,1)S(1)}, bf16[624,512]{1,0:T(8,128)(2,1)S(1)}, u32[]{:S(2)}, u32[]{:S(2)}) collective-permute-start(bf16[624,512]{1,0:T(8,128)(2,1)S(1)} %pad_maximum_fusion.1), channel_id=1, source_target_pairs={{0,1},{1,0},{2,3},{3,2},{4,5},{5,4},{6,7},{7,6},{8,9},{9,8},{10,11... | collective-permute-start | bytes 1916936 | tf_op jit(solution)/shard_map/ppermute | solution.py:906
  34.2 3.5 %collective-permute-start.5 = (bf16[6,100,512]{2,1,0:T(8,128)(2,1)S(1)}, bf16[6,100,512]{2,1,0:T(8,128)(2,1)S(1)}, u32[]{:S(2)}, u32[]{:S(2)}) collective-permute-start(bf16[6,100,512]{2,1,0:T(8,128)(2,1)S(1)} %collective-permute-done.4.own_ref), channel_id=1, source_target_pairs={{0,4},{4,0},{1,5},{5,1},{2,6},{6,2},{3,7},{7,3},{8,12},{12,8},{9,1... | collective-permute-start | bytes 1843208 | tf_op jit(solution)/shard_map/ppermute | solution.py:906
  34.2 23.4 %collective-permute-start.9 = (bf16[4,256,256]{2,1,0:T(8,128)(2,1)}, bf16[4,256,256]{2,1,0:T(8,128)(2,1)S(1)}, u32[]{:S(2)}, u32[]{:S(2)}) collective-permute-start(bf16[4,256,256]{2,1,0:T(8,128)(2,1)} %collective-permute-done.6), channel_id=1, source_target_pairs={{0,24},{8,16},{16,8},{24,0},{1,25},{9,17},{17,9},{25,1},{2,26},{10... | collective-permute-start | bytes 1572872 | tf_op jit(solution)/shard_map/ppermute | solution.py:906
  36.7 24.2 %collective-permute-start.8 = (bf16[4,256,256]{2,1,0:T(8,128)(2,1)}, bf16[4,256,256]{2,1,0:T(8,128)(2,1)S(1)}, u32[]{:S(2)}, u32[]{:S(2)}) collective-permute-start(bf16[4,256,256]{2,1,0:T(8,128)(2,1)} %collective-permute-done.6), channel_id=1, source_target_pairs={{0,16},{8,24},{16,0},{24,8},{1,17},{9,25},{17,1},{25,9},{2,18},{10... | collective-permute-start | bytes 1572872 | tf_op jit(solution)/shard_map/ppermute | solution.py:906
  37.3 23.8 %collective-permute-start.7 = (bf16[4,256,256]{2,1,0:T(8,128)(2,1)}, bf16[4,256,256]{2,1,0:T(8,128)(2,1)S(1)}, u32[]{:S(2)}, u32[]{:S(2)}) collective-permute-start(bf16[4,256,256]{2,1,0:T(8,128)(2,1)} %collective-permute-done.6), channel_id=1, source_target_pairs={{0,8},{8,0},{16,24},{24,16},{1,9},{9,1},{17,25},{25,17},{2,10},{10... | collective-permute-start | bytes 1572872 | tf_op jit(solution)/shard_map/ppermute | solution.py:906
  62.4 9.9 %collective-permute-start.10 = (bf16[4,4,256,256]{3,2,1,0:T(8,128)(2,1)S(1)}, bf16[4,4,256,256]{3,2,1,0:T(8,128)(2,1)}, u32[]{:S(2)}, u32[]{:S(2)}) collective-permute-start(bf16[4,4,256,256]{3,2,1,0:T(8,128)(2,1)S(1)} %pad_maximum_fusion.wi_ref), channel_id=1, source_target_pairs={{0,4},{4,0},{1,5},{5,1},{2,6},{6,2},{3,7},{7,3},{8,12},{12,8},{9,1... | collective-permute-start | bytes 6291464 | tf_op jit(solution)/shard_map/ppermute | solution.py:906
  71.7 11.1 %collective-permute-start.11 = (bf16[4,256,512]{2,1,0:T(8,128)(2,1)}, bf16[4,256,512]{2,1,0:T(8,128)(2,1)}, u32[]{:S(2)}, u32[]{:S(2)}) collective-permute-start(bf16[4,256,512]{2,1,0:T(8,128)(2,1)} %get-tuple-element.163), channel_id=1, source_target_pairs={{0,4},{4,0},{1,5},{5,1},{2,6},{6,2},{3,7},{7,3},{8,12},{12,8},{9,1... | collective-permute-start | bytes 3145736 | tf_op jit(solution)/shard_map/ppermute | solution.py:906
  72.2 10.6 %collective-permute-start.12 = (bf16[4,256,512]{2,1,0:T(8,128)(2,1)}, bf16[4,256,512]{2,1,0:T(8,128)(2,1)}, u32[]{:S(2)}, u32[]{:S(2)}) collective-permute-start(bf16[4,256,512]{2,1,0:T(8,128)(2,1)} %get-tuple-element.165), channel_id=1, source_target_pairs={{0,4},{4,0},{1,5},{5,1},{2,6},{6,2},{3,7},{7,3},{8,12},{12,8},{9,1... | collective-permute-start | bytes 3145736 | tf_op jit(solution)/shard_map/ppermute | solution.py:906
  81.9 22.1 %collective-permute-start.13 = (bf16[640,512]{1,0:T(8,128)(2,1)S(1)}, bf16[640,512]{1,0:T(8,128)(2,1)S(1)}, u32[]{:S(2)}, u32[]{:S(2)}) collective-permute-start(bf16[640,512]{1,0:T(8,128)(2,1)S(1)} %get-tuple-element.171), channel_id=1, source_target_pairs={{0,1},{1,0},{2,3},{3,2},{4,5},{5,4},{6,7},{7,6},{8,9},{9,8},{10,11... | collective-permute-start | bytes 1966088 | tf_op jit(solution)/shard_map/ppermute | solution.py:906
  85.2 18.8 %collective-permute-start.14 = (bf16[2,256,512]{2,1,0:T(8,128)(2,1)S(1)}, bf16[2,256,512]{2,1,0:T(8,128)(2,1)S(1)}, u32[]{:S(2)}, u32[]{:S(2)}) collective-permute-start(bf16[2,256,512]{2,1,0:T(8,128)(2,1)S(1)} %get-tuple-element.172), channel_id=1, source_target_pairs={{0,16},{8,24},{16,0},{24,8},{1,17},{9,25},{17,1},{25,9},{2,18},{10... | collective-permute-start | bytes 1572872 | tf_op jit(solution)/shard_map/ppermute | solution.py:906
  86.6 17.4 %collective-permute-start.15 = (bf16[2,1,256,512]{3,2,0,1:T(8,128)(2,1)S(1)}, bf16[2,1,256,512]{3,2,0,1:T(8,128)(2,1)S(1)}, u32[]{:S(2)}, u32[]{:S(2)}) collective-permute-start(bf16[2,1,256,512]{3,2,0,1:T(8,128)(2,1)S(1)} %bitcast.62), channel_id=1, source_target_pairs={{0,8},{8,0},{16,24},{24,16},{1,9},{9,1},{17,25},{25,17},{2,10},{10... | collective-permute-start | bytes 1572872 | tf_op jit(solution)/shard_map/ppermute | solution.py:906
  103.9 2.7 %collective-permute-start.17 = (bf16[4,256,512]{2,1,0:T(8,128)(2,1)S(1)}, bf16[4,256,512]{2,1,0:T(8,128)(2,1)S(1)}, u32[]{:S(2)}, u32[]{:S(2)}) collective-permute-start(bf16[4,256,512]{2,1,0:T(8,128)(2,1)S(1)} %get-tuple-element.189), channel_id=1, source_target_pairs={{0,4},{4,0},{1,5},{5,1},{2,6},{6,2},{3,7},{7,3},{8,12},{12,8},{9,1... | collective-permute-start | bytes 3145736 | tf_op jit(solution)/shard_map/ppermute | solution.py:906
  104.0 4.1 %collective-permute-start.16 = (bf16[4,256,512]{2,1,0:T(8,128)(2,1)S(1)}, bf16[4,256,512]{2,1,0:T(8,128)(2,1)S(1)}, u32[]{:S(2)}, u32[]{:S(2)}) collective-permute-start(bf16[4,256,512]{2,1,0:T(8,128)(2,1)S(1)} %get-tuple-element.187), channel_id=1, source_target_pairs={{0,4},{4,0},{1,5},{5,1},{2,6},{6,2},{3,7},{7,3},{8,12},{12,8},{9,1... | collective-permute-start | bytes 3145736 | tf_op jit(solution)/shard_map/ppermute | solution.py:906
  104.6 19.6 %collective-permute-start.20 = (bf16[600,512]{1,0:T(8,128)(2,1)S(1)}, bf16[600,512]{1,0:T(8,128)(2,1)S(1)}, u32[]{:S(2)}, u32[]{:S(2)}) collective-permute-start(bf16[600,512]{1,0:T(8,128)(2,1)S(1)} %get-tuple-element.200), channel_id=1, source_target_pairs={{0,1},{1,0},{2,3},{3,2},{4,5},{5,4},{6,7},{7,6},{8,9},{9,8},{10,11... | collective-permute-start | bytes 1843208 | tf_op jit(solution)/shard_map/ppermute | solution.py:906
  108.7 14.5 %collective-permute-start.19 = (bf16[2,1,256,512]{3,2,0,1:T(8,128)(2,1)S(1)}, bf16[2,1,256,512]{3,2,0,1:T(8,128)(2,1)S(1)}, u32[]{:S(2)}, u32[]{:S(2)}) collective-permute-start(bf16[2,1,256,512]{3,2,0,1:T(8,128)(2,1)S(1)} %bitcast.63), channel_id=1, source_target_pairs={{0,8},{8,0},{16,24},{24,16},{1,9},{9,1},{17,25},{25,17},{2,10},{10... | collective-permute-start | bytes 1572872 | tf_op jit(solution)/shard_map/ppermute | solution.py:906
  110.0 13.7 %collective-permute-start.18 = (bf16[2,256,512]{2,1,0:T(8,128)(2,1)S(1)}, bf16[2,256,512]{2,1,0:T(8,128)(2,1)S(1)}, u32[]{:S(2)}, u32[]{:S(2)}) collective-permute-start(bf16[2,256,512]{2,1,0:T(8,128)(2,1)S(1)} %get-tuple-element.191), channel_id=1, source_target_pairs={{0,16},{8,24},{16,0},{24,8},{1,17},{9,25},{17,1},{25,9},{2,18},{10... | collective-permute-start | bytes 1572872 | tf_op jit(solution)/shard_map/ppermute | solution.py:906
  124.2 11.6 %collective-permute-start.24 = (bf16[256,2176]{1,0:T(8,128)(2,1)S(1)}, bf16[256,2176]{1,0:T(8,128)(2,1)S(1)}, u32[]{:S(2)}, u32[]{:S(2)}) collective-permute-start(bf16[256,2176]{1,0:T(8,128)(2,1)S(1)} %get-tuple-element.217), channel_id=1, source_target_pairs={{0,4},{4,0},{1,5},{5,1},{2,6},{6,2},{3,7},{7,3},{8,12},{12,8},{9,1... | collective-permute-start | bytes 3342344 | tf_op jit(solution)/shard_map/ppermute | solution.py:906
  124.3 12.0 %collective-permute-start.25 = (bf16[3,100,512]{2,1,0:T(8,128)(2,1)S(1)}, bf16[3,100,512]{2,1,0:T(8,128)(2,1)S(1)}, u32[]{:S(2)}, u32[]{:S(2)}) collective-permute-start(bf16[3,100,512]{2,1,0:T(8,128)(2,1)S(1)} %get-tuple-element.223), channel_id=1, source_target_pairs={{0,4},{4,0},{1,5},{5,1},{2,6},{6,2},{3,7},{7,3},{8,12},{12,8},{9,1... | collective-permute-start | bytes 921608 | tf_op jit(solution)/shard_map/ppermute | solution.py:906
  125.9 10.4 %collective-permute-start.26 = (bf16[3,100,512]{2,1,0:T(8,128)(2,1)S(1)}, bf16[3,100,512]{2,1,0:T(8,128)(2,1)S(1)}, u32[]{:S(2)}, u32[]{:S(2)}) collective-permute-start(bf16[3,100,512]{2,1,0:T(8,128)(2,1)S(1)} %get-tuple-element.226), channel_id=1, source_target_pairs={{0,4},{4,0},{1,5},{5,1},{2,6},{6,2},{3,7},{7,3},{8,12},{12,8},{9,1... | collective-permute-start | bytes 921608 | tf_op jit(solution)/shard_map/ppermute | solution.py:906
  126.1 8.7 %collective-permute-start.23 = (bf16[1,256,512]{2,1,0:T(8,128)(2,1)S(1)}, bf16[1,256,512]{2,1,0:T(8,128)(2,1)S(1)}, u32[]{:S(2)}, u32[]{:S(2)}) collective-permute-start(bf16[1,256,512]{2,1,0:T(8,128)(2,1)S(1)} %get-tuple-element.291), channel_id=1, source_target_pairs={{0,16},{8,24},{16,0},{24,8},{1,17},{9,25},{17,1},{25,9},{2,18},{10... | collective-permute-start | bytes 786440 | tf_op jit(solution)/shard_map/ppermute | solution.py:906
  127.1 8.7 %collective-permute-start.22 = (bf16[1,256,512]{2,1,0:T(8,128)(2,1)S(1)}, bf16[1,256,512]{2,1,0:T(8,128)(2,1)S(1)}, u32[]{:S(2)}, u32[]{:S(2)}) collective-permute-start(bf16[1,256,512]{2,1,0:T(8,128)(2,1)S(1)} %get-tuple-element.292), channel_id=1, source_target_pairs={{0,8},{8,0},{16,24},{24,16},{1,9},{9,1},{17,25},{25,17},{2,10},{10... | collective-permute-start | bytes 786440 | tf_op jit(solution)/shard_map/ppermute | solution.py:906
  134.8 9.2 %collective-permute-start.28 = (bf16[1,256,512]{2,1,0:T(8,128)(2,1)S(1)}, bf16[1,256,512]{2,1,0:T(8,128)(2,1)S(1)}, u32[]{:S(2)}, u32[]{:S(2)}) collective-permute-start(bf16[1,256,512]{2,1,0:T(8,128)(2,1)S(1)} %get-tuple-element.289), channel_id=1, source_target_pairs={{0,16},{8,24},{16,0},{24,8},{1,17},{9,25},{17,1},{25,9},{2,18},{10... | collective-permute-start | bytes 786440 | tf_op jit(solution)/shard_map/ppermute | solution.py:906
  136.3 25.4 %collective-permute-start.27 = (bf16[2,1,256,512]{3,2,1,0:T(8,128)(2,1)S(1)}, bf16[2,1,256,512]{3,2,1,0:T(8,128)(2,1)S(1)}, u32[]{:S(2)}, u32[]{:S(2)}) collective-permute-start(bf16[2,1,256,512]{3,2,1,0:T(8,128)(2,1)S(1)} %get-tuple-element.227), channel_id=1, source_target_pairs={{0,2},{1,3},{2,0},{3,1},{4,6},{5,7},{6,4},{7,5},{8,10},{9,11},{10,... | collective-permute-start | bytes 1572872 | tf_op jit(solution)/shard_map/ppermute | solution.py:906
  138.7 19.3 %collective-permute-start.29 = (bf16[64,2176]{1,0:T(8,128)(2,1)S(1)}, bf16[64,2176]{1,0:T(8,128)(2,1)S(1)}, u32[]{:S(2)}, u32[]{:S(2)}) collective-permute-start(bf16[64,2176]{1,0:T(8,128)(2,1)S(1)} %get-tuple-element.229), channel_id=1, source_target_pairs={{0,8},{8,0},{16,24},{24,16},{1,9},{9,1},{17,25},{25,17},{2,10},{10... | collective-permute-start | bytes 835592 | tf_op jit(solution)/shard_map/ppermute | solution.py:906
  139.8 18.1 %collective-permute-start.30 = (bf16[64,2176]{1,0:T(8,128)(2,1)S(1)}, bf16[64,2176]{1,0:T(8,128)(2,1)S(1)}, u32[]{:S(2)}, u32[]{:S(2)}) collective-permute-start(bf16[64,2176]{1,0:T(8,128)(2,1)S(1)} %get-tuple-element.230), channel_id=1, source_target_pairs={{0,16},{8,24},{16,0},{24,8},{1,17},{9,25},{17,1},{25,9},{2,18},{10... | collective-permute-start | bytes 835592 | tf_op jit(solution)/shard_map/ppermute | solution.py:906
  140.8 17.2 %collective-permute-start.31 = (bf16[64,2176]{1,0:T(8,128)(2,1)S(1)}, bf16[64,2176]{1,0:T(8,128)(2,1)S(1)}, u32[]{:S(2)}, u32[]{:S(2)}) collective-permute-start(bf16[64,2176]{1,0:T(8,128)(2,1)S(1)} %get-tuple-element.231), channel_id=1, source_target_pairs={{0,24},{8,16},{16,8},{24,0},{1,25},{9,17},{17,9},{25,1},{2,26},{10... | collective-permute-start | bytes 835592 | tf_op jit(solution)/shard_map/ppermute | solution.py:906
  144.1 13.9 %collective-permute-start.21 = (bf16[1,256,512]{2,1,0:T(8,128)(2,1)S(1)}, bf16[1,256,512]{2,1,0:T(8,128)(2,1)S(1)}, u32[]{:S(2)}, u32[]{:S(2)}) collective-permute-start(bf16[1,256,512]{2,1,0:T(8,128)(2,1)S(1)} %get-tuple-element.290), channel_id=1, source_target_pairs={{0,8},{8,0},{16,24},{24,16},{1,9},{9,1},{17,25},{25,17},{2,10},{10... | collective-permute-start | bytes 786440 | tf_op jit(solution)/shard_map/ppermute | solution.py:906
  162.1 10.6 %collective-permute-start.33 = (bf16[1,1,256,512]{3,2,1,0:T(8,128)(2,1)S(1)}, bf16[1,1,256,512]{3,2,1,0:T(8,128)(2,1)S(1)}, u32[]{:S(2)}, u32[]{:S(2)}) collective-permute-start(bf16[1,1,256,512]{3,2,1,0:T(8,128)(2,1)S(1)} %bitcast.56), channel_id=1, source_target_pairs={{0,16},{8,24},{16,0},{24,8},{1,17},{9,25},{17,1},{25,9},{2,18},{10... | collective-permute-start | bytes 786440 | tf_op jit(solution)/shard_map/ppermute | solution.py:906
  163.3 9.4 %collective-permute-start.32 = (bf16[1,256,512]{2,1,0:T(8,128)(2,1)S(1)}, bf16[1,256,512]{2,1,0:T(8,128)(2,1)S(1)}, u32[]{:S(2)}, u32[]{:S(2)}) collective-permute-start(bf16[1,256,512]{2,1,0:T(8,128)(2,1)S(1)} %get-tuple-element.246.refs_0_), channel_id=1, source_target_pairs={{0,8},{8,0},{16,24},{24,16},{1,9},{9,1},{17,25},{25,17},{2,10},{10... | collective-permute-start | bytes 786440 | tf_op jit(solution)/shard_map/ppermute | solution.py:906
  164.3 4.4 %collective-permute-start.34 = (bf16[16,2176]{1,0:T(8,128)(2,1)S(1)}, bf16[16,2176]{1,0:T(8,128)(2,1)S(1)}, u32[]{:S(2)}, u32[]{:S(2)}) collective-permute-start(bf16[16,2176]{1,0:T(8,128)(2,1)S(1)} %get-tuple-element.249), channel_id=1, source_target_pairs={{0,1},{1,0},{2,3},{3,2},{4,5},{5,4},{6,7},{7,6},{8,9},{9,8},{10,11... | collective-permute-start | bytes 208904 | tf_op jit(solution)/shard_map/ppermute | solution.py:906
  164.3 6.9 %collective-permute-start.35 = (bf16[16,2176]{1,0:T(8,128)(2,1)S(1)}, bf16[16,2176]{1,0:T(8,128)(2,1)S(1)}, u32[]{:S(2)}, u32[]{:S(2)}) collective-permute-start(bf16[16,2176]{1,0:T(8,128)(2,1)S(1)} %get-tuple-element.250), channel_id=1, source_target_pairs={{0,2},{1,3},{2,0},{3,1},{4,6},{5,7},{6,4},{7,5},{8,10},{9,11},{10,... | collective-permute-start | bytes 208904 | tf_op jit(solution)/shard_map/ppermute | solution.py:906
  166.5 6.1 %collective-permute-start.36 = (bf16[16,2176]{1,0:T(8,128)(2,1)S(1)}, bf16[16,2176]{1,0:T(8,128)(2,1)S(1)}, u32[]{:S(2)}, u32[]{:S(2)}) collective-permute-start(bf16[16,2176]{1,0:T(8,128)(2,1)S(1)} %get-tuple-element.251), channel_id=1, source_target_pairs={{0,3},{1,2},{2,1},{3,0},{4,7},{5,6},{6,5},{7,4},{8,11},{9,10},{10,... | collective-permute-start | bytes 208904 | tf_op jit(solution)/shard_map/ppermute | solution.py:906
  172.8 10.9 %collective-permute-start.37 = (bf16[2,256,512]{2,1,0:T(8,128)(2,1)S(1)}, bf16[2,256,512]{2,1,0:T(8,128)(2,1)S(1)}, u32[]{:S(2)}, u32[]{:S(2)}) collective-permute-start(bf16[2,256,512]{2,1,0:T(8,128)(2,1)S(1)} %get-tuple-element.252.refs_0_), channel_id=1, source_target_pairs={{0,16},{8,24},{16,0},{24,8},{1,17},{9,25},{17,1},{25,9},{2,18},{10... | collective-permute-start | bytes 1572872 | tf_op jit(solution)/shard_map/ppermute | solution.py:906
  174.0 10.5 %collective-permute-start.38 = (bf16[2,1,256,512]{3,2,1,0:T(8,128)(2,1)S(1)}, bf16[2,1,256,512]{3,2,1,0:T(8,128)(2,1)S(1)}, u32[]{:S(2)}, u32[]{:S(2)}) collective-permute-start(bf16[2,1,256,512]{3,2,1,0:T(8,128)(2,1)S(1)} %get-tuple-element.253.refs_2_), channel_id=1, source_target_pairs={{0,8},{8,0},{16,24},{24,16},{1,9},{9,1},{17,25},{25,17},{2,10},{10... | collective-permute-start | bytes 1572872 | tf_op jit(solution)/shard_map/ppermute | solution.py:906
  174.9 6.1 %collective-permute-start.41 = (bf16[16,2176]{1,0:T(8,128)(2,1)S(1)}, bf16[16,2176]{1,0:T(8,128)(2,1)S(1)}, u32[]{:S(2)}, u32[]{:S(2)}) collective-permute-start(bf16[16,2176]{1,0:T(8,128)(2,1)S(1)} %get-tuple-element.254.refs_4_), channel_id=1, source_target_pairs={{0,3},{1,2},{2,1},{3,0},{4,7},{5,6},{6,5},{7,4},{8,11},{9,10},{10,... | collective-permute-start | bytes 208904 | tf_op jit(solution)/shard_map/ppermute | solution.py:906
  177.0 5.5 %collective-permute-start.40 = (bf16[16,2176]{1,0:T(8,128)(2,1)S(1)}, bf16[16,2176]{1,0:T(8,128)(2,1)S(1)}, u32[]{:S(2)}, u32[]{:S(2)}) collective-permute-start(bf16[16,2176]{1,0:T(8,128)(2,1)S(1)} %get-tuple-element.254.refs_4_), channel_id=1, source_target_pairs={{0,2},{1,3},{2,0},{3,1},{4,6},{5,7},{6,4},{7,5},{8,10},{9,11},{10,... | collective-permute-start | bytes 208904 | tf_op jit(solution)/shard_map/ppermute | solution.py:906
  177.0 5.5 %collective-permute-start.39 = (bf16[16,2176]{1,0:T(8,128)(2,1)S(1)}, bf16[16,2176]{1,0:T(8,128)(2,1)S(1)}, u32[]{:S(2)}, u32[]{:S(2)}) collective-permute-start(bf16[16,2176]{1,0:T(8,128)(2,1)S(1)} %get-tuple-element.254.refs_4_), channel_id=1, source_target_pairs={{0,1},{1,0},{2,3},{3,2},{4,5},{5,4},{6,7},{7,6},{8,9},{9,8},{10,11... | collective-permute-start | bytes 208904 | tf_op jit(solution)/shard_map/ppermute | solution.py:906
  184.7 4.1 %collective-permute-start.43 = (bf16[4,256,512]{2,1,0:T(8,128)(2,1)S(1)}, bf16[4,256,512]{2,1,0:T(8,128)(2,1)S(1)}, u32[]{:S(2)}, u32[]{:S(2)}) collective-permute-start(bf16[4,256,512]{2,1,0:T(8,128)(2,1)S(1)} %bitcast.47), channel_id=1, source_target_pairs={{0,4},{4,0},{1,5},{5,1},{2,6},{6,2},{3,7},{7,3},{8,12},{12,8},{9,1... | collective-permute-start | bytes 3145736 | tf_op jit(solution)/shard_map/ppermute | solution.py:906
  184.8 4.1 %collective-permute-start.42 = (bf16[4,256,512]{2,1,0:T(8,128)(2,1)S(1)}, bf16[4,256,512]{2,1,0:T(8,128)(2,1)S(1)}, u32[]{:S(2)}, u32[]{:S(2)}) collective-permute-start(bf16[4,256,512]{2,1,0:T(8,128)(2,1)S(1)} %get-tuple-element.256.im_ref), channel_id=1, source_target_pairs={{0,4},{4,0},{1,5},{5,1},{2,6},{6,2},{3,7},{7,3},{8,12},{12,8},{9,1... | collective-permute-start | bytes 3145736 | tf_op jit(solution)/shard_map/ppermute | solution.py:906
  185.3 10.5 %collective-permute-start.46 = (bf16[64,2176]{1,0:T(8,128)(2,1)S(1)}, bf16[64,2176]{1,0:T(8,128)(2,1)S(1)}, u32[]{:S(2)}, u32[]{:S(2)}) collective-permute-start(bf16[64,2176]{1,0:T(8,128)(2,1)S(1)} %get-tuple-element.260.refs_0_), channel_id=1, source_target_pairs={{0,24},{8,16},{16,8},{24,0},{1,25},{9,17},{17,9},{25,1},{2,26},{10... | collective-permute-start | bytes 835592 | tf_op jit(solution)/shard_map/ppermute | solution.py:906
  186.7 14.1 %collective-permute-start.45 = (bf16[64,2176]{1,0:T(8,128)(2,1)S(1)}, bf16[64,2176]{1,0:T(8,128)(2,1)S(1)}, u32[]{:S(2)}, u32[]{:S(2)}) collective-permute-start(bf16[64,2176]{1,0:T(8,128)(2,1)S(1)} %get-tuple-element.260.refs_0_), channel_id=1, source_target_pairs={{0,16},{8,24},{16,0},{24,8},{1,17},{9,25},{17,1},{25,9},{2,18},{10... | collective-permute-start | bytes 835592 | tf_op jit(solution)/shard_map/ppermute | solution.py:906
  187.7 13.2 %collective-permute-start.44 = (bf16[64,2176]{1,0:T(8,128)(2,1)S(1)}, bf16[64,2176]{1,0:T(8,128)(2,1)S(1)}, u32[]{:S(2)}, u32[]{:S(2)}) collective-permute-start(bf16[64,2176]{1,0:T(8,128)(2,1)S(1)} %get-tuple-element.260.refs_0_), channel_id=1, source_target_pairs={{0,8},{8,0},{16,24},{24,16},{1,9},{9,1},{17,25},{25,17},{2,10},{10... | collective-permute-start | bytes 835592 | tf_op jit(solution)/shard_map/ppermute | solution.py:906
  201.0 2.8 %collective-permute-start.47 = (bf16[256,2176]{1,0:T(8,128)(2,1)S(1)}, bf16[256,2176]{1,0:T(8,128)(2,1)S(1)}, u32[]{:S(2)}, u32[]{:S(2)}) collective-permute-start(bf16[256,2176]{1,0:T(8,128)(2,1)S(1)} %merge.15.half_ref), channel_id=1, source_target_pairs={{0,4},{4,0},{1,5},{5,1},{2,6},{6,2},{3,7},{7,3},{8,12},{12,8},{9,1... | collective-permute-start | bytes 3342344 | tf_op jit(solution)/shard_map/ppermute | solution.py:906
  (23 other events, 198.7 us)
